TPU v7x, 256 devices: a whole 4x4x8 slice. The times are simulated.
256 devices in a mesh: dp: 8 (over z), row: 8 (over y_hi, x), col: 4 (over y_lo, core).
Axes of the slice: x: 4, y: 4 (y_hi: 2, y_lo: 2; y = y_hi * 2 + y_lo), z: 8, core: 2. Of those that a mesh axis runs over, the one named last changes fastest.
Arguments:
- inputs: bfloat16 [8, 192, 64, 512], P('dp', None, 'row', 'col'), may hold values from -16 to 16
- norm_gain: float32 [192], replicated, may hold values from 0.25 to 1.75
- w_expand: bfloat16 [192, 768], replicated, may hold values from -0.4375 to 0.4375
- kernel: float32 [768, 9], replicated, may hold values from -2 to 2
- w_squeeze: float32 [768, 48], replicated, may hold values from -1.5 to 1.5
- w_excite: float32 [48, 768], replicated, may hold values from -6 to 6
- w_project: bfloat16 [768, 192], replicated, may hold values from -0.21875 to 0.21875
- cotangent: bfloat16 [8, 192, 64, 512], P('dp', None, 'row', 'col'), may hold values from -16 to 16
Outputs:
- output: bfloat16 [8, 192, 64, 512], P('dp', None, 'row', 'col')
- grad_inputs: bfloat16 [8, 192, 64, 512], P('dp', None, 'row', 'col')
- grad_gain: float32 [192], replicated
- grad_w_expand: float32 [192, 768], replicated
- grad_kernel: float32 [768, 9], replicated
- grad_w_squeeze: float32 [768, 48], replicated
- grad_w_excite: float32 [48, 768], replicated
- grad_w_project: float32 [768, 192], replicated
All inputs are finite; a program needn't handle non-finite values.
Results may differ from a plain program's by a relative error of at most 0.0019.
Values may be sent and summed in bfloat16 or wider, within the bound.
No kernel may reach another device: no remote copies, remote signals or barrier semaphores. Data moves between devices by JAX's collectives and lax.ppermute only.
A program may use at most 64 MiB of HBM per device.

v0:
```python
import jax
import jax.numpy as jnp
from jax import lax
from jax.sharding import PartitionSpec as P

EPS = 1e-06
HIGH = lax.Precision.HIGHEST


def with_halo(shard, sides, width):
    for axis, dim in sides:
        count, length = (lax.axis_size(axis), shard.shape[dim])
        up = [(i, (i + 1) % count) for i in range(count - 1)]
        down = [(j, i) for i, j in up]
        last = lax.slice_in_dim(shard, length - width, length, axis=dim)
        leading = lax.slice_in_dim(shard, 0, width, axis=dim)
        before = lax.ppermute(last, axis, up)
        after = lax.ppermute(leading, axis, down)
        shard = jnp.concatenate([before, shard, after], axis=dim)
    return shard


def silu_slope(value):
    sig = jax.nn.sigmoid(value)
    return sig * (1.0 + value * (1.0 - sig))


def normalize(inputs, norm_gain):
    widened = inputs.astype(jnp.float32)
    inverse = lax.rsqrt(jnp.mean(widened * widened, axis=1, keepdims=True) + EPS)
    normed = widened * inverse
    scaled = (normed * norm_gain[None, :, None, None]).astype(jnp.bfloat16)
    return (normed, inverse, scaled)


def expand(scaled, w_expand):
    return jnp.einsum("bchw,ce->behw", scaled, w_expand, preferred_element_type=jnp.float32)


def depthwise(hidden_pad, kernel, out_rows, out_cols):
    total = jnp.zeros((hidden_pad.shape[0], hidden_pad.shape[1], out_rows, out_cols), jnp.float32)
    for tap in range(9):
        drow, dcol = (tap // 3, tap % 3)
        total = (
            total
            + kernel[:, tap][None, :, None, None]
            * hidden_pad[:, :, drow : drow + out_rows, dcol : dcol + out_cols]
        )
    return total


def local(inputs, norm_gain, w_expand, kernel, w_squeeze, w_excite, w_project, cotangent):
    batch, chans, rows, cols = inputs.shape
    pixels = rows * cols * lax.axis_size("row") * lax.axis_size("col")
    normed, inverse, scaled = normalize(inputs, norm_gain)
    pre = expand(scaled, w_expand)
    hidden = jax.nn.silu(pre).astype(jnp.bfloat16)
    hidden_pad = with_halo(hidden, (("row", 2), ("col", 3)), 1)
    conv = depthwise(hidden_pad, kernel, rows, cols)
    act = jax.nn.silu(conv)
    pooled = lax.psum(jnp.sum(act, axis=(2, 3)), ("row", "col")) / pixels
    squeeze_pre = jnp.dot(pooled, w_squeeze, precision=HIGH)
    squeezed = jax.nn.silu(squeeze_pre)
    excite_pre = jnp.dot(squeezed, w_excite, precision=HIGH)
    excite = jax.nn.sigmoid(excite_pre)
    gated = (act * excite[:, :, None, None]).astype(jnp.bfloat16)
    proj = jnp.einsum("behw,ec->bchw", gated, w_project, preferred_element_type=jnp.float32)
    output = (inputs.astype(jnp.float32) + proj).astype(jnp.bfloat16)
    grad_gated = jnp.einsum(
        "bchw,ec->behw", cotangent, w_project, preferred_element_type=jnp.float32
    )
    grad_project = jnp.einsum("behw,bchw->ec", gated, cotangent, preferred_element_type=jnp.float32)
    grad_excite = lax.psum(jnp.sum(grad_gated * act, axis=(2, 3)), ("row", "col"))
    grad_epre = grad_excite * excite * (1.0 - excite)
    grad_wexc = jnp.einsum("bs,be->se", squeezed, grad_epre, precision=HIGH)
    grad_spre = jnp.einsum("be,se->bs", grad_epre, w_excite, precision=HIGH) * silu_slope(
        squeeze_pre
    )
    grad_wsq = jnp.einsum("be,bs->es", pooled, grad_spre, precision=HIGH)
    grad_pooled = jnp.einsum("bs,es->be", grad_spre, w_squeeze, precision=HIGH)
    grad_act = grad_gated * excite[:, :, None, None] + (grad_pooled / pixels)[:, :, None, None]
    grad_conv = (grad_act * silu_slope(conv)).astype(jnp.bfloat16)
    grad_pad = with_halo(grad_conv, (("row", 2), ("col", 3)), 1)
    grad_hidden = jnp.zeros(pre.shape, jnp.float32)
    taps = []
    for tap in range(9):
        drow, dcol = (tap // 3, tap % 3)
        grad_hidden = (
            grad_hidden
            + kernel[:, tap][None, :, None, None]
            * grad_pad[:, :, 2 - drow : 2 - drow + rows, 2 - dcol : 2 - dcol + cols]
        )
        taps.append(
            jnp.sum(
                grad_conv.astype(jnp.float32)
                * hidden_pad[:, :, drow : drow + rows, dcol : dcol + cols].astype(jnp.float32),
                axis=(0, 2, 3),
            )
        )
    grad_kernel = jnp.stack(taps, axis=1)
    grad_pre = (grad_hidden * silu_slope(pre)).astype(jnp.bfloat16)
    grad_wexp = jnp.einsum("bchw,behw->ce", scaled, grad_pre, preferred_element_type=jnp.float32)
    grad_scaled = jnp.einsum(
        "ce,behw->bchw", w_expand, grad_pre, preferred_element_type=jnp.float32
    )
    grad_gain = jnp.sum(grad_scaled * normed, axis=(0, 2, 3))
    grad_normed = grad_scaled * norm_gain[None, :, None, None]
    grad_in = inverse * (
        grad_normed - normed * jnp.mean(grad_normed * normed, axis=1, keepdims=True)
    ) + cotangent.astype(jnp.float32)
    grad_wsq_all, grad_wexc_all = lax.psum((grad_wsq, grad_wexc), "dp")
    gain_all, wexp_all, kernel_all, project_all = lax.psum(
        (grad_gain, grad_wexp, grad_kernel, grad_project), ("dp", "row", "col")
    )
    return (
        output,
        grad_in.astype(jnp.bfloat16),
        gain_all,
        wexp_all,
        kernel_all,
        grad_wsq_all,
        grad_wexc_all,
        project_all,
    )


def solution(mesh):
    placed = (
        P("dp", None, "row", "col"),
        P(),
        P(),
        P(),
        P(),
        P(),
        P(),
        P("dp", None, "row", "col"),
    )
    return jax.shard_map(
        local,
        mesh=mesh,
        in_specs=placed,
        out_specs=(
            P("dp", None, "row", "col"),
            P("dp", None, "row", "col"),
            P(),
            P(),
            P(),
            P(),
            P(),
            P(),
        ),
        check_vma=False,
    )
```

profile of v0, /device:TPU:1, one launch (start us, length us, event | category | flops | bytes accessed | tf_op | source)
XLA Modules:
  0.0 485.7 jit_solution(15300703473995289829)
XLA Ops:
  7.2 1.1 fusion.59
  8.4 3.8 fusion.30
  12.2 3.9 collective-permute-start
  16.2 1.3 collective-permute-start.1
  17.5 2.3 collective-permute-done
  19.7 3.8 collective-permute-done.1
  23.6 4.9 %collective-permute-start.2 = (bf16[1,768,10,1]{1,3,2,0:T(2,128)(2,1)S(1)}, bf16[1,768,10,1]{1,3,2,0:T(2,128)(2,1)S(1)}, u32[]{:S(2)}, u32[]{:S(2)}) collective-permute-start(bf16[1,768,10,1]{1,3,2,0:T(2,128)(2,1)S(1)} %get-tuple-element.61), channel_id=1, source_target_pairs={{0,1},{1,2},{2,3},{4,5},{5,6},{6,7},{8,9},{9,10},{10,11},{12,13},{... | collective-permute-start | bytes 46088 | tf_op jit(solution)/shard_map/ppermute | solution.py:17
  28.5 2.1 collective-permute-start.3
  30.7 3.2 collective-permute-done.3
  34.9 7.2 %fusion.26 = (f32[768]{0:T(1024)S(1)}, f32[768]{0:T(1024)S(1)}, f32[1,768,8,128]{1,3,2,0:T(8,128)}, f32[768,8,128]{0,2,1:T(8,128)}) fusion(bf16[1,768,10,129]{1,3,2,0:T(8,128)(2,1)S(1)} %get-tuple-element.60, f32[768]{0:T(1024)S(1)} %get-tuple-element.41, bf16[1,768,1,128]{1,3,2,0:T(8,128)(2,1)S(1)} %collective-permute-done.1, ...), kind=kOutput, calls=%fused_computation.48 | convolution fusion | flops 329513472 | bytes 19989504 | tf_op jit(solution)/shard_map/bchw,ec->behw/dot_general | solution.py:69
  42.1 60.9 %all-reduce.2 = (f32[1,768]{1,0:T(1,128)S(1)}, f32[1,768]{1,0:T(1,128)S(1)}) all-reduce(f32[1,768]{1,0:T(1,128)S(1)} %reduce_sum.132, f32[1,768]{1,0:T(1,128)S(1)} %reduce_sum.134), channel_id=1, replica_groups=mesh['dp'=8,'row'=8,'col'=4] {'row','col'}, use_global_device_ids=true, to_apply=%region_2.3 | all-reduce | flops 1536 | bytes 12288 | tf_op jit(solution)/shard_map/psum | solution.py:61
  103.5 3.9 fusion.46
  107.5 1.9 convolution_bitcast_fusion.1
  110.8 5.6 %fusion.24 = (f32[768]{0:T(1024)S(1)}, f32[768]{0:T(1024)S(1)}, f32[768]{0:T(1024)S(1)}, f32[768]{0:T(1024)S(1)}, f32[768]{0:T(1024)S(1)}, /*index=5*/f32[768]{0...) fusion(bf16[1,768,10,129]{1,3,2,0:T(8,128)(2,1)S(1)} %copy-done.4, ...), kind=kLoop, calls=%fused_computation.44 | loop fusion | flops 32236800 | bytes 20874240 | tf_op jit(solution)/shard_map/reduce_sum | solution.py:94
  116.4 1.4 collective-permute-start.4
  117.9 1.3 collective-permute-start.5
  120.5 3.8 collective-permute-done.5
  124.4 6.4 %collective-permute-start.6 = (bf16[1,768,10,1]{1,3,2,0:T(2,128)(2,1)S(1)}, bf16[1,768,10,1]{1,3,2,0:T(2,128)(2,1)S(1)}, u32[]{:S(2)}, u32[]{:S(2)}) collective-permute-start(bf16[1,768,10,1]{1,3,2,0:T(2,128)(2,1)S(1)} %get-tuple-element.57), channel_id=1, source_target_pairs={{1,0},{2,1},{3,2},{5,4},{6,5},{7,6},{9,8},{10,9},{11,10},{13,12},{... | collective-permute-start | bytes 46088 | tf_op jit(solution)/shard_map/ppermute | solution.py:18
  130.7 1.9 collective-permute-start.7
  133.5 1.0 copy.24
  135.8 0.9 copy-done.5
  136.7 4.7 fusion.15
  141.5 1.1 copy-done.12
  142.6 1.3 fusion.43
  144.0 2.2 fusion.58
  146.5 1.0 copy.25
  147.5 79.0 %all-reduce = (f32[192]{0:T(256)}, f32[768,9]{0,1:T(8,128)}) all-reduce(f32[192]{0:T(256)S(1)} %get-tuple-element.32, f32[768,9]{0,1:T(8,128)S(1)} %stack.39), channel_id=1, replica_groups=mesh['dp'=8,'row'=8,'col'=4] {'dp','row','col'}, use_global_device_ids=true, to_apply=%region_7.8 | all-reduce | flops 7104 | bytes 56832 | tf_op jit(solution)/shard_map/psum | solution.py:112
  226.5 245.3 %all-reduce.7.cloned.1.call-done = (f32[192,768]{1,0:T(8,128)}, f32[768,192]{0,1:T(8,128)}) async-done(((f32[192,768]{1,0:T(8,128)}, f32[768,192]{0,1:T(8,128)}), (f32[192,768]{1,0:T(8,128)}, f32[768,192]{0,1:T(8,128)})) %all-reduce.7.cloned.1.call-update) | async-done | bytes 1179664 | tf_op jit(solution)/shard_map/psum | solution.py:112
  471.8 1.9 copy.51
  473.7 1.6 copy.52
  475.3 1.6 copy.53
  476.9 1.9 copy.54
  (84 shorter events, 6.6 us)
Async XLA Ops:
  7.2 27.7 %copy-start = (bf16[768,192]{0,1:T(8,128)(2,1)S(1)}, bf16[768,192]{0,1:T(8,128)(2,1)}, u32[]{:S(2)}) copy-start(bf16[768,192]{0,1:T(8,128)(2,1)} %param.14) | copy-start | bytes 884740
  7.2 219.3 %all-reduce.9.cloned.1.call-start = ((), (), s32[]{:S(2)}) async-start(), calls=%async_computation.1 | async-start | bytes 589824 | tf_op jit(solution)/shard_map/psum | solution.py:111
  8.4 22.2 %copy-start.20 = (f32[768,9]{0,1:T(8,128)S(1)}, f32[768,9]{0,1:T(8,128)}, u32[]{:S(2)}) copy-start(f32[768,9]{0,1:T(8,128)} %param.11) | copy-start | bytes 82948
  12.2 7.5 %collective-permute-start = (bf16[1,768,1,128]{1,3,2,0:T(8,128)(2,1)S(1)}, bf16[1,768,1,128]{1,3,2,0:T(8,128)(2,1)S(1)}, u32[]{:S(2)}, u32[]{:S(2)}) collective-permute-start(bf16[1,768,1,128]{1,3,2,0:T(8,128)(2,1)S(1)} %get-tuple-element.65), channel_id=1, source_target_pairs={{0,4},{4,8},{8,12},{12,16},{16,20},{20,24},{24,28},{1,5},{5,9},{9,... | collective-permute-start | bytes 589832 | tf_op jit(solution)/shard_map/ppermute | solution.py:17
  16.2 7.4 %collective-permute-start.1 = (bf16[1,768,1,128]{1,3,2,0:T(8,128)(2,1)S(1)}, bf16[1,768,1,128]{1,3,2,0:T(8,128)(2,1)S(1)}, u32[]{:S(2)}, u32[]{:S(2)}) collective-permute-start(bf16[1,768,1,128]{1,3,2,0:T(8,128)(2,1)S(1)} %get-tuple-element.66), channel_id=1, source_target_pairs={{4,0},{8,4},{12,8},{16,12},{20,16},{24,20},{28,24},{5,1},{9,5},{13... | collective-permute-start | bytes 589832 | tf_op jit(solution)/shard_map/ppermute | solution.py:18
  19.7 15.1 %copy-start.8 = (bf16[1,768,1,128]{1,3,2,0:T(8,128)(2,1)}, bf16[1,768,1,128]{1,3,2,0:T(8,128)(2,1)S(1)}, u32[]{:S(2)}) copy-start(bf16[1,768,1,128]{1,3,2,0:T(8,128)(2,1)S(1)} %collective-permute-done) | copy-start | bytes 589828
  23.6 11.3 %copy-start.10 = (bf16[1,768,1,128]{1,3,2,0:T(8,128)(2,1)}, bf16[1,768,1,128]{1,3,2,0:T(8,128)(2,1)S(1)}, u32[]{:S(2)}) copy-start(bf16[1,768,1,128]{1,3,2,0:T(8,128)(2,1)S(1)} %collective-permute-done.1) | copy-start | bytes 589828
  23.6 7.1 %collective-permute-start.2 = (bf16[1,768,10,1]{1,3,2,0:T(2,128)(2,1)S(1)}, bf16[1,768,10,1]{1,3,2,0:T(2,128)(2,1)S(1)}, u32[]{:S(2)}, u32[]{:S(2)}) collective-permute-start(bf16[1,768,10,1]{1,3,2,0:T(2,128)(2,1)S(1)} %get-tuple-element.61), channel_id=1, source_target_pairs={{0,1},{1,2},{2,3},{4,5},{5,6},{6,7},{8,9},{9,10},{10,11},{12,13},{... | collective-permute-start | bytes 46088 | tf_op jit(solution)/shard_map/ppermute | solution.py:17
  28.5 6.3 %copy-start.17 = (bf16[1,192,8,128]{3,2,1,0:T(8,128)(2,1)S(1)}, bf16[1,192,8,128]{3,2,1,0:T(8,128)(2,1)}, u32[]{:S(2)}) copy-start(bf16[1,192,8,128]{3,2,1,0:T(8,128)(2,1)} %param.15) | copy-start | bytes 1179652
  28.5 5.3 %collective-permute-start.3 = (bf16[1,768,10,1]{1,3,2,0:T(2,128)(2,1)S(1)}, bf16[1,768,10,1]{1,3,2,0:T(2,128)(2,1)S(1)}, u32[]{:S(2)}, u32[]{:S(2)}) collective-permute-start(bf16[1,768,10,1]{1,3,2,0:T(2,128)(2,1)S(1)} %get-tuple-element.62), channel_id=1, source_target_pairs={{1,0},{2,1},{3,2},{5,4},{6,5},{7,6},{9,8},{10,9},{11,10},{13,12},{... | collective-permute-start | bytes 46088 | tf_op jit(solution)/shard_map/ppermute | solution.py:18
  34.8 7.3 %copy-start.1 = (bf16[1,768,10,129]{1,3,2,0:T(8,128)(2,1)}, bf16[1,768,10,129]{1,3,2,0:T(8,128)(2,1)S(1)}, u32[]{:S(2)}) copy-start(bf16[1,768,10,129]{1,3,2,0:T(8,128)(2,1)S(1)} %get-tuple-element.59) | copy-start | bytes 5944324
  34.8 7.3 %copy-start.3 = (bf16[1,768,10,129]{1,3,2,0:T(8,128)(2,1)}, bf16[1,768,10,129]{1,3,2,0:T(8,128)(2,1)S(1)}, u32[]{:S(2)}) copy-start(bf16[1,768,10,129]{1,3,2,0:T(8,128)(2,1)S(1)} %get-tuple-element.60) | copy-start | bytes 5944324
  34.8 68.2 %copy-start.16 = (f32[768,48]{0,1:T(8,128)S(1)}, f32[768,48]{0,1:T(8,128)}, u32[]{:S(2)}) copy-start(f32[768,48]{0,1:T(8,128)} %param.12) | copy-start | bytes 442372
  34.9 68.4 %copy-start.15 = (f32[48,768]{1,0:T(8,128)S(1)}, f32[48,768]{1,0:T(8,128)}, u32[]{:S(2)}) copy-start(f32[48,768]{1,0:T(8,128)} %param.13) | copy-start | bytes 442372
  34.9 68.6 %copy-start.13 = (bf16[1,192,8,128]{3,2,1,0:T(8,128)(2,1)S(1)}, bf16[1,192,8,128]{3,2,1,0:T(8,128)(2,1)}, u32[]{:S(2)}) copy-start(bf16[1,192,8,128]{3,2,1,0:T(8,128)(2,1)} %param.8) | copy-start | bytes 1179652
  103.5 3.9 copy-start.6
  107.4 2.5 copy-start.2
  107.4 2.5 copy-start.4
  107.4 3.4 copy-start.7
  107.4 3.4 copy-start.9
  107.5 3.4 copy-start.11
  116.4 17.1 %copy-start.19 = (bf16[1,192,8,128]{3,1,2,0:T(8,128)(2,1)S(1)}, bf16[1,192,8,128]{3,1,2,0:T(8,128)(2,1)}, u32[]{:S(2)}) copy-start(bf16[1,192,8,128]{3,1,2,0:T(8,128)(2,1)} %fusion.46) | copy-start | bytes 1179652
  116.4 4.0 collective-permute-start.4
  117.9 6.4 %collective-permute-start.5 = (bf16[1,768,1,128]{1,3,2,0:T(8,128)(2,1)S(1)}, bf16[1,768,1,128]{1,3,2,0:T(8,128)(2,1)S(1)}, u32[]{:S(2)}, u32[]{:S(2)}) collective-permute-start(bf16[1,768,1,128]{1,3,2,0:T(8,128)(2,1)S(1)} %get-tuple-element.64), channel_id=1, source_target_pairs={{4,0},{8,4},{12,8},{16,12},{20,16},{24,20},{28,24},{5,1},{9,5},{13... | collective-permute-start | bytes 589832 | tf_op jit(solution)/shard_map/ppermute | solution.py:18
  124.4 10.5 %collective-permute-start.6 = (bf16[1,768,10,1]{1,3,2,0:T(2,128)(2,1)S(1)}, bf16[1,768,10,1]{1,3,2,0:T(2,128)(2,1)S(1)}, u32[]{:S(2)}, u32[]{:S(2)}) collective-permute-start(bf16[1,768,10,1]{1,3,2,0:T(2,128)(2,1)S(1)} %get-tuple-element.57), channel_id=1, source_target_pairs={{1,0},{2,1},{3,2},{5,4},{6,5},{7,6},{9,8},{10,9},{11,10},{13,12},{... | collective-permute-start | bytes 46088 | tf_op jit(solution)/shard_map/ppermute | solution.py:18
  130.7 4.1 collective-permute-start.7
  134.5 337.3 %all-reduce.7.cloned.1.call-start = ((), (), s32[]{:S(2)}) async-start(), calls=%async_computation | async-start | bytes 2359296 | tf_op jit(solution)/shard_map/psum | solution.py:112
  134.8 1.9 copy-start.5
  136.7 5.9 %copy-start.14 = (bf16[1,192,8,128]{3,2,1,0:T(8,128)(2,1)S(1)}, bf16[1,192,8,128]{3,2,1,0:T(8,128)(2,1)}, u32[]{:S(2)}) copy-start(bf16[1,192,8,128]{3,2,1,0:T(8,128)(2,1)} %param.8) | copy-start | bytes 1179652
  136.7 5.9 %copy-start.21 = (f32[192]{0:T(256)S(1)}, f32[192]{0:T(256)}, u32[]{:S(2)}) copy-start(f32[192]{0:T(256)} %param.9) | copy-start | bytes 2308
  142.6 1.4 copy-start.22
  142.6 3.6 copy-start.18
  (1 other events, 1.2 us)
Sparse Core Ops, SparseCore 0:
  134.6 68.5 all-reduce.8
  209.3 262.5 all-reduce.6
where the time goes:
time: 488 us; the launch traced here: 486 us
  waiting for transfers between devices  259 us (53%)
  blocking collectives  140 us (29%)
  starting transfers between devices  23.5 us (5%)
  matrix products  21.3 us (4%)
  other arithmetic  15.1 us (3%)
  between operations  14.5 us (3%)
  local copies, waits for them, and re-layouts  12.4 us (3%)
    psum x1, waiting for transfers between devices, local(): lax.psum((grad_gain, grad_wexp, grad_kernel, grad_project), ('dp', 'row',...  245 us
    psum x1, blocking collectives, local(): lax.psum((grad_gain, grad_wexp, grad_kernel, grad_project), ('dp', 'row',...  79 us
    psum x1, blocking collectives, local(): pooled = lax.psum(jnp.sum(act, axis=(2, 3)), ('row', 'col')) / pixels  60.9 us
    ppermute x4, starting transfers between devices, with_halo(): before = lax.ppermute(last, axis, up)  12.2 us
    unnamed x52, local copies, waits for them, and re-layouts  12.1 us
    ppermute x4, starting transfers between devices, with_halo(): after = lax.ppermute(leading, axis, down)  11 us
    ppermute x4, waiting for transfers between devices, with_halo(): after = lax.ppermute(leading, axis, down)  10.9 us
  transfers between devices with their start and end apart: 10, of which 6 were waited for; matrix products, arithmetic and copies ran while one was open for 3% of the time, Pallas kernels for 0%

commit v1 on v0

--- a/solution.py
+++ b/solution.py
@@ -5,6 +5,7 @@
 
 EPS = 1e-06
 HIGH = lax.Precision.HIGHEST
+RC = ("row", "col")
 
 
 def with_halo(shard, sides, width):
@@ -49,6 +50,12 @@
     return total
 
 
+def gathered(block, axes, count):
+    return lax.all_to_all(
+        jnp.broadcast_to(block[None], (count,) + block.shape), axes, 0, 0, tiled=True
+    )
+
+
 def local(inputs, norm_gain, w_expand, kernel, w_squeeze, w_excite, w_project, cotangent):
     batch, chans, rows, cols = inputs.shape
     pixels = rows * cols * lax.axis_size("row") * lax.axis_size("col")
@@ -58,7 +65,15 @@
     hidden_pad = with_halo(hidden, (("row", 2), ("col", 3)), 1)
     conv = depthwise(hidden_pad, kernel, rows, cols)
     act = jax.nn.silu(conv)
-    pooled = lax.psum(jnp.sum(act, axis=(2, 3)), ("row", "col")) / pixels
+    grad_gated = jnp.einsum(
+        "bchw,ec->behw", cotangent, w_project, preferred_element_type=jnp.float32
+    )
+    sums = jnp.concatenate(
+        [jnp.sum(act, axis=(2, 3)), jnp.sum(grad_gated * act, axis=(2, 3))], axis=0
+    ).reshape(12, 128)
+    sums = jnp.sum(gathered(sums, RC, 32), axis=0).reshape(2, 768)
+    pooled = sums[:1] / pixels
+    grad_excite = sums[1:]
     squeeze_pre = jnp.dot(pooled, w_squeeze, precision=HIGH)
     squeezed = jax.nn.silu(squeeze_pre)
     excite_pre = jnp.dot(squeezed, w_excite, precision=HIGH)
@@ -66,17 +81,11 @@
     gated = (act * excite[:, :, None, None]).astype(jnp.bfloat16)
     proj = jnp.einsum("behw,ec->bchw", gated, w_project, preferred_element_type=jnp.float32)
     output = (inputs.astype(jnp.float32) + proj).astype(jnp.bfloat16)
-    grad_gated = jnp.einsum(
-        "bchw,ec->behw", cotangent, w_project, preferred_element_type=jnp.float32
-    )
-    grad_project = jnp.einsum("behw,bchw->ec", gated, cotangent, preferred_element_type=jnp.float32)
-    grad_excite = lax.psum(jnp.sum(grad_gated * act, axis=(2, 3)), ("row", "col"))
+    grad_project = jnp.einsum("behw,bchw->ce", gated, cotangent, preferred_element_type=jnp.float32)
     grad_epre = grad_excite * excite * (1.0 - excite)
-    grad_wexc = jnp.einsum("bs,be->se", squeezed, grad_epre, precision=HIGH)
     grad_spre = jnp.einsum("be,se->bs", grad_epre, w_excite, precision=HIGH) * silu_slope(
         squeeze_pre
     )
-    grad_wsq = jnp.einsum("be,bs->es", pooled, grad_spre, precision=HIGH)
     grad_pooled = jnp.einsum("bs,es->be", grad_spre, w_squeeze, precision=HIGH)
     grad_act = grad_gated * excite[:, :, None, None] + (grad_pooled / pixels)[:, :, None, None]
     grad_conv = (grad_act * silu_slope(conv)).astype(jnp.bfloat16)
@@ -97,7 +106,7 @@
                 axis=(0, 2, 3),
             )
         )
-    grad_kernel = jnp.stack(taps, axis=1)
+    grad_kernel = jnp.stack(taps, axis=0)
     grad_pre = (grad_hidden * silu_slope(pre)).astype(jnp.bfloat16)
     grad_wexp = jnp.einsum("bchw,behw->ce", scaled, grad_pre, preferred_element_type=jnp.float32)
     grad_scaled = jnp.einsum(
@@ -108,19 +117,54 @@
     grad_in = inverse * (
         grad_normed - normed * jnp.mean(grad_normed * normed, axis=1, keepdims=True)
     ) + cotangent.astype(jnp.float32)
-    grad_wsq_all, grad_wexc_all = lax.psum((grad_wsq, grad_wexc), "dp")
-    gain_all, wexp_all, kernel_all, project_all = lax.psum(
-        (grad_gain, grad_wexp, grad_kernel, grad_project), ("dp", "row", "col")
+
+    def blocks(w):
+        return w.reshape(192, 6, 128).transpose(1, 0, 2).reshape(1152, 128)
+
+    def unblock(w):
+        return w.reshape(6, 192, 128).transpose(1, 0, 2).reshape(192, 768)
+
+    big = jnp.concatenate([blocks(grad_wexp), blocks(grad_project)], axis=0).reshape(32, 72, 128)
+    small = jnp.concatenate(
+        [grad_kernel.reshape(6912), grad_gain, jnp.zeros((1088,), jnp.float32)]
+    ).reshape(32, 2, 128)
+    packed = jnp.concatenate([big, small, jnp.zeros((32, 6, 128), jnp.float32)], axis=1)
+    mine = jnp.sum(lax.all_to_all(packed, RC, 0, 0, tiled=True), axis=0)
+    vecs = jnp.concatenate(
+        [
+            pooled.reshape(768),
+            grad_epre.reshape(768),
+            squeezed.reshape(48),
+            grad_spre.reshape(48),
+            jnp.zeros((416,), jnp.float32),
+        ]
+    ).reshape(16, 128)
+    shared = gathered(jnp.concatenate([mine, vecs], axis=0), "dp", 8)
+    total = jnp.sum(shared[:, :80], axis=0)
+    vec = shared[:, 80:].reshape(8, 2048)
+    pooled_s, epre_s, squeezed_s, spre_s = (
+        vec[:, :768],
+        vec[:, 768:1536],
+        vec[:, 1536:1584],
+        vec[:, 1584:1632],
     )
+    grad_wexc = jnp.einsum("bs,be->se", squeezed_s, epre_s, precision=HIGH)
+    grad_wsq = jnp.einsum("be,bs->es", pooled_s, spre_s, precision=HIGH)
+    high = total[:74].astype(jnp.bfloat16)
+    low = (total[72:74] - lax.reduce_precision(total[72:74], 8, 7)).astype(jnp.bfloat16)
+    send = jnp.concatenate([high, low, jnp.zeros((4, 128), jnp.bfloat16)], axis=0)
+    every = gathered(send, RC, 32).astype(jnp.float32)
+    big = every[:, :72].reshape(2, 1152, 128)
+    small = (every[:, 72:74] + every[:, 74:76]).reshape(8192)
     return (
         output,
         grad_in.astype(jnp.bfloat16),
-        gain_all,
-        wexp_all,
-        kernel_all,
-        grad_wsq_all,
-        grad_wexc_all,
-        project_all,
+        small[6912:7104],
+        unblock(big[0]),
+        small[:6912].reshape(9, 768).T,
+        grad_wsq,
+        grad_wexc,
+        unblock(big[1]).T,
     )
 
 

time: 488 us -> 173 us (0.35)
  waiting for transfers between devices: 259 us -> 53.6 us
  blocking collectives: 140 us -> 17.3 us
  starting transfers between devices: 23.5 us -> 44.2 us
  between operations: 14.5 us -> 1.3 us
  other arithmetic: 15.1 us -> 20.6 us
    psum x2 -> x0, waiting for transfers between devices: 245 us -> none  [the longest x1 245 us: local(): lax.psum((grad_gain, grad_wexp, grad_kernel, grad_project), ('dp', 'row',...]
    psum x2 -> x0, blocking collectives: 140 us -> none  [the longest x1 79 us: local(): lax.psum((grad_gain, grad_wexp, grad_kernel, grad_project), ('dp', 'row',...]
    all_to_all x0 -> x3, waiting for transfers between devices: none -> 41.8 us  [the longest x2 21.2 us: gathered(): lax.all_to_all(jnp.broadcast_to(block[None], (count,) + block.shape), axe...]
    all_to_all x0 -> x3, starting transfers between devices: none -> 22.3 us  [the longest x2 13.3 us: gathered(): lax.all_to_all(jnp.broadcast_to(block[None], (count,) + block.shape), axe...]
    all_to_all x0 -> x1, blocking collectives: none -> 17.3 us  [gathered(): lax.all_to_all(jnp.broadcast_to(block[None], (count,) + block.shape), axe...]
    unnamed x52 -> x45, local copies, waits for them, and re-layouts: 12.1 us -> 4.04 us
  transfers between devices with their start and end apart: 10 -> 11, of which waited for: 6 -> 7; matrix products, arithmetic and copies ran while one was open for 3% -> 7% of each run, Pallas kernels for 0% -> 0%
where the time goes in v1:
time: 173 us; the launch traced here: 172 us
  waiting for transfers between devices  53.6 us (31%)
  starting transfers between devices  44.2 us (26%)
  matrix products  21.7 us (13%)
  other arithmetic  20.6 us (12%)
  blocking collectives  17.3 us (10%)
  local copies, waits for them, and re-layouts  13 us (8%)
    all_to_all x2, waiting for transfers between devices, gathered(): lax.all_to_all(jnp.broadcast_to(block[None], (count,) + block.shape), axe...  21.2 us
    all_to_all x1, waiting for transfers between devices, local(): mine = jnp.sum(lax.all_to_all(packed, RC, 0, 0, tiled=True), axis=0)  20.6 us
    all_to_all x1, blocking collectives, gathered(): lax.all_to_all(jnp.broadcast_to(block[None], (count,) + block.shape), axe...  17.3 us
    all_to_all x2, starting transfers between devices, gathered(): lax.all_to_all(jnp.broadcast_to(block[None], (count,) + block.shape), axe...  13.3 us
    ppermute x4, starting transfers between devices, with_halo(): before = lax.ppermute(last, axis, up)  13 us
    reduce_sum x1, other arithmetic, local(): jnp.sum(grad_conv.astype(jnp.float32) * hidden_pad[:, :, drow:drow + rows...  9.99 us
    ppermute x4, waiting for transfers between devices, with_halo(): after = lax.ppermute(leading, axis, down)  9.48 us
    all_to_all x1, starting transfers between devices, local(): mine = jnp.sum(lax.all_to_all(packed, RC, 0, 0, tiled=True), axis=0)  9.04 us
  transfers between devices with their start and end apart: 11, of which 7 were waited for; matrix products, arithmetic and copies ran while one was open for 7% of the time, Pallas kernels for 0%

profile of v1, /device:TPU:1, one launch (start us, length us, event | category | flops | bytes accessed | tf_op | source)
XLA Modules:
  0.0 171.6 jit_solution(18299834532487520555)
XLA Ops:
  0.6 1.1 fusion.66
  1.8 3.8 %fusion.30 = (bf16[768,8,128]{0,2,1:T(8,128)(2,1)S(1)}, f32[8,128,768]{2,1,0:T(8,128)}) fusion(bf16[192,768]{1,0:T(8,128)(2,1)} %param.10, f32[192]{0:T(256)} %param.9, f32[8,128]{1,0:T(8,128)S(1)} %add_rsqrt_fusion, bf16[1,192,8,128]{3,2,1,0:T(8,128)(2,1)} %param.8), kind=kOutput, calls=%fused_computation.55 | convolution fusion | flops 306708480 | bytes 5411584 | tf_op jit(solution)/shard_map/bchw,ce->behw/dot_general | solution.py:38
  5.6 3.9 %collective-permute-start = (bf16[1,768,1,128]{1,3,2,0:T(8,128)(2,1)S(1)}, bf16[1,768,1,128]{1,3,2,0:T(8,128)(2,1)S(1)}, u32[]{:S(2)}, u32[]{:S(2)}) collective-permute-start(bf16[1,768,1,128]{1,3,2,0:T(8,128)(2,1)S(1)} %get-tuple-element.80), channel_id=1, source_target_pairs={{0,4},{4,8},{8,12},{12,16},{16,20},{20,24},{24,28},{1,5},{5,9},{9,... | collective-permute-start | bytes 589832 | tf_op jit(solution)/shard_map/ppermute | solution.py:18
  9.6 1.3 collective-permute-start.1
  10.9 2.3 %collective-permute-done = bf16[1,768,1,128]{1,3,2,0:T(8,128)(2,1)S(1)} collective-permute-done((bf16[1,768,1,128]{1,3,2,0:T(8,128)(2,1)S(1)}, bf16[1,768,1,128]{1,3,2,0:T(8,128)(2,1)S(1)}, u32[]{:S(2)}, u32[]{:S(2)}) %collective-permute-start) | collective-permute-done | bytes 196640 | tf_op jit(solution)/shard_map/ppermute | solution.py:18
  13.1 3.8 %collective-permute-done.1 = bf16[1,768,1,128]{1,3,2,0:T(8,128)(2,1)S(1)} collective-permute-done((bf16[1,768,1,128]{1,3,2,0:T(8,128)(2,1)S(1)}, bf16[1,768,1,128]{1,3,2,0:T(8,128)(2,1)S(1)}, u32[]{:S(2)}, u32[]{:S(2)}) %collective-permute-start.1) | collective-permute-done | bytes 196640 | tf_op jit(solution)/shard_map/ppermute | solution.py:19
  17.0 4.9 %collective-permute-start.2 = (bf16[1,768,10,1]{1,3,2,0:T(2,128)(2,1)S(1)}, bf16[1,768,10,1]{1,3,2,0:T(2,128)(2,1)S(1)}, u32[]{:S(2)}, u32[]{:S(2)}) collective-permute-start(bf16[1,768,10,1]{1,3,2,0:T(2,128)(2,1)S(1)} %get-tuple-element.76), channel_id=1, source_target_pairs={{0,1},{1,2},{2,3},{4,5},{5,6},{6,7},{8,9},{9,10},{10,11},{12,13},{... | collective-permute-start | bytes 46088 | tf_op jit(solution)/shard_map/ppermute | solution.py:18
  22.0 2.1 %collective-permute-start.3 = (bf16[1,768,10,1]{1,3,2,0:T(2,128)(2,1)S(1)}, bf16[1,768,10,1]{1,3,2,0:T(2,128)(2,1)S(1)}, u32[]{:S(2)}, u32[]{:S(2)}) collective-permute-start(bf16[1,768,10,1]{1,3,2,0:T(2,128)(2,1)S(1)} %get-tuple-element.77), channel_id=1, source_target_pairs={{1,0},{2,1},{3,2},{5,4},{6,5},{7,6},{9,8},{10,9},{11,10},{13,12},{... | collective-permute-start | bytes 46088 | tf_op jit(solution)/shard_map/ppermute | solution.py:19
  24.1 3.2 %collective-permute-done.3 = bf16[1,768,10,1]{1,3,2,0:T(2,128)(2,1)S(1)} collective-permute-done((bf16[1,768,10,1]{1,3,2,0:T(2,128)(2,1)S(1)}, bf16[1,768,10,1]{1,3,2,0:T(2,128)(2,1)S(1)}, u32[]{:S(2)}, u32[]{:S(2)}) %collective-permute-start.3) | collective-permute-done | bytes 15392 | tf_op jit(solution)/shard_map/ppermute | solution.py:19
  28.3 7.0 %fusion.94 = (f32[768]{0:T(1024)S(1)}, f32[768]{0:T(1024)S(1)}, f32[1,768,8,128]{1,3,2,0:T(8,128)}, f32[768,8,128]{0,2,1:T(8,128)}) fusion(bf16[1,768,10,129]{1,3,2,0:T(8,128)(2,1)S(1)} %get-tuple-element.75, f32[768]{0:T(1024)S(1)} %get-tuple-element.65, bf16[1,768,1,128]{1,3,2,0:T(8,128)(2,1)S(1)} %collective-permute-done.1, ...), kind=kOutput, calls=%fused_computation.159 | convolution fusion | flops 329513472 | bytes 19989504 | tf_op jit(solution)/shard_map/bchw,ec->behw/dot_general | solution.py:68
  35.4 17.3 %all_to_all.20 = f32[32,12,128]{2,1,0:T(8,128)S(1)} all-to-all(f32[32,12,128]{2,1,0:T(8,128)S(1)} %broadcast_in_dim.17), channel_id=1, replica_groups=mesh['dp'=8,'row'=8,'col'=4] {'row','col'}, dimensions={0} | all-to-all | bytes 393216 | tf_op jit(solution)/shard_map/all_to_all | solution.py:54
  53.7 10.0 %fusion.24 = (f32[768]{0:T(1024)S(1)}, f32[768]{0:T(1024)S(1)}, f32[768]{0:T(1024)S(1)}, f32[768]{0:T(1024)S(1)}, f32[768]{0:T(1024)S(1)}, /*index=5*/f32[768]{0...) fusion(bf16[1,768,10,129]{1,3,2,0:T(8,128)(2,1)} %copy-done.2, ...), kind=kLoop, calls=%fused_computation.44 | loop fusion | flops 34596096 | bytes 22453248 | tf_op jit(solution)/shard_map/reduce_sum | solution.py:103
  63.7 2.1 %collective-permute-start.4 = (bf16[1,768,1,128]{1,3,2,0:T(8,128)(2,1)S(1)}, bf16[1,768,1,128]{1,3,2,0:T(8,128)(2,1)S(1)}, u32[]{:S(2)}, u32[]{:S(2)}) collective-permute-start(bf16[1,768,1,128]{1,3,2,0:T(8,128)(2,1)S(1)} %get-tuple-element.78), channel_id=1, source_target_pairs={{0,4},{4,8},{8,12},{12,16},{16,20},{20,24},{24,28},{1,5},{5,9},{9,... | collective-permute-start | bytes 589832 | tf_op jit(solution)/shard_map/ppermute | solution.py:18
  65.8 1.3 collective-permute-start.5
  67.2 3.0 %copy.63 = bf16[1,768,8,128]{3,2,1,0:T(8,128)(2,1)} copy(bf16[1,768,8,128]{1,3,2,0:T(8,128)(2,1)} %get-tuple-element.69) | data formatting | bytes 3145728 | tf_op jit(solution)/shard_map/convert_element_type | solution.py:81
  70.2 2.5 %collective-permute-done.5 = bf16[1,768,1,128]{1,3,2,0:T(8,128)(2,1)S(1)} collective-permute-done((bf16[1,768,1,128]{1,3,2,0:T(8,128)(2,1)S(1)}, bf16[1,768,1,128]{1,3,2,0:T(8,128)(2,1)S(1)}, u32[]{:S(2)}, u32[]{:S(2)}) %collective-permute-start.5) | collective-permute-done | bytes 196640 | tf_op jit(solution)/shard_map/ppermute | solution.py:19
  72.7 4.3 %collective-permute-start.6 = (bf16[1,768,10,1]{1,3,2,0:T(2,128)(2,1)S(1)}, bf16[1,768,10,1]{1,3,2,0:T(2,128)(2,1)S(1)}, u32[]{:S(2)}, u32[]{:S(2)}) collective-permute-start(bf16[1,768,10,1]{1,3,2,0:T(2,128)(2,1)S(1)} %get-tuple-element.72), channel_id=1, source_target_pairs={{1,0},{2,1},{3,2},{5,4},{6,5},{7,6},{9,8},{10,9},{11,10},{13,12},{... | collective-permute-start | bytes 46088 | tf_op jit(solution)/shard_map/ppermute | solution.py:19
  77.0 2.0 %collective-permute-start.7 = (bf16[1,768,10,1]{1,3,2,0:T(2,128)(2,1)S(1)}, bf16[1,768,10,1]{1,3,2,0:T(2,128)(2,1)S(1)}, u32[]{:S(2)}, u32[]{:S(2)}) collective-permute-start(bf16[1,768,10,1]{1,3,2,0:T(2,128)(2,1)S(1)} %get-tuple-element.73), channel_id=1, source_target_pairs={{0,1},{1,2},{2,3},{4,5},{5,6},{6,7},{8,9},{9,10},{10,11},{12,13},{... | collective-permute-start | bytes 46088 | tf_op jit(solution)/shard_map/ppermute | solution.py:18
  79.0 2.9 %fusion.38 = f32[6,128,192,1]{1,2,3,0:T(8,128)} fusion(bf16[6,128,8,128]{3,2,1,0:T(8,128)(2,1)} %bitcast.176, bf16[192,8,128]{2,1,0:T(8,128)(2,1)S(1)} %bitcast.183), kind=kOutput, calls=%fused_computation.73 | convolution fusion | flops 301989888 | bytes 2555904 | tf_op jit(solution)/shard_map/behw,bchw->ce/dot_general | solution.py:84
  84.0 5.6 %fusion.15 = bf16[1,768,8,128]{1,3,2,0:T(8,128)(2,1)S(1)} fusion(bf16[1,768,8,128]{1,3,2,0:T(8,128)(2,1)S(1)} %get-tuple-element.67, f32[8,128,768]{2,1,0:T(8,128)S(1)} %copy-done.4, bf16[1,768,10,129]{1,3,2,0:T(8,128)(2,1)S(1)} %get-tuple-element.71, bf16[1,768,1,128]{1,3,2,0:T(8,128)(2,1)} %copy-done.7, ...), kind=kLoop, calls=%fused_computation.35 | loop fusion | flops 29097984 | bytes 16149504 | tf_op jit(solution)/shard_map/convert_element_type | solution.py:110
  89.6 1.2 copy.61
  90.8 2.7 %fusion.65 = (f32[192]{0:T(256)S(1)}, f32[8,128]{1,0:T(8,128)S(1)}, f32[1,192,8,128]{3,1,2,0:T(8,128)}) fusion(f32[8,128]{1,0:T(8,128)S(1)} %add_rsqrt_fusion, bf16[1,192,8,128]{3,2,1,0:T(8,128)(2,1)} %param.8, f32[192]{0:T(256)S(1)} %copy-done.19, bf16[192,768]{1,0:T(8,128)(2,1)} %param.10, bf16[1,768,8,128]{1,3,2,0:T(8,128)(2,1)S(1)} %fusion.15), kind=kOutput, calls=%fused_computation.100 | convolution fusion | flops 303364928 | bytes 3057152 | tf_op jit(solution)/shard_map/ce,behw->bchw/dot_general | solution.py:112
  94.4 1.3 maximum_maximum_fusion.2
  95.7 9.0 %all-to-all-start.1 = ((f32[32,80,128]{2,1,0:T(8,128)}), f32[32,80,128]{2,1,0:T(8,128)S(1)}, u32[]{:S(2)}, u32[]{:S(2)}) async-start(f32[32,80,128]{2,1,0:T(8,128)} %maximum_maximum_fusion.2), calls=%async_computation.1 | async-start | bytes 2621440 | tf_op jit(solution)/shard_map/all_to_all | solution.py:132
  104.9 20.6 %all-to-all-done.1 = f32[32,80,128]{2,1,0:T(8,128)S(1)} async-done(((f32[32,80,128]{2,1,0:T(8,128)}), f32[32,80,128]{2,1,0:T(8,128)S(1)}, u32[]{:S(2)}, u32[]{:S(2)}) %all-to-all-start.1) | async-done | bytes 1310752 | tf_op jit(solution)/shard_map/all_to_all | solution.py:132
  126.4 8.2 %all-to-all-start.2 = ((f32[8,96,128]{2,1,0:T(8,128)}), f32[8,96,128]{2,1,0:T(8,128)S(1)}, u32[]{:S(2)}, u32[]{:S(2)}) async-start(f32[8,96,128]{2,1,0:T(8,128)} %broadcast_in_dim.21), calls=%async_computation.2 | async-start | bytes 786432 | tf_op jit(solution)/shard_map/all_to_all | solution.py:54
  134.6 1.7 %fusion.51 = bf16[1,192,8,128]{3,1,2,0:T(8,128)(2,1)S(1)} fusion(bf16[1,768,8,128]{1,3,2,0:T(8,128)(2,1)S(1)} %copy-done.3, bf16[768,192]{0,1:T(8,128)(2,1)S(1)} %copy-done, bf16[1,192,8,128]{3,2,1,0:T(8,128)(2,1)} %param.8), kind=kOutput, calls=%fused_computation.81 | convolution fusion | flops 302579712 | bytes 2654208 | tf_op jit(solution)/shard_map/behw,ec->bchw/dot_general | solution.py:82
  137.6 1.0 copy.69
  138.6 10.1 %all-to-all-done.2 = f32[8,96,128]{2,1,0:T(8,128)S(1)} async-done(((f32[8,96,128]{2,1,0:T(8,128)}), f32[8,96,128]{2,1,0:T(8,128)S(1)}, u32[]{:S(2)}, u32[]{:S(2)}) %all-to-all-start.2) | async-done | bytes 393248 | tf_op jit(solution)/shard_map/all_to_all | solution.py:54
  149.7 5.1 %all-to-all-start.3 = ((bf16[32,80,128]{2,1,0:T(8,128)(2,1)}), bf16[32,80,128]{2,1,0:T(8,128)(2,1)S(1)}, u32[]{:S(2)}, u32[]{:S(2)}) async-start(bf16[32,80,128]{2,1,0:T(8,128)(2,1)} %broadcast_in_dim.45), calls=%async_computation.3 | async-start | bytes 1310720 | tf_op jit(solution)/shard_map/all_to_all | solution.py:54
  155.9 1.0 fusion.82
  156.9 11.2 %all-to-all-done.3 = bf16[32,80,128]{2,1,0:T(8,128)(2,1)S(1)} async-done(((bf16[32,80,128]{2,1,0:T(8,128)(2,1)}), bf16[32,80,128]{2,1,0:T(8,128)(2,1)S(1)}, u32[]{:S(2)}, u32[]{:S(2)}) %all-to-all-start.3) | async-done | bytes 655392 | tf_op jit(solution)/shard_map/all_to_all | solution.py:54
  (111 shorter events, 13.0 us)
Async XLA Ops:
  0.6 27.6 %copy-start = (bf16[768,192]{0,1:T(8,128)(2,1)S(1)}, bf16[768,192]{0,1:T(8,128)(2,1)}, u32[]{:S(2)}) copy-start(bf16[768,192]{0,1:T(8,128)(2,1)} %param.14) | copy-start | bytes 884740
  1.8 22.2 %copy-start.18 = (f32[768,9]{0,1:T(8,128)S(1)}, f32[768,9]{0,1:T(8,128)}, u32[]{:S(2)}) copy-start(f32[768,9]{0,1:T(8,128)} %param.11) | copy-start | bytes 82948
  5.6 7.5 %collective-permute-start = (bf16[1,768,1,128]{1,3,2,0:T(8,128)(2,1)S(1)}, bf16[1,768,1,128]{1,3,2,0:T(8,128)(2,1)S(1)}, u32[]{:S(2)}, u32[]{:S(2)}) collective-permute-start(bf16[1,768,1,128]{1,3,2,0:T(8,128)(2,1)S(1)} %get-tuple-element.80), channel_id=1, source_target_pairs={{0,4},{4,8},{8,12},{12,16},{16,20},{20,24},{24,28},{1,5},{5,9},{9,... | collective-permute-start | bytes 589832 | tf_op jit(solution)/shard_map/ppermute | solution.py:18
  9.6 7.4 %collective-permute-start.1 = (bf16[1,768,1,128]{1,3,2,0:T(8,128)(2,1)S(1)}, bf16[1,768,1,128]{1,3,2,0:T(8,128)(2,1)S(1)}, u32[]{:S(2)}, u32[]{:S(2)}) collective-permute-start(bf16[1,768,1,128]{1,3,2,0:T(8,128)(2,1)S(1)} %get-tuple-element.81), channel_id=1, source_target_pairs={{4,0},{8,4},{12,8},{16,12},{20,16},{24,20},{28,24},{5,1},{9,5},{13... | collective-permute-start | bytes 589832 | tf_op jit(solution)/shard_map/ppermute | solution.py:19
  13.1 15.1 %copy-start.5 = (bf16[1,768,1,128]{1,3,2,0:T(8,128)(2,1)}, bf16[1,768,1,128]{1,3,2,0:T(8,128)(2,1)S(1)}, u32[]{:S(2)}) copy-start(bf16[1,768,1,128]{1,3,2,0:T(8,128)(2,1)S(1)} %collective-permute-done) | copy-start | bytes 589828
  17.0 11.3 %copy-start.6 = (bf16[1,768,1,128]{1,3,2,0:T(8,128)(2,1)}, bf16[1,768,1,128]{1,3,2,0:T(8,128)(2,1)S(1)}, u32[]{:S(2)}) copy-start(bf16[1,768,1,128]{1,3,2,0:T(8,128)(2,1)S(1)} %collective-permute-done.1) | copy-start | bytes 589828
  17.0 7.1 %collective-permute-start.2 = (bf16[1,768,10,1]{1,3,2,0:T(2,128)(2,1)S(1)}, bf16[1,768,10,1]{1,3,2,0:T(2,128)(2,1)S(1)}, u32[]{:S(2)}, u32[]{:S(2)}) collective-permute-start(bf16[1,768,10,1]{1,3,2,0:T(2,128)(2,1)S(1)} %get-tuple-element.76), channel_id=1, source_target_pairs={{0,1},{1,2},{2,3},{4,5},{5,6},{6,7},{8,9},{9,10},{10,11},{12,13},{... | collective-permute-start | bytes 46088 | tf_op jit(solution)/shard_map/ppermute | solution.py:18
  22.0 6.3 %copy-start.15 = (bf16[1,192,8,128]{3,2,1,0:T(8,128)(2,1)S(1)}, bf16[1,192,8,128]{3,2,1,0:T(8,128)(2,1)}, u32[]{:S(2)}) copy-start(bf16[1,192,8,128]{3,2,1,0:T(8,128)(2,1)} %param.15) | copy-start | bytes 1179652
  22.0 5.3 %collective-permute-start.3 = (bf16[1,768,10,1]{1,3,2,0:T(2,128)(2,1)S(1)}, bf16[1,768,10,1]{1,3,2,0:T(2,128)(2,1)S(1)}, u32[]{:S(2)}, u32[]{:S(2)}) collective-permute-start(bf16[1,768,10,1]{1,3,2,0:T(2,128)(2,1)S(1)} %get-tuple-element.77), channel_id=1, source_target_pairs={{1,0},{2,1},{3,2},{5,4},{6,5},{7,6},{9,8},{10,9},{11,10},{13,12},{... | collective-permute-start | bytes 46088 | tf_op jit(solution)/shard_map/ppermute | solution.py:19
  28.2 7.1 %copy-start.1 = (bf16[1,768,10,129]{1,3,2,0:T(8,128)(2,1)}, bf16[1,768,10,129]{1,3,2,0:T(8,128)(2,1)S(1)}, u32[]{:S(2)}) copy-start(bf16[1,768,10,129]{1,3,2,0:T(8,128)(2,1)S(1)} %get-tuple-element.74) | copy-start | bytes 5944324
  28.2 7.1 %copy-start.2 = (bf16[1,768,10,129]{1,3,2,0:T(8,128)(2,1)}, bf16[1,768,10,129]{1,3,2,0:T(8,128)(2,1)S(1)}, u32[]{:S(2)}) copy-start(bf16[1,768,10,129]{1,3,2,0:T(8,128)(2,1)S(1)} %get-tuple-element.75) | copy-start | bytes 5944324
  28.3 24.4 %copy-start.13 = (f32[768,48]{0,1:T(8,128)S(1)}, f32[768,48]{0,1:T(8,128)}, u32[]{:S(2)}) copy-start(f32[768,48]{0,1:T(8,128)} %param.12) | copy-start | bytes 442372
  28.3 24.7 %copy-start.12 = (f32[48,768]{1,0:T(8,128)S(1)}, f32[48,768]{1,0:T(8,128)}, u32[]{:S(2)}) copy-start(f32[48,768]{1,0:T(8,128)} %param.13) | copy-start | bytes 442372
  63.7 15.4 %copy-start.16 = (bf16[1,192,8,128]{3,2,1,0:T(8,128)(2,1)S(1)}, bf16[1,192,8,128]{3,2,1,0:T(8,128)(2,1)}, u32[]{:S(2)}) copy-start(bf16[1,192,8,128]{3,2,1,0:T(8,128)(2,1)} %param.15) | copy-start | bytes 1179652
  63.7 6.5 %collective-permute-start.4 = (bf16[1,768,1,128]{1,3,2,0:T(8,128)(2,1)S(1)}, bf16[1,768,1,128]{1,3,2,0:T(8,128)(2,1)S(1)}, u32[]{:S(2)}, u32[]{:S(2)}) collective-permute-start(bf16[1,768,1,128]{1,3,2,0:T(8,128)(2,1)S(1)} %get-tuple-element.78), channel_id=1, source_target_pairs={{0,4},{4,8},{8,12},{12,16},{16,20},{20,24},{24,28},{1,5},{5,9},{9,... | collective-permute-start | bytes 589832 | tf_op jit(solution)/shard_map/ppermute | solution.py:18
  65.8 6.8 %collective-permute-start.5 = (bf16[1,768,1,128]{1,3,2,0:T(8,128)(2,1)S(1)}, bf16[1,768,1,128]{1,3,2,0:T(8,128)(2,1)S(1)}, u32[]{:S(2)}, u32[]{:S(2)}) collective-permute-start(bf16[1,768,1,128]{1,3,2,0:T(8,128)(2,1)S(1)} %get-tuple-element.79), channel_id=1, source_target_pairs={{4,0},{8,4},{12,8},{16,12},{20,16},{24,20},{28,24},{5,1},{9,5},{13... | collective-permute-start | bytes 589832 | tf_op jit(solution)/shard_map/ppermute | solution.py:19
  70.2 12.9 %copy-start.7 = (bf16[1,768,1,128]{1,3,2,0:T(8,128)(2,1)}, bf16[1,768,1,128]{1,3,2,0:T(8,128)(2,1)S(1)}, u32[]{:S(2)}) copy-start(bf16[1,768,1,128]{1,3,2,0:T(8,128)(2,1)S(1)} %collective-permute-done.4) | copy-start | bytes 589828
  72.6 10.4 %copy-start.8 = (bf16[1,768,1,128]{1,3,2,0:T(8,128)(2,1)}, bf16[1,768,1,128]{1,3,2,0:T(8,128)(2,1)S(1)}, u32[]{:S(2)}) copy-start(bf16[1,768,1,128]{1,3,2,0:T(8,128)(2,1)S(1)} %collective-permute-done.5) | copy-start | bytes 589828
  72.7 9.4 %collective-permute-start.6 = (bf16[1,768,10,1]{1,3,2,0:T(2,128)(2,1)S(1)}, bf16[1,768,10,1]{1,3,2,0:T(2,128)(2,1)S(1)}, u32[]{:S(2)}, u32[]{:S(2)}) collective-permute-start(bf16[1,768,10,1]{1,3,2,0:T(2,128)(2,1)S(1)} %get-tuple-element.72), channel_id=1, source_target_pairs={{1,0},{2,1},{3,2},{5,4},{6,5},{7,6},{9,8},{10,9},{11,10},{13,12},{... | collective-permute-start | bytes 46088 | tf_op jit(solution)/shard_map/ppermute | solution.py:19
  77.0 5.1 %collective-permute-start.7 = (bf16[1,768,10,1]{1,3,2,0:T(2,128)(2,1)S(1)}, bf16[1,768,10,1]{1,3,2,0:T(2,128)(2,1)S(1)}, u32[]{:S(2)}, u32[]{:S(2)}) collective-permute-start(bf16[1,768,10,1]{1,3,2,0:T(2,128)(2,1)S(1)} %get-tuple-element.73), channel_id=1, source_target_pairs={{0,1},{1,2},{2,3},{4,5},{5,6},{6,7},{8,9},{9,10},{10,11},{12,13},{... | collective-permute-start | bytes 46088 | tf_op jit(solution)/shard_map/ppermute | solution.py:18
  82.1 1.9 %copy-start.4 = (f32[8,128,768]{2,1,0:T(8,128)S(1)}, f32[8,128,768]{2,1,0:T(8,128)}, u32[]{:S(2)}) copy-start(f32[8,128,768]{2,1,0:T(8,128)} %get-tuple-element.87) | copy-start | bytes 9437188
  89.6 1.2 copy-start.19
  90.8 2.7 %copy-start.9 = (bf16[1,192,8,128]{3,2,1,0:T(8,128)(2,1)S(1)}, bf16[1,192,8,128]{3,2,1,0:T(8,128)(2,1)}, u32[]{:S(2)}) copy-start(bf16[1,192,8,128]{3,2,1,0:T(8,128)(2,1)} %param.8) | copy-start | bytes 1179652
  90.8 3.4 %copy-start.14 = (f32[6,128,192,1]{1,2,3,0:T(8,128)S(1)}, f32[6,128,192,1]{1,2,3,0:T(8,128)}, u32[]{:S(2)}) copy-start(f32[6,128,192,1]{1,2,3,0:T(8,128)} %fusion.38) | copy-start | bytes 1769476
  95.7 38.9 %copy-start.3 = (bf16[1,768,8,128]{1,3,2,0:T(8,128)(2,1)S(1)}, bf16[1,768,8,128]{1,3,2,0:T(8,128)(2,1)}, u32[]{:S(2)}) copy-start(bf16[1,768,8,128]{1,3,2,0:T(8,128)(2,1)} %get-tuple-element.69) | copy-start | bytes 4718596
  95.7 29.8 %all-to-all-start.1 = ((f32[32,80,128]{2,1,0:T(8,128)}), f32[32,80,128]{2,1,0:T(8,128)S(1)}, u32[]{:S(2)}, u32[]{:S(2)}) async-start(f32[32,80,128]{2,1,0:T(8,128)} %maximum_maximum_fusion.2), calls=%async_computation.1 | async-start | bytes 2621440 | tf_op jit(solution)/shard_map/all_to_all | solution.py:132
  125.6 11.8 %copy-start.10 = (bf16[1,192,8,128]{3,2,1,0:T(8,128)(2,1)S(1)}, bf16[1,192,8,128]{3,2,1,0:T(8,128)(2,1)}, u32[]{:S(2)}) copy-start(bf16[1,192,8,128]{3,2,1,0:T(8,128)(2,1)} %param.8) | copy-start | bytes 1179652
  125.6 11.8 %copy-start.17 = (bf16[1,192,8,128]{3,2,1,0:T(8,128)(2,1)S(1)}, bf16[1,192,8,128]{3,2,1,0:T(8,128)(2,1)}, u32[]{:S(2)}) copy-start(bf16[1,192,8,128]{3,2,1,0:T(8,128)(2,1)} %param.15) | copy-start | bytes 1179652
  126.4 22.3 %all-to-all-start.2 = ((f32[8,96,128]{2,1,0:T(8,128)}), f32[8,96,128]{2,1,0:T(8,128)S(1)}, u32[]{:S(2)}, u32[]{:S(2)}) async-start(f32[8,96,128]{2,1,0:T(8,128)} %broadcast_in_dim.21), calls=%async_computation.2 | async-start | bytes 786432 | tf_op jit(solution)/shard_map/all_to_all | solution.py:54
  134.6 2.8 %copy-start.11 = (f32[1,192,8,128]{3,1,2,0:T(8,128)S(1)}, f32[1,192,8,128]{3,1,2,0:T(8,128)}, u32[]{:S(2)}) copy-start(f32[1,192,8,128]{3,1,2,0:T(8,128)} %get-tuple-element.89) | copy-start | bytes 2359300
  149.7 18.4 %all-to-all-start.3 = ((bf16[32,80,128]{2,1,0:T(8,128)(2,1)}), bf16[32,80,128]{2,1,0:T(8,128)(2,1)S(1)}, u32[]{:S(2)}, u32[]{:S(2)}) async-start(bf16[32,80,128]{2,1,0:T(8,128)(2,1)} %broadcast_in_dim.45), calls=%async_computation.3 | async-start | bytes 1310720 | tf_op jit(solution)/shard_map/all_to_all | solution.py:54

commit v2 on v0

v2 whole, which is shorter than its diff:
```python
import functools

import jax
import jax.numpy as jnp
from jax import lax
from jax.experimental import pallas as pl
from jax.experimental.pallas import tpu as pltpu
from jax.sharding import PartitionSpec as P

EPS = 1e-06
HIGH = lax.Precision.HIGHEST
RC = ("row", "col")
F32, BF16 = jnp.float32, jnp.bfloat16
CH, EX, SQ = 192, 768, 48
ROWS, LANES = 8, 128
EB = 128
SUB = 8
STEPS = EX // EB
XS = ROWS + 5
CS = ROWS + 3
NT = (((1,), (1,)), ((), ()))


def lane_iota(rows):
    return lax.broadcasted_iota(jnp.int32, (rows, LANES), 1)


def rounded(v):
    return v.astype(BF16).astype(F32)


def sigmoid(v):
    return 0.5 + 0.5 * jnp.tanh(0.5 * v)


def slab(s, n=1):
    return pl.ds(s * LANES, n * LANES)


def strip_kernel(x_ref, c_ref, top_ref, bot_ref, out_ref):
    lane = lane_iota(CH)
    total = jnp.zeros((CH, LANES), F32)
    for rr in range(ROWS + 4):
        if rr < 2:
            v = top_ref[rr]
        elif rr < ROWS + 2:
            v = x_ref[rr - 2]
        else:
            v = bot_ref[rr - ROWS - 2]
        v = pltpu.roll(v.astype(F32), (8 * rr + 2) % LANES, 1)
        total = jnp.where((lane >= 8 * rr) & (lane < 8 * rr + 4), v, total)
        if 1 <= rr <= ROWS + 2:
            if rr == 1:
                v = top_ref[2]
            elif rr == ROWS + 2:
                v = bot_ref[2]
            else:
                v = c_ref[rr - 2]
            v = pltpu.roll(v.astype(F32), (8 * rr + 5) % LANES, 1)
            total = jnp.where((lane >= 8 * rr + 4) & (lane < 8 * rr + 6), v, total)
    out_ref[...] = total.astype(BF16)


def input_strip(own_ref, left_ref, right_ref):
    own, left, right = (r[...].astype(F32) for r in (own_ref, left_ref, right_ref))
    pos = lane_iota(CH) % 8
    value = jnp.where(pos < 2, left, 0.0)
    value = jnp.where(pos == 2, own, value)
    value = jnp.where(pos == 4, pltpu.roll(own, 3, 1), value)
    return jnp.where((pos == 5) | (pos == 6), pltpu.roll(right, 3, 1), value)


def cotangent_strip(left_ref, right_ref):
    left, right = (r[...].astype(F32) for r in (left_ref, right_ref))
    pos = lane_iota(CH) % 8
    value = jnp.where(pos == 1, pltpu.roll(left, LANES - 3, 1), 0.0)
    return jnp.where(pos == 5, right, value)


def neighbours(v, strip, rr, first, last):
    left = jnp.where(first, pltpu.roll(strip, (LANES - 8 * rr - 1) % LANES, 1), pltpu.roll(v, 1, 1))
    right = jnp.where(
        last,
        pltpu.roll(strip, (LANES - 1 - 8 * rr - 5) % LANES, 1),
        pltpu.roll(v, LANES - 1, 1),
    )
    return left, right


def forward_kernel(
    x_ref, c_ref, top_ref, bot_ref, own_ref, left_ref, right_ref, gain_ref, wexp_ref, taps_ref,
    wproj_ref, pre_out, conv_out, sums_out, scaled_s, cot_s, pre_s, gg_s, acc_s,
):
    @pl.when(pl.program_id(0) == 0)
    def _():
        gain = gain_ref[...]
        for s in range(XS):
            if s < 2:
                x = top_ref[s].astype(F32)
            elif s < ROWS + 2:
                x = x_ref[s - 2].astype(F32)
            elif s < ROWS + 4:
                x = bot_ref[s - ROWS - 2].astype(F32)
            else:
                x = input_strip(own_ref, left_ref, right_ref)
            inverse = lax.rsqrt(jnp.sum(x * x, axis=0, keepdims=True) / CH + EPS)
            scaled_s[:, slab(s)] = (x * inverse * gain).astype(BF16)
        for r in range(ROWS):
            cot_s[:, slab(r)] = c_ref[r]

    pre_s[...] = jnp.dot(wexp_ref[...], scaled_s[...], preferred_element_type=F32)
    gg_s[...] = jnp.dot(wproj_ref[...], cot_s[...], preferred_element_type=F32)
    pre_out[...] = pre_s[:, slab(2, ROWS)]
    lane = lane_iota(SUB)
    first, last = lane == 0, lane == LANES - 1

    def body(i, carry):
        ds = pl.ds(pl.multiple_of(i * SUB, SUB), SUB)
        k = [jnp.broadcast_to(taps_ref[ds, t : t + 1], (SUB, LANES)) for t in range(9)]

        def hidden(s):
            v = pre_s[ds, slab(s)]
            return rounded(v * sigmoid(v))

        strip = hidden(XS - 1)
        acc = [None] * (ROWS + 4)
        for rr in range(ROWS + 4):
            h = hidden(rr)
            hl, hr = neighbours(h, strip, rr, first, last)
            for a in (-1, 0, 1):
                o = rr - a
                if 1 <= o <= ROWS + 2:
                    t = 3 * (a + 1)
                    term = k[t] * hl + k[t + 1] * h + k[t + 2] * hr
                    acc[o] = term if acc[o] is None else acc[o] + term
        pooled = jnp.zeros((SUB, LANES), F32)
        gexc = jnp.zeros((SUB, LANES), F32)
        for o in range(1, ROWS + 3):
            v = acc[o]
            conv_out[ds, slab(o - 1)] = v
            if 2 <= o <= ROWS + 1:
                act = v * sigmoid(v)
                pooled = pooled + act
                gexc = gexc + act * gg_s[ds, slab(o - 2)]
        edge = None
        for a in (-1, 0, 1):
            for c in (-1, 0, 1):
                shift = (-(8 * a + c)) % LANES
                term = k[3 * (a + 1) + c + 1] * (pltpu.roll(strip, shift, 1) if shift else strip)
                edge = term if edge is None else edge + term
        conv_out[ds, slab(CS - 1)] = edge
        acc_s[0, ds, :] = pooled
        acc_s[1, ds, :] = gexc
        return carry

    lax.fori_loop(0, EB // SUB, body, 0)
    ones = jnp.ones((8, LANES), F32)
    for n in range(2):
        row = lax.dot_general(ones, acc_s[n], NT, precision=HIGH, preferred_element_type=F32)
        sums_out[0, n : n + 1, :] = row[:1]


def squeeze_kernel(parts_ref, wsq_ref, wexc_ref, exc_out, gp_out, vec_out):
    pixels = 32768.0
    total = jnp.sum(parts_ref[...], axis=0)
    pooled = jnp.concatenate([total[2 * j : 2 * j + 1] for j in range(STEPS)], axis=1) / pixels
    gexc = jnp.concatenate([total[2 * j + 1 : 2 * j + 2] for j in range(STEPS)], axis=1)
    pooled = jnp.broadcast_to(pooled, (8, EX))
    gexc = jnp.broadcast_to(gexc, (8, EX))
    wsq, wexc = wsq_ref[...], wexc_ref[...]
    spre = jnp.dot(pooled, wsq, precision=HIGH, preferred_element_type=F32)
    sig = jax.nn.sigmoid(spre)
    squeezed = spre * sig
    epre = jnp.dot(squeezed, wexc, precision=HIGH, preferred_element_type=F32)
    excite = jax.nn.sigmoid(epre)
    gepre = gexc * excite * (1.0 - excite)
    gspre = lax.dot_general(gepre, wexc, NT, precision=HIGH, preferred_element_type=F32)
    gspre = gspre * (sig * (1.0 + spre * (1.0 - sig)))
    gpool = lax.dot_general(gspre, wsq, NT, precision=HIGH, preferred_element_type=F32)
    gpool = gpool / pixels
    vec_out[...] = jnp.zeros((16, LANES), F32)
    for j in range(STEPS):
        cols = slice(j * LANES, (j + 1) * LANES)
        exc_out[cols, :] = jnp.broadcast_to(excite[:1, cols], (LANES, LANES)).T
        gp_out[cols, :] = jnp.broadcast_to(gpool[:1, cols], (LANES, LANES)).T
        vec_out[j : j + 1, :] = pooled[:1, cols]
        vec_out[STEPS + j : STEPS + j + 1, :] = gepre[:1, cols]
    vec_out[12:13, :SQ] = squeezed[:1]
    vec_out[13:14, :SQ] = gspre[:1]


def backward_kernel(
    x_ref, c_ref, top_ref, bot_ref, left_ref, right_ref, gain_ref, mask_ref, pre_ref, conv_ref,
    exc_ref, gp_ref, taps_ref, wexp_ref, wproj_ref, wprojt_ref,
    out_out, gin_out, gain_out, wexp_out, wproj_out, taps_out,
    scaled_s, cot_s, inv_s, gg_s, gated_s, gpre_s, proj_s, gs_s, acc_s,
):
    step = pl.program_id(0)

    @pl.when(step == 0)
    def _():
        gain = gain_ref[...]
        for r in range(ROWS):
            x = x_ref[r].astype(F32)
            inverse = lax.rsqrt(jnp.sum(x * x, axis=0, keepdims=True) / CH + EPS)
            inv_s[r : r + 1, :] = inverse
            scaled_s[:, slab(r)] = (x * inverse * gain).astype(BF16)
            cot_s[:, slab(r + 1)] = c_ref[r]
        cot_s[:, slab(0)] = top_ref[2]
        cot_s[:, slab(ROWS + 1)] = bot_ref[2]
        cot_s[:, slab(CS - 1)] = cotangent_strip(left_ref, right_ref).astype(BF16)
        proj_s[...] = jnp.zeros_like(proj_s)
        gs_s[...] = jnp.zeros_like(gs_s)

    gg_s[...] = jnp.dot(wproj_ref[...], cot_s[...], preferred_element_type=F32)
    lane = lane_iota(SUB)
    first, last = lane == 0, lane == LANES - 1

    def body(i, carry):
        ds = pl.ds(pl.multiple_of(i * SUB, SUB), SUB)
        k = [jnp.broadcast_to(taps_ref[ds, t : t + 1], (SUB, LANES)) for t in range(9)]
        exc, gp = exc_ref[ds, :], gp_ref[ds, :]

        def grad_conv(s, mask):
            v = conv_ref[ds, slab(s)]
            sig = sigmoid(v)
            act = v * sig
            if 1 <= s <= ROWS:
                gated_s[ds, slab(s - 1)] = act * exc
            g = (gg_s[ds, slab(s)] * exc + gp) * (sig + act * (1.0 - sig))
            if mask is not None:
                g = jnp.where(mask_ref[mask : mask + 1, :] > 0.5, g, 0.0)
            return rounded(g)

        def hidden(r):
            v = pre_ref[ds, slab(r)]
            sig = sigmoid(v)
            act = v * sig
            return rounded(act), sig + act * (1.0 - sig)

        strip = grad_conv(CS - 1, 2)
        tap = [None] * 9
        state = {}
        gh = {}
        for s in range(ROWS + 2):
            g = grad_conv(s, 0 if s == 0 else 1 if s == ROWS + 1 else None)
            gl, gr = neighbours(g, strip, s + 1, first, last)
            for a in (-1, 0, 1):
                r = s + a - 1
                if 0 <= r < ROWS:
                    if r not in state:
                        state[r] = hidden(r)
                    h = state[r][0]
                    t = 3 * (a + 1)
                    term = k[t] * gr + k[t + 1] * g + k[t + 2] * gl
                    gh[r] = term if r not in gh else gh[r] + term
                    for c, v in enumerate((gr, g, gl)):
                        tap[t + c] = h * v if tap[t + c] is None else tap[t + c] + h * v
            r = s - 2
            if 0 <= r:
                gpre_s[ds, slab(r)] = gh.pop(r) * state.pop(r)[1]
        for t in range(9):
            acc_s[t, ds, :] = tap[t]
        return carry

    lax.fori_loop(0, EB // SUB, body, 0)
    gated = gated_s[...].astype(BF16)
    gpre = gpre_s[...].astype(BF16)
    wproj_out[...] = lax.dot_general(
        cot_s[:, slab(1, ROWS)], gated, NT, preferred_element_type=F32
    )
    wexp_out[...] = lax.dot_general(scaled_s[...], gpre, NT, preferred_element_type=F32)
    proj_s[...] += jnp.dot(wprojt_ref[...], gated, preferred_element_type=F32)
    gs_s[...] += jnp.dot(wexp_ref[...], gpre, preferred_element_type=F32)
    ones = jnp.ones((8, LANES), F32)
    for t in range(9):
        row = lax.dot_general(ones, acc_s[t], NT, precision=HIGH, preferred_element_type=F32)
        taps_out[t : t + 1, :] = row[:1]

    @pl.when(step == STEPS - 1)
    def _():
        gain = gain_ref[...]
        ggain = jnp.zeros((CH, LANES), F32)
        for r in range(ROWS):
            x = x_ref[r].astype(F32)
            out_out[r] = (x + proj_s[:, slab(r)]).astype(BF16)
            inverse = inv_s[r : r + 1, :]
            normed = x * inverse
            gs = gs_s[:, slab(r)]
            prod = gs * normed
            ggain = ggain + prod
            mean = jnp.sum(prod * gain, axis=0, keepdims=True) / CH
            gin = inverse * (gs * gain - normed * mean) + c_ref[r].astype(F32)
            gin_out[r] = gin.astype(BF16)
        gain_out[...] = lax.dot_general(
            jnp.ones((8, LANES), F32), ggain, NT, precision=HIGH, preferred_element_type=F32
        )


def shape(*dims, dtype=F32):
    return jax.ShapeDtypeStruct(dims, dtype)


def full(*dims):
    return pl.BlockSpec(dims, lambda j: (0,) * len(dims))


def params():
    return pltpu.CompilerParams(
        dimension_semantics=("arbitrary",), vmem_limit_bytes=40 * 1024 * 1024
    )


def gathered(block, axes, count):
    return lax.all_to_all(
        jnp.broadcast_to(block[None], (count,) + block.shape), axes, 0, 0, tiled=True
    )


def exponent(v):
    return jnp.ceil(jnp.log2(jnp.maximum(jnp.max(jnp.abs(v)), 1e-30)))


def local(inputs, norm_gain, w_expand, kernel, w_squeeze, w_excite, w_project, cotangent):
    nrow, ncol = lax.axis_size("row"), lax.axis_size("col")
    row, col = lax.axis_index("row"), lax.axis_index("col")
    x = inputs[0].transpose(1, 0, 2)
    c = cotangent[0].transpose(1, 0, 2)
    fwd_row = [(i, i + 1) for i in range(nrow - 1)]
    bwd_row = [(i + 1, i) for i in range(nrow - 1)]
    fwd_col = [(i, i + 1) for i in range(ncol - 1)]
    bwd_col = [(i + 1, i) for i in range(ncol - 1)]
    top = lax.ppermute(jnp.concatenate([x[6:8], c[7:8]], axis=0), "row", fwd_row)
    bot = lax.ppermute(jnp.concatenate([x[0:2], c[0:1]], axis=0), "row", bwd_row)
    own = pl.pallas_call(strip_kernel, out_shape=shape(CH, LANES, dtype=BF16), name="strip")(
        x, c, top, bot
    )
    left = lax.ppermute(own, "col", fwd_col)
    right = lax.ppermute(own, "col", bwd_col)

    lane = jnp.arange(LANES)
    line, pos = lane // 8, lane % 8
    top_ok, bot_ok = row > 0, row < nrow - 1
    strip_ok = ((pos == 1) & (col > 0)) | ((pos == 5) & (col < ncol - 1))
    strip_ok &= ((line > 1) | top_ok) & ((line < ROWS + 2) | bot_ok)
    mask = jnp.stack(
        [jnp.broadcast_to(top_ok, (LANES,)), jnp.broadcast_to(bot_ok, (LANES,)), strip_ok]
        + [jnp.zeros((LANES,), bool)] * 5
    ).astype(F32)
    gain = norm_gain[:, None]
    wexpt, wprojt = w_expand.T, w_project.T
    halo = full(3, CH, LANES)
    tile = full(ROWS, CH, LANES)
    edge = full(CH, LANES)
    chunk_rows = lambda width: pl.BlockSpec((EB, width), lambda j: (j, 0))
    chunk_cols = pl.BlockSpec((CH, EB), lambda j: (0, j))
    pre, conv, sums = pl.pallas_call(
        forward_kernel,
        grid=(STEPS,),
        in_specs=[tile, tile, halo, halo, edge, edge, edge, full(CH, 1),
                  chunk_rows(CH), chunk_rows(9), chunk_rows(CH)],
        out_specs=[chunk_rows(ROWS * LANES), chunk_rows(CS * LANES),
                   pl.BlockSpec((1, 2, LANES), lambda j: (j, 0, 0))],
        out_shape=[shape(EX, ROWS * LANES), shape(EX, CS * LANES), shape(STEPS, 2, LANES)],
        scratch_shapes=[
            pltpu.VMEM((CH, XS * LANES), BF16),
            pltpu.VMEM((CH, ROWS * LANES), BF16),
            pltpu.VMEM((EB, XS * LANES), F32),
            pltpu.VMEM((EB, ROWS * LANES), F32),
            pltpu.VMEM((2, EB, LANES), F32),
        ],
        compiler_params=params(),
        name="forward",
    )(x, c, top, bot, own, left, right, gain, wexpt, kernel, w_project)

    exc, gp, vec = pl.pallas_call(
        squeeze_kernel,
        out_shape=[shape(EX, LANES), shape(EX, LANES), shape(16, LANES)],
        name="squeeze",
    )(gathered(sums.reshape(2 * STEPS, LANES), RC, 32), w_squeeze, w_excite)

    out, gin, ggain, wexp, wproj, taps = pl.pallas_call(
        backward_kernel,
        grid=(STEPS,),
        in_specs=[tile, tile, halo, halo, edge, edge, full(CH, 1), full(8, LANES),
                  chunk_rows(ROWS * LANES), chunk_rows(CS * LANES), chunk_rows(LANES),
                  chunk_rows(LANES), chunk_rows(9), chunk_cols, chunk_rows(CH), chunk_cols],
        out_specs=[tile, tile, full(8, CH), pl.BlockSpec((CH, EB), lambda j: (j, 0)),
                   pl.BlockSpec((CH, EB), lambda j: (j, 0)),
                   pl.BlockSpec((9, EB), lambda j: (0, j))],
        out_shape=[shape(ROWS, CH, LANES, dtype=BF16), shape(ROWS, CH, LANES, dtype=BF16),
                   shape(8, CH), shape(STEPS * CH, EB), shape(STEPS * CH, EB), shape(9, EX)],
        scratch_shapes=[
            pltpu.VMEM((CH, ROWS * LANES), BF16),
            pltpu.VMEM((CH, CS * LANES), BF16),
            pltpu.VMEM((ROWS, LANES), F32),
            pltpu.VMEM((EB, CS * LANES), F32),
            pltpu.VMEM((EB, ROWS * LANES), F32),
            pltpu.VMEM((EB, ROWS * LANES), F32),
            pltpu.VMEM((CH, ROWS * LANES), F32),
            pltpu.VMEM((CH, ROWS * LANES), F32),
            pltpu.VMEM((9, EB, LANES), F32),
        ],
        compiler_params=params(),
        name="backward",
    )(x, c, top, bot, left, right, gain, mask, pre, conv, exc, gp, kernel, w_expand, w_project,
      wprojt)

    big = jnp.concatenate([wexp, wproj], axis=0).reshape(32, 72, 128)
    small = jnp.concatenate(
        [taps.reshape(6912), ggain[0], jnp.zeros((1088,), F32)]
    ).reshape(32, 2, 128)
    packed = jnp.concatenate([big, small, jnp.zeros((32, 6, 128), F32)], axis=1)
    mine = jnp.sum(lax.all_to_all(packed, RC, 0, 0, tiled=True), axis=0)
    shared = gathered(jnp.concatenate([mine, vec], axis=0), "dp", 8)
    total = jnp.sum(shared[:, :80], axis=0)
    vecs = shared[:, 80:].reshape(8, 2048)
    grad_wexc = jnp.einsum("bs,be->se", vecs[:, 1536:1584], vecs[:, 768:1536], precision=HIGH)
    grad_wsq = jnp.einsum("be,bs->es", vecs[:, :768], vecs[:, 1664:1712], precision=HIGH)
    e_big, e_small = exponent(total[:72]), exponent(total[72:74])
    send = jnp.concatenate(
        [
            total[:72] * jnp.exp2(-e_big),
            total[72:74] * jnp.exp2(-e_small),
            jnp.full((3, 128), e_big),
            jnp.full((3, 128), e_small),
        ],
        axis=0,
    ).astype(jnp.float16)
    every = gathered(send, RC, 32).astype(F32)
    big = (every[:, :72] * jnp.exp2(every[:, 74:75])).reshape(2, STEPS, CH, EB)
    small = (every[:, 72:74] * jnp.exp2(every[:, 77:78])).reshape(8192)
    return (
        out.transpose(1, 0, 2)[None],
        gin.transpose(1, 0, 2)[None],
        small[6912:7104],
        big[0].transpose(1, 0, 2).reshape(CH, EX),
        small[:6912].reshape(9, 768).T,
        grad_wsq,
        grad_wexc,
        big[1].transpose(0, 2, 1).reshape(EX, CH),
    )


def solution(mesh):
    placed = (
        P("dp", None, "row", "col"),
        P(),
        P(),
        P(),
        P(),
        P(),
        P(),
        P("dp", None, "row", "col"),
    )
    return jax.shard_map(
        local,
        mesh=mesh,
        in_specs=placed,
        out_specs=(
            P("dp", None, "row", "col"),
            P("dp", None, "row", "col"),
            P(),
            P(),
            P(),
            P(),
            P(),
            P(),
        ),
        check_vma=False,
    )
```

time: 488 us -> 183 us (0.38)
  waiting for transfers between devices: 259 us -> 36.4 us
  blocking collectives: 140 us -> 24.4 us
  Pallas kernels: 0 us -> 47.8 us
  matrix products: 21.3 us -> 1.97 us
  local copies, waits for them, and re-layouts: 12.4 us -> 27.5 us
  starting transfers between devices: 23.5 us -> 38.4 us
  other arithmetic: 15.1 us -> 3 us
  between operations: 14.5 us -> 2.58 us
    psum x2 -> x0, waiting for transfers between devices: 245 us -> none  [the longest x1 245 us: local(): lax.psum((grad_gain, grad_wexp, grad_kernel, grad_project), ('dp', 'row',...]
    psum x2 -> x0, blocking collectives: 140 us -> none  [the longest x1 79 us: local(): lax.psum((grad_gain, grad_wexp, grad_kernel, grad_project), ('dp', 'row',...]
    pallas_call x0 -> x4, Pallas kernels: none -> 47.8 us  [the longest x1 25 us: local(): pl.pallas_call(backward_kernel, grid=(STEPS,), in_specs=[tile, tile, halo...]
    all_to_all x0 -> x3, waiting for transfers between devices: none -> 31.3 us  [gathered(): lax.all_to_all(jnp.broadcast_to(block[None], (count,) + block.shape), axe...]
    all_to_all x0 -> x3, starting transfers between devices: none -> 24.9 us  [gathered(): lax.all_to_all(jnp.broadcast_to(block[None], (count,) + block.shape), axe...]
    all_to_all x0 -> x1, blocking collectives: none -> 24.4 us  [local(): mine = jnp.sum(lax.all_to_all(packed, RC, 0, 0, tiled=True), axis=0)]
    dot_general x10 -> x2, matrix products: 21.3 us -> 1.97 us  [the longest x1 0.99 us: local(): jnp.einsum('be,bs->es', vecs[:, :768], vecs[:, 1664:1712], precision=HIGH)]
    ppermute x8 -> x4, starting transfers between devices: 23.2 us -> 13.5 us  [the longest x1 5.42 us: local(): left = lax.ppermute(own, 'col', fwd_col)]
  transfers between devices with their start and end apart: 10 -> 7, of which waited for: 6 -> 6; matrix products, arithmetic and copies ran while one was open for 3% -> 3% of each run, Pallas kernels for 0% -> 0%
where the time goes in v2:
time: 183 us; the launch traced here: 182 us
  Pallas kernels  47.8 us (26%)
  starting transfers between devices  38.4 us (21%)
  waiting for transfers between devices  36.4 us (20%)
  local copies, waits for them, and re-layouts  27.5 us (15%)
  blocking collectives  24.4 us (13%)
  other arithmetic  3 us (2%)
  between operations  2.58 us (1%)
  matrix products  1.97 us (1%)
    all_to_all x3, waiting for transfers between devices, gathered(): lax.all_to_all(jnp.broadcast_to(block[None], (count,) + block.shape), axe...  31.3 us
    pallas_call x1, Pallas kernels, local(): pl.pallas_call(backward_kernel, grid=(STEPS,), in_specs=[tile, tile, halo...  25 us
    all_to_all x3, starting transfers between devices, gathered(): lax.all_to_all(jnp.broadcast_to(block[None], (count,) + block.shape), axe...  24.9 us
    all_to_all x1, blocking collectives, local(): mine = jnp.sum(lax.all_to_all(packed, RC, 0, 0, tiled=True), axis=0)  24.4 us
    unnamed x69, local copies, waits for them, and re-layouts  20 us
    pallas_call x1, Pallas kernels, local(): pl.pallas_call(forward_kernel, grid=(STEPS,), in_specs=[tile, tile, halo,...  17.3 us
    ppermute x1, starting transfers between devices, local(): left = lax.ppermute(own, 'col', fwd_col)  5.42 us
    ppermute x1, starting transfers between devices, local(): lax.ppermute(jnp.concatenate([x[6:8], c[7:8]], axis=0), 'row', fwd_row)  4.7 us
  transfers between devices with their start and end apart: 7, of which 6 were waited for; matrix products, arithmetic and copies ran while one was open for 3% of the time, Pallas kernels for 0%

profile of v2, /device:TPU:1, one launch (start us, length us, event | category | flops | bytes accessed | tf_op | source)
XLA Modules:
  0.0 182.0 jit_solution(1265196221915798449)
XLA Ops:
  0.6 1.3 copy_bitcast_fusion.2
  2.0 1.4 collective-permute-start.1
  3.5 4.7 %collective-permute-start = (bf16[3,192,128]{2,1,0:T(8,128)(2,1)S(1)}, bf16[3,192,128]{2,1,0:T(8,128)(2,1)S(1)}, u32[]{:S(2)}, u32[]{:S(2)}) collective-permute-start(bf16[3,192,128]{2,1,0:T(8,128)(2,1)S(1)} %pad_maximum_fusion.1), channel_id=1, source_target_pairs={{0,4},{4,8},{8,12},{12,16},{16,20},{20,24},{24,28},{1,5},{5,9},{9,... | collective-permute-start | bytes 442376 | tf_op jit(solution)/shard_map/ppermute | solution.py:333
  8.6 1.7 collective-permute-done.top_ref
  10.9 2.2 %strip.1.own_ref = bf16[192,128]{1,0:T(8,128)(2,1)} custom-call(bf16[8,192,128]{2,1,0:T(8,128)(2,1)} %copy-done, bf16[8,192,128]{2,1,0:T(8,128)(2,1)} %copy-done.2, bf16[3,192,128]{2,1,0:T(8,128)(2,1)} %copy-done.10, bf16[3,192,128]{2,1,0:T(8,128)(2,1)} %copy-done.8), custom_call_target="tpu_custom_call" | custom-call | tf_op jit(solution)/shard_map/strip/pallas_call | solution.py:335
  13.1 5.4 %collective-permute-start.2 = (bf16[192,128]{1,0:T(8,128)(2,1)}, bf16[192,128]{1,0:T(8,128)(2,1)S(1)}, u32[]{:S(2)}, u32[]{:S(2)}) collective-permute-start(bf16[192,128]{1,0:T(8,128)(2,1)} %strip.1.own_ref), channel_id=1, source_target_pairs={{0,1},{1,2},{2,3},{4,5},{5,6},{6,7},{8,9},{9,10},{10,11},{12,13},{... | collective-permute-start | bytes 147464 | tf_op jit(solution)/shard_map/ppermute | solution.py:338
  18.6 1.9 %collective-permute-start.3 = (bf16[192,128]{1,0:T(8,128)(2,1)}, bf16[192,128]{1,0:T(8,128)(2,1)S(1)}, u32[]{:S(2)}, u32[]{:S(2)}) collective-permute-start(bf16[192,128]{1,0:T(8,128)(2,1)} %strip.1.own_ref), channel_id=1, source_target_pairs={{1,0},{2,1},{3,2},{5,4},{6,5},{7,6},{9,8},{10,9},{11,10},{13,12},{... | collective-permute-start | bytes 147464 | tf_op jit(solution)/shard_map/ppermute | solution.py:339
  21.2 3.0 %collective-permute-done.3.right_ref = bf16[192,128]{1,0:T(8,128)(2,1)S(1)} collective-permute-done((bf16[192,128]{1,0:T(8,128)(2,1)}, bf16[192,128]{1,0:T(8,128)(2,1)S(1)}, u32[]{:S(2)}, u32[]{:S(2)}) %collective-permute-start.3) | collective-permute-done | bytes 49184 | tf_op jit(solution)/shard_map/ppermute | solution.py:339
  24.2 17.3 %forward.1 = (f32[768,1024]{1,0:T(8,128)S(1)}, f32[768,1408]{1,0:T(8,128)S(1)}, f32[6,2,128]{2,1,0:T(2,128)S(1)}) custom-call(bf16[8,192,128]{2,1,0:T(8,128)(2,1)S(1)} %copy-done.1, bf16[8,192,128]{2,1,0:T(8,128)(2,1)S(1)} %copy-done.3, bf16[3,192,128]{2,1,0:T(8,128)(2,1)S(1)} %copy-done.11, bf16[3,192,128]{2,1,0:T(8,128)(2,1)S(1)} %copy-done.9, ...), custom_call_target="tpu_custom_call" | custom-call | tf_op jit(solution)/shard_map/forward/pallas_call | solution.py:357
  41.5 2.0 %copy-done.4 = f32[768,1408]{1,0:T(8,128)} copy-done((f32[768,1408]{1,0:T(8,128)}, f32[768,1408]{1,0:T(8,128)S(1)}, u32[]{:S(2)}) %copy-start.4) | copy-done | bytes 4325400
  43.5 1.6 copy-done.6
  45.9 11.9 %all-to-all-start = ((f32[32,12,128]{2,1,0:T(8,128)}), f32[32,12,128]{2,1,0:T(8,128)S(1)}, u32[]{:S(2)}, u32[]{:S(2)}) async-start(f32[32,12,128]{2,1,0:T(8,128)} %broadcast_in_dim.42), calls=%async_computation | async-start | bytes 524288 | tf_op jit(solution)/shard_map/all_to_all | solution.py:315
  57.9 0.9 copy.47.wsq_ref
  59.0 7.7 %all-to-all-done.parts_ref = f32[32,12,128]{2,1,0:T(8,128)S(1)} async-done(((f32[32,12,128]{2,1,0:T(8,128)}), f32[32,12,128]{2,1,0:T(8,128)S(1)}, u32[]{:S(2)}, u32[]{:S(2)}) %all-to-all-start) | async-done | bytes 196640 | tf_op jit(solution)/shard_map/all_to_all | solution.py:315
  67.4 3.4 %squeeze.21 = (f32[768,128]{1,0:T(8,128)}, f32[768,128]{1,0:T(8,128)}, f32[16,128]{1,0:T(8,128)}) custom-call(f32[32,12,128]{2,1,0:T(8,128)} %copy-done.25, f32[768,48]{1,0:T(8,128)} %copy.47.wsq_ref, f32[48,768]{1,0:T(8,128)} %wexc_ref.1), custom_call_target="tpu_custom_call" | custom-call | tf_op jit(solution)/shard_map/squeeze/pallas_call | solution.py:376
  70.8 2.2 %copy-done.5 = f32[768,1408]{1,0:T(8,128)S(1)} copy-done((f32[768,1408]{1,0:T(8,128)S(1)}, f32[768,1408]{1,0:T(8,128)}, u32[]{:S(2)}) %copy-start.5) | copy-done | bytes 4325400
  73.0 1.9 %copy-done.7 = f32[768,1024]{1,0:T(8,128)S(1)} copy-done((f32[768,1024]{1,0:T(8,128)S(1)}, f32[768,1024]{1,0:T(8,128)}, u32[]{:S(2)}) %copy-start.7) | copy-done | bytes 3145752
  74.9 1.0 copy-done.15
  75.9 1.0 copy-done.16
  78.5 25.0 %backward.1 = (bf16[8,192,128]{2,1,0:T(8,128)(2,1)S(1)}, bf16[8,192,128]{2,1,0:T(8,128)(2,1)S(1)}, f32[8,192]{1,0:T(8,128)S(1)}, f32[1152,128]{1,0:T(8,128)S(1)}...) custom-call(bf16[8,192,128]{2,1,0:T(8,128)(2,1)S(1)} %copy-done.1, bf16[8,192,128]{2,1,0:T(8,128)(2,1)S(1)} %copy-done.3, ...), custom_call_target="tpu_custom_call" | custom-call | tf_op jit(solution)/shard_map/backward/pallas_call | solution.py:382
  106.5 1.1 pad_maximum_fusion
  107.9 24.4 %all_to_all.20 = f32[32,80,128]{2,1,0:T(8,128)S(1)} all-to-all(f32[32,80,128]{2,1,0:T(8,128)S(1)} %maximum_maximum_fusion), channel_id=1, replica_groups=mesh['dp'=8,'row'=8,'col'=4] {'row','col'}, dimensions={0} | all-to-all | bytes 2621440 | tf_op jit(solution)/shard_map/all_to_all | solution.py:414
  133.7 8.2 %all-to-all-start.2 = ((f32[8,96,128]{2,1,0:T(8,128)}), f32[8,96,128]{2,1,0:T(8,128)S(1)}, u32[]{:S(2)}, u32[]{:S(2)}) async-start(f32[8,96,128]{2,1,0:T(8,128)} %broadcast_in_dim.47), calls=%async_computation.2 | async-start | bytes 786432 | tf_op jit(solution)/shard_map/all_to_all | solution.py:315
  141.9 1.0 copy.53
  142.9 1.0 copy.54
  143.9 12.4 %all-to-all-done.2 = f32[8,96,128]{2,1,0:T(8,128)S(1)} async-done(((f32[8,96,128]{2,1,0:T(8,128)}), f32[8,96,128]{2,1,0:T(8,128)S(1)}, u32[]{:S(2)}, u32[]{:S(2)}) %all-to-all-start.2) | async-done | bytes 393248 | tf_op jit(solution)/shard_map/all_to_all | solution.py:315
  159.3 0.9 broadcast_in_dim.50
  160.3 4.8 %all-to-all-start.3 = ((f16[32,80,128]{2,1,0:T(8,128)(2,1)}), f16[32,80,128]{2,1,0:T(8,128)(2,1)S(1)}, u32[]{:S(2)}, u32[]{:S(2)}) async-start(f16[32,80,128]{2,1,0:T(8,128)(2,1)} %broadcast_in_dim.50), calls=%async_computation.3 | async-start | bytes 1310720 | tf_op jit(solution)/shard_map/all_to_all | solution.py:315
  165.1 1.0 fusion
  166.1 1.0 fusion.2
  167.1 11.2 %all-to-all-done.3 = f16[32,80,128]{2,1,0:T(8,128)(2,1)S(1)} async-done(((f16[32,80,128]{2,1,0:T(8,128)(2,1)}), f16[32,80,128]{2,1,0:T(8,128)(2,1)S(1)}, u32[]{:S(2)}, u32[]{:S(2)}) %all-to-all-start.3) | async-done | bytes 655392 | tf_op jit(solution)/shard_map/all_to_all | solution.py:315
  179.0 0.9 copy.63
  (105 shorter events, 14.0 us)
Async XLA Ops:
  1.9 8.4 %copy-start = (bf16[8,192,128]{2,1,0:T(8,128)(2,1)}, bf16[8,192,128]{2,1,0:T(8,128)(2,1)S(1)}, u32[]{:S(2)}) copy-start(bf16[8,192,128]{2,1,0:T(8,128)(2,1)S(1)} %get-tuple-element.65.x_ref) | copy-start | bytes 1179652
  1.9 8.4 %copy-start.2 = (bf16[8,192,128]{2,1,0:T(8,128)(2,1)}, bf16[8,192,128]{2,1,0:T(8,128)(2,1)S(1)}, u32[]{:S(2)}) copy-start(bf16[8,192,128]{2,1,0:T(8,128)(2,1)S(1)} %get-tuple-element.64.c_ref) | copy-start | bytes 1179652
  1.9 18.6 %copy-start.27 = (f32[768,9]{0,1:T(8,128)S(1)}, f32[768,9]{0,1:T(8,128)}, u32[]{:S(2)}) copy-start(f32[768,9]{0,1:T(8,128)} %param.11) | copy-start | bytes 82948
  1.9 18.8 %copy-start.13 = (bf16[768,192]{0,1:T(8,128)(2,1)S(1)}, bf16[768,192]{0,1:T(8,128)(2,1)}, u32[]{:S(2)}) copy-start(bf16[768,192]{0,1:T(8,128)(2,1)} %param.14) | copy-start | bytes 884740
  2.0 18.9 %copy-start.29 = (f32[192]{0:T(256)S(1)}, f32[192]{0:T(256)}, u32[]{:S(2)}) copy-start(f32[192]{0:T(256)} %param.9) | copy-start | bytes 2308
  2.0 6.6 %collective-permute-start.1 = (bf16[3,192,128]{2,1,0:T(8,128)(2,1)S(1)}, bf16[3,192,128]{2,1,0:T(8,128)(2,1)S(1)}, u32[]{:S(2)}, u32[]{:S(2)}) collective-permute-start(bf16[3,192,128]{2,1,0:T(8,128)(2,1)S(1)} %pad_maximum_fusion.2), channel_id=1, source_target_pairs={{4,0},{8,4},{12,8},{16,12},{20,16},{24,20},{28,24},{5,1},{9,5},{13... | collective-permute-start | bytes 442376 | tf_op jit(solution)/shard_map/ppermute | solution.py:334
  3.5 17.6 %copy-start.12 = (bf16[192,768]{1,0:T(8,128)(2,1)S(1)}, bf16[192,768]{1,0:T(8,128)(2,1)}, u32[]{:S(2)}) copy-start(bf16[192,768]{1,0:T(8,128)(2,1)} %wexp_ref.1) | copy-start | bytes 884740
  3.5 6.8 %collective-permute-start = (bf16[3,192,128]{2,1,0:T(8,128)(2,1)S(1)}, bf16[3,192,128]{2,1,0:T(8,128)(2,1)S(1)}, u32[]{:S(2)}, u32[]{:S(2)}) collective-permute-start(bf16[3,192,128]{2,1,0:T(8,128)(2,1)S(1)} %pad_maximum_fusion.1), channel_id=1, source_target_pairs={{0,4},{4,8},{8,12},{12,16},{16,20},{20,24},{24,28},{1,5},{5,9},{9,... | collective-permute-start | bytes 442376 | tf_op jit(solution)/shard_map/ppermute | solution.py:333
  8.6 1.7 copy-start.8
  13.1 11.1 %copy-start.1 = (bf16[8,192,128]{2,1,0:T(8,128)(2,1)S(1)}, bf16[8,192,128]{2,1,0:T(8,128)(2,1)}, u32[]{:S(2)}) copy-start(bf16[8,192,128]{2,1,0:T(8,128)(2,1)} %copy-done) | copy-start | bytes 1179652
  13.1 11.1 %copy-start.3 = (bf16[8,192,128]{2,1,0:T(8,128)(2,1)S(1)}, bf16[8,192,128]{2,1,0:T(8,128)(2,1)}, u32[]{:S(2)}) copy-start(bf16[8,192,128]{2,1,0:T(8,128)(2,1)} %copy-done.2) | copy-start | bytes 1179652
  13.1 11.1 %copy-start.9 = (bf16[3,192,128]{2,1,0:T(8,128)(2,1)S(1)}, bf16[3,192,128]{2,1,0:T(8,128)(2,1)}, u32[]{:S(2)}) copy-start(bf16[3,192,128]{2,1,0:T(8,128)(2,1)} %copy-done.8) | copy-start | bytes 442372
  13.1 11.1 %copy-start.11 = (bf16[3,192,128]{2,1,0:T(8,128)(2,1)S(1)}, bf16[3,192,128]{2,1,0:T(8,128)(2,1)}, u32[]{:S(2)}) copy-start(bf16[3,192,128]{2,1,0:T(8,128)(2,1)} %copy-done.10) | copy-start | bytes 442372
  13.1 11.1 %copy-start.23 = (bf16[192,128]{1,0:T(8,128)(2,1)S(1)}, bf16[192,128]{1,0:T(8,128)(2,1)}, u32[]{:S(2)}) copy-start(bf16[192,128]{1,0:T(8,128)(2,1)} %strip.1.own_ref) | copy-start | bytes 147460
  13.1 8.1 %collective-permute-start.2 = (bf16[192,128]{1,0:T(8,128)(2,1)}, bf16[192,128]{1,0:T(8,128)(2,1)S(1)}, u32[]{:S(2)}, u32[]{:S(2)}) collective-permute-start(bf16[192,128]{1,0:T(8,128)(2,1)} %strip.1.own_ref), channel_id=1, source_target_pairs={{0,1},{1,2},{2,3},{4,5},{5,6},{6,7},{8,9},{9,10},{10,11},{12,13},{... | collective-permute-start | bytes 147464 | tf_op jit(solution)/shard_map/ppermute | solution.py:338
  18.6 5.6 %collective-permute-start.3 = (bf16[192,128]{1,0:T(8,128)(2,1)}, bf16[192,128]{1,0:T(8,128)(2,1)S(1)}, u32[]{:S(2)}, u32[]{:S(2)}) collective-permute-start(bf16[192,128]{1,0:T(8,128)(2,1)} %strip.1.own_ref), channel_id=1, source_target_pairs={{1,0},{2,1},{3,2},{5,4},{6,5},{7,6},{9,8},{10,9},{11,10},{13,12},{... | collective-permute-start | bytes 147464 | tf_op jit(solution)/shard_map/ppermute | solution.py:339
  21.2 24.7 %copy-start.19 = (bf16[192,128]{1,0:T(8,128)(2,1)}, bf16[192,128]{1,0:T(8,128)(2,1)S(1)}, u32[]{:S(2)}) copy-start(bf16[192,128]{1,0:T(8,128)(2,1)S(1)} %collective-permute-done.2.left_ref) | copy-start | bytes 147460
  24.2 21.7 %copy-start.21 = (bf16[192,128]{1,0:T(8,128)(2,1)}, bf16[192,128]{1,0:T(8,128)(2,1)S(1)}, u32[]{:S(2)}) copy-start(bf16[192,128]{1,0:T(8,128)(2,1)S(1)} %collective-permute-done.3.right_ref) | copy-start | bytes 147460
  24.2 33.7 %copy-start.26 = (f32[768,48]{0,1:T(8,128)S(1)}, f32[768,48]{0,1:T(8,128)}, u32[]{:S(2)}) copy-start(f32[768,48]{0,1:T(8,128)} %param.12) | copy-start | bytes 442372
  41.5 2.0 %copy-start.4 = (f32[768,1408]{1,0:T(8,128)}, f32[768,1408]{1,0:T(8,128)S(1)}, u32[]{:S(2)}) copy-start(f32[768,1408]{1,0:T(8,128)S(1)} %get-tuple-element.21.conv_ref) | copy-start | bytes 12976132
  43.5 1.6 copy-start.6
  45.9 20.8 %all-to-all-start = ((f32[32,12,128]{2,1,0:T(8,128)}), f32[32,12,128]{2,1,0:T(8,128)S(1)}, u32[]{:S(2)}, u32[]{:S(2)}) async-start(f32[32,12,128]{2,1,0:T(8,128)} %broadcast_in_dim.42), calls=%async_computation | async-start | bytes 524288 | tf_op jit(solution)/shard_map/all_to_all | solution.py:315
  70.8 2.2 %copy-start.5 = (f32[768,1408]{1,0:T(8,128)S(1)}, f32[768,1408]{1,0:T(8,128)}, u32[]{:S(2)}) copy-start(f32[768,1408]{1,0:T(8,128)} %copy-done.4) | copy-start | bytes 12976132
  73.0 1.9 %copy-start.7 = (f32[768,1024]{1,0:T(8,128)S(1)}, f32[768,1024]{1,0:T(8,128)}, u32[]{:S(2)}) copy-start(f32[768,1024]{1,0:T(8,128)} %copy-done.6) | copy-start | bytes 9437188
  74.9 1.0 copy-start.15
  75.9 1.0 copy-start.16
  76.9 0.8 copy-start.20
  77.7 0.8 copy-start.22
  103.5 0.8 copy-start.14
  132.3 9.6 %copy-start.18 = (bf16[8,192,128]{2,1,0:T(8,128)(2,1)S(1)}, bf16[8,192,128]{2,1,0:T(8,128)(2,1)}, u32[]{:S(2)}) copy-start(bf16[8,192,128]{2,1,0:T(8,128)(2,1)} %copy-done.17) | copy-start | bytes 1179652
  133.7 22.6 %all-to-all-start.2 = ((f32[8,96,128]{2,1,0:T(8,128)}), f32[8,96,128]{2,1,0:T(8,128)S(1)}, u32[]{:S(2)}, u32[]{:S(2)}) async-start(f32[8,96,128]{2,1,0:T(8,128)} %broadcast_in_dim.47), calls=%async_computation.2 | async-start | bytes 786432 | tf_op jit(solution)/shard_map/all_to_all | solution.py:315
  160.3 18.0 %all-to-all-start.3 = ((f16[32,80,128]{2,1,0:T(8,128)(2,1)}), f16[32,80,128]{2,1,0:T(8,128)(2,1)S(1)}, u32[]{:S(2)}, u32[]{:S(2)}) async-start(f16[32,80,128]{2,1,0:T(8,128)(2,1)} %broadcast_in_dim.50), calls=%async_computation.3 | async-start | bytes 1310720 | tf_op jit(solution)/shard_map/all_to_all | solution.py:315
  (5 other events, 3.4 us)

commit v3 on v2

--- a/solution.py
+++ b/solution.py
@@ -13,9 +13,10 @@
 F32, BF16 = jnp.float32, jnp.bfloat16
 CH, EX, SQ = 192, 768, 48
 ROWS, LANES = 8, 128
-EB = 128
-SUB = 8
+EB = 256
+SUB = 16
 STEPS = EX // EB
+BLOCKS = EX // LANES
 XS = ROWS + 5
 CS = ROWS + 3
 NT = (((1,), (1,)), ((), ()))
@@ -27,6 +28,10 @@
 
 def rounded(v):
     return v.astype(BF16).astype(F32)
+
+
+def lane_sum(v):
+    return jnp.sum(v, axis=1, keepdims=True)
 
 
 def sigmoid(v):
@@ -64,26 +69,25 @@
 def input_strip(own_ref, left_ref, right_ref):
     own, left, right = (r[...].astype(F32) for r in (own_ref, left_ref, right_ref))
     pos = lane_iota(CH) % 8
-    value = jnp.where(pos < 2, left, 0.0)
-    value = jnp.where(pos == 2, own, value)
-    value = jnp.where(pos == 4, pltpu.roll(own, 3, 1), value)
-    return jnp.where((pos == 5) | (pos == 6), pltpu.roll(right, 3, 1), value)
+    value = jnp.where(pos == 0, pltpu.roll(own, LANES - 1, 1), 0.0)
+    value = jnp.where(pos == 1, pltpu.roll(left, 1, 1), value)
+    value = jnp.where(pos == 2, right, value)
+    value = jnp.where(pos == 3, pltpu.roll(left, 2, 1), value)
+    value = jnp.where(pos == 4, pltpu.roll(right, 1, 1), value)
+    return jnp.where(pos == 5, pltpu.roll(own, 3, 1), value)
 
 
 def cotangent_strip(left_ref, right_ref):
     left, right = (r[...].astype(F32) for r in (left_ref, right_ref))
     pos = lane_iota(CH) % 8
-    value = jnp.where(pos == 1, pltpu.roll(left, LANES - 3, 1), 0.0)
-    return jnp.where(pos == 5, right, value)
+    value = jnp.where(pos == 3, pltpu.roll(left, LANES - 1, 1), 0.0)
+    return jnp.where(pos == 2, pltpu.roll(right, LANES - 3, 1), value)
 
 
 def neighbours(v, strip, rr, first, last):
-    left = jnp.where(first, pltpu.roll(strip, (LANES - 8 * rr - 1) % LANES, 1), pltpu.roll(v, 1, 1))
-    right = jnp.where(
-        last,
-        pltpu.roll(strip, (LANES - 1 - 8 * rr - 5) % LANES, 1),
-        pltpu.roll(v, LANES - 1, 1),
-    )
+    edge = pltpu.roll(strip, (LANES - 8 * rr - 3) % LANES, 1)
+    left = jnp.where(first, edge, pltpu.roll(v, 1, 1))
+    right = jnp.where(last, edge, pltpu.roll(v, LANES - 1, 1))
     return left, right
 
 
@@ -104,23 +108,32 @@
             else:
                 x = input_strip(own_ref, left_ref, right_ref)
             inverse = lax.rsqrt(jnp.sum(x * x, axis=0, keepdims=True) / CH + EPS)
-            scaled_s[:, slab(s)] = (x * inverse * gain).astype(BF16)
+            place = s - 2 if 2 <= s < ROWS + 2 else s + ROWS if s < 2 else s
+            scaled_s[:, slab(place)] = (x * inverse * gain).astype(BF16)
         for r in range(ROWS):
             cot_s[:, slab(r)] = c_ref[r]
 
-    pre_s[...] = jnp.dot(wexp_ref[...], scaled_s[...], preferred_element_type=F32)
+    pre_out[...] = jnp.dot(
+        wexp_ref[...], scaled_s[:, slab(0, ROWS)], preferred_element_type=F32
+    )
+    pre_s[...] = jnp.dot(
+        wexp_ref[...], scaled_s[:, slab(ROWS, XS - ROWS)], preferred_element_type=F32
+    )
     gg_s[...] = jnp.dot(wproj_ref[...], cot_s[...], preferred_element_type=F32)
-    pre_out[...] = pre_s[:, slab(2, ROWS)]
     lane = lane_iota(SUB)
     first, last = lane == 0, lane == LANES - 1
 
     def body(i, carry):
         ds = pl.ds(pl.multiple_of(i * SUB, SUB), SUB)
-        k = [jnp.broadcast_to(taps_ref[ds, t : t + 1], (SUB, LANES)) for t in range(9)]
+        k = [taps_ref[ds, slab(t)] for t in range(9)]
 
         def hidden(s):
-            v = pre_s[ds, slab(s)]
-            return rounded(v * sigmoid(v))
+            if 2 <= s < ROWS + 2:
+                v = pre_out[ds, slab(s - 2)]
+            else:
+                v = pre_s[ds, slab(s if s < 2 else s - ROWS)]
+            v = 0.5 * v
+            return rounded(v + v * jnp.tanh(v))
 
         strip = hidden(XS - 1)
         acc = [None] * (ROWS + 4)
@@ -145,26 +158,23 @@
         edge = None
         for a in (-1, 0, 1):
             for c in (-1, 0, 1):
-                shift = (-(8 * a + c)) % LANES
+                shift = (-(8 * a + 2 * c)) % LANES
                 term = k[3 * (a + 1) + c + 1] * (pltpu.roll(strip, shift, 1) if shift else strip)
                 edge = term if edge is None else edge + term
         conv_out[ds, slab(CS - 1)] = edge
-        acc_s[0, ds, :] = pooled
-        acc_s[1, ds, :] = gexc
+        acc_s[ds, :] = jnp.where(first, lane_sum(pooled), lane_sum(gexc))
         return carry
 
     lax.fori_loop(0, EB // SUB, body, 0)
-    ones = jnp.ones((8, LANES), F32)
-    for n in range(2):
-        row = lax.dot_general(ones, acc_s[n], NT, precision=HIGH, preferred_element_type=F32)
-        sums_out[0, n : n + 1, :] = row[:1]
+    for n in range(EB // LANES):
+        sums_out[n] = acc_s[n * LANES : (n + 1) * LANES, :].T[:2]
 
 
 def squeeze_kernel(parts_ref, wsq_ref, wexc_ref, exc_out, gp_out, vec_out):
     pixels = 32768.0
     total = jnp.sum(parts_ref[...], axis=0)
-    pooled = jnp.concatenate([total[2 * j : 2 * j + 1] for j in range(STEPS)], axis=1) / pixels
-    gexc = jnp.concatenate([total[2 * j + 1 : 2 * j + 2] for j in range(STEPS)], axis=1)
+    pooled = jnp.concatenate([total[2 * j : 2 * j + 1] for j in range(BLOCKS)], axis=1) / pixels
+    gexc = jnp.concatenate([total[2 * j + 1 : 2 * j + 2] for j in range(BLOCKS)], axis=1)
     pooled = jnp.broadcast_to(pooled, (8, EX))
     gexc = jnp.broadcast_to(gexc, (8, EX))
     wsq, wexc = wsq_ref[...], wexc_ref[...]
@@ -179,12 +189,12 @@
     gpool = lax.dot_general(gspre, wsq, NT, precision=HIGH, preferred_element_type=F32)
     gpool = gpool / pixels
     vec_out[...] = jnp.zeros((16, LANES), F32)
-    for j in range(STEPS):
+    for j in range(BLOCKS):
         cols = slice(j * LANES, (j + 1) * LANES)
         exc_out[cols, :] = jnp.broadcast_to(excite[:1, cols], (LANES, LANES)).T
         gp_out[cols, :] = jnp.broadcast_to(gpool[:1, cols], (LANES, LANES)).T
         vec_out[j : j + 1, :] = pooled[:1, cols]
-        vec_out[STEPS + j : STEPS + j + 1, :] = gepre[:1, cols]
+        vec_out[BLOCKS + j : BLOCKS + j + 1, :] = gepre[:1, cols]
     vec_out[12:13, :SQ] = squeezed[:1]
     vec_out[13:14, :SQ] = gspre[:1]
 
@@ -218,7 +228,7 @@
 
     def body(i, carry):
         ds = pl.ds(pl.multiple_of(i * SUB, SUB), SUB)
-        k = [jnp.broadcast_to(taps_ref[ds, t : t + 1], (SUB, LANES)) for t in range(9)]
+        k = [taps_ref[ds, slab(t)] for t in range(9)]
         exc, gp = exc_ref[ds, :], gp_ref[ds, :]
 
         def grad_conv(s, mask):
@@ -259,23 +269,23 @@
             r = s - 2
             if 0 <= r:
                 gpre_s[ds, slab(r)] = gh.pop(r) * state.pop(r)[1]
+        total = jnp.zeros((SUB, LANES), F32)
         for t in range(9):
-            acc_s[t, ds, :] = tap[t]
+            total = jnp.where(lane == t, lane_sum(tap[t]), total)
+        acc_s[ds, :] = total
         return carry
 
     lax.fori_loop(0, EB // SUB, body, 0)
     gated = gated_s[...].astype(BF16)
     gpre = gpre_s[...].astype(BF16)
-    wproj_out[...] = lax.dot_general(
-        cot_s[:, slab(1, ROWS)], gated, NT, preferred_element_type=F32
-    )
-    wexp_out[...] = lax.dot_general(scaled_s[...], gpre, NT, preferred_element_type=F32)
+    wproj = lax.dot_general(cot_s[:, slab(1, ROWS)], gated, NT, preferred_element_type=F32)
+    wexp = lax.dot_general(scaled_s[...], gpre, NT, preferred_element_type=F32)
+    for n in range(EB // LANES):
+        wproj_out[n * CH : (n + 1) * CH, :] = wproj[:, n * LANES : (n + 1) * LANES]
+        wexp_out[n * CH : (n + 1) * CH, :] = wexp[:, n * LANES : (n + 1) * LANES]
+        taps_out[:, n * LANES : (n + 1) * LANES] = acc_s[n * LANES : (n + 1) * LANES, :].T[:9]
     proj_s[...] += jnp.dot(wprojt_ref[...], gated, preferred_element_type=F32)
     gs_s[...] += jnp.dot(wexp_ref[...], gpre, preferred_element_type=F32)
-    ones = jnp.ones((8, LANES), F32)
-    for t in range(9):
-        row = lax.dot_general(ones, acc_s[t], NT, precision=HIGH, preferred_element_type=F32)
-        taps_out[t : t + 1, :] = row[:1]
 
     @pl.when(step == STEPS - 1)
     def _():
@@ -292,9 +302,7 @@
             mean = jnp.sum(prod * gain, axis=0, keepdims=True) / CH
             gin = inverse * (gs * gain - normed * mean) + c_ref[r].astype(F32)
             gin_out[r] = gin.astype(BF16)
-        gain_out[...] = lax.dot_general(
-            jnp.ones((8, LANES), F32), ggain, NT, precision=HIGH, preferred_element_type=F32
-        )
+        gain_out[...] = lane_sum(ggain)
 
 
 def shape(*dims, dtype=F32):
@@ -305,9 +313,9 @@
     return pl.BlockSpec(dims, lambda j: (0,) * len(dims))
 
 
-def params():
+def params(mib, grid=True):
     return pltpu.CompilerParams(
-        dimension_semantics=("arbitrary",), vmem_limit_bytes=40 * 1024 * 1024
+        dimension_semantics=("arbitrary",) if grid else None, vmem_limit_bytes=mib * 1024 * 1024
     )
 
 
@@ -332,22 +340,26 @@
     bwd_col = [(i + 1, i) for i in range(ncol - 1)]
     top = lax.ppermute(jnp.concatenate([x[6:8], c[7:8]], axis=0), "row", fwd_row)
     bot = lax.ppermute(jnp.concatenate([x[0:2], c[0:1]], axis=0), "row", bwd_row)
-    own = pl.pallas_call(strip_kernel, out_shape=shape(CH, LANES, dtype=BF16), name="strip")(
-        x, c, top, bot
-    )
+    own = pl.pallas_call(
+        strip_kernel,
+        out_shape=shape(CH, LANES, dtype=BF16),
+        compiler_params=params(8, False),
+        name="strip",
+    )(x, c, top, bot)
     left = lax.ppermute(own, "col", fwd_col)
     right = lax.ppermute(own, "col", bwd_col)
 
     lane = jnp.arange(LANES)
     line, pos = lane // 8, lane % 8
     top_ok, bot_ok = row > 0, row < nrow - 1
-    strip_ok = ((pos == 1) & (col > 0)) | ((pos == 5) & (col < ncol - 1))
+    strip_ok = ((pos == 3) & (col > 0)) | ((pos == 2) & (col < ncol - 1))
     strip_ok &= ((line > 1) | top_ok) & ((line < ROWS + 2) | bot_ok)
     mask = jnp.stack(
         [jnp.broadcast_to(top_ok, (LANES,)), jnp.broadcast_to(bot_ok, (LANES,)), strip_ok]
         + [jnp.zeros((LANES,), bool)] * 5
     ).astype(F32)
     gain = norm_gain[:, None]
+    spread = jnp.broadcast_to(kernel[:, :, None], (EX, 9, LANES)).reshape(EX, 9 * LANES)
     wexpt, wprojt = w_expand.T, w_project.T
     halo = full(3, CH, LANES)
     tile = full(ROWS, CH, LANES)
@@ -358,38 +370,39 @@
         forward_kernel,
         grid=(STEPS,),
         in_specs=[tile, tile, halo, halo, edge, edge, edge, full(CH, 1),
-                  chunk_rows(CH), chunk_rows(9), chunk_rows(CH)],
+                  chunk_rows(CH), chunk_rows(9 * LANES), chunk_rows(CH)],
         out_specs=[chunk_rows(ROWS * LANES), chunk_rows(CS * LANES),
-                   pl.BlockSpec((1, 2, LANES), lambda j: (j, 0, 0))],
-        out_shape=[shape(EX, ROWS * LANES), shape(EX, CS * LANES), shape(STEPS, 2, LANES)],
+                   pl.BlockSpec((EB // LANES, 2, LANES), lambda j: (j, 0, 0))],
+        out_shape=[shape(EX, ROWS * LANES), shape(EX, CS * LANES), shape(BLOCKS, 2, LANES)],
         scratch_shapes=[
             pltpu.VMEM((CH, XS * LANES), BF16),
             pltpu.VMEM((CH, ROWS * LANES), BF16),
-            pltpu.VMEM((EB, XS * LANES), F32),
+            pltpu.VMEM((EB, (XS - ROWS) * LANES), F32),
             pltpu.VMEM((EB, ROWS * LANES), F32),
-            pltpu.VMEM((2, EB, LANES), F32),
+            pltpu.VMEM((EB, LANES), F32),
         ],
-        compiler_params=params(),
+        compiler_params=params(20),
         name="forward",
-    )(x, c, top, bot, own, left, right, gain, wexpt, kernel, w_project)
+    )(x, c, top, bot, own, left, right, gain, wexpt, spread, w_project)
 
     exc, gp, vec = pl.pallas_call(
         squeeze_kernel,
         out_shape=[shape(EX, LANES), shape(EX, LANES), shape(16, LANES)],
+        compiler_params=params(8, False),
         name="squeeze",
-    )(gathered(sums.reshape(2 * STEPS, LANES), RC, 32), w_squeeze, w_excite)
+    )(gathered(sums.reshape(2 * BLOCKS, LANES), RC, 32), w_squeeze, w_excite)
 
     out, gin, ggain, wexp, wproj, taps = pl.pallas_call(
         backward_kernel,
         grid=(STEPS,),
         in_specs=[tile, tile, halo, halo, edge, edge, full(CH, 1), full(8, LANES),
                   chunk_rows(ROWS * LANES), chunk_rows(CS * LANES), chunk_rows(LANES),
-                  chunk_rows(LANES), chunk_rows(9), chunk_cols, chunk_rows(CH), chunk_cols],
-        out_specs=[tile, tile, full(8, CH), pl.BlockSpec((CH, EB), lambda j: (j, 0)),
-                   pl.BlockSpec((CH, EB), lambda j: (j, 0)),
+                  chunk_rows(LANES), chunk_rows(9 * LANES), chunk_cols, chunk_rows(CH), chunk_cols],
+        out_specs=[tile, tile, full(CH, 1), pl.BlockSpec((CH * EB // LANES, LANES), lambda j: (j, 0)),
+                   pl.BlockSpec((CH * EB // LANES, LANES), lambda j: (j, 0)),
                    pl.BlockSpec((9, EB), lambda j: (0, j))],
         out_shape=[shape(ROWS, CH, LANES, dtype=BF16), shape(ROWS, CH, LANES, dtype=BF16),
-                   shape(8, CH), shape(STEPS * CH, EB), shape(STEPS * CH, EB), shape(9, EX)],
+                   shape(CH, 1), shape(BLOCKS * CH, LANES), shape(BLOCKS * CH, LANES), shape(9, EX)],
         scratch_shapes=[
             pltpu.VMEM((CH, ROWS * LANES), BF16),
             pltpu.VMEM((CH, CS * LANES), BF16),
@@ -399,16 +412,16 @@
             pltpu.VMEM((EB, ROWS * LANES), F32),
             pltpu.VMEM((CH, ROWS * LANES), F32),
             pltpu.VMEM((CH, ROWS * LANES), F32),
-            pltpu.VMEM((9, EB, LANES), F32),
+            pltpu.VMEM((EB, LANES), F32),
         ],
-        compiler_params=params(),
+        compiler_params=params(26),
         name="backward",
-    )(x, c, top, bot, left, right, gain, mask, pre, conv, exc, gp, kernel, w_expand, w_project,
+    )(x, c, top, bot, left, right, gain, mask, pre, conv, exc, gp, spread, w_expand, w_project,
       wprojt)
 
     big = jnp.concatenate([wexp, wproj], axis=0).reshape(32, 72, 128)
     small = jnp.concatenate(
-        [taps.reshape(6912), ggain[0], jnp.zeros((1088,), F32)]
+        [taps.reshape(6912), ggain[:, 0], jnp.zeros((1088,), F32)]
     ).reshape(32, 2, 128)
     packed = jnp.concatenate([big, small, jnp.zeros((32, 6, 128), F32)], axis=1)
     mine = jnp.sum(lax.all_to_all(packed, RC, 0, 0, tiled=True), axis=0)
@@ -428,7 +441,7 @@
         axis=0,
     ).astype(jnp.float16)
     every = gathered(send, RC, 32).astype(F32)
-    big = (every[:, :72] * jnp.exp2(every[:, 74:75])).reshape(2, STEPS, CH, EB)
+    big = (every[:, :72] * jnp.exp2(every[:, 74:75])).reshape(2, BLOCKS, CH, LANES)
     small = (every[:, 72:74] * jnp.exp2(every[:, 77:78])).reshape(8192)
     return (
         out.transpose(1, 0, 2)[None],

time: 183 us -> 192 us (1.049)
  local copies, waits for them, and re-layouts: 27.5 us -> 52.1 us
  Pallas kernels: 47.8 us -> 36.6 us
  waiting for transfers between devices: 36.4 us -> 30.9 us
    unnamed x69 -> x80, local copies, waits for them, and re-layouts: 20 us -> 36.9 us
    pallas_call x1, Pallas kernels: 25 us -> 17.2 us  [local(): pl.pallas_call(backward_kernel, grid=(STEPS,), in_specs=[tile, tile, halo...]
    reshape x0 -> x1, local copies, waits for them, and re-layouts: none -> 3.31 us  [local(): jnp.broadcast_to(kernel[:, :, None], (EX, 9, LANES)).reshape(EX, 9 * LANES)]
    ppermute x1, waiting for transfers between devices: 2.98 us -> 0.01 us  [local(): right = lax.ppermute(own, 'col', bwd_col)]
    all_to_all x3, waiting for transfers between devices: 31.3 us -> 28.8 us  [gathered(): lax.all_to_all(jnp.broadcast_to(block[None], (count,) + block.shape), axe...]
    broadcast_in_dim x0 -> x1, local copies, waits for them, and re-layouts: none -> 2 us  [local(): jnp.broadcast_to(kernel[:, :, None], (EX, 9, LANES)).reshape(EX, 9 * LANES)]
  transfers between devices with their start and end apart: 7 -> 7, of which waited for: 6 -> 5; matrix products, arithmetic and copies ran while one was open for 3% -> 9% of each run, Pallas kernels for 0% -> 0%
where the time goes in v3:
time: 192 us; the launch traced here: 190 us
  local copies, waits for them, and re-layouts  52.1 us (27%)
  starting transfers between devices  38.7 us (20%)
  Pallas kernels  36.6 us (19%)
  waiting for transfers between devices  30.9 us (16%)
  blocking collectives  24.4 us (13%)
  other arithmetic  3.29 us (2%)
  between operations  2.52 us (1%)
  matrix products  1.97 us (1%)
    unnamed x80, local copies, waits for them, and re-layouts  36.9 us
    all_to_all x3, waiting for transfers between devices, gathered(): lax.all_to_all(jnp.broadcast_to(block[None], (count,) + block.shape), axe...  28.8 us
    all_to_all x3, starting transfers between devices, gathered(): lax.all_to_all(jnp.broadcast_to(block[None], (count,) + block.shape), axe...  25.2 us
    all_to_all x1, blocking collectives, local(): mine = jnp.sum(lax.all_to_all(packed, RC, 0, 0, tiled=True), axis=0)  24.4 us
    pallas_call x1, Pallas kernels, local(): pl.pallas_call(backward_kernel, grid=(STEPS,), in_specs=[tile, tile, halo...  17.2 us
    pallas_call x1, Pallas kernels, local(): pl.pallas_call(forward_kernel, grid=(STEPS,), in_specs=[tile, tile, halo,...  16 us
    ppermute x1, starting transfers between devices, local(): left = lax.ppermute(own, 'col', fwd_col)  5.28 us
    ppermute x1, starting transfers between devices, local(): lax.ppermute(jnp.concatenate([x[6:8], c[7:8]], axis=0), 'row', fwd_row)  4.57 us
  transfers between devices with their start and end apart: 7, of which 5 were waited for; matrix products, arithmetic and copies ran while one was open for 9% of the time, Pallas kernels for 0%

profile of v3, /device:TPU:1, one launch (start us, length us, event | category | flops | bytes accessed | tf_op | source)
XLA Modules:
  0.0 190.5 jit_solution(10629149090822300528)
XLA Ops:
  0.6 1.3 copy_bitcast_fusion.2
  2.0 1.4 collective-permute-start.1
  3.5 4.6 %collective-permute-start = (bf16[3,192,128]{2,1,0:T(8,128)(2,1)S(1)}, bf16[3,192,128]{2,1,0:T(8,128)(2,1)S(1)}, u32[]{:S(2)}, u32[]{:S(2)}) collective-permute-start(bf16[3,192,128]{2,1,0:T(8,128)(2,1)S(1)} %pad_maximum_fusion.1), channel_id=1, source_target_pairs={{0,4},{4,8},{8,12},{12,16},{16,20},{20,24},{24,28},{1,5},{5,9},{9,... | collective-permute-start | bytes 442376 | tf_op jit(solution)/shard_map/ppermute | solution.py:341
  8.6 1.5 collective-permute-done.top_ref
  11.1 5.3 %collective-permute-start.2 = (bf16[192,128]{1,0:T(8,128)(2,1)}, bf16[192,128]{1,0:T(8,128)(2,1)}, u32[]{:S(2)}, u32[]{:S(2)}) collective-permute-start(bf16[192,128]{1,0:T(8,128)(2,1)} %strip.1.own_ref), channel_id=1, source_target_pairs={{0,1},{1,2},{2,3},{4,5},{5,6},{6,7},{8,9},{9,10},{10,11},{12,13},{... | collective-permute-start | bytes 147464 | tf_op jit(solution)/shard_map/ppermute | solution.py:349
  16.4 2.3 %collective-permute-start.3 = (bf16[192,128]{1,0:T(8,128)(2,1)}, bf16[192,128]{1,0:T(8,128)(2,1)}, u32[]{:S(2)}, u32[]{:S(2)}) collective-permute-start(bf16[192,128]{1,0:T(8,128)(2,1)} %strip.1.own_ref), channel_id=1, source_target_pairs={{1,0},{2,1},{3,2},{5,4},{6,5},{7,6},{9,8},{10,9},{11,10},{13,12},{... | collective-permute-start | bytes 147464 | tf_op jit(solution)/shard_map/ppermute | solution.py:350
  18.7 2.0 %broadcast_in_dim.47 = f32[768,9,128]{0,2,1:T(8,128)} broadcast(f32[768,9]{0,1:T(8,128)S(1)} %copy-done.34), dimensions={0,1} | broadcast | bytes 3566592 | tf_op jit(solution)/shard_map/broadcast_in_dim | solution.py:362
  20.7 3.3 %copy.44.taps_ref = f32[768,1152]{1,0:T(8,128)S(1)} copy(f32[768,1152]{0,1:T(8,128)} %bitcast.46) | data formatting | bytes 7077888 | tf_op jit(solution)/shard_map/reshape | solution.py:362
  24.0 1.9 copy.45.wproj_ref
  26.6 1.9 copy.42
  29.5 1.0 copy-done.4
  30.5 1.0 copy-done.8
  35.2 16.0 %forward.1 = (f32[768,1024]{1,0:T(8,128)S(1)}, f32[768,1408]{1,0:T(8,128)S(1)}, f32[6,2,128]{2,1,0:T(2,128)S(1)}) custom-call(bf16[8,192,128]{2,1,0:T(8,128)(2,1)S(1)} %copy-done.1, bf16[8,192,128]{2,1,0:T(8,128)(2,1)S(1)} %copy-done.4, bf16[3,192,128]{2,1,0:T(8,128)(2,1)S(1)} %copy-done.18, bf16[3,192,128]{2,1,0:T(8,128)(2,1)S(1)} %copy-done.15, ...), custom_call_target="tpu_custom_call" | custom-call | tf_op jit(solution)/shard_map/forward/pallas_call | solution.py:369
  51.2 2.0 %copy-done.6 = f32[768,1408]{1,0:T(8,128)} copy-done((f32[768,1408]{1,0:T(8,128)}, f32[768,1408]{1,0:T(8,128)S(1)}, u32[]{:S(2)}) %copy-start.6) | copy-done | bytes 4325400
  53.2 1.6 copy-done.10
  55.6 12.2 %all-to-all-start = ((f32[32,12,128]{2,1,0:T(8,128)}), f32[32,12,128]{2,1,0:T(8,128)}, u32[]{:S(2)}, u32[]{:S(2)}) async-start(f32[32,12,128]{2,1,0:T(8,128)} %broadcast_in_dim.49), calls=%async_computation | async-start | bytes 524288 | tf_op jit(solution)/shard_map/all_to_all | solution.py:323
  67.8 1.8 copy.46.wsq_ref
  71.5 5.2 %all-to-all-done.parts_ref = f32[32,12,128]{2,1,0:T(8,128)} async-done(((f32[32,12,128]{2,1,0:T(8,128)}), f32[32,12,128]{2,1,0:T(8,128)}, u32[]{:S(2)}, u32[]{:S(2)}) %all-to-all-start) | async-done | bytes 196640 | tf_op jit(solution)/shard_map/all_to_all | solution.py:323
  76.7 1.0 copy-done.12
  78.6 2.4 %squeeze.21 = (f32[768,128]{1,0:T(8,128)S(1)}, f32[768,128]{1,0:T(8,128)S(1)}, f32[16,128]{1,0:T(8,128)S(1)}) custom-call(f32[32,12,128]{2,1,0:T(8,128)} %all-to-all-done.parts_ref, f32[768,48]{1,0:T(8,128)S(1)} %copy-done.12, f32[48,768]{1,0:T(8,128)S(1)} %copy-done.30), custom_call_target="tpu_custom_call" | custom-call | tf_op jit(solution)/shard_map/squeeze/pallas_call | solution.py:388
  83.0 2.2 %copy-done.7 = f32[768,1408]{1,0:T(8,128)S(1)} copy-done((f32[768,1408]{1,0:T(8,128)S(1)}, f32[768,1408]{1,0:T(8,128)}, u32[]{:S(2)}) %copy-start.7) | copy-done | bytes 4325400
  85.2 1.0 copy-done.9
  86.2 1.9 copy-done.11
  92.7 17.2 %backward.1 = (bf16[8,192,128]{2,1,0:T(8,128)(2,1)S(1)}, bf16[8,192,128]{2,1,0:T(8,128)(2,1)S(1)}, f32[192,1]{1,0:T(8,128)S(1)}, f32[1152,128]{1,0:T(8,128)S(1)}...) custom-call(bf16[8,192,128]{2,1,0:T(8,128)(2,1)S(1)} %copy-done.2, bf16[8,192,128]{2,1,0:T(8,128)(2,1)S(1)} %copy-done.5, ...), custom_call_target="tpu_custom_call" | custom-call | tf_op jit(solution)/shard_map/backward/pallas_call | solution.py:395
  115.2 1.3 pad_maximum_fusion
  116.9 24.4 %all_to_all.20 = f32[32,80,128]{2,1,0:T(8,128)S(1)} all-to-all(f32[32,80,128]{2,1,0:T(8,128)S(1)} %maximum_maximum_fusion), channel_id=1, replica_groups=mesh['dp'=8,'row'=8,'col'=4] {'row','col'}, dimensions={0} | all-to-all | bytes 2621440 | tf_op jit(solution)/shard_map/all_to_all | solution.py:427
  142.2 8.2 %all-to-all-start.2 = ((f32[8,96,128]{2,1,0:T(8,128)}), f32[8,96,128]{2,1,0:T(8,128)S(1)}, u32[]{:S(2)}, u32[]{:S(2)}) async-start(f32[8,96,128]{2,1,0:T(8,128)} %broadcast_in_dim.54), calls=%async_computation.2 | async-start | bytes 786432 | tf_op jit(solution)/shard_map/all_to_all | solution.py:323
  150.4 1.0 copy.52
  151.4 1.0 copy.53
  152.4 12.4 %all-to-all-done.2 = f32[8,96,128]{2,1,0:T(8,128)S(1)} async-done(((f32[8,96,128]{2,1,0:T(8,128)}), f32[8,96,128]{2,1,0:T(8,128)S(1)}, u32[]{:S(2)}, u32[]{:S(2)}) %all-to-all-start.2) | async-done | bytes 393248 | tf_op jit(solution)/shard_map/all_to_all | solution.py:323
  168.7 4.8 %all-to-all-start.3 = ((f16[32,80,128]{2,1,0:T(8,128)(2,1)}), f16[32,80,128]{2,1,0:T(8,128)(2,1)S(1)}, u32[]{:S(2)}, u32[]{:S(2)}) async-start(f16[32,80,128]{2,1,0:T(8,128)(2,1)} %broadcast_in_dim.57), calls=%async_computation.3 | async-start | bytes 1310720 | tf_op jit(solution)/shard_map/all_to_all | solution.py:323
  175.5 11.2 %all-to-all-done.3 = f16[32,80,128]{2,1,0:T(8,128)(2,1)S(1)} async-done(((f16[32,80,128]{2,1,0:T(8,128)(2,1)}), f16[32,80,128]{2,1,0:T(8,128)(2,1)S(1)}, u32[]{:S(2)}, u32[]{:S(2)}) %all-to-all-start.3) | async-done | bytes 655392 | tf_op jit(solution)/shard_map/all_to_all | solution.py:323
  (118 shorter events, 31.8 us)
Async XLA Ops:
  1.9 8.2 %copy-start = (bf16[8,192,128]{2,1,0:T(8,128)(2,1)}, bf16[8,192,128]{2,1,0:T(8,128)(2,1)S(1)}, u32[]{:S(2)}) copy-start(bf16[8,192,128]{2,1,0:T(8,128)(2,1)S(1)} %get-tuple-element.65.x_ref) | copy-start | bytes 1179652
  1.9 9.2 %copy-start.3 = (bf16[8,192,128]{2,1,0:T(8,128)(2,1)}, bf16[8,192,128]{2,1,0:T(8,128)(2,1)S(1)}, u32[]{:S(2)}) copy-start(bf16[8,192,128]{2,1,0:T(8,128)(2,1)S(1)} %get-tuple-element.64.c_ref) | copy-start | bytes 1179652
  1.9 16.7 %copy-start.34 = (f32[768,9]{0,1:T(8,128)S(1)}, f32[768,9]{0,1:T(8,128)}, u32[]{:S(2)}) copy-start(f32[768,9]{0,1:T(8,128)} %param.11) | copy-start | bytes 82948
  2.0 6.6 %collective-permute-start.1 = (bf16[3,192,128]{2,1,0:T(8,128)(2,1)S(1)}, bf16[3,192,128]{2,1,0:T(8,128)(2,1)S(1)}, u32[]{:S(2)}, u32[]{:S(2)}) collective-permute-start(bf16[3,192,128]{2,1,0:T(8,128)(2,1)S(1)} %pad_maximum_fusion.2), channel_id=1, source_target_pairs={{4,0},{8,4},{12,8},{16,12},{20,16},{24,20},{28,24},{5,1},{9,5},{13... | collective-permute-start | bytes 442376 | tf_op jit(solution)/shard_map/ppermute | solution.py:342
  3.5 6.7 %collective-permute-start = (bf16[3,192,128]{2,1,0:T(8,128)(2,1)S(1)}, bf16[3,192,128]{2,1,0:T(8,128)(2,1)S(1)}, u32[]{:S(2)}, u32[]{:S(2)}) collective-permute-start(bf16[3,192,128]{2,1,0:T(8,128)(2,1)S(1)} %pad_maximum_fusion.1), channel_id=1, source_target_pairs={{0,4},{4,8},{8,12},{12,16},{16,20},{20,24},{24,28},{1,5},{5,9},{9,... | collective-permute-start | bytes 442376 | tf_op jit(solution)/shard_map/ppermute | solution.py:341
  8.6 7.8 %copy-start.14 = (bf16[3,192,128]{2,1,0:T(8,128)(2,1)}, bf16[3,192,128]{2,1,0:T(8,128)(2,1)S(1)}, u32[]{:S(2)}) copy-start(bf16[3,192,128]{2,1,0:T(8,128)(2,1)S(1)} %collective-permute-done.1.bot_ref) | copy-start | bytes 442372
  10.1 6.3 %copy-start.17 = (bf16[3,192,128]{2,1,0:T(8,128)(2,1)}, bf16[3,192,128]{2,1,0:T(8,128)(2,1)S(1)}, u32[]{:S(2)}) copy-start(bf16[3,192,128]{2,1,0:T(8,128)(2,1)S(1)} %collective-permute-done.top_ref) | copy-start | bytes 442372
  11.1 17.4 %collective-permute-start.2 = (bf16[192,128]{1,0:T(8,128)(2,1)}, bf16[192,128]{1,0:T(8,128)(2,1)}, u32[]{:S(2)}, u32[]{:S(2)}) collective-permute-start(bf16[192,128]{1,0:T(8,128)(2,1)} %strip.1.own_ref), channel_id=1, source_target_pairs={{0,1},{1,2},{2,3},{4,5},{5,6},{6,7},{8,9},{9,10},{10,11},{12,13},{... | collective-permute-start | bytes 147464 | tf_op jit(solution)/shard_map/ppermute | solution.py:349
  16.4 12.1 %collective-permute-start.3 = (bf16[192,128]{1,0:T(8,128)(2,1)}, bf16[192,128]{1,0:T(8,128)(2,1)}, u32[]{:S(2)}, u32[]{:S(2)}) collective-permute-start(bf16[192,128]{1,0:T(8,128)(2,1)} %strip.1.own_ref), channel_id=1, source_target_pairs={{1,0},{2,1},{3,2},{5,4},{6,5},{7,6},{9,8},{10,9},{11,10},{13,12},{... | collective-permute-start | bytes 147464 | tf_op jit(solution)/shard_map/ppermute | solution.py:350
  20.7 5.2 %copy-start.35 = (f32[192]{0:T(256)S(1)}, f32[192]{0:T(256)}, u32[]{:S(2)}) copy-start(f32[192]{0:T(256)} %param.9) | copy-start | bytes 2308
  28.5 1.0 copy-start.1
  29.5 1.0 copy-start.4
  30.5 1.0 copy-start.8
  31.5 1.0 copy-start.13
  32.5 0.9 copy-start.15
  33.4 0.9 copy-start.18
  51.2 2.0 %copy-start.6 = (f32[768,1408]{1,0:T(8,128)}, f32[768,1408]{1,0:T(8,128)S(1)}, u32[]{:S(2)}) copy-start(f32[768,1408]{1,0:T(8,128)S(1)} %get-tuple-element.21.conv_ref) | copy-start | bytes 12976132
  53.2 1.6 copy-start.10
  55.6 21.1 %all-to-all-start = ((f32[32,12,128]{2,1,0:T(8,128)}), f32[32,12,128]{2,1,0:T(8,128)}, u32[]{:S(2)}, u32[]{:S(2)}) async-start(f32[32,12,128]{2,1,0:T(8,128)} %broadcast_in_dim.49), calls=%async_computation | async-start | bytes 524288 | tf_op jit(solution)/shard_map/all_to_all | solution.py:323
  76.7 1.0 copy-start.12
  81.0 1.0 copy-start.2
  82.0 1.0 copy-start.5
  83.0 2.2 %copy-start.7 = (f32[768,1408]{1,0:T(8,128)S(1)}, f32[768,1408]{1,0:T(8,128)}, u32[]{:S(2)}) copy-start(f32[768,1408]{1,0:T(8,128)} %copy-done.6) | copy-start | bytes 12976132
  85.2 1.0 copy-start.9
  86.2 1.9 copy-start.11
  89.9 1.0 copy-start.20
  90.9 1.0 copy-start.21
  114.4 2.2 %copy-start.32 = (f32[192,1]{1,0:T(8,128)S(1)}, f32[192,1]{1,0:T(8,128)}, u32[]{:S(2)}) copy-start(f32[192,1]{1,0:T(8,128)} %copy-done.31) | copy-start | bytes 2308
  141.3 9.1 %copy-start.29 = (bf16[8,192,128]{2,1,0:T(8,128)(2,1)S(1)}, bf16[8,192,128]{2,1,0:T(8,128)(2,1)}, u32[]{:S(2)}) copy-start(bf16[8,192,128]{2,1,0:T(8,128)(2,1)} %copy-done.28) | copy-start | bytes 1179652
  141.4 10.0 %copy-start.27 = (bf16[8,192,128]{2,1,0:T(8,128)(2,1)S(1)}, bf16[8,192,128]{2,1,0:T(8,128)(2,1)}, u32[]{:S(2)}) copy-start(bf16[8,192,128]{2,1,0:T(8,128)(2,1)} %copy-done.26) | copy-start | bytes 1179652
  142.2 22.6 %all-to-all-start.2 = ((f32[8,96,128]{2,1,0:T(8,128)}), f32[8,96,128]{2,1,0:T(8,128)S(1)}, u32[]{:S(2)}, u32[]{:S(2)}) async-start(f32[8,96,128]{2,1,0:T(8,128)} %broadcast_in_dim.54), calls=%async_computation.2 | async-start | bytes 786432 | tf_op jit(solution)/shard_map/all_to_all | solution.py:323
  168.7 18.0 %all-to-all-start.3 = ((f16[32,80,128]{2,1,0:T(8,128)(2,1)}), f16[32,80,128]{2,1,0:T(8,128)(2,1)S(1)}, u32[]{:S(2)}, u32[]{:S(2)}) async-start(f16[32,80,128]{2,1,0:T(8,128)(2,1)} %broadcast_in_dim.57), calls=%async_computation.3 | async-start | bytes 1310720 | tf_op jit(solution)/shard_map/all_to_all | solution.py:323
  (11 other events, 8.9 us)

commit v4 on v3

--- a/solution.py
+++ b/solution.py
@@ -17,9 +17,12 @@
 SUB = 16
 STEPS = EX // EB
 BLOCKS = EX // LANES
+PARTS, PACK = 32, 80
+VMEM = 60 * 1024 * 1024
 XS = ROWS + 5
 CS = ROWS + 3
 NT = (((1,), (1,)), ((), ()))
+TN = (((0,), (0,)), ((), ()))
 
 
 def lane_iota(rows):
@@ -28,6 +31,10 @@
 
 def rounded(v):
     return v.astype(BF16).astype(F32)
+
+
+def tn_dot(a, b):
+    return lax.dot_general(a, b, TN, preferred_element_type=F32)
 
 
 def lane_sum(v):
@@ -93,7 +100,7 @@
 
 def forward_kernel(
     x_ref, c_ref, top_ref, bot_ref, own_ref, left_ref, right_ref, gain_ref, wexp_ref, taps_ref,
-    wproj_ref, pre_out, conv_out, sums_out, scaled_s, cot_s, pre_s, gg_s, acc_s,
+    wprojt_ref, pre_out, conv_out, sums_out, scaled_s, cot_s, pre_s, gg_s, acc_s,
 ):
     @pl.when(pl.program_id(0) == 0)
     def _():
@@ -113,19 +120,16 @@
         for r in range(ROWS):
             cot_s[:, slab(r)] = c_ref[r]
 
-    pre_out[...] = jnp.dot(
-        wexp_ref[...], scaled_s[:, slab(0, ROWS)], preferred_element_type=F32
-    )
-    pre_s[...] = jnp.dot(
-        wexp_ref[...], scaled_s[:, slab(ROWS, XS - ROWS)], preferred_element_type=F32
-    )
-    gg_s[...] = jnp.dot(wproj_ref[...], cot_s[...], preferred_element_type=F32)
+    wexp = wexp_ref[...]
+    pre_out[...] = tn_dot(wexp, scaled_s[:, slab(0, ROWS)])
+    pre_s[...] = tn_dot(wexp, scaled_s[:, slab(ROWS, XS - ROWS)])
+    gg_s[...] = tn_dot(wprojt_ref[...], cot_s[...])
     lane = lane_iota(SUB)
     first, last = lane == 0, lane == LANES - 1
 
     def body(i, carry):
         ds = pl.ds(pl.multiple_of(i * SUB, SUB), SUB)
-        k = [taps_ref[ds, slab(t)] for t in range(9)]
+        k = [jnp.broadcast_to(taps_ref[ds, t : t + 1], (SUB, LANES)) for t in range(9)]
 
         def hidden(s):
             if 2 <= s < ROWS + 2:
@@ -178,7 +182,7 @@
     pooled = jnp.broadcast_to(pooled, (8, EX))
     gexc = jnp.broadcast_to(gexc, (8, EX))
     wsq, wexc = wsq_ref[...], wexc_ref[...]
-    spre = jnp.dot(pooled, wsq, precision=HIGH, preferred_element_type=F32)
+    spre = lax.dot_general(pooled, wsq, NT, precision=HIGH, preferred_element_type=F32)
     sig = jax.nn.sigmoid(spre)
     squeezed = spre * sig
     epre = jnp.dot(squeezed, wexc, precision=HIGH, preferred_element_type=F32)
@@ -186,7 +190,7 @@
     gepre = gexc * excite * (1.0 - excite)
     gspre = lax.dot_general(gepre, wexc, NT, precision=HIGH, preferred_element_type=F32)
     gspre = gspre * (sig * (1.0 + spre * (1.0 - sig)))
-    gpool = lax.dot_general(gspre, wsq, NT, precision=HIGH, preferred_element_type=F32)
+    gpool = jnp.dot(gspre, wsq, precision=HIGH, preferred_element_type=F32)
     gpool = gpool / pixels
     vec_out[...] = jnp.zeros((16, LANES), F32)
     for j in range(BLOCKS):
@@ -199,10 +203,18 @@
     vec_out[13:14, :SQ] = gspre[:1]
 
 
+def big_rows(group):
+    return pl.ds(pl.multiple_of(PACK * (group // 3) + 24 * (group % 3), 8), 24)
+
+
+def small_row(row):
+    return pl.ds(PACK * (row // 2) + 72 + row % 2, 1)
+
+
 def backward_kernel(
     x_ref, c_ref, top_ref, bot_ref, left_ref, right_ref, gain_ref, mask_ref, pre_ref, conv_ref,
-    exc_ref, gp_ref, taps_ref, wexp_ref, wproj_ref, wprojt_ref,
-    out_out, gin_out, gain_out, wexp_out, wproj_out, taps_out,
+    exc_ref, gp_ref, taps_ref, wexp_ref, wprojt_ref,
+    out_out, gin_out, packed_out,
     scaled_s, cot_s, inv_s, gg_s, gated_s, gpre_s, proj_s, gs_s, acc_s,
 ):
     step = pl.program_id(0)
@@ -221,14 +233,16 @@
         cot_s[:, slab(CS - 1)] = cotangent_strip(left_ref, right_ref).astype(BF16)
         proj_s[...] = jnp.zeros_like(proj_s)
         gs_s[...] = jnp.zeros_like(gs_s)
-
-    gg_s[...] = jnp.dot(wproj_ref[...], cot_s[...], preferred_element_type=F32)
+        for d in range(PARTS):
+            packed_out[d * PACK + 72 : (d + 1) * PACK, :] = jnp.zeros((8, LANES), F32)
+
+    gg_s[...] = tn_dot(wprojt_ref[...], cot_s[...])
     lane = lane_iota(SUB)
     first, last = lane == 0, lane == LANES - 1
 
     def body(i, carry):
         ds = pl.ds(pl.multiple_of(i * SUB, SUB), SUB)
-        k = [taps_ref[ds, slab(t)] for t in range(9)]
+        k = [jnp.broadcast_to(taps_ref[ds, t : t + 1], (SUB, LANES)) for t in range(9)]
         exc, gp = exc_ref[ds, :], gp_ref[ds, :]
 
         def grad_conv(s, mask):
@@ -280,10 +294,17 @@
     gpre = gpre_s[...].astype(BF16)
     wproj = lax.dot_general(cot_s[:, slab(1, ROWS)], gated, NT, preferred_element_type=F32)
     wexp = lax.dot_general(scaled_s[...], gpre, NT, preferred_element_type=F32)
+    groups = CH // 24
     for n in range(EB // LANES):
-        wproj_out[n * CH : (n + 1) * CH, :] = wproj[:, n * LANES : (n + 1) * LANES]
-        wexp_out[n * CH : (n + 1) * CH, :] = wexp[:, n * LANES : (n + 1) * LANES]
-        taps_out[:, n * LANES : (n + 1) * LANES] = acc_s[n * LANES : (n + 1) * LANES, :].T[:9]
+        block = step * (EB // LANES) + n
+        for w, which in ((wexp, 0), (wproj, BLOCKS * groups)):
+            for i in range(groups):
+                packed_out[big_rows(which + block * groups + i), :] = w[
+                    24 * i : 24 * i + 24, n * LANES : (n + 1) * LANES
+                ]
+        taps = acc_s[n * LANES : (n + 1) * LANES, :].T
+        for t in range(9):
+            packed_out[small_row(BLOCKS * t + block), :] = taps[t : t + 1]
     proj_s[...] += jnp.dot(wprojt_ref[...], gated, preferred_element_type=F32)
     gs_s[...] += jnp.dot(wexp_ref[...], gpre, preferred_element_type=F32)
 
@@ -302,7 +323,9 @@
             mean = jnp.sum(prod * gain, axis=0, keepdims=True) / CH
             gin = inverse * (gs * gain - normed * mean) + c_ref[r].astype(F32)
             gin_out[r] = gin.astype(BF16)
-        gain_out[...] = lane_sum(ggain)
+        sums = jnp.broadcast_to(lane_sum(ggain), (CH, LANES)).T[:1]
+        packed_out[small_row(9 * BLOCKS), :] = sums[:, :LANES]
+        packed_out[pl.ds(9 * BLOCKS // 2 * PACK + 73, 1), : CH - LANES] = sums[:, LANES:]
 
 
 def shape(*dims, dtype=F32):
@@ -313,9 +336,9 @@
     return pl.BlockSpec(dims, lambda j: (0,) * len(dims))
 
 
-def params(mib, grid=True):
+def params(grid=True):
     return pltpu.CompilerParams(
-        dimension_semantics=("arbitrary",) if grid else None, vmem_limit_bytes=mib * 1024 * 1024
+        dimension_semantics=("arbitrary",) if grid else None, vmem_limit_bytes=VMEM
     )
 
 
@@ -343,24 +366,22 @@
     own = pl.pallas_call(
         strip_kernel,
         out_shape=shape(CH, LANES, dtype=BF16),
-        compiler_params=params(8, False),
+        compiler_params=params(False),
         name="strip",
     )(x, c, top, bot)
     left = lax.ppermute(own, "col", fwd_col)
     right = lax.ppermute(own, "col", bwd_col)
 
-    lane = jnp.arange(LANES)
-    line, pos = lane // 8, lane % 8
+    line = lax.broadcasted_iota(jnp.int32, (8, LANES), 1) // 8
+    pos = lax.broadcasted_iota(jnp.int32, (8, LANES), 1) % 8
+    kind = lax.broadcasted_iota(jnp.int32, (8, LANES), 0)
     top_ok, bot_ok = row > 0, row < nrow - 1
     strip_ok = ((pos == 3) & (col > 0)) | ((pos == 2) & (col < ncol - 1))
     strip_ok &= ((line > 1) | top_ok) & ((line < ROWS + 2) | bot_ok)
-    mask = jnp.stack(
-        [jnp.broadcast_to(top_ok, (LANES,)), jnp.broadcast_to(bot_ok, (LANES,)), strip_ok]
-        + [jnp.zeros((LANES,), bool)] * 5
-    ).astype(F32)
+    mask = ((kind == 0) & top_ok) | ((kind == 1) & bot_ok) | ((kind == 2) & strip_ok)
+    mask = mask.astype(F32)
     gain = norm_gain[:, None]
-    spread = jnp.broadcast_to(kernel[:, :, None], (EX, 9, LANES)).reshape(EX, 9 * LANES)
-    wexpt, wprojt = w_expand.T, w_project.T
+    wprojt = w_project.T
     halo = full(3, CH, LANES)
     tile = full(ROWS, CH, LANES)
     edge = full(CH, LANES)
@@ -370,7 +391,7 @@
         forward_kernel,
         grid=(STEPS,),
         in_specs=[tile, tile, halo, halo, edge, edge, edge, full(CH, 1),
-                  chunk_rows(CH), chunk_rows(9 * LANES), chunk_rows(CH)],
+                  chunk_cols, chunk_rows(9), chunk_cols],
         out_specs=[chunk_rows(ROWS * LANES), chunk_rows(CS * LANES),
                    pl.BlockSpec((EB // LANES, 2, LANES), lambda j: (j, 0, 0))],
         out_shape=[shape(EX, ROWS * LANES), shape(EX, CS * LANES), shape(BLOCKS, 2, LANES)],
@@ -381,28 +402,26 @@
             pltpu.VMEM((EB, ROWS * LANES), F32),
             pltpu.VMEM((EB, LANES), F32),
         ],
-        compiler_params=params(20),
+        compiler_params=params(),
         name="forward",
-    )(x, c, top, bot, own, left, right, gain, wexpt, spread, w_project)
+    )(x, c, top, bot, own, left, right, gain, w_expand, kernel, wprojt)
 
     exc, gp, vec = pl.pallas_call(
         squeeze_kernel,
         out_shape=[shape(EX, LANES), shape(EX, LANES), shape(16, LANES)],
-        compiler_params=params(8, False),
+        compiler_params=params(False),
         name="squeeze",
-    )(gathered(sums.reshape(2 * BLOCKS, LANES), RC, 32), w_squeeze, w_excite)
-
-    out, gin, ggain, wexp, wproj, taps = pl.pallas_call(
+    )(gathered(sums.reshape(2 * BLOCKS, LANES), RC, 32), w_squeeze.T, w_excite)
+
+    out, gin, packed = pl.pallas_call(
         backward_kernel,
         grid=(STEPS,),
         in_specs=[tile, tile, halo, halo, edge, edge, full(CH, 1), full(8, LANES),
                   chunk_rows(ROWS * LANES), chunk_rows(CS * LANES), chunk_rows(LANES),
-                  chunk_rows(LANES), chunk_rows(9 * LANES), chunk_cols, chunk_rows(CH), chunk_cols],
-        out_specs=[tile, tile, full(CH, 1), pl.BlockSpec((CH * EB // LANES, LANES), lambda j: (j, 0)),
-                   pl.BlockSpec((CH * EB // LANES, LANES), lambda j: (j, 0)),
-                   pl.BlockSpec((9, EB), lambda j: (0, j))],
+                  chunk_rows(LANES), chunk_rows(9), chunk_cols, chunk_cols],
+        out_specs=[tile, tile, full(PARTS * PACK, LANES)],
         out_shape=[shape(ROWS, CH, LANES, dtype=BF16), shape(ROWS, CH, LANES, dtype=BF16),
-                   shape(CH, 1), shape(BLOCKS * CH, LANES), shape(BLOCKS * CH, LANES), shape(9, EX)],
+                   shape(PARTS * PACK, LANES)],
         scratch_shapes=[
             pltpu.VMEM((CH, ROWS * LANES), BF16),
             pltpu.VMEM((CH, CS * LANES), BF16),
@@ -414,16 +433,11 @@
             pltpu.VMEM((CH, ROWS * LANES), F32),
             pltpu.VMEM((EB, LANES), F32),
         ],
-        compiler_params=params(26),
+        compiler_params=params(),
         name="backward",
-    )(x, c, top, bot, left, right, gain, mask, pre, conv, exc, gp, spread, w_expand, w_project,
-      wprojt)
-
-    big = jnp.concatenate([wexp, wproj], axis=0).reshape(32, 72, 128)
-    small = jnp.concatenate(
-        [taps.reshape(6912), ggain[:, 0], jnp.zeros((1088,), F32)]
-    ).reshape(32, 2, 128)
-    packed = jnp.concatenate([big, small, jnp.zeros((32, 6, 128), F32)], axis=1)
+    )(x, c, top, bot, left, right, gain, mask, pre, conv, exc, gp, kernel, w_expand, wprojt)
+
+    packed = packed.reshape(PARTS, PACK, LANES)
     mine = jnp.sum(lax.all_to_all(packed, RC, 0, 0, tiled=True), axis=0)
     shared = gathered(jnp.concatenate([mine, vec], axis=0), "dp", 8)
     total = jnp.sum(shared[:, :80], axis=0)

time: 192 us -> 164 us (0.85)
  local copies, waits for them, and re-layouts: 52.1 us -> 14.4 us
  Pallas kernels: 36.6 us -> 44.4 us
  waiting for transfers between devices: 30.9 us -> 36.8 us
  starting transfers between devices: 38.7 us -> 35.4 us
    unnamed x80 -> x30, local copies, waits for them, and re-layouts: 36.9 us -> 6.52 us
    reshape x2 -> x0, local copies, waits for them, and re-layouts: 4.14 us -> none  [the longest x1 3.31 us: local(): jnp.broadcast_to(kernel[:, :, None], (EX, 9, LANES)).reshape(EX, 9 * LANES)]
    pallas_call x1, Pallas kernels: 17.2 us -> 21 us  [local(): pl.pallas_call(backward_kernel, grid=(STEPS,), in_specs=[tile, tile, halo...]
    ppermute x1, waiting for transfers between devices: 0.56 us -> 3.86 us  [local(): lax.ppermute(jnp.concatenate([x[0:2], c[0:1]], axis=0), 'row', bwd_row)]
    all_to_all x3, waiting for transfers between devices: 28.8 us -> 31.8 us  [gathered(): lax.all_to_all(jnp.broadcast_to(block[None], (count,) + block.shape), axe...]
    ppermute x1, starting transfers between devices: 5.28 us -> 3.1 us  [local(): left = lax.ppermute(own, 'col', fwd_col)]
    broadcast_in_dim x3 -> x0, local copies, waits for them, and re-layouts: 2 us -> none  [the longest x1 2 us: local(): jnp.broadcast_to(kernel[:, :, None], (EX, 9, LANES)).reshape(EX, 9 * LANES)]
    pallas_call x1, Pallas kernels: 16 us -> 18 us  [local(): pl.pallas_call(forward_kernel, grid=(STEPS,), in_specs=[tile, tile, halo,...]
  transfers between devices with their start and end apart: 7 -> 7, of which waited for: 5 -> 5; matrix products, arithmetic and copies ran while one was open for 9% -> 4% of each run, Pallas kernels for 0% -> 0%
where the time goes in v4:
time: 164 us; the launch traced here: 163 us
  Pallas kernels  44.4 us (27%)
  waiting for transfers between devices  36.8 us (22%)
  starting transfers between devices  35.4 us (22%)
  blocking collectives  25 us (15%)
  local copies, waits for them, and re-layouts  14.4 us (9%)
  between operations  2.44 us (1%)
  other arithmetic  2.39 us (1%)
  matrix products  1.97 us (1%)
    all_to_all x3, waiting for transfers between devices, gathered(): lax.all_to_all(jnp.broadcast_to(block[None], (count,) + block.shape), axe...  31.8 us
    all_to_all x1, blocking collectives, local(): mine = jnp.sum(lax.all_to_all(packed, RC, 0, 0, tiled=True), axis=0)  25 us
    all_to_all x3, starting transfers between devices, gathered(): lax.all_to_all(jnp.broadcast_to(block[None], (count,) + block.shape), axe...  23.3 us
    pallas_call x1, Pallas kernels, local(): pl.pallas_call(backward_kernel, grid=(STEPS,), in_specs=[tile, tile, halo...  21 us
    pallas_call x1, Pallas kernels, local(): pl.pallas_call(forward_kernel, grid=(STEPS,), in_specs=[tile, tile, halo,...  18 us
    unnamed x30, local copies, waits for them, and re-layouts  6.52 us
    ppermute x1, starting transfers between devices, local(): lax.ppermute(jnp.concatenate([x[6:8], c[7:8]], axis=0), 'row', fwd_row)  4.07 us
    ppermute x1, waiting for transfers between devices, local(): lax.ppermute(jnp.concatenate([x[0:2], c[0:1]], axis=0), 'row', bwd_row)  3.86 us
  transfers between devices with their start and end apart: 7, of which 5 were waited for; matrix products, arithmetic and copies ran while one was open for 4% of the time, Pallas kernels for 0%

profile of v4, /device:TPU:1, one launch (start us, length us, event | category | flops | bytes accessed | tf_op | source)
XLA Modules:
  0.0 162.8 jit_solution(15556283074893811001)
XLA Ops:
  0.6 1.3 copy_bitcast_fusion.2
  2.0 4.1 %collective-permute-start = (bf16[3,192,128]{2,1,0:T(8,128)(2,1)S(1)}, bf16[3,192,128]{2,1,0:T(8,128)(2,1)S(1)}, u32[]{:S(2)}, u32[]{:S(2)}) collective-permute-start(bf16[3,192,128]{2,1,0:T(8,128)(2,1)S(1)} %pad_maximum_fusion), channel_id=1, source_target_pairs={{0,4},{4,8},{8,12},{12,16},{16,20},{20,24},{24,28},{1,5},{5,9},{9,... | collective-permute-start | bytes 442376 | tf_op jit(solution)/shard_map/ppermute | solution.py:364
  6.1 1.3 collective-permute-start.1
  7.5 1.1 collective-permute-done.top_ref
  8.6 3.9 %collective-permute-done.1.bot_ref = bf16[3,192,128]{2,1,0:T(8,128)(2,1)S(1)} collective-permute-done((bf16[3,192,128]{2,1,0:T(8,128)(2,1)S(1)}, bf16[3,192,128]{2,1,0:T(8,128)(2,1)S(1)}, u32[]{:S(2)}, u32[]{:S(2)}) %collective-permute-start.1) | collective-permute-done | bytes 147488 | tf_op jit(solution)/shard_map/ppermute | solution.py:365
  13.1 2.2 %strip.1.own_ref = bf16[192,128]{1,0:T(8,128)(2,1)} custom-call(bf16[8,192,128]{2,1,0:T(8,128)(2,1)} %copy-done, bf16[8,192,128]{2,1,0:T(8,128)(2,1)} %copy-done.1, bf16[3,192,128]{2,1,0:T(8,128)(2,1)} %copy-done.2, bf16[3,192,128]{2,1,0:T(8,128)(2,1)} %copy-done.3), custom_call_target="tpu_custom_call" | custom-call | tf_op jit(solution)/shard_map/strip/pallas_call | solution.py:366
  15.3 3.7 %collective-permute-start.3 = (bf16[192,128]{1,0:T(8,128)(2,1)}, bf16[192,128]{1,0:T(8,128)(2,1)S(1)}, u32[]{:S(2)}, u32[]{:S(2)}) collective-permute-start(bf16[192,128]{1,0:T(8,128)(2,1)} %strip.1.own_ref), channel_id=1, source_target_pairs={{1,0},{2,1},{3,2},{5,4},{6,5},{7,6},{9,8},{10,9},{11,10},{13,12},{... | collective-permute-start | bytes 147464 | tf_op jit(solution)/shard_map/ppermute | solution.py:373
  19.0 3.1 %collective-permute-start.2 = (bf16[192,128]{1,0:T(8,128)(2,1)}, bf16[192,128]{1,0:T(8,128)(2,1)S(1)}, u32[]{:S(2)}, u32[]{:S(2)}) collective-permute-start(bf16[192,128]{1,0:T(8,128)(2,1)} %strip.1.own_ref), channel_id=1, source_target_pairs={{0,1},{1,2},{2,3},{4,5},{5,6},{6,7},{8,9},{9,10},{10,11},{12,13},{... | collective-permute-start | bytes 147464 | tf_op jit(solution)/shard_map/ppermute | solution.py:372
  22.2 0.8 copy.37.gain_ref
  22.9 0.9 copy.36.taps_ref
  24.5 18.0 %forward.1 = (f32[768,1024]{1,0:T(8,128)}, f32[768,1408]{1,0:T(8,128)}, f32[6,2,128]{2,1,0:T(2,128)}) custom-call(bf16[8,192,128]{2,1,0:T(8,128)(2,1)} %copy-done, bf16[8,192,128]{2,1,0:T(8,128)(2,1)} %copy-done.1, bf16[3,192,128]{2,1,0:T(8,128)(2,1)} %copy-done.2, bf16[3,192,128]{2,1,0:T(8,128)(2,1)} %copy-done.3, bf16[192,128]{1,0:T(8,128)(2,1)} %strip.1.own_ref, ...), custom_call_target="tpu_custom_call" | custom-call | tf_op jit(solution)/shard_map/forward/pallas_call | solution.py:390
  42.5 0.7 broadcast_in_dim.35
  43.2 0.7 broadcast_in_dim.36
  43.9 10.3 %all-to-all-start = ((f32[32,12,128]{2,1,0:T(8,128)}), f32[32,12,128]{2,1,0:T(8,128)S(1)}, u32[]{:S(2)}, u32[]{:S(2)}) async-start(f32[32,12,128]{2,1,0:T(8,128)} %broadcast_in_dim.36), calls=%async_computation | async-start | bytes 524288 | tf_op jit(solution)/shard_map/all_to_all | solution.py:346
  54.2 0.7 fusion.14.mask_ref
  54.9 8.2 %all-to-all-done.parts_ref = f32[32,12,128]{2,1,0:T(8,128)S(1)} async-done(((f32[32,12,128]{2,1,0:T(8,128)}), f32[32,12,128]{2,1,0:T(8,128)S(1)}, u32[]{:S(2)}, u32[]{:S(2)}) %all-to-all-start) | async-done | bytes 196640 | tf_op jit(solution)/shard_map/all_to_all | solution.py:346
  63.0 0.7 copy-done.4
  63.7 3.2 %squeeze.17 = (f32[768,128]{1,0:T(8,128)}, f32[768,128]{1,0:T(8,128)}, f32[16,128]{1,0:T(8,128)}) custom-call(f32[32,12,128]{2,1,0:T(8,128)} %copy-done.4, f32[48,768]{1,0:T(8,128)} %bitcast.52, f32[48,768]{1,0:T(8,128)} %wexc_ref.1), custom_call_target="tpu_custom_call" | custom-call | tf_op jit(solution)/shard_map/squeeze/pallas_call | solution.py:409
  66.9 21.0 %backward.1 = (bf16[8,192,128]{2,1,0:T(8,128)(2,1)}, bf16[8,192,128]{2,1,0:T(8,128)(2,1)}, f32[2560,128]{1,0:T(8,128)}) custom-call(bf16[8,192,128]{2,1,0:T(8,128)(2,1)} %copy-done, bf16[8,192,128]{2,1,0:T(8,128)(2,1)} %copy-done.1, bf16[3,192,128]{2,1,0:T(8,128)(2,1)} %copy-done.2, bf16[3,192,128]{2,1,0:T(8,128)(2,1)} %copy-done.3, ...), custom_call_target="tpu_custom_call" | custom-call | tf_op jit(solution)/shard_map/backward/pallas_call | solution.py:416
  88.0 25.0 %all_to_all.20 = f32[32,80,128]{2,1,0:T(8,128)S(1)} all-to-all(f32[32,80,128]{2,1,0:T(8,128)} %bitcast.43), channel_id=1, replica_groups=mesh['dp'=8,'row'=8,'col'=4] {'row','col'}, dimensions={0} | all-to-all | bytes 2621440 | tf_op jit(solution)/shard_map/all_to_all | solution.py:441
  113.7 0.8 broadcast_in_dim.39
  114.5 8.2 %all-to-all-start.2 = ((f32[8,96,128]{2,1,0:T(8,128)}), f32[8,96,128]{2,1,0:T(8,128)S(1)}, u32[]{:S(2)}, u32[]{:S(2)}) async-start(f32[8,96,128]{2,1,0:T(8,128)} %broadcast_in_dim.39), calls=%async_computation.2 | async-start | bytes 786432 | tf_op jit(solution)/shard_map/all_to_all | solution.py:346
  122.7 1.0 copy.41
  123.7 1.0 copy.42
  124.7 12.4 %all-to-all-done.2 = f32[8,96,128]{2,1,0:T(8,128)S(1)} async-done(((f32[8,96,128]{2,1,0:T(8,128)}), f32[8,96,128]{2,1,0:T(8,128)S(1)}, u32[]{:S(2)}, u32[]{:S(2)}) %all-to-all-start.2) | async-done | bytes 393248 | tf_op jit(solution)/shard_map/all_to_all | solution.py:346
  140.1 1.0 broadcast_in_dim.42
  141.1 4.8 %all-to-all-start.3 = ((f16[32,80,128]{2,1,0:T(8,128)(2,1)}), f16[32,80,128]{2,1,0:T(8,128)(2,1)S(1)}, u32[]{:S(2)}, u32[]{:S(2)}) async-start(f16[32,80,128]{2,1,0:T(8,128)(2,1)} %broadcast_in_dim.42), calls=%async_computation.3 | async-start | bytes 1310720 | tf_op jit(solution)/shard_map/all_to_all | solution.py:346
  145.9 1.0 fusion
  146.9 1.0 fusion.2
  147.9 11.2 %all-to-all-done.3 = f16[32,80,128]{2,1,0:T(8,128)(2,1)S(1)} async-done(((f16[32,80,128]{2,1,0:T(8,128)(2,1)}), f16[32,80,128]{2,1,0:T(8,128)(2,1)S(1)}, u32[]{:S(2)}, u32[]{:S(2)}) %all-to-all-start.3) | async-done | bytes 655392 | tf_op jit(solution)/shard_map/all_to_all | solution.py:346
  159.5 0.9 copy.52
  161.9 0.9 copy.51
  (56 shorter events, 5.5 us)
Async XLA Ops:
  1.9 10.6 %copy-start = (bf16[8,192,128]{2,1,0:T(8,128)(2,1)}, bf16[8,192,128]{2,1,0:T(8,128)(2,1)S(1)}, u32[]{:S(2)}) copy-start(bf16[8,192,128]{2,1,0:T(8,128)(2,1)S(1)} %get-tuple-element.59.x_ref) | copy-start | bytes 1179652
  1.9 10.6 %copy-start.1 = (bf16[8,192,128]{2,1,0:T(8,128)(2,1)}, bf16[8,192,128]{2,1,0:T(8,128)(2,1)S(1)}, u32[]{:S(2)}) copy-start(bf16[8,192,128]{2,1,0:T(8,128)(2,1)S(1)} %get-tuple-element.58.c_ref) | copy-start | bytes 1179652
  1.9 20.2 %copy-start.11 = (f32[192]{0:T(256)S(1)}, f32[192]{0:T(256)}, u32[]{:S(2)}) copy-start(f32[192]{0:T(256)} %param.9) | copy-start | bytes 2308
  1.9 21.0 %copy-start.9 = (f32[768,9]{0,1:T(8,128)S(1)}, f32[768,9]{0,1:T(8,128)}, u32[]{:S(2)}) copy-start(f32[768,9]{0,1:T(8,128)} %param.11) | copy-start | bytes 82948
  2.0 6.6 %collective-permute-start = (bf16[3,192,128]{2,1,0:T(8,128)(2,1)S(1)}, bf16[3,192,128]{2,1,0:T(8,128)(2,1)S(1)}, u32[]{:S(2)}, u32[]{:S(2)}) collective-permute-start(bf16[3,192,128]{2,1,0:T(8,128)(2,1)S(1)} %pad_maximum_fusion), channel_id=1, source_target_pairs={{0,4},{4,8},{8,12},{12,16},{16,20},{20,24},{24,28},{1,5},{5,9},{9,... | collective-permute-start | bytes 442376 | tf_op jit(solution)/shard_map/ppermute | solution.py:364
  6.1 6.3 %collective-permute-start.1 = (bf16[3,192,128]{2,1,0:T(8,128)(2,1)S(1)}, bf16[3,192,128]{2,1,0:T(8,128)(2,1)S(1)}, u32[]{:S(2)}, u32[]{:S(2)}) collective-permute-start(bf16[3,192,128]{2,1,0:T(8,128)(2,1)S(1)} %pad_maximum_fusion.1), channel_id=1, source_target_pairs={{4,0},{8,4},{12,8},{16,12},{20,16},{24,20},{28,24},{5,1},{9,5},{13... | collective-permute-start | bytes 442376 | tf_op jit(solution)/shard_map/ppermute | solution.py:365
  8.6 3.9 %copy-start.2 = (bf16[3,192,128]{2,1,0:T(8,128)(2,1)}, bf16[3,192,128]{2,1,0:T(8,128)(2,1)S(1)}, u32[]{:S(2)}) copy-start(bf16[3,192,128]{2,1,0:T(8,128)(2,1)S(1)} %collective-permute-done.top_ref) | copy-start | bytes 442372
  12.5 0.7 copy-start.3
  15.3 8.6 %collective-permute-start.3 = (bf16[192,128]{1,0:T(8,128)(2,1)}, bf16[192,128]{1,0:T(8,128)(2,1)S(1)}, u32[]{:S(2)}, u32[]{:S(2)}) collective-permute-start(bf16[192,128]{1,0:T(8,128)(2,1)} %strip.1.own_ref), channel_id=1, source_target_pairs={{1,0},{2,1},{3,2},{5,4},{6,5},{7,6},{9,8},{10,9},{11,10},{13,12},{... | collective-permute-start | bytes 147464 | tf_op jit(solution)/shard_map/ppermute | solution.py:373
  19.0 4.8 %collective-permute-start.2 = (bf16[192,128]{1,0:T(8,128)(2,1)}, bf16[192,128]{1,0:T(8,128)(2,1)S(1)}, u32[]{:S(2)}, u32[]{:S(2)}) collective-permute-start(bf16[192,128]{1,0:T(8,128)(2,1)} %strip.1.own_ref), channel_id=1, source_target_pairs={{0,1},{1,2},{2,3},{4,5},{5,6},{6,7},{8,9},{9,10},{10,11},{12,13},{... | collective-permute-start | bytes 147464 | tf_op jit(solution)/shard_map/ppermute | solution.py:372
  23.9 0.6 copy-start.7
  23.9 0.6 copy-start.8
  43.9 19.1 %all-to-all-start = ((f32[32,12,128]{2,1,0:T(8,128)}), f32[32,12,128]{2,1,0:T(8,128)S(1)}, u32[]{:S(2)}, u32[]{:S(2)}) async-start(f32[32,12,128]{2,1,0:T(8,128)} %broadcast_in_dim.36), calls=%async_computation | async-start | bytes 524288 | tf_op jit(solution)/shard_map/all_to_all | solution.py:346
  63.0 0.7 copy-start.4
  113.0 0.7 copy-start.10
  113.0 9.7 %copy-start.6 = (bf16[8,192,128]{2,1,0:T(8,128)(2,1)S(1)}, bf16[8,192,128]{2,1,0:T(8,128)(2,1)}, u32[]{:S(2)}) copy-start(bf16[8,192,128]{2,1,0:T(8,128)(2,1)} %get-tuple-element.22) | copy-start | bytes 1179652
  113.1 10.6 %copy-start.5 = (bf16[8,192,128]{2,1,0:T(8,128)(2,1)S(1)}, bf16[8,192,128]{2,1,0:T(8,128)(2,1)}, u32[]{:S(2)}) copy-start(bf16[8,192,128]{2,1,0:T(8,128)(2,1)} %get-tuple-element.23) | copy-start | bytes 1179652
  114.5 22.6 %all-to-all-start.2 = ((f32[8,96,128]{2,1,0:T(8,128)}), f32[8,96,128]{2,1,0:T(8,128)S(1)}, u32[]{:S(2)}, u32[]{:S(2)}) async-start(f32[8,96,128]{2,1,0:T(8,128)} %broadcast_in_dim.39), calls=%async_computation.2 | async-start | bytes 786432 | tf_op jit(solution)/shard_map/all_to_all | solution.py:346
  141.1 18.0 %all-to-all-start.3 = ((f16[32,80,128]{2,1,0:T(8,128)(2,1)}), f16[32,80,128]{2,1,0:T(8,128)(2,1)S(1)}, u32[]{:S(2)}, u32[]{:S(2)}) async-start(f16[32,80,128]{2,1,0:T(8,128)(2,1)} %broadcast_in_dim.42), calls=%async_computation.3 | async-start | bytes 1310720 | tf_op jit(solution)/shard_map/all_to_all | solution.py:346

commit v5 on v4

--- a/solution.py
+++ b/solution.py
@@ -1,5 +1,3 @@
-import functools
-
 import jax
 import jax.numpy as jnp
 from jax import lax
@@ -19,6 +17,7 @@
 BLOCKS = EX // LANES
 PARTS, PACK = 32, 80
 VMEM = 60 * 1024 * 1024
+CHIPS = [[2 * q + core for q in range(PARTS // 2)] for core in range(2)]
 XS = ROWS + 5
 CS = ROWS + 3
 NT = (((1,), (1,)), ((), ()))
@@ -98,13 +97,27 @@
     return left, right
 
 
+def spread_gain(gain_ref):
+    return jnp.broadcast_to(gain_ref[...], (LANES, CH)).T
+
+
+def spread_taps(taps_ref, out_s):
+    for n in range(EB // LANES):
+        rows = slice(n * LANES, (n + 1) * LANES)
+        block = jnp.concatenate([taps_ref[:, rows], jnp.zeros((7, LANES), F32)], axis=0).T
+        for t in range(9):
+            out_s[rows, slab(t)] = jnp.broadcast_to(block[:, t : t + 1], (LANES, LANES))
+
+
 def forward_kernel(
     x_ref, c_ref, top_ref, bot_ref, own_ref, left_ref, right_ref, gain_ref, wexp_ref, taps_ref,
-    wprojt_ref, pre_out, conv_out, sums_out, scaled_s, cot_s, pre_s, gg_s, acc_s,
+    wprojt_ref, pre_out, conv_out, sums_out, scaled_s, cot_s, pre_s, gg_s, taps_s, acc_s,
 ):
-    @pl.when(pl.program_id(0) == 0)
+    step = pl.program_id(0)
+
+    @pl.when(step == 0)
     def _():
-        gain = gain_ref[...]
+        gain = spread_gain(gain_ref)
         for s in range(XS):
             if s < 2:
                 x = top_ref[s].astype(F32)
@@ -115,27 +128,27 @@
             else:
                 x = input_strip(own_ref, left_ref, right_ref)
             inverse = lax.rsqrt(jnp.sum(x * x, axis=0, keepdims=True) / CH + EPS)
-            place = s - 2 if 2 <= s < ROWS + 2 else s + ROWS if s < 2 else s
-            scaled_s[:, slab(place)] = (x * inverse * gain).astype(BF16)
+            scaled_s[:, slab(s)] = (x * inverse * gain).astype(BF16)
         for r in range(ROWS):
             cot_s[:, slab(r)] = c_ref[r]
-
-    wexp = wexp_ref[...]
-    pre_out[...] = tn_dot(wexp, scaled_s[:, slab(0, ROWS)])
-    pre_s[...] = tn_dot(wexp, scaled_s[:, slab(ROWS, XS - ROWS)])
-    gg_s[...] = tn_dot(wprojt_ref[...], cot_s[...])
+        pre_s[...] = tn_dot(wexp_ref[...], scaled_s[...])
+        gg_s[...] = tn_dot(wprojt_ref[...], cot_s[...])
+        sums_out[...] = jnp.zeros_like(sums_out)
+
+    spread_taps(taps_ref, taps_s)
+    base = step * EB
     lane = lane_iota(SUB)
     first, last = lane == 0, lane == LANES - 1
 
     def body(i, carry):
         ds = pl.ds(pl.multiple_of(i * SUB, SUB), SUB)
-        k = [jnp.broadcast_to(taps_ref[ds, t : t + 1], (SUB, LANES)) for t in range(9)]
+        whole = pl.ds(pl.multiple_of(base + i * SUB, SUB), SUB)
+        k = [taps_s[ds, slab(t)] for t in range(9)]
 
         def hidden(s):
+            v = pre_s[whole, slab(s)]
             if 2 <= s < ROWS + 2:
-                v = pre_out[ds, slab(s - 2)]
-            else:
-                v = pre_s[ds, slab(s if s < 2 else s - ROWS)]
+                pre_out[ds, slab(s - 2)] = v
             v = 0.5 * v
             return rounded(v + v * jnp.tanh(v))
 
@@ -156,9 +169,10 @@
             v = acc[o]
             conv_out[ds, slab(o - 1)] = v
             if 2 <= o <= ROWS + 1:
-                act = v * sigmoid(v)
+                half = 0.5 * v
+                act = half + half * jnp.tanh(half)
                 pooled = pooled + act
-                gexc = gexc + act * gg_s[ds, slab(o - 2)]
+                gexc = gexc + act * gg_s[whole, slab(o - 2)]
         edge = None
         for a in (-1, 0, 1):
             for c in (-1, 0, 1):
@@ -171,10 +185,12 @@
 
     lax.fori_loop(0, EB // SUB, body, 0)
     for n in range(EB // LANES):
-        sums_out[n] = acc_s[n * LANES : (n + 1) * LANES, :].T[:2]
-
-
-def squeeze_kernel(parts_ref, wsq_ref, wexc_ref, exc_out, gp_out, vec_out):
+        sums_out[pl.ds(2 * (step * (EB // LANES) + n), 2), :] = (
+            acc_s[n * LANES : (n + 1) * LANES, :].T[:2]
+        )
+
+
+def squeeze_excite(parts_ref, wsq_ref, wexc_ref, exc_s, gp_s, vec_out):
     pixels = 32768.0
     total = jnp.sum(parts_ref[...], axis=0)
     pooled = jnp.concatenate([total[2 * j : 2 * j + 1] for j in range(BLOCKS)], axis=1) / pixels
@@ -195,33 +211,26 @@
     vec_out[...] = jnp.zeros((16, LANES), F32)
     for j in range(BLOCKS):
         cols = slice(j * LANES, (j + 1) * LANES)
-        exc_out[cols, :] = jnp.broadcast_to(excite[:1, cols], (LANES, LANES)).T
-        gp_out[cols, :] = jnp.broadcast_to(gpool[:1, cols], (LANES, LANES)).T
+        exc_s[cols, :] = jnp.broadcast_to(excite[:1, cols], (LANES, LANES)).T
+        gp_s[cols, :] = jnp.broadcast_to(gpool[:1, cols], (LANES, LANES)).T
         vec_out[j : j + 1, :] = pooled[:1, cols]
         vec_out[BLOCKS + j : BLOCKS + j + 1, :] = gepre[:1, cols]
     vec_out[12:13, :SQ] = squeezed[:1]
     vec_out[13:14, :SQ] = gspre[:1]
 
 
-def big_rows(group):
-    return pl.ds(pl.multiple_of(PACK * (group // 3) + 24 * (group % 3), 8), 24)
-
-
-def small_row(row):
-    return pl.ds(PACK * (row // 2) + 72 + row % 2, 1)
-
-
 def backward_kernel(
-    x_ref, c_ref, top_ref, bot_ref, left_ref, right_ref, gain_ref, mask_ref, pre_ref, conv_ref,
-    exc_ref, gp_ref, taps_ref, wexp_ref, wprojt_ref,
-    out_out, gin_out, packed_out,
-    scaled_s, cot_s, inv_s, gg_s, gated_s, gpre_s, proj_s, gs_s, acc_s,
+    core_ref, parts_ref, wsq_ref, wexc_ref, x_ref, c_ref, top_ref, bot_ref, left_ref, right_ref,
+    gain_ref, mask_ref, pre_ref, conv_ref, taps_ref, wexp_ref, wprojt_ref,
+    out_out, gin_out, keep_out, send_out, vec_out,
+    packed_s, exc_s, gp_s, scaled_s, cot_s, inv_s, gg_s, gated_s, gpre_s, taps_s, acc_s, tsum_s,
 ):
     step = pl.program_id(0)
 
     @pl.when(step == 0)
     def _():
-        gain = gain_ref[...]
+        squeeze_excite(parts_ref, wsq_ref, wexc_ref, exc_s, gp_s, vec_out)
+        gain = spread_gain(gain_ref)
         for r in range(ROWS):
             x = x_ref[r].astype(F32)
             inverse = lax.rsqrt(jnp.sum(x * x, axis=0, keepdims=True) / CH + EPS)
@@ -231,35 +240,36 @@
         cot_s[:, slab(0)] = top_ref[2]
         cot_s[:, slab(ROWS + 1)] = bot_ref[2]
         cot_s[:, slab(CS - 1)] = cotangent_strip(left_ref, right_ref).astype(BF16)
-        proj_s[...] = jnp.zeros_like(proj_s)
-        gs_s[...] = jnp.zeros_like(gs_s)
-        for d in range(PARTS):
-            packed_out[d * PACK + 72 : (d + 1) * PACK, :] = jnp.zeros((8, LANES), F32)
-
-    gg_s[...] = tn_dot(wprojt_ref[...], cot_s[...])
+        gg_s[...] = tn_dot(wprojt_ref[...], cot_s[...])
+
+    spread_taps(taps_ref, taps_s)
+    base = step * EB
     lane = lane_iota(SUB)
     first, last = lane == 0, lane == LANES - 1
 
     def body(i, carry):
         ds = pl.ds(pl.multiple_of(i * SUB, SUB), SUB)
-        k = [jnp.broadcast_to(taps_ref[ds, t : t + 1], (SUB, LANES)) for t in range(9)]
-        exc, gp = exc_ref[ds, :], gp_ref[ds, :]
+        whole = pl.ds(pl.multiple_of(base + i * SUB, SUB), SUB)
+        k = [taps_s[ds, slab(t)] for t in range(9)]
+        exc, gp = exc_s[whole, :], gp_s[whole, :]
 
         def grad_conv(s, mask):
-            v = conv_ref[ds, slab(s)]
-            sig = sigmoid(v)
-            act = v * sig
+            half = 0.5 * conv_ref[ds, slab(s)]
+            t = jnp.tanh(half)
+            act = half + half * t
             if 1 <= s <= ROWS:
-                gated_s[ds, slab(s - 1)] = act * exc
-            g = (gg_s[ds, slab(s)] * exc + gp) * (sig + act * (1.0 - sig))
+                gated_s[whole, slab(s - 1)] = (act * exc).astype(BF16)
+            sig = 0.5 + 0.5 * t
+            g = (gg_s[whole, slab(s)] * exc + gp) * (sig + act * (1.0 - sig))
             if mask is not None:
                 g = jnp.where(mask_ref[mask : mask + 1, :] > 0.5, g, 0.0)
             return rounded(g)
 
         def hidden(r):
-            v = pre_ref[ds, slab(r)]
-            sig = sigmoid(v)
-            act = v * sig
+            half = 0.5 * pre_ref[ds, slab(r)]
+            t = jnp.tanh(half)
+            act = half + half * t
+            sig = 0.5 + 0.5 * t
             return rounded(act), sig + act * (1.0 - sig)
 
         strip = grad_conv(CS - 1, 2)
@@ -282,7 +292,7 @@
                         tap[t + c] = h * v if tap[t + c] is None else tap[t + c] + h * v
             r = s - 2
             if 0 <= r:
-                gpre_s[ds, slab(r)] = gh.pop(r) * state.pop(r)[1]
+                gpre_s[whole, slab(r)] = (gh.pop(r) * state.pop(r)[1]).astype(BF16)
         total = jnp.zeros((SUB, LANES), F32)
         for t in range(9):
             total = jnp.where(lane == t, lane_sum(tap[t]), total)
@@ -290,42 +300,68 @@
         return carry
 
     lax.fori_loop(0, EB // SUB, body, 0)
-    gated = gated_s[...].astype(BF16)
-    gpre = gpre_s[...].astype(BF16)
-    wproj = lax.dot_general(cot_s[:, slab(1, ROWS)], gated, NT, preferred_element_type=F32)
-    wexp = lax.dot_general(scaled_s[...], gpre, NT, preferred_element_type=F32)
-    groups = CH // 24
     for n in range(EB // LANES):
+        taps = acc_s[n * LANES : (n + 1) * LANES, :].T
         block = step * (EB // LANES) + n
-        for w, which in ((wexp, 0), (wproj, BLOCKS * groups)):
-            for i in range(groups):
-                packed_out[big_rows(which + block * groups + i), :] = w[
-                    24 * i : 24 * i + 24, n * LANES : (n + 1) * LANES
-                ]
-        taps = acc_s[n * LANES : (n + 1) * LANES, :].T
         for t in range(9):
-            packed_out[small_row(BLOCKS * t + block), :] = taps[t : t + 1]
-    proj_s[...] += jnp.dot(wprojt_ref[...], gated, preferred_element_type=F32)
-    gs_s[...] += jnp.dot(wexp_ref[...], gpre, preferred_element_type=F32)
+            tsum_s[pl.ds(BLOCKS * t + block, 1), :] = taps[t : t + 1]
 
     @pl.when(step == STEPS - 1)
     def _():
-        gain = gain_ref[...]
+        gated, gpre = gated_s[...], gpre_s[...]
+        for which, w in enumerate(
+            (
+                lax.dot_general(scaled_s[...], gpre, NT, preferred_element_type=F32),
+                lax.dot_general(cot_s[:, slab(1, ROWS)], gated, NT, preferred_element_type=F32),
+            )
+        ):
+            for n in range(BLOCKS):
+                for i in range(CH // 24):
+                    group = (which * BLOCKS + n) * (CH // 24) + i
+                    row = PACK * (group // 3) + 24 * (group % 3)
+                    packed_s[row : row + 24, :] = w[24 * i : 24 * i + 24, slab(n)]
+        proj = jnp.dot(wprojt_ref[...], gated, preferred_element_type=F32)
+        gs_all = jnp.dot(wexp_ref[...], gpre, preferred_element_type=F32)
+        gain = spread_gain(gain_ref)
         ggain = jnp.zeros((CH, LANES), F32)
         for r in range(ROWS):
             x = x_ref[r].astype(F32)
-            out_out[r] = (x + proj_s[:, slab(r)]).astype(BF16)
-            inverse = inv_s[r : r + 1, :]
-            normed = x * inverse
-            gs = gs_s[:, slab(r)]
+            out_out[r] = (x + proj[:, r * LANES : (r + 1) * LANES]).astype(BF16)
+            normed = x * inv_s[r : r + 1, :]
+            gs = gs_all[:, r * LANES : (r + 1) * LANES]
             prod = gs * normed
             ggain = ggain + prod
             mean = jnp.sum(prod * gain, axis=0, keepdims=True) / CH
-            gin = inverse * (gs * gain - normed * mean) + c_ref[r].astype(F32)
+            gin = inv_s[r : r + 1, :] * (gs * gain - normed * mean) + c_ref[r].astype(F32)
             gin_out[r] = gin.astype(BF16)
         sums = jnp.broadcast_to(lane_sum(ggain), (CH, LANES)).T[:1]
-        packed_out[small_row(9 * BLOCKS), :] = sums[:, :LANES]
-        packed_out[pl.ds(9 * BLOCKS // 2 * PACK + 73, 1), : CH - LANES] = sums[:, LANES:]
+        tsum_s[54:55, :] = sums[:, :LANES]
+        tsum_s[55:56, :] = jnp.zeros((1, LANES), F32)
+        tsum_s[55:56, : CH - LANES] = sums[:, LANES:]
+        for d in range(PARTS):
+            packed_s[d * PACK + 72 : (d + 1) * PACK, :] = jnp.zeros((8, LANES), F32)
+            if d < 28:
+                packed_s[d * PACK + 72 : d * PACK + 74, :] = tsum_s[2 * d : 2 * d + 2, :]
+        core = core_ref[0]
+        for q in range(PARTS // 2):
+            keep_out[q] = packed_s[pl.ds(pl.multiple_of(PACK * (2 * q + core), 8), PACK), :]
+            send_out[q] = packed_s[pl.ds(pl.multiple_of(PACK * (2 * q + 1 - core), 8), PACK), :]
+
+
+def scale_kernel(x_ref, out_ref):
+    x = x_ref[...]
+
+    def exponent(v):
+        top = jnp.max(jnp.max(jnp.abs(v), axis=1, keepdims=True), axis=0, keepdims=True)
+        return jnp.ceil(jnp.log2(jnp.maximum(top, 1e-30)))
+
+    row = lax.broadcasted_iota(jnp.int32, (8, LANES), 0)
+    rest = x[72:80]
+    e_big = exponent(x[:72])
+    e_small = exponent(jnp.where(row < 2, rest, 0.0))
+    out_ref[:72] = x[:72] * jnp.exp2(-e_big)
+    rest = jnp.where(row < 5, jnp.broadcast_to(e_big, (8, LANES)), jnp.broadcast_to(e_small, (8, LANES)))
+    out_ref[72:] = jnp.where(row < 2, x[72:80] * jnp.exp2(-e_small), rest)
 
 
 def shape(*dims, dtype=F32):
@@ -342,14 +378,13 @@
     )
 
 
-def gathered(block, axes, count):
-    return lax.all_to_all(
-        jnp.broadcast_to(block[None], (count,) + block.shape), axes, 0, 0, tiled=True
-    )
-
-
-def exponent(v):
-    return jnp.ceil(jnp.log2(jnp.maximum(jnp.max(jnp.abs(v)), 1e-30)))
+def gathered(block):
+    wide = jnp.broadcast_to(block[None], (PARTS // 2,) + block.shape)
+    return lax.all_to_all(wide, RC, 0, 0, tiled=True, axis_index_groups=CHIPS)
+
+
+def partner(block):
+    return lax.ppermute(block, "col", [(i, i ^ 1) for i in range(4)])
 
 
 def local(inputs, norm_gain, w_expand, kernel, w_squeeze, w_excite, w_project, cotangent):
@@ -380,81 +415,96 @@
     strip_ok &= ((line > 1) | top_ok) & ((line < ROWS + 2) | bot_ok)
     mask = ((kind == 0) & top_ok) | ((kind == 1) & bot_ok) | ((kind == 2) & strip_ok)
     mask = mask.astype(F32)
-    gain = norm_gain[:, None]
-    wprojt = w_project.T
+    gain = norm_gain[None, :]
+    wprojt, taps = w_project.T, kernel.T
     halo = full(3, CH, LANES)
     tile = full(ROWS, CH, LANES)
     edge = full(CH, LANES)
+    weight = full(CH, EX)
     chunk_rows = lambda width: pl.BlockSpec((EB, width), lambda j: (j, 0))
-    chunk_cols = pl.BlockSpec((CH, EB), lambda j: (0, j))
+    chunk_taps = pl.BlockSpec((9, EB), lambda j: (0, j))
     pre, conv, sums = pl.pallas_call(
         forward_kernel,
         grid=(STEPS,),
-        in_specs=[tile, tile, halo, halo, edge, edge, edge, full(CH, 1),
-                  chunk_cols, chunk_rows(9), chunk_cols],
-        out_specs=[chunk_rows(ROWS * LANES), chunk_rows(CS * LANES),
-                   pl.BlockSpec((EB // LANES, 2, LANES), lambda j: (j, 0, 0))],
-        out_shape=[shape(EX, ROWS * LANES), shape(EX, CS * LANES), shape(BLOCKS, 2, LANES)],
+        in_specs=[tile, tile, halo, halo, edge, edge, edge, full(1, CH), weight, chunk_taps,
+                  weight],
+        out_specs=[chunk_rows(ROWS * LANES), chunk_rows(CS * LANES), full(16, LANES)],
+        out_shape=[shape(EX, ROWS * LANES), shape(EX, CS * LANES), shape(16, LANES)],
         scratch_shapes=[
             pltpu.VMEM((CH, XS * LANES), BF16),
             pltpu.VMEM((CH, ROWS * LANES), BF16),
-            pltpu.VMEM((EB, (XS - ROWS) * LANES), F32),
-            pltpu.VMEM((EB, ROWS * LANES), F32),
+            pltpu.VMEM((EX, XS * LANES), F32),
+            pltpu.VMEM((EX, ROWS * LANES), F32),
+            pltpu.VMEM((EB, 9 * LANES), F32),
             pltpu.VMEM((EB, LANES), F32),
         ],
         compiler_params=params(),
         name="forward",
-    )(x, c, top, bot, own, left, right, gain, w_expand, kernel, wprojt)
-
-    exc, gp, vec = pl.pallas_call(
-        squeeze_kernel,
-        out_shape=[shape(EX, LANES), shape(EX, LANES), shape(16, LANES)],
-        compiler_params=params(False),
-        name="squeeze",
-    )(gathered(sums.reshape(2 * BLOCKS, LANES), RC, 32), w_squeeze.T, w_excite)
-
-    out, gin, packed = pl.pallas_call(
+    )(x, c, top, bot, own, left, right, gain, w_expand, taps, wprojt)
+
+    sums = gathered(sums + partner(sums))
+    core = (col % 2).astype(jnp.int32).reshape(1)
+    out, gin, keep, send, vec = pl.pallas_call(
         backward_kernel,
         grid=(STEPS,),
-        in_specs=[tile, tile, halo, halo, edge, edge, full(CH, 1), full(8, LANES),
-                  chunk_rows(ROWS * LANES), chunk_rows(CS * LANES), chunk_rows(LANES),
-                  chunk_rows(LANES), chunk_rows(9), chunk_cols, chunk_cols],
-        out_specs=[tile, tile, full(PARTS * PACK, LANES)],
+        in_specs=[pl.BlockSpec(memory_space=pltpu.SMEM), full(PARTS // 2, 16, LANES),
+                  full(SQ, EX), full(SQ, EX), tile, tile, halo, halo, edge, edge, full(1, CH),
+                  full(8, LANES), chunk_rows(ROWS * LANES), chunk_rows(CS * LANES), chunk_taps,
+                  weight, weight],
+        out_specs=[tile, tile, full(PARTS // 2, PACK, LANES), full(PARTS // 2, PACK, LANES),
+                   full(16, LANES)],
         out_shape=[shape(ROWS, CH, LANES, dtype=BF16), shape(ROWS, CH, LANES, dtype=BF16),
-                   shape(PARTS * PACK, LANES)],
+                   shape(PARTS // 2, PACK, LANES), shape(PARTS // 2, PACK, LANES),
+                   shape(16, LANES)],
         scratch_shapes=[
+            pltpu.VMEM((PARTS * PACK, LANES), F32),
+            pltpu.VMEM((EX, LANES), F32),
+            pltpu.VMEM((EX, LANES), F32),
             pltpu.VMEM((CH, ROWS * LANES), BF16),
             pltpu.VMEM((CH, CS * LANES), BF16),
             pltpu.VMEM((ROWS, LANES), F32),
-            pltpu.VMEM((EB, CS * LANES), F32),
-            pltpu.VMEM((EB, ROWS * LANES), F32),
-            pltpu.VMEM((EB, ROWS * LANES), F32),
-            pltpu.VMEM((CH, ROWS * LANES), F32),
-            pltpu.VMEM((CH, ROWS * LANES), F32),
+            pltpu.VMEM((EX, CS * LANES), F32),
+            pltpu.VMEM((EX, ROWS * LANES), BF16),
+            pltpu.VMEM((EX, ROWS * LANES), BF16),
+            pltpu.VMEM((EB, 9 * LANES), F32),
             pltpu.VMEM((EB, LANES), F32),
+            pltpu.VMEM((56, LANES), F32),
         ],
         compiler_params=params(),
         name="backward",
-    )(x, c, top, bot, left, right, gain, mask, pre, conv, exc, gp, kernel, w_expand, wprojt)
-
-    packed = packed.reshape(PARTS, PACK, LANES)
-    mine = jnp.sum(lax.all_to_all(packed, RC, 0, 0, tiled=True), axis=0)
-    shared = gathered(jnp.concatenate([mine, vec], axis=0), "dp", 8)
-    total = jnp.sum(shared[:, :80], axis=0)
-    vecs = shared[:, 80:].reshape(8, 2048)
+    )(core, sums, w_squeeze.T, w_excite, x, c, top, bot, left, right, gain, mask, pre, conv, taps,
+      w_expand, wprojt)
+
+    mine = lax.all_to_all(
+        keep + partner(send), RC, 0, 0, tiled=True, axis_index_groups=CHIPS
+    )
+    total = jnp.sum(mine, axis=0)
+    vecs = vec[None]
+    sample = lax.axis_index("dp")
+    for bit in (1, 2, 4):
+        both = lax.ppermute(
+            jnp.concatenate([total, vecs.reshape(16 * bit, LANES)], axis=0),
+            "dp",
+            [(i, i ^ bit) for i in range(8)],
+        )
+        total = total + both[:PACK]
+        theirs = both[PACK:].reshape(bit, 16, LANES)
+        ahead = (sample & bit) == 0
+        vecs = jnp.concatenate(
+            [jnp.where(ahead, vecs, theirs), jnp.where(ahead, theirs, vecs)], axis=0
+        )
+    vecs = vecs.reshape(8, 2048)
     grad_wexc = jnp.einsum("bs,be->se", vecs[:, 1536:1584], vecs[:, 768:1536], precision=HIGH)
     grad_wsq = jnp.einsum("be,bs->es", vecs[:, :768], vecs[:, 1664:1712], precision=HIGH)
-    e_big, e_small = exponent(total[:72]), exponent(total[72:74])
-    send = jnp.concatenate(
-        [
-            total[:72] * jnp.exp2(-e_big),
-            total[72:74] * jnp.exp2(-e_small),
-            jnp.full((3, 128), e_big),
-            jnp.full((3, 128), e_small),
-        ],
-        axis=0,
-    ).astype(jnp.float16)
-    every = gathered(send, RC, 32).astype(F32)
+    scaled = pl.pallas_call(
+        scale_kernel, out_shape=shape(PACK, LANES), compiler_params=params(False), name="scale"
+    )(total)
+    same = gathered(scaled.astype(jnp.float16))
+    other = partner(same)
+    even = core[0] == 0
+    every = jnp.stack(
+        [jnp.where(even, same, other), jnp.where(even, other, same)], axis=1
+    ).reshape(PARTS, PACK, LANES).astype(F32)
     big = (every[:, :72] * jnp.exp2(every[:, 74:75])).reshape(2, BLOCKS, CH, LANES)
     small = (every[:, 72:74] * jnp.exp2(every[:, 77:78])).reshape(8192)
     return (

time: 164 us -> 153 us (0.933)
  starting transfers between devices: 35.4 us -> 47.5 us
  waiting for transfers between devices: 36.8 us -> 25.9 us
  blocking collectives: 25 us -> 15.2 us
  local copies, waits for them, and re-layouts: 14.4 us -> 10.1 us
  other arithmetic: 2.39 us -> 4.78 us
    ppermute x0 -> x6, starting transfers between devices: none -> 19.4 us  [the longest x3 11.6 us: local(): lax.ppermute(jnp.concatenate([total, vecs.reshape(16 * bit, LANES)], axis...]
    all_to_all x3 -> x2, waiting for transfers between devices: 31.8 us -> 13.6 us  [gathered(): return lax.all_to_all(wide, RC, 0, 0, tiled=True, axis_index_groups=CHIPS)]
    all_to_all x1, blocking collectives: 25 us -> 15.2 us  [local(): lax.all_to_all(keep + partner(send), RC, 0, 0, tiled=True, axis_index_gro...]
    all_to_all x3 -> x2, starting transfers between devices: 23.3 us -> 15 us  [gathered(): return lax.all_to_all(wide, RC, 0, 0, tiled=True, axis_index_groups=CHIPS)]
    ppermute x0 -> x6, waiting for transfers between devices: none -> 6.64 us  [the longest x3 3.36 us: local(): lax.ppermute(jnp.concatenate([total, vecs.reshape(16 * bit, LANES)], axis...]
    ppermute x1, waiting for transfers between devices: 0.01 us -> 3.65 us  [local(): right = lax.ppermute(own, 'col', bwd_col)]
    ppermute x1, waiting for transfers between devices: 3.86 us -> 0.54 us  [local(): lax.ppermute(jnp.concatenate([x[0:2], c[0:1]], axis=0), 'row', bwd_row)]
    broadcast_in_dim x7 -> x2, local copies, waits for them, and re-layouts: 3.94 us -> 1.44 us  [gathered(): wide = jnp.broadcast_to(block[None], (PARTS // 2,) + block.shape)]
  transfers between devices with their start and end apart: 7 -> 12, of which waited for: 5 -> 10; matrix products, arithmetic and copies ran while one was open for 4% -> 3% of each run, Pallas kernels for 0% -> 0%
where the time goes in v5:
time: 153 us; the launch traced here: 152 us
  starting transfers between devices  47.5 us (31%)
  Pallas kernels  45.5 us (30%)
  waiting for transfers between devices  25.9 us (17%)
  blocking collectives  15.2 us (10%)
  local copies, waits for them, and re-layouts  10.1 us (7%)
  other arithmetic  4.78 us (3%)
  matrix products  1.98 us (1%)
    pallas_call x1, Pallas kernels, local(): pl.pallas_call(backward_kernel, grid=(STEPS,), in_specs=[pl.BlockSpec(mem...  23 us
    pallas_call x1, Pallas kernels, local(): pl.pallas_call(forward_kernel, grid=(STEPS,), in_specs=[tile, tile, halo,...  18.9 us
    all_to_all x1, blocking collectives, local(): lax.all_to_all(keep + partner(send), RC, 0, 0, tiled=True, axis_index_gro...  15.2 us
    all_to_all x2, starting transfers between devices, gathered(): return lax.all_to_all(wide, RC, 0, 0, tiled=True, axis_index_groups=CHIPS)  15 us
    all_to_all x2, waiting for transfers between devices, gathered(): return lax.all_to_all(wide, RC, 0, 0, tiled=True, axis_index_groups=CHIPS)  13.6 us
    ppermute x3, starting transfers between devices, local(): lax.ppermute(jnp.concatenate([total, vecs.reshape(16 * bit, LANES)], axis...  11.6 us
    ppermute x3, starting transfers between devices, partner(): return lax.ppermute(block, 'col', [(i, i ^ 1) for i in range(4)])  7.8 us
    ppermute x1, starting transfers between devices, local(): left = lax.ppermute(own, 'col', fwd_col)  5.28 us
  transfers between devices with their start and end apart: 12, of which 10 were waited for; matrix products, arithmetic and copies ran while one was open for 3% of the time, Pallas kernels for 0%

profile of v5, /device:TPU:1, one launch (start us, length us, event | category | flops | bytes accessed | tf_op | source)
XLA Modules:
  0.0 152.1 jit_solution(11880207800906526122)
XLA Ops:
  0.6 1.3 copy_bitcast_fusion.2
  2.0 1.3 collective-permute-start.1
  3.3 4.6 %collective-permute-start = (bf16[3,192,128]{2,1,0:T(8,128)(2,1)S(1)}, bf16[3,192,128]{2,1,0:T(8,128)(2,1)S(1)}, u32[]{:S(2)}, u32[]{:S(2)}) collective-permute-start(bf16[3,192,128]{2,1,0:T(8,128)(2,1)S(1)} %pad_maximum_fusion.1), channel_id=1, source_target_pairs={{0,4},{4,8},{8,12},{12,16},{16,20},{20,24},{24,28},{1,5},{5,9},{9,... | collective-permute-start | bytes 442376 | tf_op jit(solution)/shard_map/ppermute | solution.py:399
  8.4 1.5 collective-permute-done.top_ref
  10.6 2.2 %strip.1.own_ref = bf16[192,128]{1,0:T(8,128)(2,1)} custom-call(bf16[8,192,128]{2,1,0:T(8,128)(2,1)} %copy-done, bf16[8,192,128]{2,1,0:T(8,128)(2,1)} %copy-done.1, bf16[3,192,128]{2,1,0:T(8,128)(2,1)} %copy-done.3, bf16[3,192,128]{2,1,0:T(8,128)(2,1)} %copy-done.2), custom_call_target="tpu_custom_call" | custom-call | tf_op jit(solution)/shard_map/strip/pallas_call | solution.py:401
  12.8 5.3 %collective-permute-start.2 = (bf16[192,128]{1,0:T(8,128)(2,1)}, bf16[192,128]{1,0:T(8,128)(2,1)S(1)}, u32[]{:S(2)}, u32[]{:S(2)}) collective-permute-start(bf16[192,128]{1,0:T(8,128)(2,1)} %strip.1.own_ref), channel_id=1, source_target_pairs={{0,1},{1,2},{2,3},{4,5},{5,6},{6,7},{8,9},{9,10},{10,11},{12,13},{... | collective-permute-start | bytes 147464 | tf_op jit(solution)/shard_map/ppermute | solution.py:407
  18.1 1.9 %collective-permute-start.3 = (bf16[192,128]{1,0:T(8,128)(2,1)}, bf16[192,128]{1,0:T(8,128)(2,1)S(1)}, u32[]{:S(2)}, u32[]{:S(2)}) collective-permute-start(bf16[192,128]{1,0:T(8,128)(2,1)} %strip.1.own_ref), channel_id=1, source_target_pairs={{1,0},{2,1},{3,2},{5,4},{6,5},{7,6},{9,8},{10,9},{11,10},{13,12},{... | collective-permute-start | bytes 147464 | tf_op jit(solution)/shard_map/ppermute | solution.py:408
  20.1 3.6 %collective-permute-done.3.right_ref = bf16[192,128]{1,0:T(8,128)(2,1)S(1)} collective-permute-done((bf16[192,128]{1,0:T(8,128)(2,1)}, bf16[192,128]{1,0:T(8,128)(2,1)S(1)}, u32[]{:S(2)}, u32[]{:S(2)}) %collective-permute-start.3) | collective-permute-done | bytes 49184 | tf_op jit(solution)/shard_map/ppermute | solution.py:408
  24.3 18.9 %forward.1 = (f32[768,1024]{1,0:T(8,128)}, f32[768,1408]{1,0:T(8,128)}, f32[16,128]{1,0:T(8,128)}) custom-call(bf16[8,192,128]{2,1,0:T(8,128)(2,1)} %copy-done, bf16[8,192,128]{2,1,0:T(8,128)(2,1)} %copy-done.1, bf16[3,192,128]{2,1,0:T(8,128)(2,1)} %copy-done.3, bf16[3,192,128]{2,1,0:T(8,128)(2,1)} %copy-done.2, bf16[192,128]{1,0:T(8,128)(2,1)} %strip.1.own_ref, ...), custom_call_target="tpu_custom_call" | custom-call | tf_op jit(solution)/shard_map/forward/pallas_call | solution.py:426
  43.3 1.3 collective-permute-done.4
  46.0 11.5 %all-to-all-start = ((f32[16,16,128]{2,1,0:T(8,128)}), f32[16,16,128]{2,1,0:T(8,128)S(1)}, u32[]{:S(2)}, u32[]{:S(2)}) async-start(f32[16,16,128]{2,1,0:T(8,128)} %broadcast_in_dim.11), calls=%async_computation | async-start | bytes 262144 | tf_op jit(solution)/shard_map/all_to_all | solution.py:383
  58.2 6.0 %all-to-all-done.parts_ref = f32[16,16,128]{2,1,0:T(8,128)S(1)} async-done(((f32[16,16,128]{2,1,0:T(8,128)}), f32[16,16,128]{2,1,0:T(8,128)S(1)}, u32[]{:S(2)}, u32[]{:S(2)}) %all-to-all-start) | async-done | bytes 131104 | tf_op jit(solution)/shard_map/all_to_all | solution.py:383
  64.8 23.0 %backward.1 = (bf16[8,192,128]{2,1,0:T(8,128)(2,1)}, bf16[8,192,128]{2,1,0:T(8,128)(2,1)}, f32[16,80,128]{2,1,0:T(8,128)}, f32[16,80,128]{2,1,0:T(8,128)}, f32[16,128]{1,0:T(8,128)}) custom-call(s32[1]{0:T(128)} %bitcast.core_ref, f32[16,16,128]{2,1,0:T(8,128)} %copy-done.4, f32[48,768]{1,0:T(8,128)} %bitcast.64, f32[48,768]{1,0:T(8,128)} %wexc_ref.1, ...), custom_call_target="tpu_custom_call" | custom-call | tf_op jit(solution)/shard_map/backward/pallas_call | solution.py:447
  87.9 1.7 %collective-permute-start.5 = (f32[16,80,128]{2,1,0:T(8,128)}, f32[16,80,128]{2,1,0:T(8,128)S(1)}, u32[]{:S(2)}, u32[]{:S(2)}) collective-permute-start(f32[16,80,128]{2,1,0:T(8,128)} %get-tuple-element.22), channel_id=1, source_target_pairs={{0,1},{1,0},{2,3},{3,2},{4,5},{5,4},{6,7},{7,6},{8,9},{9,8},{10,11... | collective-permute-start | bytes 1966088 | tf_op jit(solution)/shard_map/ppermute | solution.py:387
  89.5 1.9 %collective-permute-done.5 = f32[16,80,128]{2,1,0:T(8,128)S(1)} collective-permute-done((f32[16,80,128]{2,1,0:T(8,128)}, f32[16,80,128]{2,1,0:T(8,128)S(1)}, u32[]{:S(2)}, u32[]{:S(2)}) %collective-permute-start.5) | collective-permute-done | bytes 655392 | tf_op jit(solution)/shard_map/ppermute | solution.py:387
  91.5 1.2 add.33
  92.6 15.2 %all_to_all.15 = f32[16,80,128]{2,1,0:T(8,128)S(1)} all-to-all(f32[16,80,128]{2,1,0:T(8,128)S(1)} %add.33), channel_id=1, replica_groups={{0,2,4,6,8,10,12,14,16,18,20,22,24,26,28,30},{1,3,5,7,9,11,13,15,17,19,..., dimensions={0} | all-to-all | bytes 1310720 | tf_op jit(solution)/shard_map/all_to_all | solution.py:478
  107.9 1.7 %collective-permute-start.6 = (f32[96,128]{1,0:T(8,128)S(1)}, f32[96,128]{1,0:T(8,128)S(1)}, u32[]{:S(2)}, u32[]{:S(2)}) collective-permute-start(f32[96,128]{1,0:T(8,128)S(1)} %pad_maximum_fusion.5), channel_id=1, source_target_pairs={{0,32},{32,0},{64,96},{96,64},{128,160},{160,128},{192,224},{224,1... | collective-permute-start | bytes 147464 | tf_op jit(solution)/shard_map/ppermute | solution.py:485
  109.6 1.5 collective-permute-done.6
  111.2 3.1 %collective-permute-start.7 = (f32[112,128]{1,0:T(8,128)S(1)}, f32[112,128]{1,0:T(8,128)S(1)}, u32[]{:S(2)}, u32[]{:S(2)}) collective-permute-start(f32[112,128]{1,0:T(8,128)S(1)} %pad_maximum_fusion.4), channel_id=1, source_target_pairs={{0,64},{32,96},{64,0},{96,32},{128,192},{160,224},{192,128},{224,1... | collective-permute-start | bytes 172040 | tf_op jit(solution)/shard_map/ppermute | solution.py:485
  114.2 1.6 %collective-permute-done.7 = f32[112,128]{1,0:T(8,128)S(1)} collective-permute-done((f32[112,128]{1,0:T(8,128)S(1)}, f32[112,128]{1,0:T(8,128)S(1)}, u32[]{:S(2)}, u32[]{:S(2)}) %collective-permute-start.7) | collective-permute-done | bytes 57376 | tf_op jit(solution)/shard_map/ppermute | solution.py:485
  115.9 6.8 %collective-permute-start.8 = (f32[144,128]{1,0:T(8,128)S(1)}, f32[144,128]{1,0:T(8,128)S(1)}, u32[]{:S(2)}, u32[]{:S(2)}) collective-permute-start(f32[144,128]{1,0:T(8,128)S(1)} %pad_maximum_fusion.3), channel_id=1, source_target_pairs={{0,128},{32,160},{64,192},{96,224},{128,0},{160,32},{192,64},{224,... | collective-permute-start | bytes 221192 | tf_op jit(solution)/shard_map/ppermute | solution.py:485
  122.7 1.0 copy.27
  123.7 1.0 copy.28
  125.6 1.5 scale.1
  128.7 3.5 %all-to-all-start.2 = ((f16[16,80,128]{2,1,0:T(8,128)(2,1)}), f16[16,80,128]{2,1,0:T(8,128)(2,1)S(1)}, u32[]{:S(2)}, u32[]{:S(2)}) async-start(f16[16,80,128]{2,1,0:T(8,128)(2,1)} %broadcast_in_dim.26), calls=%async_computation.2 | async-start | bytes 655360 | tf_op jit(solution)/shard_map/all_to_all | solution.py:383
  132.3 7.6 %all-to-all-done.2 = f16[16,80,128]{2,1,0:T(8,128)(2,1)S(1)} async-done(((f16[16,80,128]{2,1,0:T(8,128)(2,1)}), f16[16,80,128]{2,1,0:T(8,128)(2,1)S(1)}, u32[]{:S(2)}, u32[]{:S(2)}) %all-to-all-start.2) | async-done | bytes 327712 | tf_op jit(solution)/shard_map/all_to_all | solution.py:383
  139.9 6.1 %collective-permute-start.9 = (f16[16,80,128]{2,1,0:T(8,128)(2,1)S(1)}, f16[16,80,128]{2,1,0:T(8,128)(2,1)S(1)}, u32[]{:S(2)}, u32[]{:S(2)}) collective-permute-start(f16[16,80,128]{2,1,0:T(8,128)(2,1)S(1)} %all-to-all-done.2), channel_id=1, source_target_pairs={{0,1},{1,0},{2,3},{3,2},{4,5},{5,4},{6,7},{7,6},{8,9},{9,8},{10,11... | collective-permute-start | bytes 983048 | tf_op jit(solution)/shard_map/ppermute | solution.py:387
  146.0 1.0 fusion.3
  147.0 1.0 fusion.1
  149.1 0.9 copy.35
  150.0 0.9 copy.36
  (66 shorter events, 9.7 us)
Async XLA Ops:
  1.9 8.1 %copy-start = (bf16[8,192,128]{2,1,0:T(8,128)(2,1)}, bf16[8,192,128]{2,1,0:T(8,128)(2,1)S(1)}, u32[]{:S(2)}) copy-start(bf16[8,192,128]{2,1,0:T(8,128)(2,1)S(1)} %get-tuple-element.59.x_ref) | copy-start | bytes 1179652
  1.9 8.1 %copy-start.1 = (bf16[8,192,128]{2,1,0:T(8,128)(2,1)}, bf16[8,192,128]{2,1,0:T(8,128)(2,1)S(1)}, u32[]{:S(2)}) copy-start(bf16[8,192,128]{2,1,0:T(8,128)(2,1)S(1)} %get-tuple-element.58.c_ref) | copy-start | bytes 1179652
  2.0 6.5 %collective-permute-start.1 = (bf16[3,192,128]{2,1,0:T(8,128)(2,1)S(1)}, bf16[3,192,128]{2,1,0:T(8,128)(2,1)S(1)}, u32[]{:S(2)}, u32[]{:S(2)}) collective-permute-start(bf16[3,192,128]{2,1,0:T(8,128)(2,1)S(1)} %pad_maximum_fusion.2), channel_id=1, source_target_pairs={{4,0},{8,4},{12,8},{16,12},{20,16},{24,20},{28,24},{5,1},{9,5},{13... | collective-permute-start | bytes 442376 | tf_op jit(solution)/shard_map/ppermute | solution.py:400
  3.3 6.7 %collective-permute-start = (bf16[3,192,128]{2,1,0:T(8,128)(2,1)S(1)}, bf16[3,192,128]{2,1,0:T(8,128)(2,1)S(1)}, u32[]{:S(2)}, u32[]{:S(2)}) collective-permute-start(bf16[3,192,128]{2,1,0:T(8,128)(2,1)S(1)} %pad_maximum_fusion.1), channel_id=1, source_target_pairs={{0,4},{4,8},{8,12},{12,16},{16,20},{20,24},{24,28},{1,5},{5,9},{9,... | collective-permute-start | bytes 442376 | tf_op jit(solution)/shard_map/ppermute | solution.py:399
  8.4 1.5 %copy-start.2 = (bf16[3,192,128]{2,1,0:T(8,128)(2,1)}, bf16[3,192,128]{2,1,0:T(8,128)(2,1)S(1)}, u32[]{:S(2)}) copy-start(bf16[3,192,128]{2,1,0:T(8,128)(2,1)S(1)} %collective-permute-done.1.bot_ref) | copy-start | bytes 442372
  10.0 0.7 copy-start.3
  12.8 7.2 %collective-permute-start.2 = (bf16[192,128]{1,0:T(8,128)(2,1)}, bf16[192,128]{1,0:T(8,128)(2,1)S(1)}, u32[]{:S(2)}, u32[]{:S(2)}) collective-permute-start(bf16[192,128]{1,0:T(8,128)(2,1)} %strip.1.own_ref), channel_id=1, source_target_pairs={{0,1},{1,2},{2,3},{4,5},{5,6},{6,7},{8,9},{9,10},{10,11},{12,13},{... | collective-permute-start | bytes 147464 | tf_op jit(solution)/shard_map/ppermute | solution.py:407
  18.1 5.6 %collective-permute-start.3 = (bf16[192,128]{1,0:T(8,128)(2,1)}, bf16[192,128]{1,0:T(8,128)(2,1)S(1)}, u32[]{:S(2)}, u32[]{:S(2)}) collective-permute-start(bf16[192,128]{1,0:T(8,128)(2,1)} %strip.1.own_ref), channel_id=1, source_target_pairs={{1,0},{2,1},{3,2},{5,4},{6,5},{7,6},{9,8},{10,9},{11,10},{13,12},{... | collective-permute-start | bytes 147464 | tf_op jit(solution)/shard_map/ppermute | solution.py:408
  20.0 3.7 %copy-start.7 = (bf16[192,128]{1,0:T(8,128)(2,1)}, bf16[192,128]{1,0:T(8,128)(2,1)S(1)}, u32[]{:S(2)}) copy-start(bf16[192,128]{1,0:T(8,128)(2,1)S(1)} %collective-permute-done.2.left_ref) | copy-start | bytes 147460
  23.7 0.6 copy-start.8
  43.2 1.5 collective-permute-start.4
  46.0 18.2 %all-to-all-start = ((f32[16,16,128]{2,1,0:T(8,128)}), f32[16,16,128]{2,1,0:T(8,128)S(1)}, u32[]{:S(2)}, u32[]{:S(2)}) async-start(f32[16,16,128]{2,1,0:T(8,128)} %broadcast_in_dim.11), calls=%async_computation | async-start | bytes 262144 | tf_op jit(solution)/shard_map/all_to_all | solution.py:383
  64.2 0.6 copy-start.4
  87.9 3.6 %collective-permute-start.5 = (f32[16,80,128]{2,1,0:T(8,128)}, f32[16,80,128]{2,1,0:T(8,128)S(1)}, u32[]{:S(2)}, u32[]{:S(2)}) collective-permute-start(f32[16,80,128]{2,1,0:T(8,128)} %get-tuple-element.22), channel_id=1, source_target_pairs={{0,1},{1,0},{2,3},{3,2},{4,5},{5,4},{6,7},{7,6},{8,9},{9,8},{10,11... | collective-permute-start | bytes 1966088 | tf_op jit(solution)/shard_map/ppermute | solution.py:387
  92.6 15.3 %copy-start.9 = (f32[16,128]{1,0:T(8,128)S(1)}, f32[16,128]{1,0:T(8,128)}, u32[]{:S(2)}) copy-start(f32[16,128]{1,0:T(8,128)} %get-tuple-element.23) | copy-start | bytes 24580
  92.6 30.0 %copy-start.6 = (bf16[8,192,128]{2,1,0:T(8,128)(2,1)S(1)}, bf16[8,192,128]{2,1,0:T(8,128)(2,1)}, u32[]{:S(2)}) copy-start(bf16[8,192,128]{2,1,0:T(8,128)(2,1)} %get-tuple-element.19) | copy-start | bytes 1179652
  107.9 15.8 %copy-start.5 = (bf16[8,192,128]{2,1,0:T(8,128)(2,1)S(1)}, bf16[8,192,128]{2,1,0:T(8,128)(2,1)}, u32[]{:S(2)}) copy-start(bf16[8,192,128]{2,1,0:T(8,128)(2,1)} %get-tuple-element.20) | copy-start | bytes 1179652
  107.9 3.2 %collective-permute-start.6 = (f32[96,128]{1,0:T(8,128)S(1)}, f32[96,128]{1,0:T(8,128)S(1)}, u32[]{:S(2)}, u32[]{:S(2)}) collective-permute-start(f32[96,128]{1,0:T(8,128)S(1)} %pad_maximum_fusion.5), channel_id=1, source_target_pairs={{0,32},{32,0},{64,96},{96,64},{128,160},{160,128},{192,224},{224,1... | collective-permute-start | bytes 147464 | tf_op jit(solution)/shard_map/ppermute | solution.py:485
  111.2 4.6 %collective-permute-start.7 = (f32[112,128]{1,0:T(8,128)S(1)}, f32[112,128]{1,0:T(8,128)S(1)}, u32[]{:S(2)}, u32[]{:S(2)}) collective-permute-start(f32[112,128]{1,0:T(8,128)S(1)} %pad_maximum_fusion.4), channel_id=1, source_target_pairs={{0,64},{32,96},{64,0},{96,32},{128,192},{160,224},{192,128},{224,1... | collective-permute-start | bytes 172040 | tf_op jit(solution)/shard_map/ppermute | solution.py:485
  115.9 9.1 %collective-permute-start.8 = (f32[144,128]{1,0:T(8,128)S(1)}, f32[144,128]{1,0:T(8,128)S(1)}, u32[]{:S(2)}, u32[]{:S(2)}) collective-permute-start(f32[144,128]{1,0:T(8,128)S(1)} %pad_maximum_fusion.3), channel_id=1, source_target_pairs={{0,128},{32,160},{64,192},{96,224},{128,0},{160,32},{192,64},{224,... | collective-permute-start | bytes 221192 | tf_op jit(solution)/shard_map/ppermute | solution.py:485
  128.7 11.2 %all-to-all-start.2 = ((f16[16,80,128]{2,1,0:T(8,128)(2,1)}), f16[16,80,128]{2,1,0:T(8,128)(2,1)S(1)}, u32[]{:S(2)}, u32[]{:S(2)}) async-start(f16[16,80,128]{2,1,0:T(8,128)(2,1)} %broadcast_in_dim.26), calls=%async_computation.2 | async-start | bytes 655360 | tf_op jit(solution)/shard_map/all_to_all | solution.py:383
  139.9 8.1 %collective-permute-start.9 = (f16[16,80,128]{2,1,0:T(8,128)(2,1)S(1)}, f16[16,80,128]{2,1,0:T(8,128)(2,1)S(1)}, u32[]{:S(2)}, u32[]{:S(2)}) collective-permute-start(f16[16,80,128]{2,1,0:T(8,128)(2,1)S(1)} %all-to-all-done.2), channel_id=1, source_target_pairs={{0,1},{1,0},{2,3},{3,2},{4,5},{5,4},{6,7},{7,6},{8,9},{9,8},{10,11... | collective-permute-start | bytes 983048 | tf_op jit(solution)/shard_map/ppermute | solution.py:387

commit v6 on v5

--- a/solution.py
+++ b/solution.py
@@ -40,36 +40,33 @@
     return jnp.sum(v, axis=1, keepdims=True)
 
 
-def sigmoid(v):
-    return 0.5 + 0.5 * jnp.tanh(0.5 * v)
+def silu_twice_slope(half):
+    t = jnp.tanh(half)
+    act = half * (1.0 + t)
+    return act, (1.0 + t) + act * (1.0 - t)
 
 
 def slab(s, n=1):
     return pl.ds(s * LANES, n * LANES)
 
 
-def strip_kernel(x_ref, c_ref, top_ref, bot_ref, out_ref):
+def strip_kernel(x_ref, c_ref, out_ref):
     lane = lane_iota(CH)
     total = jnp.zeros((CH, LANES), F32)
-    for rr in range(ROWS + 4):
-        if rr < 2:
-            v = top_ref[rr]
-        elif rr < ROWS + 2:
-            v = x_ref[rr - 2]
-        else:
-            v = bot_ref[rr - ROWS - 2]
-        v = pltpu.roll(v.astype(F32), (8 * rr + 2) % LANES, 1)
+    for rr in range(2, ROWS + 2):
+        v = pltpu.roll(x_ref[rr - 2].astype(F32), (8 * rr + 2) % LANES, 1)
         total = jnp.where((lane >= 8 * rr) & (lane < 8 * rr + 4), v, total)
-        if 1 <= rr <= ROWS + 2:
-            if rr == 1:
-                v = top_ref[2]
-            elif rr == ROWS + 2:
-                v = bot_ref[2]
-            else:
-                v = c_ref[rr - 2]
-            v = pltpu.roll(v.astype(F32), (8 * rr + 5) % LANES, 1)
-            total = jnp.where((lane >= 8 * rr + 4) & (lane < 8 * rr + 6), v, total)
+        v = pltpu.roll(c_ref[rr - 2].astype(F32), (8 * rr + 5) % LANES, 1)
+        total = jnp.where((lane >= 8 * rr + 4) & (lane < 8 * rr + 6), v, total)
     out_ref[...] = total.astype(BF16)
+
+
+def extend_kernel(own_ref, above_ref, below_ref, out_ref):
+    lane = lane_iota(CH)
+    shift = 8 * ROWS
+    value = jnp.where(lane < 16, pltpu.roll(above_ref[...].astype(F32), LANES - shift, 1), own_ref[...].astype(F32))
+    value = jnp.where(lane >= 16 + shift, pltpu.roll(below_ref[...].astype(F32), shift, 1), value)
+    out_ref[...] = value.astype(BF16)
 
 
 def input_strip(own_ref, left_ref, right_ref):
@@ -105,6 +102,7 @@
     for n in range(EB // LANES):
         rows = slice(n * LANES, (n + 1) * LANES)
         block = jnp.concatenate([taps_ref[:, rows], jnp.zeros((7, LANES), F32)], axis=0).T
+        block = 0.5 * block
         for t in range(9):
             out_s[rows, slab(t)] = jnp.broadcast_to(block[:, t : t + 1], (LANES, LANES))
 
@@ -117,7 +115,7 @@
 
     @pl.when(step == 0)
     def _():
-        gain = spread_gain(gain_ref)
+        gain = 0.5 * spread_gain(gain_ref)
         for s in range(XS):
             if s < 2:
                 x = top_ref[s].astype(F32)
@@ -149,8 +147,7 @@
             v = pre_s[whole, slab(s)]
             if 2 <= s < ROWS + 2:
                 pre_out[ds, slab(s - 2)] = v
-            v = 0.5 * v
-            return rounded(v + v * jnp.tanh(v))
+            return rounded(v * (1.0 + jnp.tanh(v)))
 
         strip = hidden(XS - 1)
         acc = [None] * (ROWS + 4)
@@ -169,8 +166,7 @@
             v = acc[o]
             conv_out[ds, slab(o - 1)] = v
             if 2 <= o <= ROWS + 1:
-                half = 0.5 * v
-                act = half + half * jnp.tanh(half)
+                act = v * (1.0 + jnp.tanh(v))
                 pooled = pooled + act
                 gexc = gexc + act * gg_s[whole, slab(o - 2)]
         edge = None
@@ -251,26 +247,21 @@
         ds = pl.ds(pl.multiple_of(i * SUB, SUB), SUB)
         whole = pl.ds(pl.multiple_of(base + i * SUB, SUB), SUB)
         k = [taps_s[ds, slab(t)] for t in range(9)]
-        exc, gp = exc_s[whole, :], gp_s[whole, :]
+        exc, gp = exc_s[whole, :], 0.5 * gp_s[whole, :]
+        half = 0.5 * exc
 
         def grad_conv(s, mask):
-            half = 0.5 * conv_ref[ds, slab(s)]
-            t = jnp.tanh(half)
-            act = half + half * t
+            act, slope = silu_twice_slope(conv_ref[ds, slab(s)])
             if 1 <= s <= ROWS:
                 gated_s[whole, slab(s - 1)] = (act * exc).astype(BF16)
-            sig = 0.5 + 0.5 * t
-            g = (gg_s[whole, slab(s)] * exc + gp) * (sig + act * (1.0 - sig))
+            g = (gg_s[whole, slab(s)] * half + gp) * slope
             if mask is not None:
                 g = jnp.where(mask_ref[mask : mask + 1, :] > 0.5, g, 0.0)
             return rounded(g)
 
         def hidden(r):
-            half = 0.5 * pre_ref[ds, slab(r)]
-            t = jnp.tanh(half)
-            act = half + half * t
-            sig = 0.5 + 0.5 * t
-            return rounded(act), sig + act * (1.0 - sig)
+            act, slope = silu_twice_slope(pre_ref[ds, slab(r)])
+            return rounded(act), slope
 
         strip = grad_conv(CS - 1, 2)
         tap = [None] * 9
@@ -396,14 +387,22 @@
     bwd_row = [(i + 1, i) for i in range(nrow - 1)]
     fwd_col = [(i, i + 1) for i in range(ncol - 1)]
     bwd_col = [(i + 1, i) for i in range(ncol - 1)]
-    top = lax.ppermute(jnp.concatenate([x[6:8], c[7:8]], axis=0), "row", fwd_row)
-    bot = lax.ppermute(jnp.concatenate([x[0:2], c[0:1]], axis=0), "row", bwd_row)
     own = pl.pallas_call(
         strip_kernel,
         out_shape=shape(CH, LANES, dtype=BF16),
         compiler_params=params(False),
         name="strip",
-    )(x, c, top, bot)
+    )(x, c)
+    above = lax.ppermute(own, "row", fwd_row)
+    below = lax.ppermute(own, "row", bwd_row)
+    top = lax.ppermute(jnp.concatenate([x[6:8], c[7:8]], axis=0), "row", fwd_row)
+    bot = lax.ppermute(jnp.concatenate([x[0:2], c[0:1]], axis=0), "row", bwd_row)
+    own = pl.pallas_call(
+        extend_kernel,
+        out_shape=shape(CH, LANES, dtype=BF16),
+        compiler_params=params(False),
+        name="extend",
+    )(own, above, below)
     left = lax.ppermute(own, "col", fwd_col)
     right = lax.ppermute(own, "col", bwd_col)
 

time: 153 us -> 156 us (1.020)
  local copies, waits for them, and re-layouts: 10.1 us -> 13.4 us
  waiting for transfers between devices: 25.9 us -> 23.9 us
    ppermute x0 -> x2, starting transfers between devices: none -> 5.21 us  [the longest x1 3.92 us: local(): above = lax.ppermute(own, 'row', fwd_row)]
    all_to_all x2, starting transfers between devices: 15 us -> 11.7 us  [gathered(): return lax.all_to_all(wide, RC, 0, 0, tiled=True, axis_index_groups=CHIPS)]
    ppermute x1, waiting for transfers between devices: 0.01 us -> 2.35 us  [local(): left = lax.ppermute(own, 'col', fwd_col)]
    ppermute x1, waiting for transfers between devices: 3.65 us -> 1.32 us  [local(): right = lax.ppermute(own, 'col', bwd_col)]
    pallas_call x0 -> x1, Pallas kernels: none -> 1.56 us  [local(): pl.pallas_call(extend_kernel, out_shape=shape(CH, LANES, dtype=BF16), com...]
  transfers between devices with their start and end apart: 12 -> 14, of which waited for: 10 -> 9; matrix products, arithmetic and copies ran while one was open for 3% -> 4% of each run, Pallas kernels for 0% -> 1%
where the time goes in v6:
time: 156 us; the launch traced here: 155 us
  starting transfers between devices  48.8 us (31%)
  Pallas kernels  46.3 us (30%)
  waiting for transfers between devices  23.9 us (15%)
  blocking collectives  15.2 us (10%)
  local copies, waits for them, and re-layouts  13.4 us (9%)
  other arithmetic  4.78 us (3%)
  matrix products  1.98 us (1%)
    pallas_call x1, Pallas kernels, local(): pl.pallas_call(backward_kernel, grid=(STEPS,), in_specs=[pl.BlockSpec(mem...  22.5 us
    pallas_call x1, Pallas kernels, local(): pl.pallas_call(forward_kernel, grid=(STEPS,), in_specs=[tile, tile, halo,...  18.7 us
    all_to_all x1, blocking collectives, local(): lax.all_to_all(keep + partner(send), RC, 0, 0, tiled=True, axis_index_gro...  15.2 us
    all_to_all x2, waiting for transfers between devices, gathered(): return lax.all_to_all(wide, RC, 0, 0, tiled=True, axis_index_groups=CHIPS)  13.6 us
    all_to_all x2, starting transfers between devices, gathered(): return lax.all_to_all(wide, RC, 0, 0, tiled=True, axis_index_groups=CHIPS)  11.7 us
    ppermute x3, starting transfers between devices, local(): lax.ppermute(jnp.concatenate([total, vecs.reshape(16 * bit, LANES)], axis...  11.6 us
    ppermute x3, starting transfers between devices, partner(): return lax.ppermute(block, 'col', [(i, i ^ 1) for i in range(4)])  7.8 us
    unnamed x23, local copies, waits for them, and re-layouts  5.52 us
  transfers between devices with their start and end apart: 14, of which 9 were waited for; matrix products, arithmetic and copies ran while one was open for 4% of the time, Pallas kernels for 1%

profile of v6, /device:TPU:1, one launch (start us, length us, event | category | flops | bytes accessed | tf_op | source)
XLA Modules:
  0.0 155.3 jit_solution(6212563396048290118)
XLA Ops:
  0.6 2.1 %copy_bitcast_fusion.2 = (bf16[8,192,128]{2,1,0:T(8,128)(2,1)}, bf16[8,192,128]{2,1,0:T(8,128)(2,1)}) fusion(bf16[1,192,8,128]{3,2,1,0:T(8,128)(2,1)} %param.15, bf16[1,192,8,128]{3,2,1,0:T(8,128)(2,1)} %param.8), kind=kLoop, calls=%fused_computation.5 | loop fusion | bytes 1572864 | tf_op jit(solution)/shard_map/transpose | solution.py:385
  2.8 2.0 %strip.1.own_ref = bf16[192,128]{1,0:T(8,128)(2,1)} custom-call(bf16[8,192,128]{2,1,0:T(8,128)(2,1)} %get-tuple-element.59.x_ref, bf16[8,192,128]{2,1,0:T(8,128)(2,1)} %get-tuple-element.58.c_ref), custom_call_target="tpu_custom_call" | custom-call | tf_op jit(solution)/shard_map/strip/pallas_call | solution.py:390
  4.8 3.9 %collective-permute-start.2 = (bf16[192,128]{1,0:T(8,128)(2,1)}, bf16[192,128]{1,0:T(8,128)(2,1)S(1)}, u32[]{:S(2)}, u32[]{:S(2)}) collective-permute-start(bf16[192,128]{1,0:T(8,128)(2,1)} %strip.1.own_ref), channel_id=1, source_target_pairs={{0,4},{4,8},{8,12},{12,16},{16,20},{20,24},{24,28},{1,5},{5,9},{9,... | collective-permute-start | bytes 147464 | tf_op jit(solution)/shard_map/ppermute | solution.py:396
  8.7 1.3 collective-permute-start.3
  11.8 1.3 collective-permute-start.1
  13.1 4.6 %collective-permute-start = (bf16[3,192,128]{2,1,0:T(8,128)(2,1)S(1)}, bf16[3,192,128]{2,1,0:T(8,128)(2,1)S(1)}, u32[]{:S(2)}, u32[]{:S(2)}) collective-permute-start(bf16[3,192,128]{2,1,0:T(8,128)(2,1)S(1)} %pad_maximum_fusion.1), channel_id=1, source_target_pairs={{0,4},{4,8},{8,12},{12,16},{16,20},{20,24},{24,28},{1,5},{5,9},{9,... | collective-permute-start | bytes 442376 | tf_op jit(solution)/shard_map/ppermute | solution.py:398
  19.0 1.6 %extend.1.own_ref = bf16[192,128]{1,0:T(8,128)(2,1)} custom-call(bf16[192,128]{1,0:T(8,128)(2,1)} %strip.1.own_ref, bf16[192,128]{1,0:T(8,128)(2,1)} %copy-done.7, bf16[192,128]{1,0:T(8,128)(2,1)} %copy-done.8), custom_call_target="tpu_custom_call" | custom-call | tf_op jit(solution)/shard_map/extend/pallas_call | solution.py:400
  20.6 4.6 %collective-permute-start.4 = (bf16[192,128]{1,0:T(8,128)(2,1)}, bf16[192,128]{1,0:T(8,128)(2,1)S(1)}, u32[]{:S(2)}, u32[]{:S(2)}) collective-permute-start(bf16[192,128]{1,0:T(8,128)(2,1)} %extend.1.own_ref), channel_id=1, source_target_pairs={{0,1},{1,2},{2,3},{4,5},{5,6},{6,7},{8,9},{9,10},{10,11},{12,13},{... | collective-permute-start | bytes 147464 | tf_op jit(solution)/shard_map/ppermute | solution.py:406
  25.2 1.9 %collective-permute-start.5 = (bf16[192,128]{1,0:T(8,128)(2,1)}, bf16[192,128]{1,0:T(8,128)(2,1)S(1)}, u32[]{:S(2)}, u32[]{:S(2)}) collective-permute-start(bf16[192,128]{1,0:T(8,128)(2,1)} %extend.1.own_ref), channel_id=1, source_target_pairs={{1,0},{2,1},{3,2},{5,4},{6,5},{7,6},{9,8},{10,9},{11,10},{13,12},{... | collective-permute-start | bytes 147464 | tf_op jit(solution)/shard_map/ppermute | solution.py:407
  27.2 2.3 %collective-permute-done.4.left_ref = bf16[192,128]{1,0:T(8,128)(2,1)S(1)} collective-permute-done((bf16[192,128]{1,0:T(8,128)(2,1)}, bf16[192,128]{1,0:T(8,128)(2,1)S(1)}, u32[]{:S(2)}, u32[]{:S(2)}) %collective-permute-start.4) | collective-permute-done | bytes 49184 | tf_op jit(solution)/shard_map/ppermute | solution.py:406
  29.5 1.3 collective-permute-done.5.right_ref
  31.6 18.7 %forward.1 = (f32[768,1024]{1,0:T(8,128)}, f32[768,1408]{1,0:T(8,128)}, f32[16,128]{1,0:T(8,128)}) custom-call(bf16[8,192,128]{2,1,0:T(8,128)(2,1)} %get-tuple-element.59.x_ref, bf16[8,192,128]{2,1,0:T(8,128)(2,1)} %get-tuple-element.58.c_ref, bf16[3,192,128]{2,1,0:T(8,128)(2,1)} %copy-done.1, bf16[3,192,128]{2,1,0:T(8,128)(2,1)} %copy-done, ...), custom_call_target="tpu_custom_call" | custom-call | tf_op jit(solution)/shard_map/forward/pallas_call | solution.py:425
  50.4 1.3 collective-permute-done.6
  53.1 8.2 %all-to-all-start = ((f32[16,16,128]{2,1,0:T(8,128)}), f32[16,16,128]{2,1,0:T(8,128)S(1)}, u32[]{:S(2)}, u32[]{:S(2)}) async-start(f32[16,16,128]{2,1,0:T(8,128)} %broadcast_in_dim.11), calls=%async_computation | async-start | bytes 262144 | tf_op jit(solution)/shard_map/all_to_all | solution.py:374
  62.0 6.0 %all-to-all-done.parts_ref = f32[16,16,128]{2,1,0:T(8,128)S(1)} async-done(((f32[16,16,128]{2,1,0:T(8,128)}), f32[16,16,128]{2,1,0:T(8,128)S(1)}, u32[]{:S(2)}, u32[]{:S(2)}) %all-to-all-start) | async-done | bytes 131104 | tf_op jit(solution)/shard_map/all_to_all | solution.py:374
  68.6 22.5 %backward.1 = (bf16[8,192,128]{2,1,0:T(8,128)(2,1)}, bf16[8,192,128]{2,1,0:T(8,128)(2,1)}, f32[16,80,128]{2,1,0:T(8,128)}, f32[16,80,128]{2,1,0:T(8,128)}, f32[16,128]{1,0:T(8,128)}) custom-call(s32[1]{0:T(128)} %bitcast.core_ref, f32[16,16,128]{2,1,0:T(8,128)} %copy-done.2, f32[48,768]{1,0:T(8,128)} %bitcast.64, f32[48,768]{1,0:T(8,128)} %wexc_ref.1, ...), custom_call_target="tpu_custom_call" | custom-call | tf_op jit(solution)/shard_map/backward/pallas_call | solution.py:446
  91.1 1.7 %collective-permute-start.7 = (f32[16,80,128]{2,1,0:T(8,128)}, f32[16,80,128]{2,1,0:T(8,128)S(1)}, u32[]{:S(2)}, u32[]{:S(2)}) collective-permute-start(f32[16,80,128]{2,1,0:T(8,128)} %get-tuple-element.22), channel_id=1, source_target_pairs={{0,1},{1,0},{2,3},{3,2},{4,5},{5,4},{6,7},{7,6},{8,9},{9,8},{10,11... | collective-permute-start | bytes 1966088 | tf_op jit(solution)/shard_map/ppermute | solution.py:378
  92.8 1.9 %collective-permute-done.7 = f32[16,80,128]{2,1,0:T(8,128)S(1)} collective-permute-done((f32[16,80,128]{2,1,0:T(8,128)}, f32[16,80,128]{2,1,0:T(8,128)S(1)}, u32[]{:S(2)}, u32[]{:S(2)}) %collective-permute-start.7) | collective-permute-done | bytes 655392 | tf_op jit(solution)/shard_map/ppermute | solution.py:378
  94.7 1.2 add.33
  95.9 15.2 %all_to_all.15 = f32[16,80,128]{2,1,0:T(8,128)S(1)} all-to-all(f32[16,80,128]{2,1,0:T(8,128)S(1)} %add.33), channel_id=1, replica_groups={{0,2,4,6,8,10,12,14,16,18,20,22,24,26,28,30},{1,3,5,7,9,11,13,15,17,19,..., dimensions={0} | all-to-all | bytes 1310720 | tf_op jit(solution)/shard_map/all_to_all | solution.py:477
  111.1 1.7 %collective-permute-start.8 = (f32[96,128]{1,0:T(8,128)S(1)}, f32[96,128]{1,0:T(8,128)S(1)}, u32[]{:S(2)}, u32[]{:S(2)}) collective-permute-start(f32[96,128]{1,0:T(8,128)S(1)} %pad_maximum_fusion.5), channel_id=1, source_target_pairs={{0,32},{32,0},{64,96},{96,64},{128,160},{160,128},{192,224},{224,1... | collective-permute-start | bytes 147464 | tf_op jit(solution)/shard_map/ppermute | solution.py:484
  112.9 1.5 collective-permute-done.8
  114.4 3.1 %collective-permute-start.9 = (f32[112,128]{1,0:T(8,128)S(1)}, f32[112,128]{1,0:T(8,128)S(1)}, u32[]{:S(2)}, u32[]{:S(2)}) collective-permute-start(f32[112,128]{1,0:T(8,128)S(1)} %pad_maximum_fusion.4), channel_id=1, source_target_pairs={{0,64},{32,96},{64,0},{96,32},{128,192},{160,224},{192,128},{224,1... | collective-permute-start | bytes 172040 | tf_op jit(solution)/shard_map/ppermute | solution.py:484
  117.5 1.6 %collective-permute-done.9 = f32[112,128]{1,0:T(8,128)S(1)} collective-permute-done((f32[112,128]{1,0:T(8,128)S(1)}, f32[112,128]{1,0:T(8,128)S(1)}, u32[]{:S(2)}, u32[]{:S(2)}) %collective-permute-start.9) | collective-permute-done | bytes 57376 | tf_op jit(solution)/shard_map/ppermute | solution.py:484
  119.1 6.8 %collective-permute-start.10 = (f32[144,128]{1,0:T(8,128)S(1)}, f32[144,128]{1,0:T(8,128)S(1)}, u32[]{:S(2)}, u32[]{:S(2)}) collective-permute-start(f32[144,128]{1,0:T(8,128)S(1)} %pad_maximum_fusion.3), channel_id=1, source_target_pairs={{0,128},{32,160},{64,192},{96,224},{128,0},{160,32},{192,64},{224,... | collective-permute-start | bytes 221192 | tf_op jit(solution)/shard_map/ppermute | solution.py:484
  125.9 1.0 copy.27
  126.9 1.0 copy.28
  128.9 1.5 scale.1
  131.9 3.5 %all-to-all-start.2 = ((f16[16,80,128]{2,1,0:T(8,128)(2,1)}), f16[16,80,128]{2,1,0:T(8,128)(2,1)S(1)}, u32[]{:S(2)}, u32[]{:S(2)}) async-start(f16[16,80,128]{2,1,0:T(8,128)(2,1)} %broadcast_in_dim.26), calls=%async_computation.2 | async-start | bytes 655360 | tf_op jit(solution)/shard_map/all_to_all | solution.py:374
  135.5 7.6 %all-to-all-done.2 = f16[16,80,128]{2,1,0:T(8,128)(2,1)S(1)} async-done(((f16[16,80,128]{2,1,0:T(8,128)(2,1)}), f16[16,80,128]{2,1,0:T(8,128)(2,1)S(1)}, u32[]{:S(2)}, u32[]{:S(2)}) %all-to-all-start.2) | async-done | bytes 327712 | tf_op jit(solution)/shard_map/all_to_all | solution.py:374
  143.1 6.1 %collective-permute-start.11 = (f16[16,80,128]{2,1,0:T(8,128)(2,1)S(1)}, f16[16,80,128]{2,1,0:T(8,128)(2,1)S(1)}, u32[]{:S(2)}, u32[]{:S(2)}) collective-permute-start(f16[16,80,128]{2,1,0:T(8,128)(2,1)S(1)} %all-to-all-done.2), channel_id=1, source_target_pairs={{0,1},{1,0},{2,3},{3,2},{4,5},{5,4},{6,7},{7,6},{8,9},{9,8},{10,11... | collective-permute-start | bytes 983048 | tf_op jit(solution)/shard_map/ppermute | solution.py:378
  150.2 1.0 fusion.1
  (71 shorter events, 14.3 us)
Async XLA Ops:
  4.8 13.0 %collective-permute-start.2 = (bf16[192,128]{1,0:T(8,128)(2,1)}, bf16[192,128]{1,0:T(8,128)(2,1)S(1)}, u32[]{:S(2)}, u32[]{:S(2)}) collective-permute-start(bf16[192,128]{1,0:T(8,128)(2,1)} %strip.1.own_ref), channel_id=1, source_target_pairs={{0,4},{4,8},{8,12},{12,16},{16,20},{20,24},{24,28},{1,5},{5,9},{9,... | collective-permute-start | bytes 147464 | tf_op jit(solution)/shard_map/ppermute | solution.py:396
  8.7 9.1 %collective-permute-start.3 = (bf16[192,128]{1,0:T(8,128)(2,1)}, bf16[192,128]{1,0:T(8,128)(2,1)S(1)}, u32[]{:S(2)}, u32[]{:S(2)}) collective-permute-start(bf16[192,128]{1,0:T(8,128)(2,1)} %strip.1.own_ref), channel_id=1, source_target_pairs={{4,0},{8,4},{12,8},{16,12},{20,16},{24,20},{28,24},{5,1},{9,5},{13... | collective-permute-start | bytes 147464 | tf_op jit(solution)/shard_map/ppermute | solution.py:397
  11.8 19.0 %collective-permute-start.1 = (bf16[3,192,128]{2,1,0:T(8,128)(2,1)S(1)}, bf16[3,192,128]{2,1,0:T(8,128)(2,1)S(1)}, u32[]{:S(2)}, u32[]{:S(2)}) collective-permute-start(bf16[3,192,128]{2,1,0:T(8,128)(2,1)S(1)} %pad_maximum_fusion.2), channel_id=1, source_target_pairs={{4,0},{8,4},{12,8},{16,12},{20,16},{24,20},{28,24},{5,1},{9,5},{13... | collective-permute-start | bytes 442376 | tf_op jit(solution)/shard_map/ppermute | solution.py:399
  13.1 17.7 %collective-permute-start = (bf16[3,192,128]{2,1,0:T(8,128)(2,1)S(1)}, bf16[3,192,128]{2,1,0:T(8,128)(2,1)S(1)}, u32[]{:S(2)}, u32[]{:S(2)}) collective-permute-start(bf16[3,192,128]{2,1,0:T(8,128)(2,1)S(1)} %pad_maximum_fusion.1), channel_id=1, source_target_pairs={{0,4},{4,8},{8,12},{12,16},{16,20},{20,24},{24,28},{1,5},{5,9},{9,... | collective-permute-start | bytes 442376 | tf_op jit(solution)/shard_map/ppermute | solution.py:398
  17.8 0.6 copy-start.7
  18.4 0.6 copy-start.8
  20.6 8.9 %collective-permute-start.4 = (bf16[192,128]{1,0:T(8,128)(2,1)}, bf16[192,128]{1,0:T(8,128)(2,1)S(1)}, u32[]{:S(2)}, u32[]{:S(2)}) collective-permute-start(bf16[192,128]{1,0:T(8,128)(2,1)} %extend.1.own_ref), channel_id=1, source_target_pairs={{0,1},{1,2},{2,3},{4,5},{5,6},{6,7},{8,9},{9,10},{10,11},{12,13},{... | collective-permute-start | bytes 147464 | tf_op jit(solution)/shard_map/ppermute | solution.py:406
  25.2 5.6 %collective-permute-start.5 = (bf16[192,128]{1,0:T(8,128)(2,1)}, bf16[192,128]{1,0:T(8,128)(2,1)S(1)}, u32[]{:S(2)}, u32[]{:S(2)}) collective-permute-start(bf16[192,128]{1,0:T(8,128)(2,1)} %extend.1.own_ref), channel_id=1, source_target_pairs={{1,0},{2,1},{3,2},{5,4},{6,5},{7,6},{9,8},{10,9},{11,10},{13,12},{... | collective-permute-start | bytes 147464 | tf_op jit(solution)/shard_map/ppermute | solution.py:407
  29.5 1.4 copy-start.5
  30.8 0.6 copy-start.6
  30.8 0.7 copy-start
  30.8 0.7 copy-start.1
  50.3 1.5 collective-permute-start.6
  53.1 14.9 %all-to-all-start = ((f32[16,16,128]{2,1,0:T(8,128)}), f32[16,16,128]{2,1,0:T(8,128)S(1)}, u32[]{:S(2)}, u32[]{:S(2)}) async-start(f32[16,16,128]{2,1,0:T(8,128)} %broadcast_in_dim.11), calls=%async_computation | async-start | bytes 262144 | tf_op jit(solution)/shard_map/all_to_all | solution.py:374
  68.0 0.7 copy-start.2
  91.1 3.6 %collective-permute-start.7 = (f32[16,80,128]{2,1,0:T(8,128)}, f32[16,80,128]{2,1,0:T(8,128)S(1)}, u32[]{:S(2)}, u32[]{:S(2)}) collective-permute-start(f32[16,80,128]{2,1,0:T(8,128)} %get-tuple-element.22), channel_id=1, source_target_pairs={{0,1},{1,0},{2,3},{3,2},{4,5},{5,4},{6,7},{7,6},{8,9},{9,8},{10,11... | collective-permute-start | bytes 1966088 | tf_op jit(solution)/shard_map/ppermute | solution.py:378
  95.9 15.3 %copy-start.9 = (f32[16,128]{1,0:T(8,128)S(1)}, f32[16,128]{1,0:T(8,128)}, u32[]{:S(2)}) copy-start(f32[16,128]{1,0:T(8,128)} %get-tuple-element.23) | copy-start | bytes 24580
  95.9 30.0 %copy-start.4 = (bf16[8,192,128]{2,1,0:T(8,128)(2,1)S(1)}, bf16[8,192,128]{2,1,0:T(8,128)(2,1)}, u32[]{:S(2)}) copy-start(bf16[8,192,128]{2,1,0:T(8,128)(2,1)} %get-tuple-element.19) | copy-start | bytes 1179652
  111.1 15.8 %copy-start.3 = (bf16[8,192,128]{2,1,0:T(8,128)(2,1)S(1)}, bf16[8,192,128]{2,1,0:T(8,128)(2,1)}, u32[]{:S(2)}) copy-start(bf16[8,192,128]{2,1,0:T(8,128)(2,1)} %get-tuple-element.20) | copy-start | bytes 1179652
  111.1 3.2 %collective-permute-start.8 = (f32[96,128]{1,0:T(8,128)S(1)}, f32[96,128]{1,0:T(8,128)S(1)}, u32[]{:S(2)}, u32[]{:S(2)}) collective-permute-start(f32[96,128]{1,0:T(8,128)S(1)} %pad_maximum_fusion.5), channel_id=1, source_target_pairs={{0,32},{32,0},{64,96},{96,64},{128,160},{160,128},{192,224},{224,1... | collective-permute-start | bytes 147464 | tf_op jit(solution)/shard_map/ppermute | solution.py:484
  114.4 4.6 %collective-permute-start.9 = (f32[112,128]{1,0:T(8,128)S(1)}, f32[112,128]{1,0:T(8,128)S(1)}, u32[]{:S(2)}, u32[]{:S(2)}) collective-permute-start(f32[112,128]{1,0:T(8,128)S(1)} %pad_maximum_fusion.4), channel_id=1, source_target_pairs={{0,64},{32,96},{64,0},{96,32},{128,192},{160,224},{192,128},{224,1... | collective-permute-start | bytes 172040 | tf_op jit(solution)/shard_map/ppermute | solution.py:484
  119.1 9.2 %collective-permute-start.10 = (f32[144,128]{1,0:T(8,128)S(1)}, f32[144,128]{1,0:T(8,128)S(1)}, u32[]{:S(2)}, u32[]{:S(2)}) collective-permute-start(f32[144,128]{1,0:T(8,128)S(1)} %pad_maximum_fusion.3), channel_id=1, source_target_pairs={{0,128},{32,160},{64,192},{96,224},{128,0},{160,32},{192,64},{224,... | collective-permute-start | bytes 221192 | tf_op jit(solution)/shard_map/ppermute | solution.py:484
  131.9 11.2 %all-to-all-start.2 = ((f16[16,80,128]{2,1,0:T(8,128)(2,1)}), f16[16,80,128]{2,1,0:T(8,128)(2,1)S(1)}, u32[]{:S(2)}, u32[]{:S(2)}) async-start(f16[16,80,128]{2,1,0:T(8,128)(2,1)} %broadcast_in_dim.26), calls=%async_computation.2 | async-start | bytes 655360 | tf_op jit(solution)/shard_map/all_to_all | solution.py:374
  143.1 8.1 %collective-permute-start.11 = (f16[16,80,128]{2,1,0:T(8,128)(2,1)S(1)}, f16[16,80,128]{2,1,0:T(8,128)(2,1)S(1)}, u32[]{:S(2)}, u32[]{:S(2)}) collective-permute-start(f16[16,80,128]{2,1,0:T(8,128)(2,1)S(1)} %all-to-all-done.2), channel_id=1, source_target_pairs={{0,1},{1,0},{2,3},{3,2},{4,5},{5,4},{6,7},{7,6},{8,9},{9,8},{10,11... | collective-permute-start | bytes 983048 | tf_op jit(solution)/shard_map/ppermute | solution.py:378

commit v7 on v5

--- a/solution.py
+++ b/solution.py
@@ -40,15 +40,17 @@
     return jnp.sum(v, axis=1, keepdims=True)
 
 
-def sigmoid(v):
-    return 0.5 + 0.5 * jnp.tanh(0.5 * v)
+def silu_twice_slope(half):
+    t = jnp.tanh(half)
+    act = half * (1.0 + t)
+    return act, (1.0 + t) + act * (1.0 - t)
 
 
 def slab(s, n=1):
     return pl.ds(s * LANES, n * LANES)
 
 
-def strip_kernel(x_ref, c_ref, top_ref, bot_ref, out_ref):
+def strip_kernel(x_ref, c_ref, top_ref, bot_ref, after_ref, out_ref):
     lane = lane_iota(CH)
     total = jnp.zeros((CH, LANES), F32)
     for rr in range(ROWS + 4):
@@ -105,52 +107,70 @@
     for n in range(EB // LANES):
         rows = slice(n * LANES, (n + 1) * LANES)
         block = jnp.concatenate([taps_ref[:, rows], jnp.zeros((7, LANES), F32)], axis=0).T
+        block = 0.5 * block
         for t in range(9):
             out_s[rows, slab(t)] = jnp.broadcast_to(block[:, t : t + 1], (LANES, LANES))
 
 
+def expand_kernel(
+    x_ref, c_ref, gain_ref, wexp_ref, wprojt_ref, scaled_out, inv_out, pre_out, hid_out, gg_out, cot_s
+):
+    @pl.when(pl.program_id(0) == 0)
+    def _():
+        gain = spread_gain(gain_ref)
+        for r in range(ROWS):
+            x = x_ref[r].astype(F32)
+            inverse = lax.rsqrt(jnp.sum(x * x, axis=0, keepdims=True) / CH + EPS)
+            inv_out[r : r + 1, :] = inverse
+            scaled_out[:, slab(r)] = (x * inverse * gain).astype(BF16)
+            cot_s[:, slab(r)] = c_ref[r]
+
+    pre_out[...] = tn_dot(wexp_ref[...] * 0.5, scaled_out[...])
+    gg_out[...] = tn_dot(wprojt_ref[...], cot_s[...])
+
+    def body(i, carry):
+        ds = pl.ds(pl.multiple_of(i * SUB, SUB), SUB)
+        v = pre_out[ds, :]
+        hid_out[ds, :] = (v * (1.0 + jnp.tanh(v))).astype(BF16)
+        return carry
+
+    lax.fori_loop(0, EB // SUB, body, 0)
+
+
 def forward_kernel(
-    x_ref, c_ref, top_ref, bot_ref, own_ref, left_ref, right_ref, gain_ref, wexp_ref, taps_ref,
-    wprojt_ref, pre_out, conv_out, sums_out, scaled_s, cot_s, pre_s, gg_s, taps_s, acc_s,
+    top_ref, bot_ref, own_ref, left_ref, right_ref, gain_ref, wexp_ref, taps_ref, hid_ref, gg_ref,
+    conv_out, sums_out, scaled_s, pre_s, taps_s, acc_s,
 ):
     step = pl.program_id(0)
 
     @pl.when(step == 0)
     def _():
-        gain = spread_gain(gain_ref)
-        for s in range(XS):
+        gain = 0.5 * spread_gain(gain_ref)
+        for s in range(XS - ROWS):
             if s < 2:
                 x = top_ref[s].astype(F32)
-            elif s < ROWS + 2:
-                x = x_ref[s - 2].astype(F32)
-            elif s < ROWS + 4:
-                x = bot_ref[s - ROWS - 2].astype(F32)
+            elif s < 4:
+                x = bot_ref[s - 2].astype(F32)
             else:
                 x = input_strip(own_ref, left_ref, right_ref)
             inverse = lax.rsqrt(jnp.sum(x * x, axis=0, keepdims=True) / CH + EPS)
             scaled_s[:, slab(s)] = (x * inverse * gain).astype(BF16)
-        for r in range(ROWS):
-            cot_s[:, slab(r)] = c_ref[r]
-        pre_s[...] = tn_dot(wexp_ref[...], scaled_s[...])
-        gg_s[...] = tn_dot(wprojt_ref[...], cot_s[...])
         sums_out[...] = jnp.zeros_like(sums_out)
 
+    pre_s[...] = tn_dot(wexp_ref[...], scaled_s[...])
     spread_taps(taps_ref, taps_s)
-    base = step * EB
     lane = lane_iota(SUB)
     first, last = lane == 0, lane == LANES - 1
 
     def body(i, carry):
         ds = pl.ds(pl.multiple_of(i * SUB, SUB), SUB)
-        whole = pl.ds(pl.multiple_of(base + i * SUB, SUB), SUB)
         k = [taps_s[ds, slab(t)] for t in range(9)]
 
         def hidden(s):
-            v = pre_s[whole, slab(s)]
             if 2 <= s < ROWS + 2:
-                pre_out[ds, slab(s - 2)] = v
-            v = 0.5 * v
-            return rounded(v + v * jnp.tanh(v))
+                return hid_ref[ds, slab(s - 2)].astype(F32)
+            v = pre_s[ds, slab(s if s < 2 else s - ROWS)]
+            return rounded(v * (1.0 + jnp.tanh(v)))
 
         strip = hidden(XS - 1)
         acc = [None] * (ROWS + 4)
@@ -169,10 +189,9 @@
             v = acc[o]
             conv_out[ds, slab(o - 1)] = v
             if 2 <= o <= ROWS + 1:
-                half = 0.5 * v
-                act = half + half * jnp.tanh(half)
+                act = v * (1.0 + jnp.tanh(v))
                 pooled = pooled + act
-                gexc = gexc + act * gg_s[whole, slab(o - 2)]
+                gexc = gexc + act * gg_ref[ds, slab(o - 2)]
         edge = None
         for a in (-1, 0, 1):
             for c in (-1, 0, 1):
@@ -221,26 +240,21 @@
 
 def backward_kernel(
     core_ref, parts_ref, wsq_ref, wexc_ref, x_ref, c_ref, top_ref, bot_ref, left_ref, right_ref,
-    gain_ref, mask_ref, pre_ref, conv_ref, taps_ref, wexp_ref, wprojt_ref,
+    gain_ref, mask_ref, scaled_ref, inv_ref, gg_ref, pre_ref, conv_ref, taps_ref, wexp_ref, wprojt_ref,
     out_out, gin_out, keep_out, send_out, vec_out,
-    packed_s, exc_s, gp_s, scaled_s, cot_s, inv_s, gg_s, gated_s, gpre_s, taps_s, acc_s, tsum_s,
+    packed_s, exc_s, gp_s, rim_s, cot_s, gg_s, gated_s, gpre_s, taps_s, acc_s, tsum_s,
 ):
     step = pl.program_id(0)
 
     @pl.when(step == 0)
     def _():
         squeeze_excite(parts_ref, wsq_ref, wexc_ref, exc_s, gp_s, vec_out)
-        gain = spread_gain(gain_ref)
         for r in range(ROWS):
-            x = x_ref[r].astype(F32)
-            inverse = lax.rsqrt(jnp.sum(x * x, axis=0, keepdims=True) / CH + EPS)
-            inv_s[r : r + 1, :] = inverse
-            scaled_s[:, slab(r)] = (x * inverse * gain).astype(BF16)
-            cot_s[:, slab(r + 1)] = c_ref[r]
-        cot_s[:, slab(0)] = top_ref[2]
-        cot_s[:, slab(ROWS + 1)] = bot_ref[2]
-        cot_s[:, slab(CS - 1)] = cotangent_strip(left_ref, right_ref).astype(BF16)
-        gg_s[...] = tn_dot(wprojt_ref[...], cot_s[...])
+            cot_s[:, slab(r)] = c_ref[r]
+        rim_s[:, slab(0)] = top_ref[2]
+        rim_s[:, slab(1)] = bot_ref[2]
+        rim_s[:, slab(2)] = cotangent_strip(left_ref, right_ref).astype(BF16)
+        gg_s[...] = tn_dot(wprojt_ref[...], rim_s[...])
 
     spread_taps(taps_ref, taps_s)
     base = step * EB
@@ -251,26 +265,25 @@
         ds = pl.ds(pl.multiple_of(i * SUB, SUB), SUB)
         whole = pl.ds(pl.multiple_of(base + i * SUB, SUB), SUB)
         k = [taps_s[ds, slab(t)] for t in range(9)]
-        exc, gp = exc_s[whole, :], gp_s[whole, :]
+        exc, gp = exc_s[whole, :], 0.5 * gp_s[whole, :]
+        half = 0.5 * exc
 
         def grad_conv(s, mask):
-            half = 0.5 * conv_ref[ds, slab(s)]
-            t = jnp.tanh(half)
-            act = half + half * t
+            act, slope = silu_twice_slope(conv_ref[ds, slab(s)])
             if 1 <= s <= ROWS:
                 gated_s[whole, slab(s - 1)] = (act * exc).astype(BF16)
-            sig = 0.5 + 0.5 * t
-            g = (gg_s[whole, slab(s)] * exc + gp) * (sig + act * (1.0 - sig))
+            if 1 <= s <= ROWS:
+                g = gg_ref[ds, slab(s - 1)]
+            else:
+                g = gg_s[whole, slab(0 if s == 0 else s - ROWS)]
+            g = (g * half + gp) * slope
             if mask is not None:
                 g = jnp.where(mask_ref[mask : mask + 1, :] > 0.5, g, 0.0)
             return rounded(g)
 
         def hidden(r):
-            half = 0.5 * pre_ref[ds, slab(r)]
-            t = jnp.tanh(half)
-            act = half + half * t
-            sig = 0.5 + 0.5 * t
-            return rounded(act), sig + act * (1.0 - sig)
+            act, slope = silu_twice_slope(pre_ref[ds, slab(r)])
+            return rounded(act), slope
 
         strip = grad_conv(CS - 1, 2)
         tap = [None] * 9
@@ -311,8 +324,8 @@
         gated, gpre = gated_s[...], gpre_s[...]
         for which, w in enumerate(
             (
-                lax.dot_general(scaled_s[...], gpre, NT, preferred_element_type=F32),
-                lax.dot_general(cot_s[:, slab(1, ROWS)], gated, NT, preferred_element_type=F32),
+                lax.dot_general(scaled_ref[...], gpre, NT, preferred_element_type=F32),
+                lax.dot_general(cot_s[...], gated, NT, preferred_element_type=F32),
             )
         ):
             for n in range(BLOCKS):
@@ -327,12 +340,12 @@
         for r in range(ROWS):
             x = x_ref[r].astype(F32)
             out_out[r] = (x + proj[:, r * LANES : (r + 1) * LANES]).astype(BF16)
-            normed = x * inv_s[r : r + 1, :]
+            normed = x * inv_ref[r : r + 1, :]
             gs = gs_all[:, r * LANES : (r + 1) * LANES]
             prod = gs * normed
             ggain = ggain + prod
             mean = jnp.sum(prod * gain, axis=0, keepdims=True) / CH
-            gin = inv_s[r : r + 1, :] * (gs * gain - normed * mean) + c_ref[r].astype(F32)
+            gin = inv_ref[r : r + 1, :] * (gs * gain - normed * mean) + c_ref[r].astype(F32)
             gin_out[r] = gin.astype(BF16)
         sums = jnp.broadcast_to(lane_sum(ggain), (CH, LANES)).T[:1]
         tsum_s[54:55, :] = sums[:, :LANES]
@@ -378,6 +391,10 @@
     )
 
 
+def cost(flops, moved):
+    return pl.CostEstimate(flops=int(flops), bytes_accessed=int(moved), transcendentals=0)
+
+
 def gathered(block):
     wide = jnp.broadcast_to(block[None], (PARTS // 2,) + block.shape)
     return lax.all_to_all(wide, RC, 0, 0, tiled=True, axis_index_groups=CHIPS)
@@ -398,12 +415,36 @@
     bwd_col = [(i + 1, i) for i in range(ncol - 1)]
     top = lax.ppermute(jnp.concatenate([x[6:8], c[7:8]], axis=0), "row", fwd_row)
     bot = lax.ppermute(jnp.concatenate([x[0:2], c[0:1]], axis=0), "row", bwd_row)
+    gain = norm_gain[None, :]
+    wprojt, taps = w_project.T, kernel.T
+    halo = full(3, CH, LANES)
+    tile = full(ROWS, CH, LANES)
+    edge = full(CH, LANES)
+    weight = full(CH, EX)
+    chunk_rows = lambda width: pl.BlockSpec((EB, width), lambda j: (j, 0))
+    chunk_cols = pl.BlockSpec((CH, EB), lambda j: (0, j))
+    chunk_taps = pl.BlockSpec((9, EB), lambda j: (0, j))
+    scaled, inv, pre, hid, gg = pl.pallas_call(
+        expand_kernel,
+        grid=(STEPS,),
+        in_specs=[tile, tile, full(1, CH), chunk_cols, chunk_cols],
+        out_specs=[full(CH, ROWS * LANES), full(ROWS, LANES), chunk_rows(ROWS * LANES),
+                   chunk_rows(ROWS * LANES), chunk_rows(ROWS * LANES)],
+        out_shape=[shape(CH, ROWS * LANES, dtype=BF16), shape(ROWS, LANES),
+                   shape(EX, ROWS * LANES), shape(EX, ROWS * LANES, dtype=BF16),
+                   shape(EX, ROWS * LANES)],
+        scratch_shapes=[pltpu.VMEM((CH, ROWS * LANES), BF16)],
+        compiler_params=params(),
+        cost_estimate=cost(600e6, 10e6),
+        name="expand",
+    )(x, c, gain, w_expand, wprojt)
     own = pl.pallas_call(
         strip_kernel,
         out_shape=shape(CH, LANES, dtype=BF16),
         compiler_params=params(False),
+        cost_estimate=cost(1e6, 1e6),
         name="strip",
-    )(x, c, top, bot)
+    )(x, c, top, bot, inv)
     left = lax.ppermute(own, "col", fwd_col)
     right = lax.ppermute(own, "col", bwd_col)
 
@@ -415,32 +456,23 @@
     strip_ok &= ((line > 1) | top_ok) & ((line < ROWS + 2) | bot_ok)
     mask = ((kind == 0) & top_ok) | ((kind == 1) & bot_ok) | ((kind == 2) & strip_ok)
     mask = mask.astype(F32)
-    gain = norm_gain[None, :]
-    wprojt, taps = w_project.T, kernel.T
-    halo = full(3, CH, LANES)
-    tile = full(ROWS, CH, LANES)
-    edge = full(CH, LANES)
-    weight = full(CH, EX)
-    chunk_rows = lambda width: pl.BlockSpec((EB, width), lambda j: (j, 0))
-    chunk_taps = pl.BlockSpec((9, EB), lambda j: (0, j))
-    pre, conv, sums = pl.pallas_call(
+    conv, sums = pl.pallas_call(
         forward_kernel,
         grid=(STEPS,),
-        in_specs=[tile, tile, halo, halo, edge, edge, edge, full(1, CH), weight, chunk_taps,
-                  weight],
-        out_specs=[chunk_rows(ROWS * LANES), chunk_rows(CS * LANES), full(16, LANES)],
-        out_shape=[shape(EX, ROWS * LANES), shape(EX, CS * LANES), shape(16, LANES)],
+        in_specs=[halo, halo, edge, edge, edge, full(1, CH), chunk_cols, chunk_taps,
+                  chunk_rows(ROWS * LANES), chunk_rows(ROWS * LANES)],
+        out_specs=[chunk_rows(CS * LANES), full(16, LANES)],
+        out_shape=[shape(EX, CS * LANES), shape(16, LANES)],
         scratch_shapes=[
-            pltpu.VMEM((CH, XS * LANES), BF16),
-            pltpu.VMEM((CH, ROWS * LANES), BF16),
-            pltpu.VMEM((EX, XS * LANES), F32),
-            pltpu.VMEM((EX, ROWS * LANES), F32),
+            pltpu.VMEM((CH, (XS - ROWS) * LANES), BF16),
+            pltpu.VMEM((EB, (XS - ROWS) * LANES), F32),
             pltpu.VMEM((EB, 9 * LANES), F32),
             pltpu.VMEM((EB, LANES), F32),
         ],
         compiler_params=params(),
+        cost_estimate=cost(200e6, 12e6),
         name="forward",
-    )(x, c, top, bot, own, left, right, gain, w_expand, taps, wprojt)
+    )(top, bot, own, left, right, gain, w_expand, taps, hid, gg)
 
     sums = gathered(sums + partner(sums))
     core = (col % 2).astype(jnp.int32).reshape(1)
@@ -449,7 +481,8 @@
         grid=(STEPS,),
         in_specs=[pl.BlockSpec(memory_space=pltpu.SMEM), full(PARTS // 2, 16, LANES),
                   full(SQ, EX), full(SQ, EX), tile, tile, halo, halo, edge, edge, full(1, CH),
-                  full(8, LANES), chunk_rows(ROWS * LANES), chunk_rows(CS * LANES), chunk_taps,
+                  full(8, LANES), full(CH, ROWS * LANES), full(ROWS, LANES),
+                  chunk_rows(ROWS * LANES), chunk_rows(ROWS * LANES), chunk_rows(CS * LANES), chunk_taps,
                   weight, weight],
         out_specs=[tile, tile, full(PARTS // 2, PACK, LANES), full(PARTS // 2, PACK, LANES),
                    full(16, LANES)],
@@ -460,10 +493,9 @@
             pltpu.VMEM((PARTS * PACK, LANES), F32),
             pltpu.VMEM((EX, LANES), F32),
             pltpu.VMEM((EX, LANES), F32),
+            pltpu.VMEM((CH, 3 * LANES), BF16),
             pltpu.VMEM((CH, ROWS * LANES), BF16),
-            pltpu.VMEM((CH, CS * LANES), BF16),
-            pltpu.VMEM((ROWS, LANES), F32),
-            pltpu.VMEM((EX, CS * LANES), F32),
+            pltpu.VMEM((EX, 3 * LANES), F32),
             pltpu.VMEM((EX, ROWS * LANES), BF16),
             pltpu.VMEM((EX, ROWS * LANES), BF16),
             pltpu.VMEM((EB, 9 * LANES), F32),
@@ -471,8 +503,9 @@
             pltpu.VMEM((56, LANES), F32),
         ],
         compiler_params=params(),
+        cost_estimate=cost(1500e6, 16e6),
         name="backward",
-    )(core, sums, w_squeeze.T, w_excite, x, c, top, bot, left, right, gain, mask, pre, conv, taps,
+    )(core, sums, w_squeeze.T, w_excite, x, c, top, bot, left, right, gain, mask, scaled, inv, gg, pre, conv, taps,
       w_expand, wprojt)
 
     mine = lax.all_to_all(

time: 153 us -> 150 us (0.980)
  starting transfers between devices: 47.5 us -> 43.2 us
  Pallas kernels: 45.5 us -> 49.5 us
  waiting for transfers between devices: 25.9 us -> 23.9 us
    pallas_call x1 -> x2, Pallas kernels: 18.9 us -> 23.7 us  [the longest x1 17.4 us: local(): pl.pallas_call(forward_kernel, grid=(STEPS,), in_specs=[halo, halo, edge,...]
    all_to_all x2, starting transfers between devices: 15 us -> 11.4 us  [gathered(): return lax.all_to_all(wide, RC, 0, 0, tiled=True, axis_index_groups=CHIPS)]
  transfers between devices with their start and end apart: 12 -> 12, of which waited for: 10 -> 8; matrix products, arithmetic and copies ran while one was open for 3% -> 3% of each run, Pallas kernels for 0% -> 4%
where the time goes in v7:
time: 150 us
  Pallas kernels  49.5 us (33%)
  starting transfers between devices  43.2 us (29%)
  waiting for transfers between devices  23.9 us (16%)
  blocking collectives  15.2 us (10%)
  local copies, waits for them, and re-layouts  10.2 us (7%)
  other arithmetic  4.77 us (3%)
  matrix products  1.98 us (1%)
    pallas_call x1, Pallas kernels, local(): pl.pallas_call(backward_kernel, grid=(STEPS,), in_specs=[pl.BlockSpec(mem...  22.1 us
    pallas_call x1, Pallas kernels, local(): pl.pallas_call(forward_kernel, grid=(STEPS,), in_specs=[halo, halo, edge,...  17.4 us
    all_to_all x1, blocking collectives, local(): lax.all_to_all(keep + partner(send), RC, 0, 0, tiled=True, axis_index_gro...  15.2 us
    all_to_all x2, waiting for transfers between devices, gathered(): return lax.all_to_all(wide, RC, 0, 0, tiled=True, axis_index_groups=CHIPS)  13.6 us
    ppermute x3, starting transfers between devices, local(): lax.ppermute(jnp.concatenate([total, vecs.reshape(16 * bit, LANES)], axis...  11.6 us
    all_to_all x2, starting transfers between devices, gathered(): return lax.all_to_all(wide, RC, 0, 0, tiled=True, axis_index_groups=CHIPS)  11.4 us
    ppermute x3, starting transfers between devices, partner(): return lax.ppermute(block, 'col', [(i, i ^ 1) for i in range(4)])  7.79 us
    pallas_call x1, Pallas kernels, local(): pl.pallas_call(expand_kernel, grid=(STEPS,), in_specs=[tile, tile, full(1...  6.3 us
  transfers between devices with their start and end apart: 12, of which 8 were waited for; matrix products, arithmetic and copies ran while one was open for 3% of the time, Pallas kernels for 4%

profile of v7, /device:TPU:1, one launch (start us, length us, event | category | flops | bytes accessed | tf_op | source)
XLA Modules:
  0.0 149.8 jit_solution(1289007093953774311)
XLA Ops:
  0.6 1.3 copy_bitcast_fusion.2
  2.0 1.3 collective-permute-start.1
  3.3 4.6 %collective-permute-start = (bf16[3,192,128]{2,1,0:T(8,128)(2,1)S(1)}, bf16[3,192,128]{2,1,0:T(8,128)(2,1)S(1)}, u32[]{:S(2)}, u32[]{:S(2)}) collective-permute-start(bf16[3,192,128]{2,1,0:T(8,128)(2,1)S(1)} %pad_maximum_fusion.1), channel_id=1, source_target_pairs={{0,4},{4,8},{8,12},{12,16},{16,20},{20,24},{24,28},{1,5},{5,9},{9,... | collective-permute-start | bytes 442376 | tf_op jit(solution)/shard_map/ppermute | solution.py:416
  7.9 6.3 %expand.1 = (bf16[192,1024]{1,0:T(8,128)(2,1)}, f32[8,128]{1,0:T(8,128)}, f32[768,1024]{1,0:T(8,128)}, bf16[768,1024]{1,0:T(8,128)(2,1)}, f32[768,1024]{1,0:T(8,128)}) custom-call(bf16[8,192,128]{2,1,0:T(8,128)(2,1)} %copy-done, bf16[8,192,128]{2,1,0:T(8,128)(2,1)} %copy-done.1, f32[1,192]{1,0:T(1,128)} %bitcast.77, bf16[192,768]{1,0:T(8,128)(2,1)} %wexp_ref.5, ...), custom_call_target="tpu_custom_call" | custom-call | flops 600000000 | bytes 10000000 | tf_op jit(solution)/shard_map/expand/pallas_call | solution.py:427
  14.9 2.2 %strip.1.own_ref = bf16[192,128]{1,0:T(8,128)(2,1)} custom-call(bf16[8,192,128]{2,1,0:T(8,128)(2,1)} %copy-done, bf16[8,192,128]{2,1,0:T(8,128)(2,1)} %copy-done.1, bf16[3,192,128]{2,1,0:T(8,128)(2,1)} %copy-done.3, bf16[3,192,128]{2,1,0:T(8,128)(2,1)} %copy-done.2, f32[8,128]{1,0:T(8,128)} %get-tuple-element.20.after_ref.inv_ref), custom_call_target="tpu_custom_call" | custom-call | flops 1000000 | bytes 1000000 | tf_op jit(solution)/shard_map/strip/pallas_call | solution.py:441
  17.1 4.6 %collective-permute-start.2 = (bf16[192,128]{1,0:T(8,128)(2,1)}, bf16[192,128]{1,0:T(8,128)(2,1)S(1)}, u32[]{:S(2)}, u32[]{:S(2)}) collective-permute-start(bf16[192,128]{1,0:T(8,128)(2,1)} %strip.1.own_ref), channel_id=1, source_target_pairs={{0,1},{1,2},{2,3},{4,5},{5,6},{6,7},{8,9},{9,10},{10,11},{12,13},{... | collective-permute-start | bytes 147464 | tf_op jit(solution)/shard_map/ppermute | solution.py:448
  21.7 1.9 %collective-permute-start.3 = (bf16[192,128]{1,0:T(8,128)(2,1)}, bf16[192,128]{1,0:T(8,128)(2,1)S(1)}, u32[]{:S(2)}, u32[]{:S(2)}) collective-permute-start(bf16[192,128]{1,0:T(8,128)(2,1)} %strip.1.own_ref), channel_id=1, source_target_pairs={{1,0},{2,1},{3,2},{5,4},{6,5},{7,6},{9,8},{10,9},{11,10},{13,12},{... | collective-permute-start | bytes 147464 | tf_op jit(solution)/shard_map/ppermute | solution.py:449
  23.7 3.6 %collective-permute-done.3.right_ref = bf16[192,128]{1,0:T(8,128)(2,1)S(1)} collective-permute-done((bf16[192,128]{1,0:T(8,128)(2,1)}, bf16[192,128]{1,0:T(8,128)(2,1)S(1)}, u32[]{:S(2)}, u32[]{:S(2)}) %collective-permute-start.3) | collective-permute-done | bytes 49184 | tf_op jit(solution)/shard_map/ppermute | solution.py:449
  27.9 17.4 %forward.1 = (f32[768,1408]{1,0:T(8,128)}, f32[16,128]{1,0:T(8,128)}) custom-call(bf16[3,192,128]{2,1,0:T(8,128)(2,1)} %copy-done.3, bf16[3,192,128]{2,1,0:T(8,128)(2,1)} %copy-done.2, bf16[192,128]{1,0:T(8,128)(2,1)} %strip.1.own_ref, bf16[192,128]{1,0:T(8,128)(2,1)} %copy-done.7, bf16[192,128]{1,0:T(8,128)(2,1)} %copy-done.8, f32[1,192]{1,0:T(1,128)} %bitcast.78, ...), custom_call_target="tpu_custom_call" | custom-call | flops 200000000 | bytes 12000000 | tf_op jit(solution)/shard_map/forward/pallas_call | solution.py:459
  45.4 1.3 collective-permute-done.4
  48.1 7.9 %all-to-all-start = ((f32[16,16,128]{2,1,0:T(8,128)}), f32[16,16,128]{2,1,0:T(8,128)S(1)}, u32[]{:S(2)}, u32[]{:S(2)}) async-start(f32[16,16,128]{2,1,0:T(8,128)} %broadcast_in_dim.11), calls=%async_computation | async-start | bytes 262144 | tf_op jit(solution)/shard_map/all_to_all | solution.py:400
  56.7 6.0 %all-to-all-done.parts_ref = f32[16,16,128]{2,1,0:T(8,128)S(1)} async-done(((f32[16,16,128]{2,1,0:T(8,128)}), f32[16,16,128]{2,1,0:T(8,128)S(1)}, u32[]{:S(2)}, u32[]{:S(2)}) %all-to-all-start) | async-done | bytes 131104 | tf_op jit(solution)/shard_map/all_to_all | solution.py:400
  63.4 22.1 %backward.1 = (bf16[8,192,128]{2,1,0:T(8,128)(2,1)}, bf16[8,192,128]{2,1,0:T(8,128)(2,1)}, f32[16,80,128]{2,1,0:T(8,128)}, f32[16,80,128]{2,1,0:T(8,128)}, f32[16,128]{1,0:T(8,128)}) custom-call(s32[1]{0:T(128)} %bitcast.core_ref, f32[16,16,128]{2,1,0:T(8,128)} %copy-done.4, f32[48,768]{1,0:T(8,128)} %bitcast.64, f32[48,768]{1,0:T(8,128)} %wexc_ref.1, ...), custom_call_target="tpu_custom_call" | custom-call | flops 1500000000 | bytes 16000000 | tf_op jit(solution)/shard_map/backward/pallas_call | solution.py:479
  85.5 1.7 %collective-permute-start.5 = (f32[16,80,128]{2,1,0:T(8,128)}, f32[16,80,128]{2,1,0:T(8,128)S(1)}, u32[]{:S(2)}, u32[]{:S(2)}) collective-permute-start(f32[16,80,128]{2,1,0:T(8,128)} %get-tuple-element.30), channel_id=1, source_target_pairs={{0,1},{1,0},{2,3},{3,2},{4,5},{5,4},{6,7},{7,6},{8,9},{9,8},{10,11... | collective-permute-start | bytes 1966088 | tf_op jit(solution)/shard_map/ppermute | solution.py:404
  87.2 1.9 %collective-permute-done.5 = f32[16,80,128]{2,1,0:T(8,128)S(1)} collective-permute-done((f32[16,80,128]{2,1,0:T(8,128)}, f32[16,80,128]{2,1,0:T(8,128)S(1)}, u32[]{:S(2)}, u32[]{:S(2)}) %collective-permute-start.5) | collective-permute-done | bytes 655392 | tf_op jit(solution)/shard_map/ppermute | solution.py:404
  89.1 1.2 add.33
  90.3 15.2 %all_to_all.15 = f32[16,80,128]{2,1,0:T(8,128)S(1)} all-to-all(f32[16,80,128]{2,1,0:T(8,128)S(1)} %add.33), channel_id=1, replica_groups={{0,2,4,6,8,10,12,14,16,18,20,22,24,26,28,30},{1,3,5,7,9,11,13,15,17,19,..., dimensions={0} | all-to-all | bytes 1310720 | tf_op jit(solution)/shard_map/all_to_all | solution.py:511
  105.6 1.7 %collective-permute-start.6 = (f32[96,128]{1,0:T(8,128)S(1)}, f32[96,128]{1,0:T(8,128)S(1)}, u32[]{:S(2)}, u32[]{:S(2)}) collective-permute-start(f32[96,128]{1,0:T(8,128)S(1)} %pad_maximum_fusion.5), channel_id=1, source_target_pairs={{0,32},{32,0},{64,96},{96,64},{128,160},{160,128},{192,224},{224,1... | collective-permute-start | bytes 147464 | tf_op jit(solution)/shard_map/ppermute | solution.py:518
  107.3 1.5 collective-permute-done.6
  108.8 3.1 %collective-permute-start.7 = (f32[112,128]{1,0:T(8,128)S(1)}, f32[112,128]{1,0:T(8,128)S(1)}, u32[]{:S(2)}, u32[]{:S(2)}) collective-permute-start(f32[112,128]{1,0:T(8,128)S(1)} %pad_maximum_fusion.4), channel_id=1, source_target_pairs={{0,64},{32,96},{64,0},{96,32},{128,192},{160,224},{192,128},{224,1... | collective-permute-start | bytes 172040 | tf_op jit(solution)/shard_map/ppermute | solution.py:518
  111.9 1.6 %collective-permute-done.7 = f32[112,128]{1,0:T(8,128)S(1)} collective-permute-done((f32[112,128]{1,0:T(8,128)S(1)}, f32[112,128]{1,0:T(8,128)S(1)}, u32[]{:S(2)}, u32[]{:S(2)}) %collective-permute-start.7) | collective-permute-done | bytes 57376 | tf_op jit(solution)/shard_map/ppermute | solution.py:518
  113.5 6.8 %collective-permute-start.8 = (f32[144,128]{1,0:T(8,128)S(1)}, f32[144,128]{1,0:T(8,128)S(1)}, u32[]{:S(2)}, u32[]{:S(2)}) collective-permute-start(f32[144,128]{1,0:T(8,128)S(1)} %pad_maximum_fusion.3), channel_id=1, source_target_pairs={{0,128},{32,160},{64,192},{96,224},{128,0},{160,32},{192,64},{224,... | collective-permute-start | bytes 221192 | tf_op jit(solution)/shard_map/ppermute | solution.py:518
  120.3 1.0 copy.27
  121.3 1.0 copy.28
  123.3 1.5 %scale.1 = f32[80,128]{1,0:T(8,128)} custom-call(f32[80,128]{1,0:T(8,128)} %slice_add_fusion.x_ref), custom_call_target="tpu_custom_call" | custom-call | tf_op jit(solution)/shard_map/scale/pallas_call | solution.py:532
  126.4 3.5 %all-to-all-start.2 = ((f16[16,80,128]{2,1,0:T(8,128)(2,1)}), f16[16,80,128]{2,1,0:T(8,128)(2,1)S(1)}, u32[]{:S(2)}, u32[]{:S(2)}) async-start(f16[16,80,128]{2,1,0:T(8,128)(2,1)} %broadcast_in_dim.26), calls=%async_computation.2 | async-start | bytes 655360 | tf_op jit(solution)/shard_map/all_to_all | solution.py:400
  130.0 7.6 %all-to-all-done.2 = f16[16,80,128]{2,1,0:T(8,128)(2,1)S(1)} async-done(((f16[16,80,128]{2,1,0:T(8,128)(2,1)}), f16[16,80,128]{2,1,0:T(8,128)(2,1)S(1)}, u32[]{:S(2)}, u32[]{:S(2)}) %all-to-all-start.2) | async-done | bytes 327712 | tf_op jit(solution)/shard_map/all_to_all | solution.py:400
  137.5 6.1 %collective-permute-start.9 = (f16[16,80,128]{2,1,0:T(8,128)(2,1)S(1)}, f16[16,80,128]{2,1,0:T(8,128)(2,1)S(1)}, u32[]{:S(2)}, u32[]{:S(2)}) collective-permute-start(f16[16,80,128]{2,1,0:T(8,128)(2,1)S(1)} %all-to-all-done.2), channel_id=1, source_target_pairs={{0,1},{1,0},{2,3},{3,2},{4,5},{5,4},{6,7},{7,6},{8,9},{9,8},{10,11... | collective-permute-start | bytes 983048 | tf_op jit(solution)/shard_map/ppermute | solution.py:404
  143.6 1.0 fusion.3
  144.6 1.0 fusion.1
  146.7 0.9 copy.35
  147.7 0.9 copy.36
  (67 shorter events, 9.2 us)
Async XLA Ops:
  1.9 6.0 %copy-start = (bf16[8,192,128]{2,1,0:T(8,128)(2,1)}, bf16[8,192,128]{2,1,0:T(8,128)(2,1)S(1)}, u32[]{:S(2)}) copy-start(bf16[8,192,128]{2,1,0:T(8,128)(2,1)S(1)} %get-tuple-element.67.x_ref) | copy-start | bytes 1179652
  1.9 6.0 %copy-start.1 = (bf16[8,192,128]{2,1,0:T(8,128)(2,1)}, bf16[8,192,128]{2,1,0:T(8,128)(2,1)S(1)}, u32[]{:S(2)}) copy-start(bf16[8,192,128]{2,1,0:T(8,128)(2,1)S(1)} %get-tuple-element.66.c_ref) | copy-start | bytes 1179652
  2.0 12.2 %collective-permute-start.1 = (bf16[3,192,128]{2,1,0:T(8,128)(2,1)S(1)}, bf16[3,192,128]{2,1,0:T(8,128)(2,1)S(1)}, u32[]{:S(2)}, u32[]{:S(2)}) collective-permute-start(bf16[3,192,128]{2,1,0:T(8,128)(2,1)S(1)} %pad_maximum_fusion.2), channel_id=1, source_target_pairs={{4,0},{8,4},{12,8},{16,12},{20,16},{24,20},{28,24},{5,1},{9,5},{13... | collective-permute-start | bytes 442376 | tf_op jit(solution)/shard_map/ppermute | solution.py:417
  3.3 10.9 %collective-permute-start = (bf16[3,192,128]{2,1,0:T(8,128)(2,1)S(1)}, bf16[3,192,128]{2,1,0:T(8,128)(2,1)S(1)}, u32[]{:S(2)}, u32[]{:S(2)}) collective-permute-start(bf16[3,192,128]{2,1,0:T(8,128)(2,1)S(1)} %pad_maximum_fusion.1), channel_id=1, source_target_pairs={{0,4},{4,8},{8,12},{12,16},{16,20},{20,24},{24,28},{1,5},{5,9},{9,... | collective-permute-start | bytes 442376 | tf_op jit(solution)/shard_map/ppermute | solution.py:416
  14.2 0.7 copy-start.2
  14.3 0.7 copy-start.3
  17.1 6.5 %collective-permute-start.2 = (bf16[192,128]{1,0:T(8,128)(2,1)}, bf16[192,128]{1,0:T(8,128)(2,1)S(1)}, u32[]{:S(2)}, u32[]{:S(2)}) collective-permute-start(bf16[192,128]{1,0:T(8,128)(2,1)} %strip.1.own_ref), channel_id=1, source_target_pairs={{0,1},{1,2},{2,3},{4,5},{5,6},{6,7},{8,9},{9,10},{10,11},{12,13},{... | collective-permute-start | bytes 147464 | tf_op jit(solution)/shard_map/ppermute | solution.py:448
  21.7 5.6 %collective-permute-start.3 = (bf16[192,128]{1,0:T(8,128)(2,1)}, bf16[192,128]{1,0:T(8,128)(2,1)S(1)}, u32[]{:S(2)}, u32[]{:S(2)}) collective-permute-start(bf16[192,128]{1,0:T(8,128)(2,1)} %strip.1.own_ref), channel_id=1, source_target_pairs={{1,0},{2,1},{3,2},{5,4},{6,5},{7,6},{9,8},{10,9},{11,10},{13,12},{... | collective-permute-start | bytes 147464 | tf_op jit(solution)/shard_map/ppermute | solution.py:449
  23.7 3.7 %copy-start.7 = (bf16[192,128]{1,0:T(8,128)(2,1)}, bf16[192,128]{1,0:T(8,128)(2,1)S(1)}, u32[]{:S(2)}) copy-start(bf16[192,128]{1,0:T(8,128)(2,1)S(1)} %collective-permute-done.2.left_ref) | copy-start | bytes 147460
  27.3 0.6 copy-start.8
  45.3 1.4 collective-permute-start.4
  48.1 14.6 %all-to-all-start = ((f32[16,16,128]{2,1,0:T(8,128)}), f32[16,16,128]{2,1,0:T(8,128)S(1)}, u32[]{:S(2)}, u32[]{:S(2)}) async-start(f32[16,16,128]{2,1,0:T(8,128)} %broadcast_in_dim.11), calls=%async_computation | async-start | bytes 262144 | tf_op jit(solution)/shard_map/all_to_all | solution.py:400
  62.7 0.7 copy-start.4
  85.5 3.6 %collective-permute-start.5 = (f32[16,80,128]{2,1,0:T(8,128)}, f32[16,80,128]{2,1,0:T(8,128)S(1)}, u32[]{:S(2)}, u32[]{:S(2)}) collective-permute-start(f32[16,80,128]{2,1,0:T(8,128)} %get-tuple-element.30), channel_id=1, source_target_pairs={{0,1},{1,0},{2,3},{3,2},{4,5},{5,4},{6,7},{7,6},{8,9},{9,8},{10,11... | collective-permute-start | bytes 1966088 | tf_op jit(solution)/shard_map/ppermute | solution.py:404
  90.3 15.3 %copy-start.9 = (f32[16,128]{1,0:T(8,128)S(1)}, f32[16,128]{1,0:T(8,128)}, u32[]{:S(2)}) copy-start(f32[16,128]{1,0:T(8,128)} %get-tuple-element.31) | copy-start | bytes 24580
  90.3 30.0 %copy-start.6 = (bf16[8,192,128]{2,1,0:T(8,128)(2,1)S(1)}, bf16[8,192,128]{2,1,0:T(8,128)(2,1)}, u32[]{:S(2)}) copy-start(bf16[8,192,128]{2,1,0:T(8,128)(2,1)} %get-tuple-element.27) | copy-start | bytes 1179652
  105.5 15.8 %copy-start.5 = (bf16[8,192,128]{2,1,0:T(8,128)(2,1)S(1)}, bf16[8,192,128]{2,1,0:T(8,128)(2,1)}, u32[]{:S(2)}) copy-start(bf16[8,192,128]{2,1,0:T(8,128)(2,1)} %get-tuple-element.28) | copy-start | bytes 1179652
  105.6 3.2 %collective-permute-start.6 = (f32[96,128]{1,0:T(8,128)S(1)}, f32[96,128]{1,0:T(8,128)S(1)}, u32[]{:S(2)}, u32[]{:S(2)}) collective-permute-start(f32[96,128]{1,0:T(8,128)S(1)} %pad_maximum_fusion.5), channel_id=1, source_target_pairs={{0,32},{32,0},{64,96},{96,64},{128,160},{160,128},{192,224},{224,1... | collective-permute-start | bytes 147464 | tf_op jit(solution)/shard_map/ppermute | solution.py:518
  108.8 4.6 %collective-permute-start.7 = (f32[112,128]{1,0:T(8,128)S(1)}, f32[112,128]{1,0:T(8,128)S(1)}, u32[]{:S(2)}, u32[]{:S(2)}) collective-permute-start(f32[112,128]{1,0:T(8,128)S(1)} %pad_maximum_fusion.4), channel_id=1, source_target_pairs={{0,64},{32,96},{64,0},{96,32},{128,192},{160,224},{192,128},{224,1... | collective-permute-start | bytes 172040 | tf_op jit(solution)/shard_map/ppermute | solution.py:518
  113.5 9.2 %collective-permute-start.8 = (f32[144,128]{1,0:T(8,128)S(1)}, f32[144,128]{1,0:T(8,128)S(1)}, u32[]{:S(2)}, u32[]{:S(2)}) collective-permute-start(f32[144,128]{1,0:T(8,128)S(1)} %pad_maximum_fusion.3), channel_id=1, source_target_pairs={{0,128},{32,160},{64,192},{96,224},{128,0},{160,32},{192,64},{224,... | collective-permute-start | bytes 221192 | tf_op jit(solution)/shard_map/ppermute | solution.py:518
  126.4 11.2 %all-to-all-start.2 = ((f16[16,80,128]{2,1,0:T(8,128)(2,1)}), f16[16,80,128]{2,1,0:T(8,128)(2,1)S(1)}, u32[]{:S(2)}, u32[]{:S(2)}) async-start(f16[16,80,128]{2,1,0:T(8,128)(2,1)} %broadcast_in_dim.26), calls=%async_computation.2 | async-start | bytes 655360 | tf_op jit(solution)/shard_map/all_to_all | solution.py:400
  137.5 8.1 %collective-permute-start.9 = (f16[16,80,128]{2,1,0:T(8,128)(2,1)S(1)}, f16[16,80,128]{2,1,0:T(8,128)(2,1)S(1)}, u32[]{:S(2)}, u32[]{:S(2)}) collective-permute-start(f16[16,80,128]{2,1,0:T(8,128)(2,1)S(1)} %all-to-all-done.2), channel_id=1, source_target_pairs={{0,1},{1,0},{2,3},{3,2},{4,5},{5,4},{6,7},{7,6},{8,9},{9,8},{10,11... | collective-permute-start | bytes 983048 | tf_op jit(solution)/shard_map/ppermute | solution.py:404

commit v8 on v7

--- a/solution.py
+++ b/solution.py
@@ -112,6 +112,31 @@
             out_s[rows, slab(t)] = jnp.broadcast_to(block[:, t : t + 1], (LANES, LANES))
 
 
+class Chunks:
+    def __init__(self, pairs, sems):
+        self.pairs, self.sems = pairs, sems
+
+    def copies(self, step):
+        rows = pl.ds(pl.multiple_of(step * EB, EB), EB)
+        slot = step % 2
+        return [
+            pltpu.make_async_copy(src.at[rows, :], dst.at[slot], self.sems.at[n, slot])
+            for n, (src, dst) in enumerate(self.pairs)
+        ]
+
+    def start(self, step):
+        for copy in self.copies(step):
+            copy.start()
+
+    def advance(self, step):
+        for copy in self.copies(step):
+            copy.wait()
+
+        @pl.when(step < STEPS - 1)
+        def _():
+            self.start(step + 1)
+
+
 def expand_kernel(
     x_ref, c_ref, gain_ref, wexp_ref, wprojt_ref, scaled_out, inv_out, pre_out, hid_out, gg_out, cot_s
 ):
@@ -138,13 +163,16 @@
 
 
 def forward_kernel(
-    top_ref, bot_ref, own_ref, left_ref, right_ref, gain_ref, wexp_ref, taps_ref, hid_ref, gg_ref,
-    conv_out, sums_out, scaled_s, pre_s, taps_s, acc_s,
+    top_ref, bot_ref, own_ref, left_ref, right_ref, gain_ref, wexp_ref, taps_ref, hid_any, gg_any,
+    conv_out, sums_out, scaled_s, pre_s, taps_s, acc_s, hid_s, gg_s, sems,
 ):
     step = pl.program_id(0)
+    chunks = Chunks(((hid_any, hid_s), (gg_any, gg_s)), sems)
+    hid_ref, gg_ref = hid_s.at[step % 2], gg_s.at[step % 2]
 
     @pl.when(step == 0)
     def _():
+        chunks.start(0)
         gain = 0.5 * spread_gain(gain_ref)
         for s in range(XS - ROWS):
             if s < 2:
@@ -159,6 +187,7 @@
 
     pre_s[...] = tn_dot(wexp_ref[...], scaled_s[...])
     spread_taps(taps_ref, taps_s)
+    chunks.advance(step)
     lane = lane_iota(SUB)
     first, last = lane == 0, lane == LANES - 1
 
@@ -199,14 +228,15 @@
                 term = k[3 * (a + 1) + c + 1] * (pltpu.roll(strip, shift, 1) if shift else strip)
                 edge = term if edge is None else edge + term
         conv_out[ds, slab(CS - 1)] = edge
-        acc_s[ds, :] = jnp.where(first, lane_sum(pooled), lane_sum(gexc))
+        acc_s[0, ds, :] = pooled
+        acc_s[1, ds, :] = gexc
         return carry
 
     lax.fori_loop(0, EB // SUB, body, 0)
     for n in range(EB // LANES):
-        sums_out[pl.ds(2 * (step * (EB // LANES) + n), 2), :] = (
-            acc_s[n * LANES : (n + 1) * LANES, :].T[:2]
-        )
+        for kind in range(2):
+            row = jnp.sum(acc_s[kind, n * LANES : (n + 1) * LANES, :].T, axis=0, keepdims=True)
+            sums_out[pl.ds(2 * (step * (EB // LANES) + n) + kind, 1), :] = row
 
 
 def squeeze_excite(parts_ref, wsq_ref, wexc_ref, exc_s, gp_s, vec_out):
@@ -240,14 +270,18 @@
 
 def backward_kernel(
     core_ref, parts_ref, wsq_ref, wexc_ref, x_ref, c_ref, top_ref, bot_ref, left_ref, right_ref,
-    gain_ref, mask_ref, scaled_ref, inv_ref, gg_ref, pre_ref, conv_ref, taps_ref, wexp_ref, wprojt_ref,
-    out_out, gin_out, keep_out, send_out, vec_out,
+    gain_ref, mask_ref, scaled_ref, inv_ref, gg_any, pre_any, conv_any, taps_ref, wexp_ref, wprojt_ref,
+    out_out, gin_out, keep_any, send_any, vec_out,
     packed_s, exc_s, gp_s, rim_s, cot_s, gg_s, gated_s, gpre_s, taps_s, acc_s, tsum_s,
+    ggc_s, prec_s, convc_s, sems, out_sems,
 ):
     step = pl.program_id(0)
+    chunks = Chunks(((gg_any, ggc_s), (pre_any, prec_s), (conv_any, convc_s)), sems)
+    gg_ref, pre_ref, conv_ref = (r.at[step % 2] for r in (ggc_s, prec_s, convc_s))
 
     @pl.when(step == 0)
     def _():
+        chunks.start(0)
         squeeze_excite(parts_ref, wsq_ref, wexc_ref, exc_s, gp_s, vec_out)
         for r in range(ROWS):
             cot_s[:, slab(r)] = c_ref[r]
@@ -257,6 +291,7 @@
         gg_s[...] = tn_dot(wprojt_ref[...], rim_s[...])
 
     spread_taps(taps_ref, taps_s)
+    chunks.advance(step)
     base = step * EB
     lane = lane_iota(SUB)
     first, last = lane == 0, lane == LANES - 1
@@ -331,34 +366,44 @@
             for n in range(BLOCKS):
                 for i in range(CH // 24):
                     group = (which * BLOCKS + n) * (CH // 24) + i
-                    row = PACK * (group // 3) + 24 * (group % 3)
+                    part = group // 3
+                    row = PACK * (part % 2 * PARTS // 2 + part // 2) + 24 * (group % 3)
                     packed_s[row : row + 24, :] = w[24 * i : 24 * i + 24, slab(n)]
-        proj = jnp.dot(wprojt_ref[...], gated, preferred_element_type=F32)
         gs_all = jnp.dot(wexp_ref[...], gpre, preferred_element_type=F32)
-        gain = spread_gain(gain_ref)
         ggain = jnp.zeros((CH, LANES), F32)
         for r in range(ROWS):
-            x = x_ref[r].astype(F32)
-            out_out[r] = (x + proj[:, r * LANES : (r + 1) * LANES]).astype(BF16)
-            normed = x * inv_ref[r : r + 1, :]
-            gs = gs_all[:, r * LANES : (r + 1) * LANES]
-            prod = gs * normed
-            ggain = ggain + prod
-            mean = jnp.sum(prod * gain, axis=0, keepdims=True) / CH
-            gin = inv_ref[r : r + 1, :] * (gs * gain - normed * mean) + c_ref[r].astype(F32)
-            gin_out[r] = gin.astype(BF16)
+            normed = x_ref[r].astype(F32) * inv_ref[r : r + 1, :]
+            ggain = ggain + gs_all[:, r * LANES : (r + 1) * LANES] * normed
         sums = jnp.broadcast_to(lane_sum(ggain), (CH, LANES)).T[:1]
         tsum_s[54:55, :] = sums[:, :LANES]
         tsum_s[55:56, :] = jnp.zeros((1, LANES), F32)
         tsum_s[55:56, : CH - LANES] = sums[:, LANES:]
         for d in range(PARTS):
-            packed_s[d * PACK + 72 : (d + 1) * PACK, :] = jnp.zeros((8, LANES), F32)
+            rows = slice((d % 2 * PARTS // 2 + d // 2) * PACK + 72, (d % 2 * PARTS // 2 + d // 2 + 1) * PACK)
+            packed_s[rows, :] = jnp.zeros((8, LANES), F32)
             if d < 28:
-                packed_s[d * PACK + 72 : d * PACK + 74, :] = tsum_s[2 * d : 2 * d + 2, :]
-        core = core_ref[0]
-        for q in range(PARTS // 2):
-            keep_out[q] = packed_s[pl.ds(pl.multiple_of(PACK * (2 * q + core), 8), PACK), :]
-            send_out[q] = packed_s[pl.ds(pl.multiple_of(PACK * (2 * q + 1 - core), 8), PACK), :]
+                packed_s[rows.start : rows.start + 2, :] = tsum_s[2 * d : 2 * d + 2, :]
+        core, half = core_ref[0], PARTS // 2 * PACK
+        sends = [
+            pltpu.make_async_copy(
+                packed_s.at[pl.ds(pl.multiple_of(half * which, 8), half), :], dst, out_sems.at[n]
+            )
+            for n, (which, dst) in enumerate(((core, keep_any), (1 - core, send_any)))
+        ]
+        for copy in sends:
+            copy.start()
+        proj = jnp.dot(wprojt_ref[...], gated, preferred_element_type=F32)
+        gain = spread_gain(gain_ref)
+        for r in range(ROWS):
+            x = x_ref[r].astype(F32)
+            out_out[r] = (x + proj[:, r * LANES : (r + 1) * LANES]).astype(BF16)
+            inverse = inv_ref[r : r + 1, :]
+            normed = x * inverse
+            gnormed = gs_all[:, r * LANES : (r + 1) * LANES] * gain
+            mean = jnp.sum(gnormed * normed, axis=0, keepdims=True) / CH
+            gin_out[r] = (inverse * (gnormed - normed * mean) + c_ref[r].astype(F32)).astype(BF16)
+        for copy in sends:
+            copy.wait()
 
 
 def scale_kernel(x_ref, out_ref):
@@ -372,9 +417,32 @@
     rest = x[72:80]
     e_big = exponent(x[:72])
     e_small = exponent(jnp.where(row < 2, rest, 0.0))
-    out_ref[:72] = x[:72] * jnp.exp2(-e_big)
-    rest = jnp.where(row < 5, jnp.broadcast_to(e_big, (8, LANES)), jnp.broadcast_to(e_small, (8, LANES)))
-    out_ref[72:] = jnp.where(row < 2, x[72:80] * jnp.exp2(-e_small), rest)
+    big = x[:72] * jnp.exp2(-e_big)
+    tail = jnp.where(row < 5, jnp.broadcast_to(e_big, (8, LANES)), jnp.broadcast_to(e_small, (8, LANES)))
+    tail = jnp.where(row < 2, rest * jnp.exp2(-e_small), tail)
+    for q in range(PARTS // 2):
+        out_ref[q, :72] = big
+        out_ref[q, 72:] = tail
+
+
+def to_half(v):
+    row = lax.broadcasted_iota(jnp.int32, (1, PACK, 1), 1)
+    size = jnp.abs(v)
+
+    def exponent(where):
+        top = jnp.max(jnp.where(where, size, 0.0), axis=(1, 2), keepdims=True)
+        return jnp.ceil(jnp.log2(jnp.maximum(top, 1e-30)))
+
+    e_big, e_small = exponent(row < 72), exponent((row >= 72) & (row < 74))
+    scaled = v * jnp.where(row < 72, jnp.exp2(-e_big), jnp.exp2(-e_small))
+    return jnp.where(row < 74, scaled, jnp.where(row < 77, e_big, e_small)).astype(jnp.float16)
+
+
+def from_half(h):
+    v = h.astype(F32)
+    row = lax.broadcasted_iota(jnp.int32, (1, PACK, 1), 1)
+    scale = jnp.where(row < 72, jnp.exp2(v[:, 74:75]), jnp.exp2(v[:, 77:78]))
+    return jnp.where(row < 74, v * scale, 0.0)
 
 
 def shape(*dims, dtype=F32):
@@ -395,9 +463,12 @@
     return pl.CostEstimate(flops=int(flops), bytes_accessed=int(moved), transcendentals=0)
 
 
+def exchanged(blocks):
+    return lax.all_to_all(blocks, RC, 0, 0, tiled=True, axis_index_groups=CHIPS)
+
+
 def gathered(block):
-    wide = jnp.broadcast_to(block[None], (PARTS // 2,) + block.shape)
-    return lax.all_to_all(wide, RC, 0, 0, tiled=True, axis_index_groups=CHIPS)
+    return exchanged(jnp.broadcast_to(block[None], (PARTS // 2,) + block.shape))
 
 
 def partner(block):
@@ -421,6 +492,7 @@
     tile = full(ROWS, CH, LANES)
     edge = full(CH, LANES)
     weight = full(CH, EX)
+    anywhere = pl.BlockSpec(memory_space=pl.ANY)
     chunk_rows = lambda width: pl.BlockSpec((EB, width), lambda j: (j, 0))
     chunk_cols = pl.BlockSpec((CH, EB), lambda j: (0, j))
     chunk_taps = pl.BlockSpec((9, EB), lambda j: (0, j))
@@ -460,14 +532,17 @@
         forward_kernel,
         grid=(STEPS,),
         in_specs=[halo, halo, edge, edge, edge, full(1, CH), chunk_cols, chunk_taps,
-                  chunk_rows(ROWS * LANES), chunk_rows(ROWS * LANES)],
+                  anywhere, anywhere],
         out_specs=[chunk_rows(CS * LANES), full(16, LANES)],
         out_shape=[shape(EX, CS * LANES), shape(16, LANES)],
         scratch_shapes=[
             pltpu.VMEM((CH, (XS - ROWS) * LANES), BF16),
             pltpu.VMEM((EB, (XS - ROWS) * LANES), F32),
             pltpu.VMEM((EB, 9 * LANES), F32),
-            pltpu.VMEM((EB, LANES), F32),
+            pltpu.VMEM((2, EB, LANES), F32),
+            pltpu.VMEM((2, EB, ROWS * LANES), BF16),
+            pltpu.VMEM((2, EB, ROWS * LANES), F32),
+            pltpu.SemaphoreType.DMA((2, 2)),
         ],
         compiler_params=params(),
         cost_estimate=cost(200e6, 12e6),
@@ -482,12 +557,11 @@
         in_specs=[pl.BlockSpec(memory_space=pltpu.SMEM), full(PARTS // 2, 16, LANES),
                   full(SQ, EX), full(SQ, EX), tile, tile, halo, halo, edge, edge, full(1, CH),
                   full(8, LANES), full(CH, ROWS * LANES), full(ROWS, LANES),
-                  chunk_rows(ROWS * LANES), chunk_rows(ROWS * LANES), chunk_rows(CS * LANES), chunk_taps,
+                  anywhere, anywhere, anywhere, chunk_taps,
                   weight, weight],
-        out_specs=[tile, tile, full(PARTS // 2, PACK, LANES), full(PARTS // 2, PACK, LANES),
-                   full(16, LANES)],
+        out_specs=[tile, tile, anywhere, anywhere, full(16, LANES)],
         out_shape=[shape(ROWS, CH, LANES, dtype=BF16), shape(ROWS, CH, LANES, dtype=BF16),
-                   shape(PARTS // 2, PACK, LANES), shape(PARTS // 2, PACK, LANES),
+                   shape(PARTS // 2 * PACK, LANES), shape(PARTS // 2 * PACK, LANES),
                    shape(16, LANES)],
         scratch_shapes=[
             pltpu.VMEM((PARTS * PACK, LANES), F32),
@@ -501,6 +575,11 @@
             pltpu.VMEM((EB, 9 * LANES), F32),
             pltpu.VMEM((EB, LANES), F32),
             pltpu.VMEM((56, LANES), F32),
+            pltpu.VMEM((2, EB, ROWS * LANES), F32),
+            pltpu.VMEM((2, EB, ROWS * LANES), F32),
+            pltpu.VMEM((2, EB, CS * LANES), F32),
+            pltpu.SemaphoreType.DMA((3, 2)),
+            pltpu.SemaphoreType.DMA((2,)),
         ],
         compiler_params=params(),
         cost_estimate=cost(1500e6, 16e6),
@@ -508,10 +587,9 @@
     )(core, sums, w_squeeze.T, w_excite, x, c, top, bot, left, right, gain, mask, scaled, inv, gg, pre, conv, taps,
       w_expand, wprojt)
 
-    mine = lax.all_to_all(
-        keep + partner(send), RC, 0, 0, tiled=True, axis_index_groups=CHIPS
-    )
-    total = jnp.sum(mine, axis=0)
+    halves = to_half((keep + partner(send)).reshape(PARTS // 2, PACK, LANES))
+    mine = exchanged(halves)
+    total = jnp.sum(from_half(mine), axis=0)
     vecs = vec[None]
     sample = lax.axis_index("dp")
     for bit in (1, 2, 4):
@@ -530,9 +608,12 @@
     grad_wexc = jnp.einsum("bs,be->se", vecs[:, 1536:1584], vecs[:, 768:1536], precision=HIGH)
     grad_wsq = jnp.einsum("be,bs->es", vecs[:, :768], vecs[:, 1664:1712], precision=HIGH)
     scaled = pl.pallas_call(
-        scale_kernel, out_shape=shape(PACK, LANES), compiler_params=params(False), name="scale"
+        scale_kernel,
+        out_shape=shape(PARTS // 2, PACK, LANES),
+        compiler_params=params(False),
+        name="scale",
     )(total)
-    same = gathered(scaled.astype(jnp.float16))
+    same = exchanged(scaled.astype(jnp.float16))
     other = partner(same)
     even = core[0] == 0
     every = jnp.stack(

time: 150 us -> 145 us (0.967)
  Pallas kernels: 49.5 us -> 44.4 us
  blocking collectives: 15.2 us -> 11.6 us
  other arithmetic: 4.77 us -> 8.01 us
    pallas_call x1, Pallas kernels: 17.4 us -> 12.8 us  [local(): pl.pallas_call(forward_kernel, grid=(STEPS,), in_specs=[halo, halo, edge,...]
    all_to_all x1, blocking collectives: 15.2 us -> 11.6 us  [exchanged(): return lax.all_to_all(blocks, RC, 0, 0, tiled=True, axis_index_groups=CHIPS)]
    reduce_max x0 -> x3, other arithmetic: none -> 2.58 us  [exponent(): top = jnp.max(jnp.where(where, size, 0.0), axis=(1, 2), keepdims=True)]
    convert_element_type x1 -> x3, other arithmetic: 0.78 us -> 2.34 us  [the longest x1 1.85 us: local(): same = exchanged(scaled.astype(jnp.float16))]
where the time goes in v8:
time: 145 us; the launch traced here: 144 us
  Pallas kernels  44.4 us (31%)
  starting transfers between devices  43.2 us (30%)
  waiting for transfers between devices  23.7 us (16%)
  blocking collectives  11.6 us (8%)
  local copies, waits for them, and re-layouts  9.86 us (7%)
  other arithmetic  8.01 us (6%)
  matrix products  1.99 us (1%)
    pallas_call x1, Pallas kernels, local(): pl.pallas_call(backward_kernel, grid=(STEPS,), in_specs=[pl.BlockSpec(mem...  21.3 us
    all_to_all x2, waiting for transfers between devices, exchanged(): return lax.all_to_all(blocks, RC, 0, 0, tiled=True, axis_index_groups=CHIPS)  13.6 us
    pallas_call x1, Pallas kernels, local(): pl.pallas_call(forward_kernel, grid=(STEPS,), in_specs=[halo, halo, edge,...  12.8 us
    ppermute x3, starting transfers between devices, local(): lax.ppermute(jnp.concatenate([total, vecs.reshape(16 * bit, LANES)], axis...  11.6 us
    all_to_all x1, blocking collectives, exchanged(): return lax.all_to_all(blocks, RC, 0, 0, tiled=True, axis_index_groups=CHIPS)  11.6 us
    all_to_all x2, starting transfers between devices, exchanged(): return lax.all_to_all(blocks, RC, 0, 0, tiled=True, axis_index_groups=CHIPS)  11.4 us
    ppermute x3, starting transfers between devices, partner(): return lax.ppermute(block, 'col', [(i, i ^ 1) for i in range(4)])  7.88 us
    pallas_call x1, Pallas kernels, local(): pl.pallas_call(expand_kernel, grid=(STEPS,), in_specs=[tile, tile, full(1...  6.36 us
  transfers between devices with their start and end apart: 12, of which 8 were waited for; matrix products, arithmetic and copies ran while one was open for 3% of the time, Pallas kernels for 4%

profile of v8, /device:TPU:1, one launch (start us, length us, event | category | flops | bytes accessed | tf_op | source)
XLA Modules:
  0.0 143.9 jit_solution(10407966868408901061)
XLA Ops:
  0.6 1.3 copy_bitcast_fusion.2
  2.0 1.3 collective-permute-start.1
  3.3 4.6 %collective-permute-start = (bf16[3,192,128]{2,1,0:T(8,128)(2,1)S(1)}, bf16[3,192,128]{2,1,0:T(8,128)(2,1)S(1)}, u32[]{:S(2)}, u32[]{:S(2)}) collective-permute-start(bf16[3,192,128]{2,1,0:T(8,128)(2,1)S(1)} %pad_maximum_fusion), channel_id=1, source_target_pairs={{0,4},{4,8},{8,12},{12,16},{16,20},{20,24},{24,28},{1,5},{5,9},{9,... | collective-permute-start | bytes 442376 | tf_op jit(solution)/shard_map/ppermute | solution.py:487
  7.9 6.4 %expand.1 = (bf16[192,1024]{1,0:T(8,128)(2,1)}, f32[8,128]{1,0:T(8,128)}, f32[768,1024]{1,0:T(8,128)}, bf16[768,1024]{1,0:T(8,128)(2,1)}, f32[768,1024]{1,0:T(8,128)}) custom-call(bf16[8,192,128]{2,1,0:T(8,128)(2,1)} %copy-done, bf16[8,192,128]{2,1,0:T(8,128)(2,1)} %copy-done.1, f32[1,192]{1,0:T(1,128)} %bitcast.82, bf16[192,768]{1,0:T(8,128)(2,1)} %wexp_ref.5, ...), custom_call_target="tpu_custom_call" | custom-call | flops 600000000 | bytes 10000000 | tf_op jit(solution)/shard_map/expand/pallas_call | solution.py:499
  15.0 2.2 %strip.1.own_ref = bf16[192,128]{1,0:T(8,128)(2,1)} custom-call(bf16[8,192,128]{2,1,0:T(8,128)(2,1)} %copy-done, bf16[8,192,128]{2,1,0:T(8,128)(2,1)} %copy-done.1, bf16[3,192,128]{2,1,0:T(8,128)(2,1)} %copy-done.3, bf16[3,192,128]{2,1,0:T(8,128)(2,1)} %copy-done.2, f32[8,128]{1,0:T(8,128)} %get-tuple-element.20.after_ref.inv_ref), custom_call_target="tpu_custom_call" | custom-call | flops 1000000 | bytes 1000000 | tf_op jit(solution)/shard_map/strip/pallas_call | solution.py:513
  17.2 4.6 %collective-permute-start.2 = (bf16[192,128]{1,0:T(8,128)(2,1)}, bf16[192,128]{1,0:T(8,128)(2,1)S(1)}, u32[]{:S(2)}, u32[]{:S(2)}) collective-permute-start(bf16[192,128]{1,0:T(8,128)(2,1)} %strip.1.own_ref), channel_id=1, source_target_pairs={{0,1},{1,2},{2,3},{4,5},{5,6},{6,7},{8,9},{9,10},{10,11},{12,13},{... | collective-permute-start | bytes 147464 | tf_op jit(solution)/shard_map/ppermute | solution.py:520
  21.8 1.9 %collective-permute-start.3 = (bf16[192,128]{1,0:T(8,128)(2,1)}, bf16[192,128]{1,0:T(8,128)(2,1)S(1)}, u32[]{:S(2)}, u32[]{:S(2)}) collective-permute-start(bf16[192,128]{1,0:T(8,128)(2,1)} %strip.1.own_ref), channel_id=1, source_target_pairs={{1,0},{2,1},{3,2},{5,4},{6,5},{7,6},{9,8},{10,9},{11,10},{13,12},{... | collective-permute-start | bytes 147464 | tf_op jit(solution)/shard_map/ppermute | solution.py:521
  23.7 3.6 %collective-permute-done.3.right_ref = bf16[192,128]{1,0:T(8,128)(2,1)S(1)} collective-permute-done((bf16[192,128]{1,0:T(8,128)(2,1)}, bf16[192,128]{1,0:T(8,128)(2,1)S(1)}, u32[]{:S(2)}, u32[]{:S(2)}) %collective-permute-start.3) | collective-permute-done | bytes 49184 | tf_op jit(solution)/shard_map/ppermute | solution.py:521
  28.0 12.8 %forward.1 = (f32[768,1408]{1,0:T(8,128)}, f32[16,128]{1,0:T(8,128)}) custom-call(bf16[3,192,128]{2,1,0:T(8,128)(2,1)} %copy-done.3, bf16[3,192,128]{2,1,0:T(8,128)(2,1)} %copy-done.2, bf16[192,128]{1,0:T(8,128)(2,1)} %strip.1.own_ref, bf16[192,128]{1,0:T(8,128)(2,1)} %copy-done.7, bf16[192,128]{1,0:T(8,128)(2,1)} %copy-done.8, f32[1,192]{1,0:T(1,128)} %bitcast.83, ...), custom_call_target="tpu_custom_call" | custom-call | flops 200000000 | bytes 12000000 | tf_op jit(solution)/shard_map/forward/pallas_call | solution.py:531
  41.0 1.3 collective-permute-done.4
  43.7 7.8 %all-to-all-start = ((f32[16,16,128]{2,1,0:T(8,128)}), f32[16,16,128]{2,1,0:T(8,128)S(1)}, u32[]{:S(2)}, u32[]{:S(2)}) async-start(f32[16,16,128]{2,1,0:T(8,128)} %broadcast_in_dim.136), calls=%async_computation | async-start | bytes 262144 | tf_op jit(solution)/shard_map/all_to_all | solution.py:467
  52.2 6.0 %all-to-all-done.parts_ref = f32[16,16,128]{2,1,0:T(8,128)S(1)} async-done(((f32[16,16,128]{2,1,0:T(8,128)}), f32[16,16,128]{2,1,0:T(8,128)S(1)}, u32[]{:S(2)}, u32[]{:S(2)}) %all-to-all-start) | async-done | bytes 131104 | tf_op jit(solution)/shard_map/all_to_all | solution.py:467
  58.8 21.3 %backward.1 = (bf16[8,192,128]{2,1,0:T(8,128)(2,1)}, bf16[8,192,128]{2,1,0:T(8,128)(2,1)}, f32[1280,128]{1,0:T(8,128)}, f32[1280,128]{1,0:T(8,128)}, f32[16,128]{1,0:T(8,128)}) custom-call(s32[1]{0:T(128)} %bitcast.core_ref, f32[16,16,128]{2,1,0:T(8,128)} %copy-done.4, f32[48,768]{1,0:T(8,128)} %bitcast.67, f32[48,768]{1,0:T(8,128)} %wexc_ref.1, ...), custom_call_target="tpu_custom_call" | custom-call | flops 1500000000 | bytes 16000000 | tf_op jit(solution)/shard_map/backward/pallas_call | solution.py:554
  80.2 1.7 %collective-permute-start.5 = (f32[1280,128]{1,0:T(8,128)}, f32[1280,128]{1,0:T(8,128)S(1)}, u32[]{:S(2)}, u32[]{:S(2)}) collective-permute-start(f32[1280,128]{1,0:T(8,128)} %get-tuple-element.30), channel_id=1, source_target_pairs={{0,1},{1,0},{2,3},{3,2},{4,5},{5,4},{6,7},{7,6},{8,9},{9,8},{10,11... | collective-permute-start | bytes 1966088 | tf_op jit(solution)/shard_map/ppermute | solution.py:475
  82.0 1.7 %collective-permute-done.5 = f32[1280,128]{1,0:T(8,128)S(1)} collective-permute-done((f32[1280,128]{1,0:T(8,128)}, f32[1280,128]{1,0:T(8,128)S(1)}, u32[]{:S(2)}, u32[]{:S(2)}) %collective-permute-start.5) | collective-permute-done | bytes 655392 | tf_op jit(solution)/shard_map/ppermute | solution.py:475
  83.8 2.3 %select_reduce_fusion.2 = (f32[1280]{0:T(1024)S(1)}, f32[1280]{0:T(1024)S(1)}, f32[1280,128]{1,0:T(8,128)S(1)}) fusion(pred[1280]{0:T(1024)(128)(4,1)S(1)} %broadcast_in_dim.141, pred[1280]{0:T(1024)(128)(4,1)S(1)} %broadcast_in_dim.146, f32[1280,128]{1,0:T(8,128)} %get-tuple-element.29, f32[1280,128]{1,0:T(8,128)S(1)} %collective-permute-done.5), kind=kLoop, calls=%fused_computation.5 | loop fusion | flops 980480 | bytes 1978880 | tf_op jit(solution)/shard_map/reduce_max | solution.py:433
  87.1 11.6 %all_to_all.15 = f16[16,80,128]{2,1,0:T(8,128)(2,1)S(1)} all-to-all(f16[16,80,128]{2,1,0:T(8,128)(2,1)S(1)} %select_convert_fusion), channel_id=1, replica_groups={{0,2,4,6,8,10,12,14,16,18,20,22,24,26,28,30},{1,3,5,7,9,11,13,15,17,19,..., dimensions={0} | all-to-all | bytes 655360 | tf_op jit(solution)/shard_map/all_to_all | solution.py:467
  99.1 1.7 %collective-permute-start.6 = (f32[96,128]{1,0:T(8,128)S(1)}, f32[96,128]{1,0:T(8,128)S(1)}, u32[]{:S(2)}, u32[]{:S(2)}) collective-permute-start(f32[96,128]{1,0:T(8,128)S(1)} %pad_maximum_fusion.4), channel_id=1, source_target_pairs={{0,32},{32,0},{64,96},{96,64},{128,160},{160,128},{192,224},{224,1... | collective-permute-start | bytes 147464 | tf_op jit(solution)/shard_map/ppermute | solution.py:596
  100.8 1.5 %collective-permute-done.6 = f32[96,128]{1,0:T(8,128)S(1)} collective-permute-done((f32[96,128]{1,0:T(8,128)S(1)}, f32[96,128]{1,0:T(8,128)S(1)}, u32[]{:S(2)}, u32[]{:S(2)}) %collective-permute-start.6) | collective-permute-done | bytes 49184 | tf_op jit(solution)/shard_map/ppermute | solution.py:596
  102.3 3.1 %collective-permute-start.7 = (f32[112,128]{1,0:T(8,128)S(1)}, f32[112,128]{1,0:T(8,128)S(1)}, u32[]{:S(2)}, u32[]{:S(2)}) collective-permute-start(f32[112,128]{1,0:T(8,128)S(1)} %pad_maximum_fusion.3), channel_id=1, source_target_pairs={{0,64},{32,96},{64,0},{96,32},{128,192},{160,224},{192,128},{224,1... | collective-permute-start | bytes 172040 | tf_op jit(solution)/shard_map/ppermute | solution.py:596
  105.4 1.6 %collective-permute-done.7 = f32[112,128]{1,0:T(8,128)S(1)} collective-permute-done((f32[112,128]{1,0:T(8,128)S(1)}, f32[112,128]{1,0:T(8,128)S(1)}, u32[]{:S(2)}, u32[]{:S(2)}) %collective-permute-start.7) | collective-permute-done | bytes 57376 | tf_op jit(solution)/shard_map/ppermute | solution.py:596
  107.0 6.8 %collective-permute-start.8 = (f32[144,128]{1,0:T(8,128)S(1)}, f32[144,128]{1,0:T(8,128)S(1)}, u32[]{:S(2)}, u32[]{:S(2)}) collective-permute-start(f32[144,128]{1,0:T(8,128)S(1)} %pad_maximum_fusion.2), channel_id=1, source_target_pairs={{0,128},{32,160},{64,192},{96,224},{128,0},{160,32},{192,64},{224,... | collective-permute-start | bytes 221192 | tf_op jit(solution)/shard_map/ppermute | solution.py:596
  113.8 1.0 copy.33
  114.8 1.0 copy.34
  116.9 1.8 %scale.1 = f32[16,80,128]{2,1,0:T(8,128)} custom-call(f32[80,128]{1,0:T(8,128)} %slice_add_fusion.x_ref), custom_call_target="tpu_custom_call" | custom-call | tf_op jit(solution)/shard_map/scale/pallas_call | solution.py:610
  118.6 1.9 %convert_element_type.21 = f16[16,80,128]{2,1,0:T(8,128)(2,1)} convert(f32[16,80,128]{2,1,0:T(8,128)} %scale.1) | non-fusion elementwise | flops 163840 | bytes 983040 | tf_op jit(solution)/shard_map/convert_element_type | solution.py:616
  120.5 3.5 %all-to-all-start.2 = ((f16[16,80,128]{2,1,0:T(8,128)(2,1)}), f16[16,80,128]{2,1,0:T(8,128)(2,1)S(1)}, u32[]{:S(2)}, u32[]{:S(2)}) async-start(f16[16,80,128]{2,1,0:T(8,128)(2,1)} %convert_element_type.21), calls=%async_computation.2 | async-start | bytes 655360 | tf_op jit(solution)/shard_map/all_to_all | solution.py:467
  124.1 7.6 %all-to-all-done.2 = f16[16,80,128]{2,1,0:T(8,128)(2,1)S(1)} async-done(((f16[16,80,128]{2,1,0:T(8,128)(2,1)}), f16[16,80,128]{2,1,0:T(8,128)(2,1)S(1)}, u32[]{:S(2)}, u32[]{:S(2)}) %all-to-all-start.2) | async-done | bytes 327712 | tf_op jit(solution)/shard_map/all_to_all | solution.py:467
  131.7 6.1 %collective-permute-start.9 = (f16[16,80,128]{2,1,0:T(8,128)(2,1)S(1)}, f16[16,80,128]{2,1,0:T(8,128)(2,1)S(1)}, u32[]{:S(2)}, u32[]{:S(2)}) collective-permute-start(f16[16,80,128]{2,1,0:T(8,128)(2,1)S(1)} %all-to-all-done.2), channel_id=1, source_target_pairs={{0,1},{1,0},{2,3},{3,2},{4,5},{5,4},{6,7},{7,6},{8,9},{9,8},{10,11... | collective-permute-start | bytes 983048 | tf_op jit(solution)/shard_map/ppermute | solution.py:475
  137.8 1.0 fusion.3
  138.8 1.0 fusion.1
  140.8 0.9 copy.41
  (84 shorter events, 10.0 us)
Async XLA Ops:
  1.9 6.0 %copy-start = (bf16[8,192,128]{2,1,0:T(8,128)(2,1)}, bf16[8,192,128]{2,1,0:T(8,128)(2,1)S(1)}, u32[]{:S(2)}) copy-start(bf16[8,192,128]{2,1,0:T(8,128)(2,1)S(1)} %get-tuple-element.84.x_ref) | copy-start | bytes 1179652
  1.9 6.0 %copy-start.1 = (bf16[8,192,128]{2,1,0:T(8,128)(2,1)}, bf16[8,192,128]{2,1,0:T(8,128)(2,1)S(1)}, u32[]{:S(2)}) copy-start(bf16[8,192,128]{2,1,0:T(8,128)(2,1)S(1)} %get-tuple-element.83.c_ref) | copy-start | bytes 1179652
  2.0 12.3 %collective-permute-start.1 = (bf16[3,192,128]{2,1,0:T(8,128)(2,1)S(1)}, bf16[3,192,128]{2,1,0:T(8,128)(2,1)S(1)}, u32[]{:S(2)}, u32[]{:S(2)}) collective-permute-start(bf16[3,192,128]{2,1,0:T(8,128)(2,1)S(1)} %pad_maximum_fusion.1), channel_id=1, source_target_pairs={{4,0},{8,4},{12,8},{16,12},{20,16},{24,20},{28,24},{5,1},{9,5},{13... | collective-permute-start | bytes 442376 | tf_op jit(solution)/shard_map/ppermute | solution.py:488
  3.3 11.0 %collective-permute-start = (bf16[3,192,128]{2,1,0:T(8,128)(2,1)S(1)}, bf16[3,192,128]{2,1,0:T(8,128)(2,1)S(1)}, u32[]{:S(2)}, u32[]{:S(2)}) collective-permute-start(bf16[3,192,128]{2,1,0:T(8,128)(2,1)S(1)} %pad_maximum_fusion), channel_id=1, source_target_pairs={{0,4},{4,8},{8,12},{12,16},{16,20},{20,24},{24,28},{1,5},{5,9},{9,... | collective-permute-start | bytes 442376 | tf_op jit(solution)/shard_map/ppermute | solution.py:487
  14.3 0.7 copy-start.2
  14.3 0.7 copy-start.3
  17.2 6.5 %collective-permute-start.2 = (bf16[192,128]{1,0:T(8,128)(2,1)}, bf16[192,128]{1,0:T(8,128)(2,1)S(1)}, u32[]{:S(2)}, u32[]{:S(2)}) collective-permute-start(bf16[192,128]{1,0:T(8,128)(2,1)} %strip.1.own_ref), channel_id=1, source_target_pairs={{0,1},{1,2},{2,3},{4,5},{5,6},{6,7},{8,9},{9,10},{10,11},{12,13},{... | collective-permute-start | bytes 147464 | tf_op jit(solution)/shard_map/ppermute | solution.py:520
  21.8 5.6 %collective-permute-start.3 = (bf16[192,128]{1,0:T(8,128)(2,1)}, bf16[192,128]{1,0:T(8,128)(2,1)S(1)}, u32[]{:S(2)}, u32[]{:S(2)}) collective-permute-start(bf16[192,128]{1,0:T(8,128)(2,1)} %strip.1.own_ref), channel_id=1, source_target_pairs={{1,0},{2,1},{3,2},{5,4},{6,5},{7,6},{9,8},{10,9},{11,10},{13,12},{... | collective-permute-start | bytes 147464 | tf_op jit(solution)/shard_map/ppermute | solution.py:521
  23.7 3.7 %copy-start.7 = (bf16[192,128]{1,0:T(8,128)(2,1)}, bf16[192,128]{1,0:T(8,128)(2,1)S(1)}, u32[]{:S(2)}) copy-start(bf16[192,128]{1,0:T(8,128)(2,1)S(1)} %collective-permute-done.2.left_ref) | copy-start | bytes 147460
  27.4 0.6 copy-start.8
  40.8 1.5 %collective-permute-start.4 = (f32[16,128]{1,0:T(8,128)}, f32[16,128]{1,0:T(8,128)S(1)}, u32[]{:S(2)}, u32[]{:S(2)}) collective-permute-start(f32[16,128]{1,0:T(8,128)} %get-tuple-element.23), channel_id=1, source_target_pairs={{0,1},{1,0},{2,3},{3,2},{4,5},{5,4},{6,7},{7,6},{8,9},{9,8},{10,11... | collective-permute-start | bytes 24584 | tf_op jit(solution)/shard_map/ppermute | solution.py:475
  43.7 14.5 %all-to-all-start = ((f32[16,16,128]{2,1,0:T(8,128)}), f32[16,16,128]{2,1,0:T(8,128)S(1)}, u32[]{:S(2)}, u32[]{:S(2)}) async-start(f32[16,16,128]{2,1,0:T(8,128)} %broadcast_in_dim.136), calls=%async_computation | async-start | bytes 262144 | tf_op jit(solution)/shard_map/all_to_all | solution.py:467
  58.2 0.6 copy-start.4
  80.2 3.6 %collective-permute-start.5 = (f32[1280,128]{1,0:T(8,128)}, f32[1280,128]{1,0:T(8,128)S(1)}, u32[]{:S(2)}, u32[]{:S(2)}) collective-permute-start(f32[1280,128]{1,0:T(8,128)} %get-tuple-element.30), channel_id=1, source_target_pairs={{0,1},{1,0},{2,3},{3,2},{4,5},{5,4},{6,7},{7,6},{8,9},{9,8},{10,11... | collective-permute-start | bytes 1966088 | tf_op jit(solution)/shard_map/ppermute | solution.py:475
  86.7 12.4 %copy-start.9 = (f32[16,128]{1,0:T(8,128)S(1)}, f32[16,128]{1,0:T(8,128)}, u32[]{:S(2)}) copy-start(f32[16,128]{1,0:T(8,128)} %get-tuple-element.31) | copy-start | bytes 24580
  87.1 26.7 %copy-start.6 = (bf16[8,192,128]{2,1,0:T(8,128)(2,1)S(1)}, bf16[8,192,128]{2,1,0:T(8,128)(2,1)}, u32[]{:S(2)}) copy-start(bf16[8,192,128]{2,1,0:T(8,128)(2,1)} %get-tuple-element.27) | copy-start | bytes 1179652
  98.7 16.2 %copy-start.5 = (bf16[8,192,128]{2,1,0:T(8,128)(2,1)S(1)}, bf16[8,192,128]{2,1,0:T(8,128)(2,1)}, u32[]{:S(2)}) copy-start(bf16[8,192,128]{2,1,0:T(8,128)(2,1)} %get-tuple-element.28) | copy-start | bytes 1179652
  99.1 3.2 %collective-permute-start.6 = (f32[96,128]{1,0:T(8,128)S(1)}, f32[96,128]{1,0:T(8,128)S(1)}, u32[]{:S(2)}, u32[]{:S(2)}) collective-permute-start(f32[96,128]{1,0:T(8,128)S(1)} %pad_maximum_fusion.4), channel_id=1, source_target_pairs={{0,32},{32,0},{64,96},{96,64},{128,160},{160,128},{192,224},{224,1... | collective-permute-start | bytes 147464 | tf_op jit(solution)/shard_map/ppermute | solution.py:596
  102.3 4.6 %collective-permute-start.7 = (f32[112,128]{1,0:T(8,128)S(1)}, f32[112,128]{1,0:T(8,128)S(1)}, u32[]{:S(2)}, u32[]{:S(2)}) collective-permute-start(f32[112,128]{1,0:T(8,128)S(1)} %pad_maximum_fusion.3), channel_id=1, source_target_pairs={{0,64},{32,96},{64,0},{96,32},{128,192},{160,224},{192,128},{224,1... | collective-permute-start | bytes 172040 | tf_op jit(solution)/shard_map/ppermute | solution.py:596
  107.0 9.2 %collective-permute-start.8 = (f32[144,128]{1,0:T(8,128)S(1)}, f32[144,128]{1,0:T(8,128)S(1)}, u32[]{:S(2)}, u32[]{:S(2)}) collective-permute-start(f32[144,128]{1,0:T(8,128)S(1)} %pad_maximum_fusion.2), channel_id=1, source_target_pairs={{0,128},{32,160},{64,192},{96,224},{128,0},{160,32},{192,64},{224,... | collective-permute-start | bytes 221192 | tf_op jit(solution)/shard_map/ppermute | solution.py:596
  120.5 11.2 %all-to-all-start.2 = ((f16[16,80,128]{2,1,0:T(8,128)(2,1)}), f16[16,80,128]{2,1,0:T(8,128)(2,1)S(1)}, u32[]{:S(2)}, u32[]{:S(2)}) async-start(f16[16,80,128]{2,1,0:T(8,128)(2,1)} %convert_element_type.21), calls=%async_computation.2 | async-start | bytes 655360 | tf_op jit(solution)/shard_map/all_to_all | solution.py:467
  131.7 8.1 %collective-permute-start.9 = (f16[16,80,128]{2,1,0:T(8,128)(2,1)S(1)}, f16[16,80,128]{2,1,0:T(8,128)(2,1)S(1)}, u32[]{:S(2)}, u32[]{:S(2)}) collective-permute-start(f16[16,80,128]{2,1,0:T(8,128)(2,1)S(1)} %all-to-all-done.2), channel_id=1, source_target_pairs={{0,1},{1,0},{2,3},{3,2},{4,5},{5,4},{6,7},{7,6},{8,9},{9,8},{10,11... | collective-permute-start | bytes 983048 | tf_op jit(solution)/shard_map/ppermute | solution.py:475

commit v9 on v8

--- a/solution.py
+++ b/solution.py
@@ -50,28 +50,27 @@
     return pl.ds(s * LANES, n * LANES)
 
 
-def strip_kernel(x_ref, c_ref, top_ref, bot_ref, after_ref, out_ref):
+def strip_lines(lines, total):
     lane = lane_iota(CH)
-    total = jnp.zeros((CH, LANES), F32)
-    for rr in range(ROWS + 4):
-        if rr < 2:
-            v = top_ref[rr]
-        elif rr < ROWS + 2:
-            v = x_ref[rr - 2]
-        else:
-            v = bot_ref[rr - ROWS - 2]
-        v = pltpu.roll(v.astype(F32), (8 * rr + 2) % LANES, 1)
-        total = jnp.where((lane >= 8 * rr) & (lane < 8 * rr + 4), v, total)
-        if 1 <= rr <= ROWS + 2:
-            if rr == 1:
-                v = top_ref[2]
-            elif rr == ROWS + 2:
-                v = bot_ref[2]
-            else:
-                v = c_ref[rr - 2]
-            v = pltpu.roll(v.astype(F32), (8 * rr + 5) % LANES, 1)
+    for rr, x, c in lines:
+        if x is not None:
+            v = pltpu.roll(x.astype(F32), (8 * rr + 2) % LANES, 1)
+            total = jnp.where((lane >= 8 * rr) & (lane < 8 * rr + 4), v, total)
+        if c is not None:
+            v = pltpu.roll(c.astype(F32), (8 * rr + 5) % LANES, 1)
             total = jnp.where((lane >= 8 * rr + 4) & (lane < 8 * rr + 6), v, total)
-    out_ref[...] = total.astype(BF16)
+    return total
+
+
+def strip_kernel(part_ref, top_ref, bot_ref, out_ref):
+    last = ROWS + 2
+    lines = [
+        (0, top_ref[0], None),
+        (1, top_ref[1], top_ref[2]),
+        (last, bot_ref[0], bot_ref[2]),
+        (last + 1, bot_ref[1], None),
+    ]
+    out_ref[...] = strip_lines(lines, part_ref[...].astype(F32)).astype(BF16)
 
 
 def input_strip(own_ref, left_ref, right_ref):
@@ -138,7 +137,8 @@
 
 
 def expand_kernel(
-    x_ref, c_ref, gain_ref, wexp_ref, wprojt_ref, scaled_out, inv_out, pre_out, hid_out, gg_out, cot_s
+    x_ref, c_ref, gain_ref, wexp_ref, wprojt_ref,
+    scaled_out, inv_out, part_out, pre_out, hid_out, gg_out, cot_s,
 ):
     @pl.when(pl.program_id(0) == 0)
     def _():
@@ -149,6 +149,8 @@
             inv_out[r : r + 1, :] = inverse
             scaled_out[:, slab(r)] = (x * inverse * gain).astype(BF16)
             cot_s[:, slab(r)] = c_ref[r]
+        lines = [(r + 2, x_ref[r], c_ref[r]) for r in range(ROWS)]
+        part_out[...] = strip_lines(lines, jnp.zeros((CH, LANES), F32)).astype(BF16)
 
     pre_out[...] = tn_dot(wexp_ref[...] * 0.5, scaled_out[...])
     gg_out[...] = tn_dot(wprojt_ref[...], cot_s[...])
@@ -363,12 +365,12 @@
                 lax.dot_general(cot_s[...], gated, NT, preferred_element_type=F32),
             )
         ):
-            for n in range(BLOCKS):
-                for i in range(CH // 24):
-                    group = (which * BLOCKS + n) * (CH // 24) + i
-                    part = group // 3
-                    row = PACK * (part % 2 * PARTS // 2 + part // 2) + 24 * (group % 3)
-                    packed_s[row : row + 24, :] = w[24 * i : 24 * i + 24, slab(n)]
+            for i in range(CH // 8):
+                for n in range(BLOCKS):
+                    group = (which * (CH // 8) + i) * BLOCKS + n
+                    part = group // 9
+                    row = PACK * (part % 2 * PARTS // 2 + part // 2) + 8 * (group % 9)
+                    packed_s[row : row + 8, :] = w[8 * i : 8 * i + 8, slab(n)]
         gs_all = jnp.dot(wexp_ref[...], gpre, preferred_element_type=F32)
         ggain = jnp.zeros((CH, LANES), F32)
         for r in range(ROWS):
@@ -406,25 +408,6 @@
             copy.wait()
 
 
-def scale_kernel(x_ref, out_ref):
-    x = x_ref[...]
-
-    def exponent(v):
-        top = jnp.max(jnp.max(jnp.abs(v), axis=1, keepdims=True), axis=0, keepdims=True)
-        return jnp.ceil(jnp.log2(jnp.maximum(top, 1e-30)))
-
-    row = lax.broadcasted_iota(jnp.int32, (8, LANES), 0)
-    rest = x[72:80]
-    e_big = exponent(x[:72])
-    e_small = exponent(jnp.where(row < 2, rest, 0.0))
-    big = x[:72] * jnp.exp2(-e_big)
-    tail = jnp.where(row < 5, jnp.broadcast_to(e_big, (8, LANES)), jnp.broadcast_to(e_small, (8, LANES)))
-    tail = jnp.where(row < 2, rest * jnp.exp2(-e_small), tail)
-    for q in range(PARTS // 2):
-        out_ref[q, :72] = big
-        out_ref[q, 72:] = tail
-
-
 def to_half(v):
     row = lax.broadcasted_iota(jnp.int32, (1, PACK, 1), 1)
     size = jnp.abs(v)
@@ -496,13 +479,14 @@
     chunk_rows = lambda width: pl.BlockSpec((EB, width), lambda j: (j, 0))
     chunk_cols = pl.BlockSpec((CH, EB), lambda j: (0, j))
     chunk_taps = pl.BlockSpec((9, EB), lambda j: (0, j))
-    scaled, inv, pre, hid, gg = pl.pallas_call(
+    scaled, inv, part, pre, hid, gg = pl.pallas_call(
         expand_kernel,
         grid=(STEPS,),
         in_specs=[tile, tile, full(1, CH), chunk_cols, chunk_cols],
-        out_specs=[full(CH, ROWS * LANES), full(ROWS, LANES), chunk_rows(ROWS * LANES),
+        out_specs=[full(CH, ROWS * LANES), full(ROWS, LANES), edge, chunk_rows(ROWS * LANES),
                    chunk_rows(ROWS * LANES), chunk_rows(ROWS * LANES)],
         out_shape=[shape(CH, ROWS * LANES, dtype=BF16), shape(ROWS, LANES),
+                   shape(CH, LANES, dtype=BF16),
                    shape(EX, ROWS * LANES), shape(EX, ROWS * LANES, dtype=BF16),
                    shape(EX, ROWS * LANES)],
         scratch_shapes=[pltpu.VMEM((CH, ROWS * LANES), BF16)],
@@ -516,7 +500,7 @@
         compiler_params=params(False),
         cost_estimate=cost(1e6, 1e6),
         name="strip",
-    )(x, c, top, bot, inv)
+    )(part, top, bot)
     left = lax.ppermute(own, "col", fwd_col)
     right = lax.ppermute(own, "col", bwd_col)
 
@@ -607,29 +591,24 @@
     vecs = vecs.reshape(8, 2048)
     grad_wexc = jnp.einsum("bs,be->se", vecs[:, 1536:1584], vecs[:, 768:1536], precision=HIGH)
     grad_wsq = jnp.einsum("be,bs->es", vecs[:, :768], vecs[:, 1664:1712], precision=HIGH)
-    scaled = pl.pallas_call(
-        scale_kernel,
-        out_shape=shape(PARTS // 2, PACK, LANES),
-        compiler_params=params(False),
-        name="scale",
-    )(total)
-    same = exchanged(scaled.astype(jnp.float16))
+    same = gathered(to_half(total[None])[0])
     other = partner(same)
     even = core[0] == 0
     every = jnp.stack(
         [jnp.where(even, same, other), jnp.where(even, other, same)], axis=1
     ).reshape(PARTS, PACK, LANES).astype(F32)
-    big = (every[:, :72] * jnp.exp2(every[:, 74:75])).reshape(2, BLOCKS, CH, LANES)
+    big = (every[:, :72] * jnp.exp2(every[:, 74:75])).reshape(2, CH // 8, BLOCKS, 8, LANES)
+    big = big.transpose(0, 1, 3, 2, 4).reshape(2, CH, EX)
     small = (every[:, 72:74] * jnp.exp2(every[:, 77:78])).reshape(8192)
     return (
         out.transpose(1, 0, 2)[None],
         gin.transpose(1, 0, 2)[None],
         small[6912:7104],
-        big[0].transpose(1, 0, 2).reshape(CH, EX),
+        big[0],
         small[:6912].reshape(9, 768).T,
         grad_wsq,
         grad_wexc,
-        big[1].transpose(0, 2, 1).reshape(EX, CH),
+        big[1].T,
     )
 
 

time: 145 us -> 142 us (0.979)
  Pallas kernels: 44.4 us -> 42.4 us
  between operations: 1.07 us -> 2.56 us
  other arithmetic: 8.01 us -> 6.53 us
    convert_element_type x1 -> x0, other arithmetic: 1.85 us -> none  [local(): same = exchanged(scaled.astype(jnp.float16))]
    pallas_call x1 -> x0, Pallas kernels: 1.76 us -> none  [local(): pl.pallas_call(scale_kernel, out_shape=shape(PARTS // 2, PACK, LANES), co...]
    unnamed x23 -> x22, local copies, waits for them, and re-layouts: 4.9 us -> 3.99 us
    reduce_max x3 -> x4, other arithmetic: 2.58 us -> 3.27 us  [exponent(): top = jnp.max(jnp.where(where, size, 0.0), axis=(1, 2), keepdims=True)]
  transfers between devices with their start and end apart: 12 -> 12, of which waited for: 8 -> 8; matrix products, arithmetic and copies ran while one was open for 3% -> 4% of each run, Pallas kernels for 4% -> 5%
where the time goes in v9:
time: 142 us; the launch traced here: 141 us
  starting transfers between devices  43 us (30%)
  Pallas kernels  42.4 us (30%)
  waiting for transfers between devices  23.7 us (17%)
  blocking collectives  11.6 us (8%)
  local copies, waits for them, and re-layouts  9.39 us (7%)
  other arithmetic  6.53 us (5%)
  between operations  2.56 us (2%)
  matrix products  1.99 us (1%)
    pallas_call x1, Pallas kernels, local(): pl.pallas_call(backward_kernel, grid=(STEPS,), in_specs=[pl.BlockSpec(mem...  21.3 us
    all_to_all x2, waiting for transfers between devices, exchanged(): return lax.all_to_all(blocks, RC, 0, 0, tiled=True, axis_index_groups=CHIPS)  13.6 us
    pallas_call x1, Pallas kernels, local(): pl.pallas_call(forward_kernel, grid=(STEPS,), in_specs=[halo, halo, edge,...  12.8 us
    ppermute x3, starting transfers between devices, local(): lax.ppermute(jnp.concatenate([total, vecs.reshape(16 * bit, LANES)], axis...  11.6 us
    all_to_all x1, blocking collectives, exchanged(): return lax.all_to_all(blocks, RC, 0, 0, tiled=True, axis_index_groups=CHIPS)  11.6 us
    all_to_all x2, starting transfers between devices, exchanged(): return lax.all_to_all(blocks, RC, 0, 0, tiled=True, axis_index_groups=CHIPS)  11.2 us
    ppermute x3, starting transfers between devices, partner(): return lax.ppermute(block, 'col', [(i, i ^ 1) for i in range(4)])  7.88 us
    pallas_call x1, Pallas kernels, local(): pl.pallas_call(expand_kernel, grid=(STEPS,), in_specs=[tile, tile, full(1...  6.52 us
  transfers between devices with their start and end apart: 12, of which 8 were waited for; matrix products, arithmetic and copies ran while one was open for 4% of the time, Pallas kernels for 5%

profile of v9, /device:TPU:1, one launch (start us, length us, event | category | flops | bytes accessed | tf_op | source)
XLA Modules:
  0.0 141.2 jit_solution(6300939807671821374)
XLA Ops:
  0.6 1.3 copy_bitcast_fusion
  2.0 1.3 collective-permute-start.1
  3.3 4.6 %collective-permute-start = (bf16[3,192,128]{2,1,0:T(8,128)(2,1)S(1)}, bf16[3,192,128]{2,1,0:T(8,128)(2,1)S(1)}, u32[]{:S(2)}, u32[]{:S(2)}) collective-permute-start(bf16[3,192,128]{2,1,0:T(8,128)(2,1)S(1)} %pad_maximum_fusion.1), channel_id=1, source_target_pairs={{0,4},{4,8},{8,12},{12,16},{16,20},{20,24},{24,28},{1,5},{5,9},{9,... | collective-permute-start | bytes 442376 | tf_op jit(solution)/shard_map/ppermute | solution.py:470
  7.9 6.5 %expand.1 = (bf16[192,1024]{1,0:T(8,128)(2,1)}, f32[8,128]{1,0:T(8,128)}, bf16[192,128]{1,0:T(8,128)(2,1)}, f32[768,1024]{1,0:T(8,128)}, bf16[768,1024]{1,0:T(8,128)(2,1)}, /*index=5*/f32[768,1024]{1,0:T(8,128)}) custom-call(bf16[8,192,128]{2,1,0:T(8,128)(2,1)} %copy-done, bf16[8,192,128]{2,1,0:T(8,128)(2,1)} %copy-done.1, f32[1,192]{1,0:T(1,128)} %bitcast.75, ...), custom_call_target="tpu_custom_call" | custom-call | flops 600000000 | bytes 10000000 | tf_op jit(solution)/shard_map/expand/pallas_call | solution.py:482
  15.2 1.8 %strip.1.own_ref = bf16[192,128]{1,0:T(8,128)(2,1)} custom-call(bf16[192,128]{1,0:T(8,128)(2,1)} %get-tuple-element.21.part_ref, bf16[3,192,128]{2,1,0:T(8,128)(2,1)} %copy-done.3, bf16[3,192,128]{2,1,0:T(8,128)(2,1)} %copy-done.2), custom_call_target="tpu_custom_call" | custom-call | flops 1000000 | bytes 1000000 | tf_op jit(solution)/shard_map/strip/pallas_call | solution.py:497
  16.9 4.6 %collective-permute-start.2 = (bf16[192,128]{1,0:T(8,128)(2,1)}, bf16[192,128]{1,0:T(8,128)(2,1)S(1)}, u32[]{:S(2)}, u32[]{:S(2)}) collective-permute-start(bf16[192,128]{1,0:T(8,128)(2,1)} %strip.1.own_ref), channel_id=1, source_target_pairs={{0,1},{1,2},{2,3},{4,5},{5,6},{6,7},{8,9},{9,10},{10,11},{12,13},{... | collective-permute-start | bytes 147464 | tf_op jit(solution)/shard_map/ppermute | solution.py:504
  21.5 1.9 %collective-permute-start.3 = (bf16[192,128]{1,0:T(8,128)(2,1)}, bf16[192,128]{1,0:T(8,128)(2,1)S(1)}, u32[]{:S(2)}, u32[]{:S(2)}) collective-permute-start(bf16[192,128]{1,0:T(8,128)(2,1)} %strip.1.own_ref), channel_id=1, source_target_pairs={{1,0},{2,1},{3,2},{5,4},{6,5},{7,6},{9,8},{10,9},{11,10},{13,12},{... | collective-permute-start | bytes 147464 | tf_op jit(solution)/shard_map/ppermute | solution.py:505
  23.5 3.6 %collective-permute-done.3.right_ref = bf16[192,128]{1,0:T(8,128)(2,1)S(1)} collective-permute-done((bf16[192,128]{1,0:T(8,128)(2,1)}, bf16[192,128]{1,0:T(8,128)(2,1)S(1)}, u32[]{:S(2)}, u32[]{:S(2)}) %collective-permute-start.3) | collective-permute-done | bytes 49184 | tf_op jit(solution)/shard_map/ppermute | solution.py:505
  27.7 12.8 %forward.1 = (f32[768,1408]{1,0:T(8,128)}, f32[16,128]{1,0:T(8,128)}) custom-call(bf16[3,192,128]{2,1,0:T(8,128)(2,1)} %copy-done.3, bf16[3,192,128]{2,1,0:T(8,128)(2,1)} %copy-done.2, bf16[192,128]{1,0:T(8,128)(2,1)} %strip.1.own_ref, bf16[192,128]{1,0:T(8,128)(2,1)} %copy-done.7, bf16[192,128]{1,0:T(8,128)(2,1)} %copy-done.8, f32[1,192]{1,0:T(1,128)} %bitcast.76, ...), custom_call_target="tpu_custom_call" | custom-call | flops 200000000 | bytes 12000000 | tf_op jit(solution)/shard_map/forward/pallas_call | solution.py:515
  40.7 1.3 collective-permute-done.4
  42.0 0.7 add.31
  43.4 7.7 %all-to-all-start = ((f32[16,16,128]{2,1,0:T(8,128)}), f32[16,16,128]{2,1,0:T(8,128)S(1)}, u32[]{:S(2)}, u32[]{:S(2)}) async-start(f32[16,16,128]{2,1,0:T(8,128)} %broadcast_in_dim.208), calls=%async_computation | async-start | bytes 262144 | tf_op jit(solution)/shard_map/all_to_all | solution.py:450
  51.7 6.0 %all-to-all-done.parts_ref = f32[16,16,128]{2,1,0:T(8,128)S(1)} async-done(((f32[16,16,128]{2,1,0:T(8,128)}), f32[16,16,128]{2,1,0:T(8,128)S(1)}, u32[]{:S(2)}, u32[]{:S(2)}) %all-to-all-start) | async-done | bytes 131104 | tf_op jit(solution)/shard_map/all_to_all | solution.py:450
  58.4 21.3 %backward.1 = (bf16[8,192,128]{2,1,0:T(8,128)(2,1)}, bf16[8,192,128]{2,1,0:T(8,128)(2,1)}, f32[1280,128]{1,0:T(8,128)}, f32[1280,128]{1,0:T(8,128)}, f32[16,128]{1,0:T(8,128)}) custom-call(s32[1]{0:T(128)} %bitcast.core_ref, f32[16,16,128]{2,1,0:T(8,128)} %copy-done.4, f32[48,768]{1,0:T(8,128)} %bitcast.60, f32[48,768]{1,0:T(8,128)} %wexc_ref.1, ...), custom_call_target="tpu_custom_call" | custom-call | flops 1500000000 | bytes 16000000 | tf_op jit(solution)/shard_map/backward/pallas_call | solution.py:538
  79.7 1.7 %collective-permute-start.5 = (f32[1280,128]{1,0:T(8,128)}, f32[1280,128]{1,0:T(8,128)S(1)}, u32[]{:S(2)}, u32[]{:S(2)}) collective-permute-start(f32[1280,128]{1,0:T(8,128)} %get-tuple-element.32), channel_id=1, source_target_pairs={{0,1},{1,0},{2,3},{3,2},{4,5},{5,4},{6,7},{7,6},{8,9},{9,8},{10,11... | collective-permute-start | bytes 1966088 | tf_op jit(solution)/shard_map/ppermute | solution.py:458
  81.6 1.7 %collective-permute-done.5 = f32[1280,128]{1,0:T(8,128)S(1)} collective-permute-done((f32[1280,128]{1,0:T(8,128)}, f32[1280,128]{1,0:T(8,128)S(1)}, u32[]{:S(2)}, u32[]{:S(2)}) %collective-permute-start.5) | collective-permute-done | bytes 655392 | tf_op jit(solution)/shard_map/ppermute | solution.py:458
  83.3 2.3 %select_reduce_fusion.2 = (f32[1280]{0:T(1024)S(1)}, f32[1280]{0:T(1024)S(1)}, f32[1280,128]{1,0:T(8,128)S(1)}) fusion(pred[1280]{0:T(1024)(128)(4,1)S(1)} %broadcast_in_dim.214, pred[1280]{0:T(1024)(128)(4,1)S(1)} %broadcast_in_dim.219, f32[1280,128]{1,0:T(8,128)} %get-tuple-element.31, f32[1280,128]{1,0:T(8,128)S(1)} %collective-permute-done.5), kind=kLoop, calls=%fused_computation.6 | loop fusion | flops 980480 | bytes 1978880 | tf_op jit(solution)/shard_map/reduce_max | solution.py:416
  86.7 11.6 %all_to_all.15 = f16[16,80,128]{2,1,0:T(8,128)(2,1)S(1)} all-to-all(f16[16,80,128]{2,1,0:T(8,128)(2,1)S(1)} %select_convert_fusion), channel_id=1, replica_groups={{0,2,4,6,8,10,12,14,16,18,20,22,24,26,28,30},{1,3,5,7,9,11,13,15,17,19,..., dimensions={0} | all-to-all | bytes 655360 | tf_op jit(solution)/shard_map/all_to_all | solution.py:450
  98.7 1.7 %collective-permute-start.6 = (f32[96,128]{1,0:T(8,128)S(1)}, f32[96,128]{1,0:T(8,128)S(1)}, u32[]{:S(2)}, u32[]{:S(2)}) collective-permute-start(f32[96,128]{1,0:T(8,128)S(1)} %pad_maximum_fusion.5), channel_id=1, source_target_pairs={{0,32},{32,0},{64,96},{96,64},{128,160},{160,128},{192,224},{224,1... | collective-permute-start | bytes 147464 | tf_op jit(solution)/shard_map/ppermute | solution.py:580
  100.4 1.5 %collective-permute-done.6 = f32[96,128]{1,0:T(8,128)S(1)} collective-permute-done((f32[96,128]{1,0:T(8,128)S(1)}, f32[96,128]{1,0:T(8,128)S(1)}, u32[]{:S(2)}, u32[]{:S(2)}) %collective-permute-start.6) | collective-permute-done | bytes 49184 | tf_op jit(solution)/shard_map/ppermute | solution.py:580
  101.9 3.1 %collective-permute-start.7 = (f32[112,128]{1,0:T(8,128)S(1)}, f32[112,128]{1,0:T(8,128)S(1)}, u32[]{:S(2)}, u32[]{:S(2)}) collective-permute-start(f32[112,128]{1,0:T(8,128)S(1)} %pad_maximum_fusion.4), channel_id=1, source_target_pairs={{0,64},{32,96},{64,0},{96,32},{128,192},{160,224},{192,128},{224,1... | collective-permute-start | bytes 172040 | tf_op jit(solution)/shard_map/ppermute | solution.py:580
  105.0 1.6 %collective-permute-done.7 = f32[112,128]{1,0:T(8,128)S(1)} collective-permute-done((f32[112,128]{1,0:T(8,128)S(1)}, f32[112,128]{1,0:T(8,128)S(1)}, u32[]{:S(2)}, u32[]{:S(2)}) %collective-permute-start.7) | collective-permute-done | bytes 57376 | tf_op jit(solution)/shard_map/ppermute | solution.py:580
  106.6 6.8 %collective-permute-start.8 = (f32[144,128]{1,0:T(8,128)S(1)}, f32[144,128]{1,0:T(8,128)S(1)}, u32[]{:S(2)}, u32[]{:S(2)}) collective-permute-start(f32[144,128]{1,0:T(8,128)S(1)} %pad_maximum_fusion.3), channel_id=1, source_target_pairs={{0,128},{32,160},{64,192},{96,224},{128,0},{160,32},{192,64},{224,... | collective-permute-start | bytes 221192 | tf_op jit(solution)/shard_map/ppermute | solution.py:580
  113.4 1.0 copy.24
  114.4 1.0 copy.25
  118.1 0.8 broadcast_in_dim.242
  118.9 3.5 %all-to-all-start.2 = ((f16[16,80,128]{2,1,0:T(8,128)(2,1)}), f16[16,80,128]{2,1,0:T(8,128)(2,1)S(1)}, u32[]{:S(2)}, u32[]{:S(2)}) async-start(f16[16,80,128]{2,1,0:T(8,128)(2,1)} %broadcast_in_dim.242), calls=%async_computation.2 | async-start | bytes 655360 | tf_op jit(solution)/shard_map/all_to_all | solution.py:450
  122.5 7.6 %all-to-all-done.2 = f16[16,80,128]{2,1,0:T(8,128)(2,1)S(1)} async-done(((f16[16,80,128]{2,1,0:T(8,128)(2,1)}), f16[16,80,128]{2,1,0:T(8,128)(2,1)S(1)}, u32[]{:S(2)}, u32[]{:S(2)}) %all-to-all-start.2) | async-done | bytes 327712 | tf_op jit(solution)/shard_map/all_to_all | solution.py:450
  130.1 6.1 %collective-permute-start.9 = (f16[16,80,128]{2,1,0:T(8,128)(2,1)S(1)}, f16[16,80,128]{2,1,0:T(8,128)(2,1)S(1)}, u32[]{:S(2)}, u32[]{:S(2)}) collective-permute-start(f16[16,80,128]{2,1,0:T(8,128)(2,1)S(1)} %all-to-all-done.2), channel_id=1, source_target_pairs={{0,1},{1,0},{2,3},{3,2},{4,5},{5,4},{6,7},{7,6},{8,9},{9,8},{10,11... | collective-permute-start | bytes 983048 | tf_op jit(solution)/shard_map/ppermute | solution.py:458
  136.2 1.0 fusion.3
  137.2 1.0 fusion.1
  138.9 1.1 slice_bitcast_fusion
  (83 shorter events, 8.3 us)
Async XLA Ops:
  1.9 6.0 %copy-start = (bf16[8,192,128]{2,1,0:T(8,128)(2,1)}, bf16[8,192,128]{2,1,0:T(8,128)(2,1)S(1)}, u32[]{:S(2)}) copy-start(bf16[8,192,128]{2,1,0:T(8,128)(2,1)S(1)} %get-tuple-element.80.x_ref) | copy-start | bytes 1179652
  1.9 6.0 %copy-start.1 = (bf16[8,192,128]{2,1,0:T(8,128)(2,1)}, bf16[8,192,128]{2,1,0:T(8,128)(2,1)S(1)}, u32[]{:S(2)}) copy-start(bf16[8,192,128]{2,1,0:T(8,128)(2,1)S(1)} %get-tuple-element.79.c_ref) | copy-start | bytes 1179652
  2.0 12.5 %collective-permute-start.1 = (bf16[3,192,128]{2,1,0:T(8,128)(2,1)S(1)}, bf16[3,192,128]{2,1,0:T(8,128)(2,1)S(1)}, u32[]{:S(2)}, u32[]{:S(2)}) collective-permute-start(bf16[3,192,128]{2,1,0:T(8,128)(2,1)S(1)} %pad_maximum_fusion.2), channel_id=1, source_target_pairs={{4,0},{8,4},{12,8},{16,12},{20,16},{24,20},{28,24},{5,1},{9,5},{13... | collective-permute-start | bytes 442376 | tf_op jit(solution)/shard_map/ppermute | solution.py:471
  3.3 11.2 %collective-permute-start = (bf16[3,192,128]{2,1,0:T(8,128)(2,1)S(1)}, bf16[3,192,128]{2,1,0:T(8,128)(2,1)S(1)}, u32[]{:S(2)}, u32[]{:S(2)}) collective-permute-start(bf16[3,192,128]{2,1,0:T(8,128)(2,1)S(1)} %pad_maximum_fusion.1), channel_id=1, source_target_pairs={{0,4},{4,8},{8,12},{12,16},{16,20},{20,24},{24,28},{1,5},{5,9},{9,... | collective-permute-start | bytes 442376 | tf_op jit(solution)/shard_map/ppermute | solution.py:470
  14.5 0.7 copy-start.2
  14.5 0.7 copy-start.3
  16.9 6.5 %collective-permute-start.2 = (bf16[192,128]{1,0:T(8,128)(2,1)}, bf16[192,128]{1,0:T(8,128)(2,1)S(1)}, u32[]{:S(2)}, u32[]{:S(2)}) collective-permute-start(bf16[192,128]{1,0:T(8,128)(2,1)} %strip.1.own_ref), channel_id=1, source_target_pairs={{0,1},{1,2},{2,3},{4,5},{5,6},{6,7},{8,9},{9,10},{10,11},{12,13},{... | collective-permute-start | bytes 147464 | tf_op jit(solution)/shard_map/ppermute | solution.py:504
  21.5 5.6 %collective-permute-start.3 = (bf16[192,128]{1,0:T(8,128)(2,1)}, bf16[192,128]{1,0:T(8,128)(2,1)S(1)}, u32[]{:S(2)}, u32[]{:S(2)}) collective-permute-start(bf16[192,128]{1,0:T(8,128)(2,1)} %strip.1.own_ref), channel_id=1, source_target_pairs={{1,0},{2,1},{3,2},{5,4},{6,5},{7,6},{9,8},{10,9},{11,10},{13,12},{... | collective-permute-start | bytes 147464 | tf_op jit(solution)/shard_map/ppermute | solution.py:505
  23.5 3.7 %copy-start.7 = (bf16[192,128]{1,0:T(8,128)(2,1)}, bf16[192,128]{1,0:T(8,128)(2,1)S(1)}, u32[]{:S(2)}) copy-start(bf16[192,128]{1,0:T(8,128)(2,1)S(1)} %collective-permute-done.2.left_ref) | copy-start | bytes 147460
  27.1 0.6 copy-start.8
  40.5 1.5 %collective-permute-start.4 = (f32[16,128]{1,0:T(8,128)}, f32[16,128]{1,0:T(8,128)S(1)}, u32[]{:S(2)}, u32[]{:S(2)}) collective-permute-start(f32[16,128]{1,0:T(8,128)} %get-tuple-element.24), channel_id=1, source_target_pairs={{0,1},{1,0},{2,3},{3,2},{4,5},{5,4},{6,7},{7,6},{8,9},{9,8},{10,11... | collective-permute-start | bytes 24584 | tf_op jit(solution)/shard_map/ppermute | solution.py:458
  43.4 14.4 %all-to-all-start = ((f32[16,16,128]{2,1,0:T(8,128)}), f32[16,16,128]{2,1,0:T(8,128)S(1)}, u32[]{:S(2)}, u32[]{:S(2)}) async-start(f32[16,16,128]{2,1,0:T(8,128)} %broadcast_in_dim.208), calls=%async_computation | async-start | bytes 262144 | tf_op jit(solution)/shard_map/all_to_all | solution.py:450
  57.8 0.7 copy-start.4
  79.7 3.6 %collective-permute-start.5 = (f32[1280,128]{1,0:T(8,128)}, f32[1280,128]{1,0:T(8,128)S(1)}, u32[]{:S(2)}, u32[]{:S(2)}) collective-permute-start(f32[1280,128]{1,0:T(8,128)} %get-tuple-element.32), channel_id=1, source_target_pairs={{0,1},{1,0},{2,3},{3,2},{4,5},{5,4},{6,7},{7,6},{8,9},{9,8},{10,11... | collective-permute-start | bytes 1966088 | tf_op jit(solution)/shard_map/ppermute | solution.py:458
  86.3 12.4 %copy-start.9 = (f32[16,128]{1,0:T(8,128)S(1)}, f32[16,128]{1,0:T(8,128)}, u32[]{:S(2)}) copy-start(f32[16,128]{1,0:T(8,128)} %get-tuple-element.33) | copy-start | bytes 24580
  86.7 26.7 %copy-start.6 = (bf16[8,192,128]{2,1,0:T(8,128)(2,1)S(1)}, bf16[8,192,128]{2,1,0:T(8,128)(2,1)}, u32[]{:S(2)}) copy-start(bf16[8,192,128]{2,1,0:T(8,128)(2,1)} %get-tuple-element.29) | copy-start | bytes 1179652
  98.3 16.2 %copy-start.5 = (bf16[8,192,128]{2,1,0:T(8,128)(2,1)S(1)}, bf16[8,192,128]{2,1,0:T(8,128)(2,1)}, u32[]{:S(2)}) copy-start(bf16[8,192,128]{2,1,0:T(8,128)(2,1)} %get-tuple-element.30) | copy-start | bytes 1179652
  98.7 3.2 %collective-permute-start.6 = (f32[96,128]{1,0:T(8,128)S(1)}, f32[96,128]{1,0:T(8,128)S(1)}, u32[]{:S(2)}, u32[]{:S(2)}) collective-permute-start(f32[96,128]{1,0:T(8,128)S(1)} %pad_maximum_fusion.5), channel_id=1, source_target_pairs={{0,32},{32,0},{64,96},{96,64},{128,160},{160,128},{192,224},{224,1... | collective-permute-start | bytes 147464 | tf_op jit(solution)/shard_map/ppermute | solution.py:580
  101.9 4.6 %collective-permute-start.7 = (f32[112,128]{1,0:T(8,128)S(1)}, f32[112,128]{1,0:T(8,128)S(1)}, u32[]{:S(2)}, u32[]{:S(2)}) collective-permute-start(f32[112,128]{1,0:T(8,128)S(1)} %pad_maximum_fusion.4), channel_id=1, source_target_pairs={{0,64},{32,96},{64,0},{96,32},{128,192},{160,224},{192,128},{224,1... | collective-permute-start | bytes 172040 | tf_op jit(solution)/shard_map/ppermute | solution.py:580
  106.6 9.2 %collective-permute-start.8 = (f32[144,128]{1,0:T(8,128)S(1)}, f32[144,128]{1,0:T(8,128)S(1)}, u32[]{:S(2)}, u32[]{:S(2)}) collective-permute-start(f32[144,128]{1,0:T(8,128)S(1)} %pad_maximum_fusion.3), channel_id=1, source_target_pairs={{0,128},{32,160},{64,192},{96,224},{128,0},{160,32},{192,64},{224,... | collective-permute-start | bytes 221192 | tf_op jit(solution)/shard_map/ppermute | solution.py:580
  118.9 11.2 %all-to-all-start.2 = ((f16[16,80,128]{2,1,0:T(8,128)(2,1)}), f16[16,80,128]{2,1,0:T(8,128)(2,1)S(1)}, u32[]{:S(2)}, u32[]{:S(2)}) async-start(f16[16,80,128]{2,1,0:T(8,128)(2,1)} %broadcast_in_dim.242), calls=%async_computation.2 | async-start | bytes 655360 | tf_op jit(solution)/shard_map/all_to_all | solution.py:450
  130.1 8.1 %collective-permute-start.9 = (f16[16,80,128]{2,1,0:T(8,128)(2,1)S(1)}, f16[16,80,128]{2,1,0:T(8,128)(2,1)S(1)}, u32[]{:S(2)}, u32[]{:S(2)}) collective-permute-start(f16[16,80,128]{2,1,0:T(8,128)(2,1)S(1)} %all-to-all-done.2), channel_id=1, source_target_pairs={{0,1},{1,0},{2,3},{3,2},{4,5},{5,4},{6,7},{7,6},{8,9},{9,8},{10,11... | collective-permute-start | bytes 983048 | tf_op jit(solution)/shard_map/ppermute | solution.py:458

commit v10 on v9

--- a/solution.py
+++ b/solution.py
@@ -16,7 +16,7 @@
 STEPS = EX // EB
 BLOCKS = EX // LANES
 PARTS, PACK = 32, 80
-VMEM = 60 * 1024 * 1024
+VMEM_KIB = 60 * 1024
 CHIPS = [[2 * q + core for q in range(PARTS // 2)] for core in range(2)]
 XS = ROWS + 5
 CS = ROWS + 3
@@ -161,7 +161,7 @@
         hid_out[ds, :] = (v * (1.0 + jnp.tanh(v))).astype(BF16)
         return carry
 
-    lax.fori_loop(0, EB // SUB, body, 0)
+    lax.fori_loop(0, EB // SUB, body, 0, unroll=4)
 
 
 def forward_kernel(
@@ -234,7 +234,7 @@
         acc_s[1, ds, :] = gexc
         return carry
 
-    lax.fori_loop(0, EB // SUB, body, 0)
+    lax.fori_loop(0, EB // SUB, body, 0, unroll=8)
     for n in range(EB // LANES):
         for kind in range(2):
             row = jnp.sum(acc_s[kind, n * LANES : (n + 1) * LANES, :].T, axis=0, keepdims=True)
@@ -349,7 +349,7 @@
         acc_s[ds, :] = total
         return carry
 
-    lax.fori_loop(0, EB // SUB, body, 0)
+    lax.fori_loop(0, EB // SUB, body, 0, unroll=2)
     for n in range(EB // LANES):
         taps = acc_s[n * LANES : (n + 1) * LANES, :].T
         block = step * (EB // LANES) + n
@@ -436,9 +436,9 @@
     return pl.BlockSpec(dims, lambda j: (0,) * len(dims))
 
 
-def params(grid=True):
+def params(grid=True, kib=VMEM_KIB):
     return pltpu.CompilerParams(
-        dimension_semantics=("arbitrary",) if grid else None, vmem_limit_bytes=VMEM
+        dimension_semantics=("arbitrary",) if grid else None, vmem_limit_bytes=kib * 1024
     )
 
 
@@ -497,7 +497,7 @@
     own = pl.pallas_call(
         strip_kernel,
         out_shape=shape(CH, LANES, dtype=BF16),
-        compiler_params=params(False),
+        compiler_params=params(False, 4096),
         cost_estimate=cost(1e6, 1e6),
         name="strip",
     )(part, top, bot)

time: 142 us -> 135 us (0.951)
  Pallas kernels: 42.4 us -> 34.8 us
    pallas_call x1, Pallas kernels: 21.3 us -> 18.4 us  [local(): pl.pallas_call(backward_kernel, grid=(STEPS,), in_specs=[pl.BlockSpec(mem...]
    pallas_call x1, Pallas kernels: 12.8 us -> 10.1 us  [local(): pl.pallas_call(forward_kernel, grid=(STEPS,), in_specs=[halo, halo, edge,...]
    pallas_call x1, Pallas kernels: 1.77 us -> 0.14 us  [local(): pl.pallas_call(strip_kernel, out_shape=shape(CH, LANES, dtype=BF16), comp...]
    unnamed x22 -> x26, local copies, waits for them, and re-layouts: 3.99 us -> 4.16 us
where the time goes in v10:
time: 135 us; the launch traced here: 134 us
  starting transfers between devices  43.7 us (32%)
  Pallas kernels  34.8 us (26%)
  waiting for transfers between devices  23.4 us (17%)
  blocking collectives  11.6 us (9%)
  local copies, waits for them, and re-layouts  9.56 us (7%)
  other arithmetic  6.54 us (5%)
  between operations  2.59 us (2%)
  matrix products  1.98 us (1%)
    pallas_call x1, Pallas kernels, local(): pl.pallas_call(backward_kernel, grid=(STEPS,), in_specs=[pl.BlockSpec(mem...  18.4 us
    all_to_all x2, waiting for transfers between devices, exchanged(): return lax.all_to_all(blocks, RC, 0, 0, tiled=True, axis_index_groups=CHIPS)  13.6 us
    ppermute x3, starting transfers between devices, local(): lax.ppermute(jnp.concatenate([total, vecs.reshape(16 * bit, LANES)], axis...  11.8 us
    all_to_all x1, blocking collectives, exchanged(): return lax.all_to_all(blocks, RC, 0, 0, tiled=True, axis_index_groups=CHIPS)  11.6 us
    all_to_all x2, starting transfers between devices, exchanged(): return lax.all_to_all(blocks, RC, 0, 0, tiled=True, axis_index_groups=CHIPS)  11.5 us
    pallas_call x1, Pallas kernels, local(): pl.pallas_call(forward_kernel, grid=(STEPS,), in_specs=[halo, halo, edge,...  10.1 us
    ppermute x3, starting transfers between devices, partner(): return lax.ppermute(block, 'col', [(i, i ^ 1) for i in range(4)])  8.05 us
    pallas_call x1, Pallas kernels, local(): pl.pallas_call(expand_kernel, grid=(STEPS,), in_specs=[tile, tile, full(1...  6.19 us
  transfers between devices with their start and end apart: 12, of which 8 were waited for; matrix products, arithmetic and copies ran while one was open for 4% of the time, Pallas kernels for 5%

profile of v10, /device:TPU:1, one launch (start us, length us, event | category | flops | bytes accessed | tf_op | source)
XLA Modules:
  0.0 134.1 jit_solution(3740128555850951619)
XLA Ops:
  0.6 1.3 copy_bitcast_fusion
  2.0 1.3 collective-permute-start.1
  3.3 4.6 %collective-permute-start = (bf16[3,192,128]{2,1,0:T(8,128)(2,1)S(1)}, bf16[3,192,128]{2,1,0:T(8,128)(2,1)S(1)}, u32[]{:S(2)}, u32[]{:S(2)}) collective-permute-start(bf16[3,192,128]{2,1,0:T(8,128)(2,1)S(1)} %pad_maximum_fusion.1), channel_id=1, source_target_pairs={{0,4},{4,8},{8,12},{12,16},{16,20},{20,24},{24,28},{1,5},{5,9},{9,... | collective-permute-start | bytes 442376 | tf_op jit(solution)/shard_map/ppermute | solution.py:470
  7.9 6.2 %expand.1 = (bf16[192,1024]{1,0:T(8,128)(2,1)}, f32[8,128]{1,0:T(8,128)}, bf16[192,128]{1,0:T(8,128)(2,1)}, f32[768,1024]{1,0:T(8,128)}, bf16[768,1024]{1,0:T(8,128)(2,1)}, /*index=5*/f32[768,1024]{1,0:T(8,128)}) custom-call(bf16[8,192,128]{2,1,0:T(8,128)(2,1)} %copy-done.4, bf16[8,192,128]{2,1,0:T(8,128)(2,1)} %copy-done.5, f32[1,192]{1,0:T(1,128)} %bitcast.75, ...), custom_call_target="tpu_custom_call" | custom-call | flops 600000000 | bytes 10000000 | tf_op jit(solution)/shard_map/expand/pallas_call | solution.py:482
  14.2 0.8 copy-done.3
  15.2 4.6 %collective-permute-start.2 = (bf16[192,128]{1,0:T(8,128)(2,1)S(1)}, bf16[192,128]{1,0:T(8,128)(2,1)S(1)}, u32[]{:S(2)}, u32[]{:S(2)}) collective-permute-start(bf16[192,128]{1,0:T(8,128)(2,1)S(1)} %strip.1.own_ref), channel_id=1, source_target_pairs={{0,1},{1,2},{2,3},{4,5},{5,6},{6,7},{8,9},{9,10},{10,11},{12,13},{... | collective-permute-start | bytes 147464 | tf_op jit(solution)/shard_map/ppermute | solution.py:504
  19.8 1.9 %collective-permute-start.3 = (bf16[192,128]{1,0:T(8,128)(2,1)S(1)}, bf16[192,128]{1,0:T(8,128)(2,1)S(1)}, u32[]{:S(2)}, u32[]{:S(2)}) collective-permute-start(bf16[192,128]{1,0:T(8,128)(2,1)S(1)} %strip.1.own_ref), channel_id=1, source_target_pairs={{1,0},{2,1},{3,2},{5,4},{6,5},{7,6},{9,8},{10,9},{11,10},{13,12},{... | collective-permute-start | bytes 147464 | tf_op jit(solution)/shard_map/ppermute | solution.py:505
  21.7 3.4 %collective-permute-done.3.right_ref = bf16[192,128]{1,0:T(8,128)(2,1)S(1)} collective-permute-done((bf16[192,128]{1,0:T(8,128)(2,1)S(1)}, bf16[192,128]{1,0:T(8,128)(2,1)S(1)}, u32[]{:S(2)}, u32[]{:S(2)}) %collective-permute-start.3) | collective-permute-done | bytes 49184 | tf_op jit(solution)/shard_map/ppermute | solution.py:505
  25.8 10.1 %forward.1 = (f32[768,1408]{1,0:T(8,128)}, f32[16,128]{1,0:T(8,128)}) custom-call(bf16[3,192,128]{2,1,0:T(8,128)(2,1)} %copy-done.1, bf16[3,192,128]{2,1,0:T(8,128)(2,1)} %copy-done, bf16[192,128]{1,0:T(8,128)(2,1)} %copy-done.2, bf16[192,128]{1,0:T(8,128)(2,1)} %copy-done.9, bf16[192,128]{1,0:T(8,128)(2,1)} %copy-done.10, f32[1,192]{1,0:T(1,128)} %bitcast.76, ...), custom_call_target="tpu_custom_call" | custom-call | flops 200000000 | bytes 12000000 | tf_op jit(solution)/shard_map/forward/pallas_call | solution.py:515
  36.0 1.3 collective-permute-done.4
  37.4 0.7 add.31
  38.7 8.0 %all-to-all-start = ((f32[16,16,128]{2,1,0:T(8,128)}), f32[16,16,128]{2,1,0:T(8,128)S(1)}, u32[]{:S(2)}, u32[]{:S(2)}) async-start(f32[16,16,128]{2,1,0:T(8,128)} %broadcast_in_dim.208), calls=%async_computation | async-start | bytes 262144 | tf_op jit(solution)/shard_map/all_to_all | solution.py:450
  47.4 6.0 %all-to-all-done.parts_ref = f32[16,16,128]{2,1,0:T(8,128)S(1)} async-done(((f32[16,16,128]{2,1,0:T(8,128)}), f32[16,16,128]{2,1,0:T(8,128)S(1)}, u32[]{:S(2)}, u32[]{:S(2)}) %all-to-all-start) | async-done | bytes 131104 | tf_op jit(solution)/shard_map/all_to_all | solution.py:450
  54.1 18.4 %backward.1 = (bf16[8,192,128]{2,1,0:T(8,128)(2,1)}, bf16[8,192,128]{2,1,0:T(8,128)(2,1)}, f32[1280,128]{1,0:T(8,128)}, f32[1280,128]{1,0:T(8,128)}, f32[16,128]{1,0:T(8,128)}) custom-call(s32[1]{0:T(128)} %bitcast.core_ref, f32[16,16,128]{2,1,0:T(8,128)} %copy-done.6, f32[48,768]{1,0:T(8,128)} %bitcast.60, f32[48,768]{1,0:T(8,128)} %wexc_ref.1, ...), custom_call_target="tpu_custom_call" | custom-call | flops 1500000000 | bytes 16000000 | tf_op jit(solution)/shard_map/backward/pallas_call | solution.py:538
  72.4 1.7 %collective-permute-start.5 = (f32[1280,128]{1,0:T(8,128)}, f32[1280,128]{1,0:T(8,128)S(1)}, u32[]{:S(2)}, u32[]{:S(2)}) collective-permute-start(f32[1280,128]{1,0:T(8,128)} %get-tuple-element.32), channel_id=1, source_target_pairs={{0,1},{1,0},{2,3},{3,2},{4,5},{5,4},{6,7},{7,6},{8,9},{9,8},{10,11... | collective-permute-start | bytes 1966088 | tf_op jit(solution)/shard_map/ppermute | solution.py:458
  74.3 1.7 %collective-permute-done.5 = f32[1280,128]{1,0:T(8,128)S(1)} collective-permute-done((f32[1280,128]{1,0:T(8,128)}, f32[1280,128]{1,0:T(8,128)S(1)}, u32[]{:S(2)}, u32[]{:S(2)}) %collective-permute-start.5) | collective-permute-done | bytes 655392 | tf_op jit(solution)/shard_map/ppermute | solution.py:458
  76.0 2.3 %select_reduce_fusion.2 = (f32[1280]{0:T(1024)S(1)}, f32[1280]{0:T(1024)S(1)}, f32[1280,128]{1,0:T(8,128)S(1)}) fusion(pred[1280]{0:T(1024)(128)(4,1)S(1)} %broadcast_in_dim.214, pred[1280]{0:T(1024)(128)(4,1)S(1)} %broadcast_in_dim.219, f32[1280,128]{1,0:T(8,128)} %get-tuple-element.31, f32[1280,128]{1,0:T(8,128)S(1)} %collective-permute-done.5), kind=kLoop, calls=%fused_computation.6 | loop fusion | flops 980480 | bytes 1978880 | tf_op jit(solution)/shard_map/reduce_max | solution.py:416
  79.4 11.6 %all_to_all.15 = f16[16,80,128]{2,1,0:T(8,128)(2,1)S(1)} all-to-all(f16[16,80,128]{2,1,0:T(8,128)(2,1)S(1)} %select_convert_fusion), channel_id=1, replica_groups={{0,2,4,6,8,10,12,14,16,18,20,22,24,26,28,30},{1,3,5,7,9,11,13,15,17,19,..., dimensions={0} | all-to-all | bytes 655360 | tf_op jit(solution)/shard_map/all_to_all | solution.py:450
  91.4 1.7 %collective-permute-start.6 = (f32[96,128]{1,0:T(8,128)S(1)}, f32[96,128]{1,0:T(8,128)S(1)}, u32[]{:S(2)}, u32[]{:S(2)}) collective-permute-start(f32[96,128]{1,0:T(8,128)S(1)} %pad_maximum_fusion.5), channel_id=1, source_target_pairs={{0,32},{32,0},{64,96},{96,64},{128,160},{160,128},{192,224},{224,1... | collective-permute-start | bytes 147464 | tf_op jit(solution)/shard_map/ppermute | solution.py:580
  93.1 1.5 %collective-permute-done.6 = f32[96,128]{1,0:T(8,128)S(1)} collective-permute-done((f32[96,128]{1,0:T(8,128)S(1)}, f32[96,128]{1,0:T(8,128)S(1)}, u32[]{:S(2)}, u32[]{:S(2)}) %collective-permute-start.6) | collective-permute-done | bytes 49184 | tf_op jit(solution)/shard_map/ppermute | solution.py:580
  94.6 3.1 %collective-permute-start.7 = (f32[112,128]{1,0:T(8,128)S(1)}, f32[112,128]{1,0:T(8,128)S(1)}, u32[]{:S(2)}, u32[]{:S(2)}) collective-permute-start(f32[112,128]{1,0:T(8,128)S(1)} %pad_maximum_fusion.4), channel_id=1, source_target_pairs={{0,64},{32,96},{64,0},{96,32},{128,192},{160,224},{192,128},{224,1... | collective-permute-start | bytes 172040 | tf_op jit(solution)/shard_map/ppermute | solution.py:580
  97.7 1.6 %collective-permute-done.7 = f32[112,128]{1,0:T(8,128)S(1)} collective-permute-done((f32[112,128]{1,0:T(8,128)S(1)}, f32[112,128]{1,0:T(8,128)S(1)}, u32[]{:S(2)}, u32[]{:S(2)}) %collective-permute-start.7) | collective-permute-done | bytes 57376 | tf_op jit(solution)/shard_map/ppermute | solution.py:580
  99.3 7.0 %collective-permute-start.8 = (f32[144,128]{1,0:T(8,128)S(1)}, f32[144,128]{1,0:T(8,128)S(1)}, u32[]{:S(2)}, u32[]{:S(2)}) collective-permute-start(f32[144,128]{1,0:T(8,128)S(1)} %pad_maximum_fusion.3), channel_id=1, source_target_pairs={{0,128},{32,160},{64,192},{96,224},{128,0},{160,32},{192,64},{224,... | collective-permute-start | bytes 221192 | tf_op jit(solution)/shard_map/ppermute | solution.py:580
  106.3 1.0 copy.24
  107.3 1.0 copy.25
  110.8 0.8 broadcast_in_dim.242
  111.6 3.5 %all-to-all-start.2 = ((f16[16,80,128]{2,1,0:T(8,128)(2,1)}), f16[16,80,128]{2,1,0:T(8,128)(2,1)S(1)}, u32[]{:S(2)}, u32[]{:S(2)}) async-start(f16[16,80,128]{2,1,0:T(8,128)(2,1)} %broadcast_in_dim.242), calls=%async_computation.2 | async-start | bytes 655360 | tf_op jit(solution)/shard_map/all_to_all | solution.py:450
  115.2 7.6 %all-to-all-done.2 = f16[16,80,128]{2,1,0:T(8,128)(2,1)S(1)} async-done(((f16[16,80,128]{2,1,0:T(8,128)(2,1)}), f16[16,80,128]{2,1,0:T(8,128)(2,1)S(1)}, u32[]{:S(2)}, u32[]{:S(2)}) %all-to-all-start.2) | async-done | bytes 327712 | tf_op jit(solution)/shard_map/all_to_all | solution.py:450
  122.8 6.3 %collective-permute-start.9 = (f16[16,80,128]{2,1,0:T(8,128)(2,1)S(1)}, f16[16,80,128]{2,1,0:T(8,128)(2,1)S(1)}, u32[]{:S(2)}, u32[]{:S(2)}) collective-permute-start(f16[16,80,128]{2,1,0:T(8,128)(2,1)S(1)} %all-to-all-done.2), channel_id=1, source_target_pairs={{0,1},{1,0},{2,3},{3,2},{4,5},{5,4},{6,7},{7,6},{8,9},{9,8},{10,11... | collective-permute-start | bytes 983048 | tf_op jit(solution)/shard_map/ppermute | solution.py:458
  129.1 1.0 fusion.3
  130.1 1.0 fusion.1
  131.8 1.1 slice_bitcast_fusion
  (87 shorter events, 7.5 us)
Async XLA Ops:
  1.9 6.0 %copy-start.4 = (bf16[8,192,128]{2,1,0:T(8,128)(2,1)}, bf16[8,192,128]{2,1,0:T(8,128)(2,1)S(1)}, u32[]{:S(2)}) copy-start(bf16[8,192,128]{2,1,0:T(8,128)(2,1)S(1)} %get-tuple-element.80.x_ref) | copy-start | bytes 1179652
  1.9 6.0 %copy-start.5 = (bf16[8,192,128]{2,1,0:T(8,128)(2,1)}, bf16[8,192,128]{2,1,0:T(8,128)(2,1)S(1)}, u32[]{:S(2)}) copy-start(bf16[8,192,128]{2,1,0:T(8,128)(2,1)S(1)} %get-tuple-element.79.c_ref) | copy-start | bytes 1179652
  2.0 12.1 %collective-permute-start.1 = (bf16[3,192,128]{2,1,0:T(8,128)(2,1)S(1)}, bf16[3,192,128]{2,1,0:T(8,128)(2,1)S(1)}, u32[]{:S(2)}, u32[]{:S(2)}) collective-permute-start(bf16[3,192,128]{2,1,0:T(8,128)(2,1)S(1)} %pad_maximum_fusion.2), channel_id=1, source_target_pairs={{4,0},{8,4},{12,8},{16,12},{20,16},{24,20},{28,24},{5,1},{9,5},{13... | collective-permute-start | bytes 442376 | tf_op jit(solution)/shard_map/ppermute | solution.py:471
  3.3 10.8 %collective-permute-start = (bf16[3,192,128]{2,1,0:T(8,128)(2,1)S(1)}, bf16[3,192,128]{2,1,0:T(8,128)(2,1)S(1)}, u32[]{:S(2)}, u32[]{:S(2)}) collective-permute-start(bf16[3,192,128]{2,1,0:T(8,128)(2,1)S(1)} %pad_maximum_fusion.1), channel_id=1, source_target_pairs={{0,4},{4,8},{8,12},{12,16},{16,20},{20,24},{24,28},{1,5},{5,9},{9,... | collective-permute-start | bytes 442376 | tf_op jit(solution)/shard_map/ppermute | solution.py:470
  14.1 11.0 %copy-start = (bf16[3,192,128]{2,1,0:T(8,128)(2,1)}, bf16[3,192,128]{2,1,0:T(8,128)(2,1)S(1)}, u32[]{:S(2)}) copy-start(bf16[3,192,128]{2,1,0:T(8,128)(2,1)S(1)} %collective-permute-done.1.bot_ref) | copy-start | bytes 442372
  14.2 11.0 %copy-start.1 = (bf16[3,192,128]{2,1,0:T(8,128)(2,1)}, bf16[3,192,128]{2,1,0:T(8,128)(2,1)S(1)}, u32[]{:S(2)}) copy-start(bf16[3,192,128]{2,1,0:T(8,128)(2,1)S(1)} %collective-permute-done.top_ref) | copy-start | bytes 442372
  14.2 0.9 copy-start.3
  15.2 10.0 %copy-start.2 = (bf16[192,128]{1,0:T(8,128)(2,1)}, bf16[192,128]{1,0:T(8,128)(2,1)S(1)}, u32[]{:S(2)}) copy-start(bf16[192,128]{1,0:T(8,128)(2,1)S(1)} %strip.1.own_ref) | copy-start | bytes 147460
  15.2 6.5 %collective-permute-start.2 = (bf16[192,128]{1,0:T(8,128)(2,1)S(1)}, bf16[192,128]{1,0:T(8,128)(2,1)S(1)}, u32[]{:S(2)}, u32[]{:S(2)}) collective-permute-start(bf16[192,128]{1,0:T(8,128)(2,1)S(1)} %strip.1.own_ref), channel_id=1, source_target_pairs={{0,1},{1,2},{2,3},{4,5},{5,6},{6,7},{8,9},{9,10},{10,11},{12,13},{... | collective-permute-start | bytes 147464 | tf_op jit(solution)/shard_map/ppermute | solution.py:504
  19.8 5.4 %collective-permute-start.3 = (bf16[192,128]{1,0:T(8,128)(2,1)S(1)}, bf16[192,128]{1,0:T(8,128)(2,1)S(1)}, u32[]{:S(2)}, u32[]{:S(2)}) collective-permute-start(bf16[192,128]{1,0:T(8,128)(2,1)S(1)} %strip.1.own_ref), channel_id=1, source_target_pairs={{1,0},{2,1},{3,2},{5,4},{6,5},{7,6},{9,8},{10,9},{11,10},{13,12},{... | collective-permute-start | bytes 147464 | tf_op jit(solution)/shard_map/ppermute | solution.py:505
  21.7 3.5 %copy-start.9 = (bf16[192,128]{1,0:T(8,128)(2,1)}, bf16[192,128]{1,0:T(8,128)(2,1)S(1)}, u32[]{:S(2)}) copy-start(bf16[192,128]{1,0:T(8,128)(2,1)S(1)} %collective-permute-done.2.left_ref) | copy-start | bytes 147460
  25.2 0.6 copy-start.10
  35.9 1.5 %collective-permute-start.4 = (f32[16,128]{1,0:T(8,128)}, f32[16,128]{1,0:T(8,128)S(1)}, u32[]{:S(2)}, u32[]{:S(2)}) collective-permute-start(f32[16,128]{1,0:T(8,128)} %get-tuple-element.24), channel_id=1, source_target_pairs={{0,1},{1,0},{2,3},{3,2},{4,5},{5,4},{6,7},{7,6},{8,9},{9,8},{10,11... | collective-permute-start | bytes 24584 | tf_op jit(solution)/shard_map/ppermute | solution.py:458
  38.7 14.7 %all-to-all-start = ((f32[16,16,128]{2,1,0:T(8,128)}), f32[16,16,128]{2,1,0:T(8,128)S(1)}, u32[]{:S(2)}, u32[]{:S(2)}) async-start(f32[16,16,128]{2,1,0:T(8,128)} %broadcast_in_dim.208), calls=%async_computation | async-start | bytes 262144 | tf_op jit(solution)/shard_map/all_to_all | solution.py:450
  53.4 0.7 copy-start.6
  72.4 3.6 %collective-permute-start.5 = (f32[1280,128]{1,0:T(8,128)}, f32[1280,128]{1,0:T(8,128)S(1)}, u32[]{:S(2)}, u32[]{:S(2)}) collective-permute-start(f32[1280,128]{1,0:T(8,128)} %get-tuple-element.32), channel_id=1, source_target_pairs={{0,1},{1,0},{2,3},{3,2},{4,5},{5,4},{6,7},{7,6},{8,9},{9,8},{10,11... | collective-permute-start | bytes 1966088 | tf_op jit(solution)/shard_map/ppermute | solution.py:458
  78.9 12.4 %copy-start.11 = (f32[16,128]{1,0:T(8,128)S(1)}, f32[16,128]{1,0:T(8,128)}, u32[]{:S(2)}) copy-start(f32[16,128]{1,0:T(8,128)} %get-tuple-element.33) | copy-start | bytes 24580
  79.4 26.9 %copy-start.8 = (bf16[8,192,128]{2,1,0:T(8,128)(2,1)S(1)}, bf16[8,192,128]{2,1,0:T(8,128)(2,1)}, u32[]{:S(2)}) copy-start(bf16[8,192,128]{2,1,0:T(8,128)(2,1)} %get-tuple-element.29) | copy-start | bytes 1179652
  91.0 16.3 %copy-start.7 = (bf16[8,192,128]{2,1,0:T(8,128)(2,1)S(1)}, bf16[8,192,128]{2,1,0:T(8,128)(2,1)}, u32[]{:S(2)}) copy-start(bf16[8,192,128]{2,1,0:T(8,128)(2,1)} %get-tuple-element.30) | copy-start | bytes 1179652
  91.4 3.2 %collective-permute-start.6 = (f32[96,128]{1,0:T(8,128)S(1)}, f32[96,128]{1,0:T(8,128)S(1)}, u32[]{:S(2)}, u32[]{:S(2)}) collective-permute-start(f32[96,128]{1,0:T(8,128)S(1)} %pad_maximum_fusion.5), channel_id=1, source_target_pairs={{0,32},{32,0},{64,96},{96,64},{128,160},{160,128},{192,224},{224,1... | collective-permute-start | bytes 147464 | tf_op jit(solution)/shard_map/ppermute | solution.py:580
  94.6 4.6 %collective-permute-start.7 = (f32[112,128]{1,0:T(8,128)S(1)}, f32[112,128]{1,0:T(8,128)S(1)}, u32[]{:S(2)}, u32[]{:S(2)}) collective-permute-start(f32[112,128]{1,0:T(8,128)S(1)} %pad_maximum_fusion.4), channel_id=1, source_target_pairs={{0,64},{32,96},{64,0},{96,32},{128,192},{160,224},{192,128},{224,1... | collective-permute-start | bytes 172040 | tf_op jit(solution)/shard_map/ppermute | solution.py:580
  99.3 9.2 %collective-permute-start.8 = (f32[144,128]{1,0:T(8,128)S(1)}, f32[144,128]{1,0:T(8,128)S(1)}, u32[]{:S(2)}, u32[]{:S(2)}) collective-permute-start(f32[144,128]{1,0:T(8,128)S(1)} %pad_maximum_fusion.3), channel_id=1, source_target_pairs={{0,128},{32,160},{64,192},{96,224},{128,0},{160,32},{192,64},{224,... | collective-permute-start | bytes 221192 | tf_op jit(solution)/shard_map/ppermute | solution.py:580
  111.6 11.2 %all-to-all-start.2 = ((f16[16,80,128]{2,1,0:T(8,128)(2,1)}), f16[16,80,128]{2,1,0:T(8,128)(2,1)S(1)}, u32[]{:S(2)}, u32[]{:S(2)}) async-start(f16[16,80,128]{2,1,0:T(8,128)(2,1)} %broadcast_in_dim.242), calls=%async_computation.2 | async-start | bytes 655360 | tf_op jit(solution)/shard_map/all_to_all | solution.py:450
  122.8 8.3 %collective-permute-start.9 = (f16[16,80,128]{2,1,0:T(8,128)(2,1)S(1)}, f16[16,80,128]{2,1,0:T(8,128)(2,1)S(1)}, u32[]{:S(2)}, u32[]{:S(2)}) collective-permute-start(f16[16,80,128]{2,1,0:T(8,128)(2,1)S(1)} %all-to-all-done.2), channel_id=1, source_target_pairs={{0,1},{1,0},{2,3},{3,2},{4,5},{5,4},{6,7},{7,6},{8,9},{9,8},{10,11... | collective-permute-start | bytes 983048 | tf_op jit(solution)/shard_map/ppermute | solution.py:458

commit v11 on v10

--- a/solution.py
+++ b/solution.py
@@ -380,11 +380,17 @@
         tsum_s[54:55, :] = sums[:, :LANES]
         tsum_s[55:56, :] = jnp.zeros((1, LANES), F32)
         tsum_s[55:56, : CH - LANES] = sums[:, LANES:]
+        spare = lax.broadcasted_iota(jnp.int32, (8, LANES), 0)
         for d in range(PARTS):
-            rows = slice((d % 2 * PARTS // 2 + d // 2) * PACK + 72, (d % 2 * PARTS // 2 + d // 2 + 1) * PACK)
-            packed_s[rows, :] = jnp.zeros((8, LANES), F32)
+            base = (d % 2 * PARTS // 2 + d // 2) * PACK
+            packed_s[base + 72 : base + PACK, :] = jnp.zeros((8, LANES), F32)
             if d < 28:
-                packed_s[rows.start : rows.start + 2, :] = tsum_s[2 * d : 2 * d + 2, :]
+                packed_s[base + 72 : base + 74, :] = tsum_s[2 * d : 2 * d + 2, :]
+            tail = packed_s[base + 72 : base + PACK, :]
+            big = jnp.max(jnp.abs(packed_s[base : base + 72, :]), axis=0, keepdims=True)
+            tail = jnp.where(spare == 2, big, tail)
+            small = jnp.max(jnp.where(spare < 2, jnp.abs(tail), 0.0), axis=0, keepdims=True)
+            packed_s[base + 72 : base + PACK, :] = jnp.where(spare == 3, small, tail)
         core, half = core_ref[0], PARTS // 2 * PACK
         sends = [
             pltpu.make_async_copy(
@@ -408,15 +414,12 @@
             copy.wait()
 
 
-def to_half(v):
+def to_half(v, big, small):
     row = lax.broadcasted_iota(jnp.int32, (1, PACK, 1), 1)
-    size = jnp.abs(v)
-
-    def exponent(where):
-        top = jnp.max(jnp.where(where, size, 0.0), axis=(1, 2), keepdims=True)
-        return jnp.ceil(jnp.log2(jnp.maximum(top, 1e-30)))
-
-    e_big, e_small = exponent(row < 72), exponent((row >= 72) & (row < 74))
+    e_big, e_small = (
+        jnp.ceil(jnp.log2(jnp.maximum(jnp.max(m, axis=(1, 2), keepdims=True), 1e-30)))
+        for m in (big, small)
+    )
     scaled = v * jnp.where(row < 72, jnp.exp2(-e_big), jnp.exp2(-e_small))
     return jnp.where(row < 74, scaled, jnp.where(row < 77, e_big, e_small)).astype(jnp.float16)
 
@@ -571,27 +574,30 @@
     )(core, sums, w_squeeze.T, w_excite, x, c, top, bot, left, right, gain, mask, scaled, inv, gg, pre, conv, taps,
       w_expand, wprojt)
 
-    halves = to_half((keep + partner(send)).reshape(PARTS // 2, PACK, LANES))
+    pair = (keep + partner(send)).reshape(PARTS // 2, PACK, LANES)
+    halves = to_half(pair, pair[:, 74:75], pair[:, 75:76])
     mine = exchanged(halves)
     total = jnp.sum(from_half(mine), axis=0)
     vecs = vec[None]
     sample = lax.axis_index("dp")
-    for bit in (1, 2, 4):
+    members = 1
+    for bit in (4, 2, 1):
         both = lax.ppermute(
-            jnp.concatenate([total, vecs.reshape(16 * bit, LANES)], axis=0),
+            jnp.concatenate([total, vecs.reshape(16 * members, LANES)], axis=0),
             "dp",
             [(i, i ^ bit) for i in range(8)],
         )
         total = total + both[:PACK]
-        theirs = both[PACK:].reshape(bit, 16, LANES)
+        theirs = both[PACK:].reshape(members, 16, LANES)
         ahead = (sample & bit) == 0
         vecs = jnp.concatenate(
             [jnp.where(ahead, vecs, theirs), jnp.where(ahead, theirs, vecs)], axis=0
         )
+        members *= 2
     vecs = vecs.reshape(8, 2048)
     grad_wexc = jnp.einsum("bs,be->se", vecs[:, 1536:1584], vecs[:, 768:1536], precision=HIGH)
     grad_wsq = jnp.einsum("be,bs->es", vecs[:, :768], vecs[:, 1664:1712], precision=HIGH)
-    same = gathered(to_half(total[None])[0])
+    same = gathered(to_half(total[None], jnp.abs(total[None, :72]), jnp.abs(total[None, 72:74]))[0])
     other = partner(same)
     even = core[0] == 0
     every = jnp.stack(

time: 135 us -> 133 us (0.985)
  starting transfers between devices: 43.7 us -> 39.5 us
  waiting for transfers between devices: 23.4 us -> 26.5 us
    ppermute x3, starting transfers between devices: 11.8 us -> 8.62 us  [local(): lax.ppermute(jnp.concatenate([total, vecs.reshape(16 * members, LANES)],...]
    ppermute x3, waiting for transfers between devices: 3.25 us -> 6.23 us  [local(): lax.ppermute(jnp.concatenate([total, vecs.reshape(16 * members, LANES)],...]
    reduce_max x4 -> x3, other arithmetic: 3.27 us -> 1.41 us  [to_half(): jnp.max(m, axis=(1, 2), keepdims=True)]
where the time goes in v11:
time: 133 us; the launch traced here: 132 us
  starting transfers between devices  39.5 us (30%)
  Pallas kernels  34.8 us (26%)
  waiting for transfers between devices  26.5 us (20%)
  blocking collectives  11.6 us (9%)
  local copies, waits for them, and re-layouts  9.21 us (7%)
  other arithmetic  5.82 us (4%)
  between operations  2.61 us (2%)
  matrix products  1.99 us (1%)
    pallas_call x1, Pallas kernels, local(): pl.pallas_call(backward_kernel, grid=(STEPS,), in_specs=[pl.BlockSpec(mem...  18.3 us
    all_to_all x2, waiting for transfers between devices, exchanged(): return lax.all_to_all(blocks, RC, 0, 0, tiled=True, axis_index_groups=CHIPS)  13.6 us
    all_to_all x1, blocking collectives, exchanged(): return lax.all_to_all(blocks, RC, 0, 0, tiled=True, axis_index_groups=CHIPS)  11.6 us
    all_to_all x2, starting transfers between devices, exchanged(): return lax.all_to_all(blocks, RC, 0, 0, tiled=True, axis_index_groups=CHIPS)  11.5 us
    pallas_call x1, Pallas kernels, local(): pl.pallas_call(forward_kernel, grid=(STEPS,), in_specs=[halo, halo, edge,...  10.1 us
    ppermute x3, starting transfers between devices, local(): lax.ppermute(jnp.concatenate([total, vecs.reshape(16 * members, LANES)],...  8.62 us
    ppermute x3, starting transfers between devices, partner(): return lax.ppermute(block, 'col', [(i, i ^ 1) for i in range(4)])  7.05 us
    ppermute x3, waiting for transfers between devices, local(): lax.ppermute(jnp.concatenate([total, vecs.reshape(16 * members, LANES)],...  6.23 us
  transfers between devices with their start and end apart: 12, of which 8 were waited for; matrix products, arithmetic and copies ran while one was open for 4% of the time, Pallas kernels for 5%

profile of v11, /device:TPU:1, one launch (start us, length us, event | category | flops | bytes accessed | tf_op | source)
XLA Modules:
  0.0 132.0 jit_solution(4204119826118811158)
XLA Ops:
  0.6 1.3 copy_bitcast_fusion
  2.0 1.3 collective-permute-start.1
  3.3 4.6 %collective-permute-start = (bf16[3,192,128]{2,1,0:T(8,128)(2,1)S(1)}, bf16[3,192,128]{2,1,0:T(8,128)(2,1)S(1)}, u32[]{:S(2)}, u32[]{:S(2)}) collective-permute-start(bf16[3,192,128]{2,1,0:T(8,128)(2,1)S(1)} %pad_maximum_fusion.1), channel_id=1, source_target_pairs={{0,4},{4,8},{8,12},{12,16},{16,20},{20,24},{24,28},{1,5},{5,9},{9,... | collective-permute-start | bytes 442376 | tf_op jit(solution)/shard_map/ppermute | solution.py:473
  7.9 6.2 %expand.1 = (bf16[192,1024]{1,0:T(8,128)(2,1)}, f32[8,128]{1,0:T(8,128)}, bf16[192,128]{1,0:T(8,128)(2,1)}, f32[768,1024]{1,0:T(8,128)}, bf16[768,1024]{1,0:T(8,128)(2,1)}, /*index=5*/f32[768,1024]{1,0:T(8,128)}) custom-call(bf16[8,192,128]{2,1,0:T(8,128)(2,1)} %copy-done.4, bf16[8,192,128]{2,1,0:T(8,128)(2,1)} %copy-done.5, f32[1,192]{1,0:T(1,128)} %bitcast.76, ...), custom_call_target="tpu_custom_call" | custom-call | flops 600000000 | bytes 10000000 | tf_op jit(solution)/shard_map/expand/pallas_call | solution.py:485
  14.2 0.8 copy-done.3
  15.2 4.6 %collective-permute-start.2 = (bf16[192,128]{1,0:T(8,128)(2,1)S(1)}, bf16[192,128]{1,0:T(8,128)(2,1)S(1)}, u32[]{:S(2)}, u32[]{:S(2)}) collective-permute-start(bf16[192,128]{1,0:T(8,128)(2,1)S(1)} %strip.1.own_ref), channel_id=1, source_target_pairs={{0,1},{1,2},{2,3},{4,5},{5,6},{6,7},{8,9},{9,10},{10,11},{12,13},{... | collective-permute-start | bytes 147464 | tf_op jit(solution)/shard_map/ppermute | solution.py:507
  19.8 1.9 %collective-permute-start.3 = (bf16[192,128]{1,0:T(8,128)(2,1)S(1)}, bf16[192,128]{1,0:T(8,128)(2,1)S(1)}, u32[]{:S(2)}, u32[]{:S(2)}) collective-permute-start(bf16[192,128]{1,0:T(8,128)(2,1)S(1)} %strip.1.own_ref), channel_id=1, source_target_pairs={{1,0},{2,1},{3,2},{5,4},{6,5},{7,6},{9,8},{10,9},{11,10},{13,12},{... | collective-permute-start | bytes 147464 | tf_op jit(solution)/shard_map/ppermute | solution.py:508
  21.8 3.4 %collective-permute-done.3.right_ref = bf16[192,128]{1,0:T(8,128)(2,1)S(1)} collective-permute-done((bf16[192,128]{1,0:T(8,128)(2,1)S(1)}, bf16[192,128]{1,0:T(8,128)(2,1)S(1)}, u32[]{:S(2)}, u32[]{:S(2)}) %collective-permute-start.3) | collective-permute-done | bytes 49184 | tf_op jit(solution)/shard_map/ppermute | solution.py:508
  25.8 10.1 %forward.1 = (f32[768,1408]{1,0:T(8,128)}, f32[16,128]{1,0:T(8,128)}) custom-call(bf16[3,192,128]{2,1,0:T(8,128)(2,1)} %copy-done.1, bf16[3,192,128]{2,1,0:T(8,128)(2,1)} %copy-done, bf16[192,128]{1,0:T(8,128)(2,1)} %copy-done.2, bf16[192,128]{1,0:T(8,128)(2,1)} %copy-done.9, bf16[192,128]{1,0:T(8,128)(2,1)} %copy-done.10, f32[1,192]{1,0:T(1,128)} %bitcast.77, ...), custom_call_target="tpu_custom_call" | custom-call | flops 200000000 | bytes 12000000 | tf_op jit(solution)/shard_map/forward/pallas_call | solution.py:518
  36.1 1.3 %collective-permute-done.4 = f32[16,128]{1,0:T(8,128)S(1)} collective-permute-done((f32[16,128]{1,0:T(8,128)}, f32[16,128]{1,0:T(8,128)S(1)}, u32[]{:S(2)}, u32[]{:S(2)}) %collective-permute-start.4) | collective-permute-done | bytes 8224 | tf_op jit(solution)/shard_map/ppermute | solution.py:461
  37.4 0.7 add.31
  38.8 8.0 %all-to-all-start = ((f32[16,16,128]{2,1,0:T(8,128)}), f32[16,16,128]{2,1,0:T(8,128)S(1)}, u32[]{:S(2)}, u32[]{:S(2)}) async-start(f32[16,16,128]{2,1,0:T(8,128)} %broadcast_in_dim.170), calls=%async_computation | async-start | bytes 262144 | tf_op jit(solution)/shard_map/all_to_all | solution.py:453
  47.4 6.0 %all-to-all-done.parts_ref = f32[16,16,128]{2,1,0:T(8,128)S(1)} async-done(((f32[16,16,128]{2,1,0:T(8,128)}), f32[16,16,128]{2,1,0:T(8,128)S(1)}, u32[]{:S(2)}, u32[]{:S(2)}) %all-to-all-start) | async-done | bytes 131104 | tf_op jit(solution)/shard_map/all_to_all | solution.py:453
  54.1 18.3 %backward.1 = (bf16[8,192,128]{2,1,0:T(8,128)(2,1)}, bf16[8,192,128]{2,1,0:T(8,128)(2,1)}, f32[1280,128]{1,0:T(8,128)}, f32[1280,128]{1,0:T(8,128)}, f32[16,128]{1,0:T(8,128)}) custom-call(s32[1]{0:T(128)} %bitcast.core_ref, f32[16,16,128]{2,1,0:T(8,128)} %copy-done.6, f32[48,768]{1,0:T(8,128)} %bitcast.61, f32[48,768]{1,0:T(8,128)} %wexc_ref.1, ...), custom_call_target="tpu_custom_call" | custom-call | flops 1500000000 | bytes 16000000 | tf_op jit(solution)/shard_map/backward/pallas_call | solution.py:541
  72.4 1.7 %collective-permute-start.5 = (f32[1280,128]{1,0:T(8,128)}, f32[1280,128]{1,0:T(8,128)S(1)}, u32[]{:S(2)}, u32[]{:S(2)}) collective-permute-start(f32[1280,128]{1,0:T(8,128)} %get-tuple-element.32), channel_id=1, source_target_pairs={{0,1},{1,0},{2,3},{3,2},{4,5},{5,4},{6,7},{7,6},{8,9},{9,8},{10,11... | collective-permute-start | bytes 1966088 | tf_op jit(solution)/shard_map/ppermute | solution.py:461
  74.1 1.9 %collective-permute-done.5 = f32[1280,128]{1,0:T(8,128)S(1)} collective-permute-done((f32[1280,128]{1,0:T(8,128)}, f32[1280,128]{1,0:T(8,128)S(1)}, u32[]{:S(2)}, u32[]{:S(2)}) %collective-permute-start.5) | collective-permute-done | bytes 655392 | tf_op jit(solution)/shard_map/ppermute | solution.py:461
  76.0 1.2 add.33
  78.0 11.6 %all_to_all.15 = f16[16,80,128]{2,1,0:T(8,128)(2,1)S(1)} all-to-all(f16[16,80,128]{2,1,0:T(8,128)(2,1)S(1)} %select_convert_fusion), channel_id=1, replica_groups={{0,2,4,6,8,10,12,14,16,18,20,22,24,26,28,30},{1,3,5,7,9,11,13,15,17,19,..., dimensions={0} | all-to-all | bytes 655360 | tf_op jit(solution)/shard_map/all_to_all | solution.py:453
  89.9 7.0 %collective-permute-start.6 = (f32[96,128]{1,0:T(8,128)S(1)}, f32[96,128]{1,0:T(8,128)S(1)}, u32[]{:S(2)}, u32[]{:S(2)}) collective-permute-start(f32[96,128]{1,0:T(8,128)S(1)} %pad_maximum_fusion.5), channel_id=1, source_target_pairs={{0,128},{32,160},{64,192},{96,224},{128,0},{160,32},{192,64},{224,... | collective-permute-start | bytes 147464 | tf_op jit(solution)/shard_map/ppermute | solution.py:585
  96.9 1.5 %collective-permute-done.6 = f32[96,128]{1,0:T(8,128)S(1)} collective-permute-done((f32[96,128]{1,0:T(8,128)S(1)}, f32[96,128]{1,0:T(8,128)S(1)}, u32[]{:S(2)}, u32[]{:S(2)}) %collective-permute-start.6) | collective-permute-done | bytes 49184 | tf_op jit(solution)/shard_map/ppermute | solution.py:585
  98.4 1.5 %collective-permute-start.7 = (f32[112,128]{1,0:T(8,128)S(1)}, f32[112,128]{1,0:T(8,128)S(1)}, u32[]{:S(2)}, u32[]{:S(2)}) collective-permute-start(f32[112,128]{1,0:T(8,128)S(1)} %pad_maximum_fusion.4), channel_id=1, source_target_pairs={{0,64},{32,96},{64,0},{96,32},{128,192},{160,224},{192,128},{224,1... | collective-permute-start | bytes 172040 | tf_op jit(solution)/shard_map/ppermute | solution.py:585
  100.0 3.6 %collective-permute-done.7 = f32[112,128]{1,0:T(8,128)S(1)} collective-permute-done((f32[112,128]{1,0:T(8,128)S(1)}, f32[112,128]{1,0:T(8,128)S(1)}, u32[]{:S(2)}, u32[]{:S(2)}) %collective-permute-start.7) | collective-permute-done | bytes 57376 | tf_op jit(solution)/shard_map/ppermute | solution.py:585
  103.7 1.0 copy.19
  104.7 1.0 copy.20
  105.8 1.1 collective-permute-done.8
  109.7 0.8 broadcast_in_dim.195
  110.5 3.5 %all-to-all-start.2 = ((f16[16,80,128]{2,1,0:T(8,128)(2,1)}), f16[16,80,128]{2,1,0:T(8,128)(2,1)S(1)}, u32[]{:S(2)}, u32[]{:S(2)}) async-start(f16[16,80,128]{2,1,0:T(8,128)(2,1)} %broadcast_in_dim.195), calls=%async_computation.2 | async-start | bytes 655360 | tf_op jit(solution)/shard_map/all_to_all | solution.py:453
  114.1 7.6 %all-to-all-done.2 = f16[16,80,128]{2,1,0:T(8,128)(2,1)S(1)} async-done(((f16[16,80,128]{2,1,0:T(8,128)(2,1)}), f16[16,80,128]{2,1,0:T(8,128)(2,1)S(1)}, u32[]{:S(2)}, u32[]{:S(2)}) %all-to-all-start.2) | async-done | bytes 327712 | tf_op jit(solution)/shard_map/all_to_all | solution.py:453
  121.7 5.3 %collective-permute-start.9 = (f16[16,80,128]{2,1,0:T(8,128)(2,1)S(1)}, f16[16,80,128]{2,1,0:T(8,128)(2,1)S(1)}, u32[]{:S(2)}, u32[]{:S(2)}) collective-permute-start(f16[16,80,128]{2,1,0:T(8,128)(2,1)S(1)} %all-to-all-done.2), channel_id=1, source_target_pairs={{0,1},{1,0},{2,3},{3,2},{4,5},{5,4},{6,7},{7,6},{8,9},{9,8},{10,11... | collective-permute-start | bytes 983048 | tf_op jit(solution)/shard_map/ppermute | solution.py:461
  127.0 1.0 fusion.4
  128.0 1.0 fusion.2
  129.7 1.1 slice_bitcast_fusion
  (82 shorter events, 7.5 us)
Async XLA Ops:
  1.9 6.0 %copy-start.4 = (bf16[8,192,128]{2,1,0:T(8,128)(2,1)}, bf16[8,192,128]{2,1,0:T(8,128)(2,1)S(1)}, u32[]{:S(2)}) copy-start(bf16[8,192,128]{2,1,0:T(8,128)(2,1)S(1)} %get-tuple-element.69.x_ref) | copy-start | bytes 1179652
  1.9 6.0 %copy-start.5 = (bf16[8,192,128]{2,1,0:T(8,128)(2,1)}, bf16[8,192,128]{2,1,0:T(8,128)(2,1)S(1)}, u32[]{:S(2)}) copy-start(bf16[8,192,128]{2,1,0:T(8,128)(2,1)S(1)} %get-tuple-element.68.c_ref) | copy-start | bytes 1179652
  2.0 12.2 %collective-permute-start.1 = (bf16[3,192,128]{2,1,0:T(8,128)(2,1)S(1)}, bf16[3,192,128]{2,1,0:T(8,128)(2,1)S(1)}, u32[]{:S(2)}, u32[]{:S(2)}) collective-permute-start(bf16[3,192,128]{2,1,0:T(8,128)(2,1)S(1)} %pad_maximum_fusion.2), channel_id=1, source_target_pairs={{4,0},{8,4},{12,8},{16,12},{20,16},{24,20},{28,24},{5,1},{9,5},{13... | collective-permute-start | bytes 442376 | tf_op jit(solution)/shard_map/ppermute | solution.py:474
  3.3 10.9 %collective-permute-start = (bf16[3,192,128]{2,1,0:T(8,128)(2,1)S(1)}, bf16[3,192,128]{2,1,0:T(8,128)(2,1)S(1)}, u32[]{:S(2)}, u32[]{:S(2)}) collective-permute-start(bf16[3,192,128]{2,1,0:T(8,128)(2,1)S(1)} %pad_maximum_fusion.1), channel_id=1, source_target_pairs={{0,4},{4,8},{8,12},{12,16},{16,20},{20,24},{24,28},{1,5},{5,9},{9,... | collective-permute-start | bytes 442376 | tf_op jit(solution)/shard_map/ppermute | solution.py:473
  14.2 11.0 %copy-start = (bf16[3,192,128]{2,1,0:T(8,128)(2,1)}, bf16[3,192,128]{2,1,0:T(8,128)(2,1)S(1)}, u32[]{:S(2)}) copy-start(bf16[3,192,128]{2,1,0:T(8,128)(2,1)S(1)} %collective-permute-done.1.bot_ref) | copy-start | bytes 442372
  14.2 11.0 %copy-start.1 = (bf16[3,192,128]{2,1,0:T(8,128)(2,1)}, bf16[3,192,128]{2,1,0:T(8,128)(2,1)S(1)}, u32[]{:S(2)}) copy-start(bf16[3,192,128]{2,1,0:T(8,128)(2,1)S(1)} %collective-permute-done.top_ref) | copy-start | bytes 442372
  14.2 0.9 copy-start.3
  15.2 10.0 %copy-start.2 = (bf16[192,128]{1,0:T(8,128)(2,1)}, bf16[192,128]{1,0:T(8,128)(2,1)S(1)}, u32[]{:S(2)}) copy-start(bf16[192,128]{1,0:T(8,128)(2,1)S(1)} %strip.1.own_ref) | copy-start | bytes 147460
  15.2 6.5 %collective-permute-start.2 = (bf16[192,128]{1,0:T(8,128)(2,1)S(1)}, bf16[192,128]{1,0:T(8,128)(2,1)S(1)}, u32[]{:S(2)}, u32[]{:S(2)}) collective-permute-start(bf16[192,128]{1,0:T(8,128)(2,1)S(1)} %strip.1.own_ref), channel_id=1, source_target_pairs={{0,1},{1,2},{2,3},{4,5},{5,6},{6,7},{8,9},{9,10},{10,11},{12,13},{... | collective-permute-start | bytes 147464 | tf_op jit(solution)/shard_map/ppermute | solution.py:507
  19.8 5.4 %collective-permute-start.3 = (bf16[192,128]{1,0:T(8,128)(2,1)S(1)}, bf16[192,128]{1,0:T(8,128)(2,1)S(1)}, u32[]{:S(2)}, u32[]{:S(2)}) collective-permute-start(bf16[192,128]{1,0:T(8,128)(2,1)S(1)} %strip.1.own_ref), channel_id=1, source_target_pairs={{1,0},{2,1},{3,2},{5,4},{6,5},{7,6},{9,8},{10,9},{11,10},{13,12},{... | collective-permute-start | bytes 147464 | tf_op jit(solution)/shard_map/ppermute | solution.py:508
  21.8 3.5 %copy-start.9 = (bf16[192,128]{1,0:T(8,128)(2,1)}, bf16[192,128]{1,0:T(8,128)(2,1)S(1)}, u32[]{:S(2)}) copy-start(bf16[192,128]{1,0:T(8,128)(2,1)S(1)} %collective-permute-done.2.left_ref) | copy-start | bytes 147460
  25.2 0.6 copy-start.10
  35.9 1.5 %collective-permute-start.4 = (f32[16,128]{1,0:T(8,128)}, f32[16,128]{1,0:T(8,128)S(1)}, u32[]{:S(2)}, u32[]{:S(2)}) collective-permute-start(f32[16,128]{1,0:T(8,128)} %get-tuple-element.24), channel_id=1, source_target_pairs={{0,1},{1,0},{2,3},{3,2},{4,5},{5,4},{6,7},{7,6},{8,9},{9,8},{10,11... | collective-permute-start | bytes 24584 | tf_op jit(solution)/shard_map/ppermute | solution.py:461
  38.8 14.7 %all-to-all-start = ((f32[16,16,128]{2,1,0:T(8,128)}), f32[16,16,128]{2,1,0:T(8,128)S(1)}, u32[]{:S(2)}, u32[]{:S(2)}) async-start(f32[16,16,128]{2,1,0:T(8,128)} %broadcast_in_dim.170), calls=%async_computation | async-start | bytes 262144 | tf_op jit(solution)/shard_map/all_to_all | solution.py:453
  53.4 0.7 copy-start.6
  72.4 3.6 %collective-permute-start.5 = (f32[1280,128]{1,0:T(8,128)}, f32[1280,128]{1,0:T(8,128)S(1)}, u32[]{:S(2)}, u32[]{:S(2)}) collective-permute-start(f32[1280,128]{1,0:T(8,128)} %get-tuple-element.32), channel_id=1, source_target_pairs={{0,1},{1,0},{2,3},{3,2},{4,5},{5,4},{6,7},{7,6},{8,9},{9,8},{10,11... | collective-permute-start | bytes 1966088 | tf_op jit(solution)/shard_map/ppermute | solution.py:461
  77.5 12.4 %copy-start.11 = (f32[16,128]{1,0:T(8,128)S(1)}, f32[16,128]{1,0:T(8,128)}, u32[]{:S(2)}) copy-start(f32[16,128]{1,0:T(8,128)} %get-tuple-element.33) | copy-start | bytes 24580
  77.9 25.8 %copy-start.8 = (bf16[8,192,128]{2,1,0:T(8,128)(2,1)S(1)}, bf16[8,192,128]{2,1,0:T(8,128)(2,1)}, u32[]{:S(2)}) copy-start(bf16[8,192,128]{2,1,0:T(8,128)(2,1)} %get-tuple-element.29) | copy-start | bytes 1179652
  89.5 15.2 %copy-start.7 = (bf16[8,192,128]{2,1,0:T(8,128)(2,1)S(1)}, bf16[8,192,128]{2,1,0:T(8,128)(2,1)}, u32[]{:S(2)}) copy-start(bf16[8,192,128]{2,1,0:T(8,128)(2,1)} %get-tuple-element.30) | copy-start | bytes 1179652
  89.9 8.5 %collective-permute-start.6 = (f32[96,128]{1,0:T(8,128)S(1)}, f32[96,128]{1,0:T(8,128)S(1)}, u32[]{:S(2)}, u32[]{:S(2)}) collective-permute-start(f32[96,128]{1,0:T(8,128)S(1)} %pad_maximum_fusion.5), channel_id=1, source_target_pairs={{0,128},{32,160},{64,192},{96,224},{128,0},{160,32},{192,64},{224,... | collective-permute-start | bytes 147464 | tf_op jit(solution)/shard_map/ppermute | solution.py:585
  98.4 5.1 %collective-permute-start.7 = (f32[112,128]{1,0:T(8,128)S(1)}, f32[112,128]{1,0:T(8,128)S(1)}, u32[]{:S(2)}, u32[]{:S(2)}) collective-permute-start(f32[112,128]{1,0:T(8,128)S(1)} %pad_maximum_fusion.4), channel_id=1, source_target_pairs={{0,64},{32,96},{64,0},{96,32},{128,192},{160,224},{192,128},{224,1... | collective-permute-start | bytes 172040 | tf_op jit(solution)/shard_map/ppermute | solution.py:585
  103.6 3.3 %collective-permute-start.8 = (f32[144,128]{1,0:T(8,128)S(1)}, f32[144,128]{1,0:T(8,128)S(1)}, u32[]{:S(2)}, u32[]{:S(2)}) collective-permute-start(f32[144,128]{1,0:T(8,128)S(1)} %pad_maximum_fusion.3), channel_id=1, source_target_pairs={{0,32},{32,0},{64,96},{96,64},{128,160},{160,128},{192,224},{224,1... | collective-permute-start | bytes 221192 | tf_op jit(solution)/shard_map/ppermute | solution.py:585
  110.5 11.2 %all-to-all-start.2 = ((f16[16,80,128]{2,1,0:T(8,128)(2,1)}), f16[16,80,128]{2,1,0:T(8,128)(2,1)S(1)}, u32[]{:S(2)}, u32[]{:S(2)}) async-start(f16[16,80,128]{2,1,0:T(8,128)(2,1)} %broadcast_in_dim.195), calls=%async_computation.2 | async-start | bytes 655360 | tf_op jit(solution)/shard_map/all_to_all | solution.py:453
  121.7 7.3 %collective-permute-start.9 = (f16[16,80,128]{2,1,0:T(8,128)(2,1)S(1)}, f16[16,80,128]{2,1,0:T(8,128)(2,1)S(1)}, u32[]{:S(2)}, u32[]{:S(2)}) collective-permute-start(f16[16,80,128]{2,1,0:T(8,128)(2,1)S(1)} %all-to-all-done.2), channel_id=1, source_target_pairs={{0,1},{1,0},{2,3},{3,2},{4,5},{5,4},{6,7},{7,6},{8,9},{9,8},{10,11... | collective-permute-start | bytes 983048 | tf_op jit(solution)/shard_map/ppermute | solution.py:461

commit v12 on v11

--- a/solution.py
+++ b/solution.py
@@ -414,10 +414,13 @@
             copy.wait()
 
 
+TOP = 15.0
+
+
 def to_half(v, big, small):
     row = lax.broadcasted_iota(jnp.int32, (1, PACK, 1), 1)
     e_big, e_small = (
-        jnp.ceil(jnp.log2(jnp.maximum(jnp.max(m, axis=(1, 2), keepdims=True), 1e-30)))
+        jnp.ceil(jnp.log2(jnp.maximum(jnp.max(m, axis=(1, 2), keepdims=True), 1e-30))) - TOP
         for m in (big, small)
     )
     scaled = v * jnp.where(row < 72, jnp.exp2(-e_big), jnp.exp2(-e_small))
@@ -427,8 +430,9 @@
 def from_half(h):
     v = h.astype(F32)
     row = lax.broadcasted_iota(jnp.int32, (1, PACK, 1), 1)
-    scale = jnp.where(row < 72, jnp.exp2(v[:, 74:75]), jnp.exp2(v[:, 77:78]))
-    return jnp.where(row < 74, v * scale, 0.0)
+    s_big, s_small = jnp.exp2(v[:, 74:75]), jnp.exp2(v[:, 77:78])
+    bounds = jnp.where(row == 74, s_big, jnp.where(row == 75, s_small, 0.0)) * 2.0**TOP
+    return jnp.where(row < 74, v * jnp.where(row < 72, s_big, s_small), bounds)
 
 
 def shape(*dims, dtype=F32):
@@ -574,8 +578,11 @@
     )(core, sums, w_squeeze.T, w_excite, x, c, top, bot, left, right, gain, mask, scaled, inv, gg, pre, conv, taps,
       w_expand, wprojt)
 
-    pair = (keep + partner(send)).reshape(PARTS // 2, PACK, LANES)
-    halves = to_half(pair, pair[:, 74:75], pair[:, 75:76])
+    keep = keep.reshape(PARTS // 2, PACK, LANES)
+    sent = partner(send).reshape(PARTS // 2, PACK, LANES)
+    halves = to_half(
+        keep + sent, keep[:, 74:75] + sent[:, 74:75], keep[:, 75:76] + sent[:, 75:76]
+    )
     mine = exchanged(halves)
     total = jnp.sum(from_half(mine), axis=0)
     vecs = vec[None]
@@ -597,7 +604,7 @@
     vecs = vecs.reshape(8, 2048)
     grad_wexc = jnp.einsum("bs,be->se", vecs[:, 1536:1584], vecs[:, 768:1536], precision=HIGH)
     grad_wsq = jnp.einsum("be,bs->es", vecs[:, :768], vecs[:, 1664:1712], precision=HIGH)
-    same = gathered(to_half(total[None], jnp.abs(total[None, :72]), jnp.abs(total[None, 72:74]))[0])
+    same = gathered(to_half(total[None], total[None, 74:75], total[None, 75:76])[0])
     other = partner(same)
     even = core[0] == 0
     every = jnp.stack(

time: 133 us -> 135 us (1.015)
  blocking collectives: 11.6 us -> 0 us
  waiting for transfers between devices: 26.5 us -> 34.7 us
  starting transfers between devices: 39.5 us -> 43.9 us
    all_to_all x1 -> x0, blocking collectives: 11.6 us -> none  [exchanged(): return lax.all_to_all(blocks, RC, 0, 0, tiled=True, axis_index_groups=CHIPS)]
    all_to_all x2 -> x3, waiting for transfers between devices: 13.6 us -> 22.2 us  [exchanged(): return lax.all_to_all(blocks, RC, 0, 0, tiled=True, axis_index_groups=CHIPS)]
    all_to_all x2 -> x3, starting transfers between devices: 11.5 us -> 15.2 us  [exchanged(): return lax.all_to_all(blocks, RC, 0, 0, tiled=True, axis_index_groups=CHIPS)]
    convert_element_type x2, other arithmetic: 0.53 us -> 2.35 us  [to_half(): jnp.where(row < 74, scaled, jnp.where(row < 77, e_big, e_small))]
  transfers between devices with their start and end apart: 12 -> 13, of which waited for: 8 -> 9; matrix products, arithmetic and copies ran while one was open for 4% -> 4% of each run, Pallas kernels for 5% -> 5%
where the time goes in v12:
time: 135 us; the launch traced here: 134 us
  starting transfers between devices  43.9 us (33%)
  Pallas kernels  34.7 us (26%)
  waiting for transfers between devices  34.7 us (26%)
  local copies, waits for them, and re-layouts  9.21 us (7%)
  other arithmetic  6.87 us (5%)
  between operations  2.6 us (2%)
  matrix products  1.98 us (1%)
    all_to_all x3, waiting for transfers between devices, exchanged(): return lax.all_to_all(blocks, RC, 0, 0, tiled=True, axis_index_groups=CHIPS)  22.2 us
    pallas_call x1, Pallas kernels, local(): pl.pallas_call(backward_kernel, grid=(STEPS,), in_specs=[pl.BlockSpec(mem...  18.3 us
    all_to_all x3, starting transfers between devices, exchanged(): return lax.all_to_all(blocks, RC, 0, 0, tiled=True, axis_index_groups=CHIPS)  15.2 us
    pallas_call x1, Pallas kernels, local(): pl.pallas_call(forward_kernel, grid=(STEPS,), in_specs=[halo, halo, edge,...  10.1 us
    ppermute x3, starting transfers between devices, local(): lax.ppermute(jnp.concatenate([total, vecs.reshape(16 * members, LANES)],...  8.88 us
    ppermute x3, starting transfers between devices, partner(): return lax.ppermute(block, 'col', [(i, i ^ 1) for i in range(4)])  7.48 us
    pallas_call x1, Pallas kernels, local(): pl.pallas_call(expand_kernel, grid=(STEPS,), in_specs=[tile, tile, full(1...  6.21 us
    ppermute x3, waiting for transfers between devices, local(): lax.ppermute(jnp.concatenate([total, vecs.reshape(16 * members, LANES)],...  5.78 us
  transfers between devices with their start and end apart: 13, of which 9 were waited for; matrix products, arithmetic and copies ran while one was open for 4% of the time, Pallas kernels for 5%

profile of v12, /device:TPU:1, one launch (start us, length us, event | category | flops | bytes accessed | tf_op | source)
XLA Modules:
  0.0 134.0 jit_solution(16188668119175169671)
XLA Ops:
  0.6 1.3 copy_bitcast_fusion
  2.0 1.3 collective-permute-start.1
  3.3 4.6 %collective-permute-start = (bf16[3,192,128]{2,1,0:T(8,128)(2,1)S(1)}, bf16[3,192,128]{2,1,0:T(8,128)(2,1)S(1)}, u32[]{:S(2)}, u32[]{:S(2)}) collective-permute-start(bf16[3,192,128]{2,1,0:T(8,128)(2,1)S(1)} %pad_maximum_fusion.1), channel_id=1, source_target_pairs={{0,4},{4,8},{8,12},{12,16},{16,20},{20,24},{24,28},{1,5},{5,9},{9,... | collective-permute-start | bytes 442376 | tf_op jit(solution)/shard_map/ppermute | solution.py:477
  7.9 6.2 %expand.1 = (bf16[192,1024]{1,0:T(8,128)(2,1)}, f32[8,128]{1,0:T(8,128)}, bf16[192,128]{1,0:T(8,128)(2,1)}, f32[768,1024]{1,0:T(8,128)}, bf16[768,1024]{1,0:T(8,128)(2,1)}, /*index=5*/f32[768,1024]{1,0:T(8,128)}) custom-call(bf16[8,192,128]{2,1,0:T(8,128)(2,1)} %copy-done.4, bf16[8,192,128]{2,1,0:T(8,128)(2,1)} %copy-done.5, f32[1,192]{1,0:T(1,128)} %bitcast.79, ...), custom_call_target="tpu_custom_call" | custom-call | flops 600000000 | bytes 10000000 | tf_op jit(solution)/shard_map/expand/pallas_call | solution.py:489
  14.2 0.8 copy-done.3
  15.2 4.6 %collective-permute-start.2 = (bf16[192,128]{1,0:T(8,128)(2,1)S(1)}, bf16[192,128]{1,0:T(8,128)(2,1)S(1)}, u32[]{:S(2)}, u32[]{:S(2)}) collective-permute-start(bf16[192,128]{1,0:T(8,128)(2,1)S(1)} %strip.1.own_ref), channel_id=1, source_target_pairs={{0,1},{1,2},{2,3},{4,5},{5,6},{6,7},{8,9},{9,10},{10,11},{12,13},{... | collective-permute-start | bytes 147464 | tf_op jit(solution)/shard_map/ppermute | solution.py:511
  19.8 1.9 %collective-permute-start.3 = (bf16[192,128]{1,0:T(8,128)(2,1)S(1)}, bf16[192,128]{1,0:T(8,128)(2,1)S(1)}, u32[]{:S(2)}, u32[]{:S(2)}) collective-permute-start(bf16[192,128]{1,0:T(8,128)(2,1)S(1)} %strip.1.own_ref), channel_id=1, source_target_pairs={{1,0},{2,1},{3,2},{5,4},{6,5},{7,6},{9,8},{10,9},{11,10},{13,12},{... | collective-permute-start | bytes 147464 | tf_op jit(solution)/shard_map/ppermute | solution.py:512
  21.7 3.4 %collective-permute-done.3.right_ref = bf16[192,128]{1,0:T(8,128)(2,1)S(1)} collective-permute-done((bf16[192,128]{1,0:T(8,128)(2,1)S(1)}, bf16[192,128]{1,0:T(8,128)(2,1)S(1)}, u32[]{:S(2)}, u32[]{:S(2)}) %collective-permute-start.3) | collective-permute-done | bytes 49184 | tf_op jit(solution)/shard_map/ppermute | solution.py:512
  25.8 10.1 %forward.1 = (f32[768,1408]{1,0:T(8,128)}, f32[16,128]{1,0:T(8,128)}) custom-call(bf16[3,192,128]{2,1,0:T(8,128)(2,1)} %copy-done.1, bf16[3,192,128]{2,1,0:T(8,128)(2,1)} %copy-done, bf16[192,128]{1,0:T(8,128)(2,1)} %copy-done.2, bf16[192,128]{1,0:T(8,128)(2,1)} %copy-done.9, bf16[192,128]{1,0:T(8,128)(2,1)} %copy-done.10, f32[1,192]{1,0:T(1,128)} %bitcast.80, ...), custom_call_target="tpu_custom_call" | custom-call | flops 200000000 | bytes 12000000 | tf_op jit(solution)/shard_map/forward/pallas_call | solution.py:522
  36.0 1.3 collective-permute-done.4
  38.7 8.0 %all-to-all-start = ((f32[16,16,128]{2,1,0:T(8,128)}), f32[16,16,128]{2,1,0:T(8,128)S(1)}, u32[]{:S(2)}, u32[]{:S(2)}) async-start(f32[16,16,128]{2,1,0:T(8,128)} %broadcast_in_dim.202), calls=%async_computation | async-start | bytes 262144 | tf_op jit(solution)/shard_map/all_to_all | solution.py:457
  47.4 6.0 %all-to-all-done.parts_ref = f32[16,16,128]{2,1,0:T(8,128)S(1)} async-done(((f32[16,16,128]{2,1,0:T(8,128)}), f32[16,16,128]{2,1,0:T(8,128)S(1)}, u32[]{:S(2)}, u32[]{:S(2)}) %all-to-all-start) | async-done | bytes 131104 | tf_op jit(solution)/shard_map/all_to_all | solution.py:457
  54.1 18.3 %backward.1 = (bf16[8,192,128]{2,1,0:T(8,128)(2,1)}, bf16[8,192,128]{2,1,0:T(8,128)(2,1)}, f32[1280,128]{1,0:T(8,128)}, f32[1280,128]{1,0:T(8,128)}, f32[16,128]{1,0:T(8,128)}) custom-call(s32[1]{0:T(128)} %bitcast.core_ref, f32[16,16,128]{2,1,0:T(8,128)} %copy-done.6, f32[48,768]{1,0:T(8,128)} %bitcast.64, f32[48,768]{1,0:T(8,128)} %wexc_ref.1, ...), custom_call_target="tpu_custom_call" | custom-call | flops 1500000000 | bytes 16000000 | tf_op jit(solution)/shard_map/backward/pallas_call | solution.py:545
  72.4 1.7 %collective-permute-start.5 = (f32[1280,128]{1,0:T(8,128)}, f32[1280,128]{1,0:T(8,128)S(1)}, u32[]{:S(2)}, u32[]{:S(2)}) collective-permute-start(f32[1280,128]{1,0:T(8,128)} %get-tuple-element.32), channel_id=1, source_target_pairs={{0,1},{1,0},{2,3},{3,2},{4,5},{5,4},{6,7},{7,6},{8,9},{9,8},{10,11... | collective-permute-start | bytes 1966088 | tf_op jit(solution)/shard_map/ppermute | solution.py:465
  74.0 1.9 %collective-permute-done.5 = f32[1280,128]{1,0:T(8,128)S(1)} collective-permute-done((f32[1280,128]{1,0:T(8,128)}, f32[1280,128]{1,0:T(8,128)S(1)}, u32[]{:S(2)}, u32[]{:S(2)}) %collective-permute-start.5) | collective-permute-done | bytes 655392 | tf_op jit(solution)/shard_map/ppermute | solution.py:465
  75.9 1.1 fusion.11
  77.2 2.3 %select_convert_fusion = f16[16,80,128]{2,1,0:T(8,128)(2,1)} fusion(f32[16,80,128]{2,1,0:T(8,128)} %bitcast.54, f32[16,80,128]{2,1,0:T(8,128)S(1)} %bitcast.56, f32[16,80]{1,0:T(8,128)S(1)} %broadcast_select_fusion.4, f32[16,80]{1,0:T(8,128)S(1)} %broadcast_select_fusion.5, pred[80]{0:T(512)(128)(4,1)S(1)} %iota_compare_fusion.4), kind=kLoop, calls=%fused_computation.4 | loop fusion | flops 655360 | bytes 1648720 | tf_op jit(solution)/shard_map/convert_element_type | solution.py:427
  79.5 3.7 %all-to-all-start.1 = ((f16[16,80,128]{2,1,0:T(8,128)(2,1)}), f16[16,80,128]{2,1,0:T(8,128)(2,1)S(1)}, u32[]{:S(2)}, u32[]{:S(2)}) async-start(f16[16,80,128]{2,1,0:T(8,128)(2,1)} %select_convert_fusion), calls=%async_computation.1 | async-start | bytes 655360 | tf_op jit(solution)/shard_map/all_to_all | solution.py:457
  83.2 8.6 %all-to-all-done.1 = f16[16,80,128]{2,1,0:T(8,128)(2,1)S(1)} async-done(((f16[16,80,128]{2,1,0:T(8,128)(2,1)}), f16[16,80,128]{2,1,0:T(8,128)(2,1)S(1)}, u32[]{:S(2)}, u32[]{:S(2)}) %all-to-all-start.1) | async-done | bytes 327712 | tf_op jit(solution)/shard_map/all_to_all | solution.py:457
  92.3 7.0 %collective-permute-start.6 = (f32[96,128]{1,0:T(8,128)S(1)}, f32[96,128]{1,0:T(8,128)S(1)}, u32[]{:S(2)}, u32[]{:S(2)}) collective-permute-start(f32[96,128]{1,0:T(8,128)S(1)} %pad_maximum_fusion.5), channel_id=1, source_target_pairs={{0,128},{32,160},{64,192},{96,224},{128,0},{160,32},{192,64},{224,... | collective-permute-start | bytes 147464 | tf_op jit(solution)/shard_map/ppermute | solution.py:592
  99.3 1.5 %collective-permute-done.6 = f32[96,128]{1,0:T(8,128)S(1)} collective-permute-done((f32[96,128]{1,0:T(8,128)S(1)}, f32[96,128]{1,0:T(8,128)S(1)}, u32[]{:S(2)}, u32[]{:S(2)}) %collective-permute-start.6) | collective-permute-done | bytes 49184 | tf_op jit(solution)/shard_map/ppermute | solution.py:592
  100.8 1.5 %collective-permute-start.7 = (f32[112,128]{1,0:T(8,128)S(1)}, f32[112,128]{1,0:T(8,128)S(1)}, u32[]{:S(2)}, u32[]{:S(2)}) collective-permute-start(f32[112,128]{1,0:T(8,128)S(1)} %pad_maximum_fusion.4), channel_id=1, source_target_pairs={{0,64},{32,96},{64,0},{96,32},{128,192},{160,224},{192,128},{224,1... | collective-permute-start | bytes 172040 | tf_op jit(solution)/shard_map/ppermute | solution.py:592
  102.3 3.2 %collective-permute-done.7 = f32[112,128]{1,0:T(8,128)S(1)} collective-permute-done((f32[112,128]{1,0:T(8,128)S(1)}, f32[112,128]{1,0:T(8,128)S(1)}, u32[]{:S(2)}, u32[]{:S(2)}) %collective-permute-start.7) | collective-permute-done | bytes 57376 | tf_op jit(solution)/shard_map/ppermute | solution.py:592
  105.9 1.0 copy.19
  106.9 1.0 copy.20
  108.0 1.1 collective-permute-done.8
  112.1 3.5 %all-to-all-start.2 = ((f16[16,80,128]{2,1,0:T(8,128)(2,1)}), f16[16,80,128]{2,1,0:T(8,128)(2,1)S(1)}, u32[]{:S(2)}, u32[]{:S(2)}) async-start(f16[16,80,128]{2,1,0:T(8,128)(2,1)} %broadcast_in_dim.231), calls=%async_computation.2 | async-start | bytes 655360 | tf_op jit(solution)/shard_map/all_to_all | solution.py:457
  115.7 7.6 %all-to-all-done.2 = f16[16,80,128]{2,1,0:T(8,128)(2,1)S(1)} async-done(((f16[16,80,128]{2,1,0:T(8,128)(2,1)}), f16[16,80,128]{2,1,0:T(8,128)(2,1)S(1)}, u32[]{:S(2)}, u32[]{:S(2)}) %all-to-all-start.2) | async-done | bytes 327712 | tf_op jit(solution)/shard_map/all_to_all | solution.py:457
  123.3 5.7 %collective-permute-start.9 = (f16[16,80,128]{2,1,0:T(8,128)(2,1)S(1)}, f16[16,80,128]{2,1,0:T(8,128)(2,1)S(1)}, u32[]{:S(2)}, u32[]{:S(2)}) collective-permute-start(f16[16,80,128]{2,1,0:T(8,128)(2,1)S(1)} %all-to-all-done.2), channel_id=1, source_target_pairs={{0,1},{1,0},{2,3},{3,2},{4,5},{5,4},{6,7},{7,6},{8,9},{9,8},{10,11... | collective-permute-start | bytes 983048 | tf_op jit(solution)/shard_map/ppermute | solution.py:465
  129.0 1.0 fusion.3
  130.0 1.0 fusion.1
  131.7 1.1 slice_bitcast_fusion
  (82 shorter events, 8.1 us)
Async XLA Ops:
  1.9 6.0 %copy-start.4 = (bf16[8,192,128]{2,1,0:T(8,128)(2,1)}, bf16[8,192,128]{2,1,0:T(8,128)(2,1)S(1)}, u32[]{:S(2)}) copy-start(bf16[8,192,128]{2,1,0:T(8,128)(2,1)S(1)} %get-tuple-element.71.x_ref) | copy-start | bytes 1179652
  1.9 6.0 %copy-start.5 = (bf16[8,192,128]{2,1,0:T(8,128)(2,1)}, bf16[8,192,128]{2,1,0:T(8,128)(2,1)S(1)}, u32[]{:S(2)}) copy-start(bf16[8,192,128]{2,1,0:T(8,128)(2,1)S(1)} %get-tuple-element.70.c_ref) | copy-start | bytes 1179652
  2.0 12.2 %collective-permute-start.1 = (bf16[3,192,128]{2,1,0:T(8,128)(2,1)S(1)}, bf16[3,192,128]{2,1,0:T(8,128)(2,1)S(1)}, u32[]{:S(2)}, u32[]{:S(2)}) collective-permute-start(bf16[3,192,128]{2,1,0:T(8,128)(2,1)S(1)} %pad_maximum_fusion.2), channel_id=1, source_target_pairs={{4,0},{8,4},{12,8},{16,12},{20,16},{24,20},{28,24},{5,1},{9,5},{13... | collective-permute-start | bytes 442376 | tf_op jit(solution)/shard_map/ppermute | solution.py:478
  3.3 10.9 %collective-permute-start = (bf16[3,192,128]{2,1,0:T(8,128)(2,1)S(1)}, bf16[3,192,128]{2,1,0:T(8,128)(2,1)S(1)}, u32[]{:S(2)}, u32[]{:S(2)}) collective-permute-start(bf16[3,192,128]{2,1,0:T(8,128)(2,1)S(1)} %pad_maximum_fusion.1), channel_id=1, source_target_pairs={{0,4},{4,8},{8,12},{12,16},{16,20},{20,24},{24,28},{1,5},{5,9},{9,... | collective-permute-start | bytes 442376 | tf_op jit(solution)/shard_map/ppermute | solution.py:477
  14.1 11.0 %copy-start = (bf16[3,192,128]{2,1,0:T(8,128)(2,1)}, bf16[3,192,128]{2,1,0:T(8,128)(2,1)S(1)}, u32[]{:S(2)}) copy-start(bf16[3,192,128]{2,1,0:T(8,128)(2,1)S(1)} %collective-permute-done.1.bot_ref) | copy-start | bytes 442372
  14.2 11.0 %copy-start.1 = (bf16[3,192,128]{2,1,0:T(8,128)(2,1)}, bf16[3,192,128]{2,1,0:T(8,128)(2,1)S(1)}, u32[]{:S(2)}) copy-start(bf16[3,192,128]{2,1,0:T(8,128)(2,1)S(1)} %collective-permute-done.top_ref) | copy-start | bytes 442372
  14.2 0.9 copy-start.3
  15.2 10.0 %copy-start.2 = (bf16[192,128]{1,0:T(8,128)(2,1)}, bf16[192,128]{1,0:T(8,128)(2,1)S(1)}, u32[]{:S(2)}) copy-start(bf16[192,128]{1,0:T(8,128)(2,1)S(1)} %strip.1.own_ref) | copy-start | bytes 147460
  15.2 6.5 %collective-permute-start.2 = (bf16[192,128]{1,0:T(8,128)(2,1)S(1)}, bf16[192,128]{1,0:T(8,128)(2,1)S(1)}, u32[]{:S(2)}, u32[]{:S(2)}) collective-permute-start(bf16[192,128]{1,0:T(8,128)(2,1)S(1)} %strip.1.own_ref), channel_id=1, source_target_pairs={{0,1},{1,2},{2,3},{4,5},{5,6},{6,7},{8,9},{9,10},{10,11},{12,13},{... | collective-permute-start | bytes 147464 | tf_op jit(solution)/shard_map/ppermute | solution.py:511
  19.8 5.4 %collective-permute-start.3 = (bf16[192,128]{1,0:T(8,128)(2,1)S(1)}, bf16[192,128]{1,0:T(8,128)(2,1)S(1)}, u32[]{:S(2)}, u32[]{:S(2)}) collective-permute-start(bf16[192,128]{1,0:T(8,128)(2,1)S(1)} %strip.1.own_ref), channel_id=1, source_target_pairs={{1,0},{2,1},{3,2},{5,4},{6,5},{7,6},{9,8},{10,9},{11,10},{13,12},{... | collective-permute-start | bytes 147464 | tf_op jit(solution)/shard_map/ppermute | solution.py:512
  21.7 3.5 %copy-start.9 = (bf16[192,128]{1,0:T(8,128)(2,1)}, bf16[192,128]{1,0:T(8,128)(2,1)S(1)}, u32[]{:S(2)}) copy-start(bf16[192,128]{1,0:T(8,128)(2,1)S(1)} %collective-permute-done.2.left_ref) | copy-start | bytes 147460
  25.2 0.6 copy-start.10
  35.9 1.5 %collective-permute-start.4 = (f32[16,128]{1,0:T(8,128)}, f32[16,128]{1,0:T(8,128)S(1)}, u32[]{:S(2)}, u32[]{:S(2)}) collective-permute-start(f32[16,128]{1,0:T(8,128)} %get-tuple-element.24), channel_id=1, source_target_pairs={{0,1},{1,0},{2,3},{3,2},{4,5},{5,4},{6,7},{7,6},{8,9},{9,8},{10,11... | collective-permute-start | bytes 24584 | tf_op jit(solution)/shard_map/ppermute | solution.py:465
  38.7 14.7 %all-to-all-start = ((f32[16,16,128]{2,1,0:T(8,128)}), f32[16,16,128]{2,1,0:T(8,128)S(1)}, u32[]{:S(2)}, u32[]{:S(2)}) async-start(f32[16,16,128]{2,1,0:T(8,128)} %broadcast_in_dim.202), calls=%async_computation | async-start | bytes 262144 | tf_op jit(solution)/shard_map/all_to_all | solution.py:457
  53.4 0.7 copy-start.6
  72.4 3.6 %collective-permute-start.5 = (f32[1280,128]{1,0:T(8,128)}, f32[1280,128]{1,0:T(8,128)S(1)}, u32[]{:S(2)}, u32[]{:S(2)}) collective-permute-start(f32[1280,128]{1,0:T(8,128)} %get-tuple-element.32), channel_id=1, source_target_pairs={{0,1},{1,0},{2,3},{3,2},{4,5},{5,4},{6,7},{7,6},{8,9},{9,8},{10,11... | collective-permute-start | bytes 1966088 | tf_op jit(solution)/shard_map/ppermute | solution.py:465
  79.5 12.8 %copy-start.11 = (f32[16,128]{1,0:T(8,128)S(1)}, f32[16,128]{1,0:T(8,128)}, u32[]{:S(2)}) copy-start(f32[16,128]{1,0:T(8,128)} %get-tuple-element.33) | copy-start | bytes 24580
  79.5 12.3 %all-to-all-start.1 = ((f16[16,80,128]{2,1,0:T(8,128)(2,1)}), f16[16,80,128]{2,1,0:T(8,128)(2,1)S(1)}, u32[]{:S(2)}, u32[]{:S(2)}) async-start(f16[16,80,128]{2,1,0:T(8,128)(2,1)} %select_convert_fusion), calls=%async_computation.1 | async-start | bytes 655360 | tf_op jit(solution)/shard_map/all_to_all | solution.py:457
  83.2 22.8 %copy-start.8 = (bf16[8,192,128]{2,1,0:T(8,128)(2,1)S(1)}, bf16[8,192,128]{2,1,0:T(8,128)(2,1)}, u32[]{:S(2)}) copy-start(bf16[8,192,128]{2,1,0:T(8,128)(2,1)} %get-tuple-element.29) | copy-start | bytes 1179652
  83.2 23.7 %copy-start.7 = (bf16[8,192,128]{2,1,0:T(8,128)(2,1)S(1)}, bf16[8,192,128]{2,1,0:T(8,128)(2,1)}, u32[]{:S(2)}) copy-start(bf16[8,192,128]{2,1,0:T(8,128)(2,1)} %get-tuple-element.30) | copy-start | bytes 1179652
  92.3 8.5 %collective-permute-start.6 = (f32[96,128]{1,0:T(8,128)S(1)}, f32[96,128]{1,0:T(8,128)S(1)}, u32[]{:S(2)}, u32[]{:S(2)}) collective-permute-start(f32[96,128]{1,0:T(8,128)S(1)} %pad_maximum_fusion.5), channel_id=1, source_target_pairs={{0,128},{32,160},{64,192},{96,224},{128,0},{160,32},{192,64},{224,... | collective-permute-start | bytes 147464 | tf_op jit(solution)/shard_map/ppermute | solution.py:592
  100.8 4.7 %collective-permute-start.7 = (f32[112,128]{1,0:T(8,128)S(1)}, f32[112,128]{1,0:T(8,128)S(1)}, u32[]{:S(2)}, u32[]{:S(2)}) collective-permute-start(f32[112,128]{1,0:T(8,128)S(1)} %pad_maximum_fusion.4), channel_id=1, source_target_pairs={{0,64},{32,96},{64,0},{96,32},{128,192},{160,224},{192,128},{224,1... | collective-permute-start | bytes 172040 | tf_op jit(solution)/shard_map/ppermute | solution.py:592
  105.6 3.5 %collective-permute-start.8 = (f32[144,128]{1,0:T(8,128)S(1)}, f32[144,128]{1,0:T(8,128)S(1)}, u32[]{:S(2)}, u32[]{:S(2)}) collective-permute-start(f32[144,128]{1,0:T(8,128)S(1)} %pad_maximum_fusion.3), channel_id=1, source_target_pairs={{0,32},{32,0},{64,96},{96,64},{128,160},{160,128},{192,224},{224,1... | collective-permute-start | bytes 221192 | tf_op jit(solution)/shard_map/ppermute | solution.py:592
  112.1 11.2 %all-to-all-start.2 = ((f16[16,80,128]{2,1,0:T(8,128)(2,1)}), f16[16,80,128]{2,1,0:T(8,128)(2,1)S(1)}, u32[]{:S(2)}, u32[]{:S(2)}) async-start(f16[16,80,128]{2,1,0:T(8,128)(2,1)} %broadcast_in_dim.231), calls=%async_computation.2 | async-start | bytes 655360 | tf_op jit(solution)/shard_map/all_to_all | solution.py:457
  123.3 7.7 %collective-permute-start.9 = (f16[16,80,128]{2,1,0:T(8,128)(2,1)S(1)}, f16[16,80,128]{2,1,0:T(8,128)(2,1)S(1)}, u32[]{:S(2)}, u32[]{:S(2)}) collective-permute-start(f16[16,80,128]{2,1,0:T(8,128)(2,1)S(1)} %all-to-all-done.2), channel_id=1, source_target_pairs={{0,1},{1,0},{2,3},{3,2},{4,5},{5,4},{6,7},{7,6},{8,9},{9,8},{10,11... | collective-permute-start | bytes 983048 | tf_op jit(solution)/shard_map/ppermute | solution.py:465

commit v13 on v11

--- a/solution.py
+++ b/solution.py
@@ -414,6 +414,22 @@
             copy.wait()
 
 
+def scale_kernel(x_ref, out_ref):
+    def exponent(v):
+        top = jnp.max(jnp.max(jnp.abs(v), axis=0, keepdims=True), axis=1, keepdims=True)
+        return jnp.ceil(jnp.log2(jnp.maximum(jnp.broadcast_to(top, (8, LANES)), 1e-30)))
+
+    row = lax.broadcasted_iota(jnp.int32, (8, LANES), 0)
+    rest = x_ref[72:80, :]
+    e_big = exponent(x_ref[:72, :])
+    e_small = exponent(jnp.where(row < 2, rest, 0.0))
+    factor = jnp.exp2(-e_big)
+    for i in range(9):
+        out_ref[8 * i : 8 * i + 8, :] = x_ref[8 * i : 8 * i + 8, :] * factor
+    tail = jnp.where(row < 5, e_big, e_small)
+    out_ref[72:80, :] = jnp.where(row < 2, rest * jnp.exp2(-e_small), tail)
+
+
 def to_half(v, big, small):
     row = lax.broadcasted_iota(jnp.int32, (1, PACK, 1), 1)
     e_big, e_small = (
@@ -597,7 +613,14 @@
     vecs = vecs.reshape(8, 2048)
     grad_wexc = jnp.einsum("bs,be->se", vecs[:, 1536:1584], vecs[:, 768:1536], precision=HIGH)
     grad_wsq = jnp.einsum("be,bs->es", vecs[:, :768], vecs[:, 1664:1712], precision=HIGH)
-    same = gathered(to_half(total[None], jnp.abs(total[None, :72]), jnp.abs(total[None, 72:74]))[0])
+    scaled = pl.pallas_call(
+        scale_kernel,
+        out_shape=shape(PACK, LANES),
+        compiler_params=params(False, 4096),
+        cost_estimate=cost(1e5, 1e5),
+        name="scale",
+    )(total)
+    same = gathered(scaled.astype(jnp.float16))
     other = partner(same)
     even = core[0] == 0
     every = jnp.stack(

time: 133 us -> 130 us (0.977)
  between operations: 2.61 us -> 1.12 us
where the time goes in v13:
time: 130 us; the launch traced here: 129 us
  starting transfers between devices  39.6 us (30%)
  Pallas kernels  34.8 us (27%)
  waiting for transfers between devices  26.5 us (20%)
  blocking collectives  11.6 us (9%)
  local copies, waits for them, and re-layouts  9.21 us (7%)
  other arithmetic  4.53 us (3%)
  matrix products  1.98 us (2%)
    pallas_call x1, Pallas kernels, local(): pl.pallas_call(backward_kernel, grid=(STEPS,), in_specs=[pl.BlockSpec(mem...  18.3 us
    all_to_all x2, waiting for transfers between devices, exchanged(): return lax.all_to_all(blocks, RC, 0, 0, tiled=True, axis_index_groups=CHIPS)  13.6 us
    all_to_all x1, blocking collectives, exchanged(): return lax.all_to_all(blocks, RC, 0, 0, tiled=True, axis_index_groups=CHIPS)  11.6 us
    all_to_all x2, starting transfers between devices, exchanged(): return lax.all_to_all(blocks, RC, 0, 0, tiled=True, axis_index_groups=CHIPS)  11.5 us
    pallas_call x1, Pallas kernels, local(): pl.pallas_call(forward_kernel, grid=(STEPS,), in_specs=[halo, halo, edge,...  10.1 us
    ppermute x3, starting transfers between devices, local(): lax.ppermute(jnp.concatenate([total, vecs.reshape(16 * members, LANES)],...  8.63 us
    ppermute x3, starting transfers between devices, partner(): return lax.ppermute(block, 'col', [(i, i ^ 1) for i in range(4)])  7.06 us
    ppermute x3, waiting for transfers between devices, local(): lax.ppermute(jnp.concatenate([total, vecs.reshape(16 * members, LANES)],...  6.24 us
  transfers between devices with their start and end apart: 12, of which 8 were waited for; matrix products, arithmetic and copies ran while one was open for 4% of the time, Pallas kernels for 5%

profile of v13, /device:TPU:1, one launch (start us, length us, event | category | flops | bytes accessed | tf_op | source)
XLA Modules:
  0.0 129.3 jit_solution(13417516901421695234)
XLA Ops:
  0.6 1.3 copy_bitcast_fusion
  2.0 1.3 collective-permute-start.1
  3.3 4.6 %collective-permute-start = (bf16[3,192,128]{2,1,0:T(8,128)(2,1)S(1)}, bf16[3,192,128]{2,1,0:T(8,128)(2,1)S(1)}, u32[]{:S(2)}, u32[]{:S(2)}) collective-permute-start(bf16[3,192,128]{2,1,0:T(8,128)(2,1)S(1)} %pad_maximum_fusion.1), channel_id=1, source_target_pairs={{0,4},{4,8},{8,12},{12,16},{16,20},{20,24},{24,28},{1,5},{5,9},{9,... | collective-permute-start | bytes 442376 | tf_op jit(solution)/shard_map/ppermute | solution.py:489
  7.9 6.2 %expand.1 = (bf16[192,1024]{1,0:T(8,128)(2,1)}, f32[8,128]{1,0:T(8,128)}, bf16[192,128]{1,0:T(8,128)(2,1)}, f32[768,1024]{1,0:T(8,128)}, bf16[768,1024]{1,0:T(8,128)(2,1)}, /*index=5*/f32[768,1024]{1,0:T(8,128)}) custom-call(bf16[8,192,128]{2,1,0:T(8,128)(2,1)} %copy-done.4, bf16[8,192,128]{2,1,0:T(8,128)(2,1)} %copy-done.5, f32[1,192]{1,0:T(1,128)} %bitcast.76, ...), custom_call_target="tpu_custom_call" | custom-call | flops 600000000 | bytes 10000000 | tf_op jit(solution)/shard_map/expand/pallas_call | solution.py:501
  14.2 0.8 copy-done.3
  15.2 4.6 %collective-permute-start.2 = (bf16[192,128]{1,0:T(8,128)(2,1)S(1)}, bf16[192,128]{1,0:T(8,128)(2,1)S(1)}, u32[]{:S(2)}, u32[]{:S(2)}) collective-permute-start(bf16[192,128]{1,0:T(8,128)(2,1)S(1)} %strip.1.own_ref), channel_id=1, source_target_pairs={{0,1},{1,2},{2,3},{4,5},{5,6},{6,7},{8,9},{9,10},{10,11},{12,13},{... | collective-permute-start | bytes 147464 | tf_op jit(solution)/shard_map/ppermute | solution.py:523
  19.8 1.9 %collective-permute-start.3 = (bf16[192,128]{1,0:T(8,128)(2,1)S(1)}, bf16[192,128]{1,0:T(8,128)(2,1)S(1)}, u32[]{:S(2)}, u32[]{:S(2)}) collective-permute-start(bf16[192,128]{1,0:T(8,128)(2,1)S(1)} %strip.1.own_ref), channel_id=1, source_target_pairs={{1,0},{2,1},{3,2},{5,4},{6,5},{7,6},{9,8},{10,9},{11,10},{13,12},{... | collective-permute-start | bytes 147464 | tf_op jit(solution)/shard_map/ppermute | solution.py:524
  21.7 3.4 %collective-permute-done.3.right_ref = bf16[192,128]{1,0:T(8,128)(2,1)S(1)} collective-permute-done((bf16[192,128]{1,0:T(8,128)(2,1)S(1)}, bf16[192,128]{1,0:T(8,128)(2,1)S(1)}, u32[]{:S(2)}, u32[]{:S(2)}) %collective-permute-start.3) | collective-permute-done | bytes 49184 | tf_op jit(solution)/shard_map/ppermute | solution.py:524
  25.8 10.1 %forward.1 = (f32[768,1408]{1,0:T(8,128)}, f32[16,128]{1,0:T(8,128)}) custom-call(bf16[3,192,128]{2,1,0:T(8,128)(2,1)} %copy-done.1, bf16[3,192,128]{2,1,0:T(8,128)(2,1)} %copy-done, bf16[192,128]{1,0:T(8,128)(2,1)} %copy-done.2, bf16[192,128]{1,0:T(8,128)(2,1)} %copy-done.9, bf16[192,128]{1,0:T(8,128)(2,1)} %copy-done.10, f32[1,192]{1,0:T(1,128)} %bitcast.77, ...), custom_call_target="tpu_custom_call" | custom-call | flops 200000000 | bytes 12000000 | tf_op jit(solution)/shard_map/forward/pallas_call | solution.py:534
  36.0 1.3 %collective-permute-done.4 = f32[16,128]{1,0:T(8,128)S(1)} collective-permute-done((f32[16,128]{1,0:T(8,128)}, f32[16,128]{1,0:T(8,128)S(1)}, u32[]{:S(2)}, u32[]{:S(2)}) %collective-permute-start.4) | collective-permute-done | bytes 8224 | tf_op jit(solution)/shard_map/ppermute | solution.py:477
  37.4 0.7 add.31
  38.7 8.0 %all-to-all-start = ((f32[16,16,128]{2,1,0:T(8,128)}), f32[16,16,128]{2,1,0:T(8,128)S(1)}, u32[]{:S(2)}, u32[]{:S(2)}) async-start(f32[16,16,128]{2,1,0:T(8,128)} %broadcast_in_dim.120), calls=%async_computation | async-start | bytes 262144 | tf_op jit(solution)/shard_map/all_to_all | solution.py:469
  47.4 6.0 %all-to-all-done.parts_ref = f32[16,16,128]{2,1,0:T(8,128)S(1)} async-done(((f32[16,16,128]{2,1,0:T(8,128)}), f32[16,16,128]{2,1,0:T(8,128)S(1)}, u32[]{:S(2)}, u32[]{:S(2)}) %all-to-all-start) | async-done | bytes 131104 | tf_op jit(solution)/shard_map/all_to_all | solution.py:469
  54.1 18.3 %backward.1 = (bf16[8,192,128]{2,1,0:T(8,128)(2,1)}, bf16[8,192,128]{2,1,0:T(8,128)(2,1)}, f32[1280,128]{1,0:T(8,128)}, f32[1280,128]{1,0:T(8,128)}, f32[16,128]{1,0:T(8,128)}) custom-call(s32[1]{0:T(128)} %bitcast.core_ref, f32[16,16,128]{2,1,0:T(8,128)} %copy-done.6, f32[48,768]{1,0:T(8,128)} %bitcast.61, f32[48,768]{1,0:T(8,128)} %wexc_ref.1, ...), custom_call_target="tpu_custom_call" | custom-call | flops 1500000000 | bytes 16000000 | tf_op jit(solution)/shard_map/backward/pallas_call | solution.py:557
  72.4 1.7 %collective-permute-start.5 = (f32[1280,128]{1,0:T(8,128)}, f32[1280,128]{1,0:T(8,128)S(1)}, u32[]{:S(2)}, u32[]{:S(2)}) collective-permute-start(f32[1280,128]{1,0:T(8,128)} %get-tuple-element.32), channel_id=1, source_target_pairs={{0,1},{1,0},{2,3},{3,2},{4,5},{5,4},{6,7},{7,6},{8,9},{9,8},{10,11... | collective-permute-start | bytes 1966088 | tf_op jit(solution)/shard_map/ppermute | solution.py:477
  74.1 1.9 %collective-permute-done.5 = f32[1280,128]{1,0:T(8,128)S(1)} collective-permute-done((f32[1280,128]{1,0:T(8,128)}, f32[1280,128]{1,0:T(8,128)S(1)}, u32[]{:S(2)}, u32[]{:S(2)}) %collective-permute-start.5) | collective-permute-done | bytes 655392 | tf_op jit(solution)/shard_map/ppermute | solution.py:477
  76.0 1.2 add.33
  78.0 11.6 %all_to_all.15 = f16[16,80,128]{2,1,0:T(8,128)(2,1)S(1)} all-to-all(f16[16,80,128]{2,1,0:T(8,128)(2,1)S(1)} %select_convert_fusion), channel_id=1, replica_groups={{0,2,4,6,8,10,12,14,16,18,20,22,24,26,28,30},{1,3,5,7,9,11,13,15,17,19,..., dimensions={0} | all-to-all | bytes 655360 | tf_op jit(solution)/shard_map/all_to_all | solution.py:469
  89.9 7.0 %collective-permute-start.6 = (f32[96,128]{1,0:T(8,128)S(1)}, f32[96,128]{1,0:T(8,128)S(1)}, u32[]{:S(2)}, u32[]{:S(2)}) collective-permute-start(f32[96,128]{1,0:T(8,128)S(1)} %pad_maximum_fusion.5), channel_id=1, source_target_pairs={{0,128},{32,160},{64,192},{96,224},{128,0},{160,32},{192,64},{224,... | collective-permute-start | bytes 147464 | tf_op jit(solution)/shard_map/ppermute | solution.py:601
  96.9 1.5 %collective-permute-done.6 = f32[96,128]{1,0:T(8,128)S(1)} collective-permute-done((f32[96,128]{1,0:T(8,128)S(1)}, f32[96,128]{1,0:T(8,128)S(1)}, u32[]{:S(2)}, u32[]{:S(2)}) %collective-permute-start.6) | collective-permute-done | bytes 49184 | tf_op jit(solution)/shard_map/ppermute | solution.py:601
  98.4 1.5 %collective-permute-start.7 = (f32[112,128]{1,0:T(8,128)S(1)}, f32[112,128]{1,0:T(8,128)S(1)}, u32[]{:S(2)}, u32[]{:S(2)}) collective-permute-start(f32[112,128]{1,0:T(8,128)S(1)} %pad_maximum_fusion.4), channel_id=1, source_target_pairs={{0,64},{32,96},{64,0},{96,32},{128,192},{160,224},{192,128},{224,1... | collective-permute-start | bytes 172040 | tf_op jit(solution)/shard_map/ppermute | solution.py:601
  100.0 3.6 %collective-permute-done.7 = f32[112,128]{1,0:T(8,128)S(1)} collective-permute-done((f32[112,128]{1,0:T(8,128)S(1)}, f32[112,128]{1,0:T(8,128)S(1)}, u32[]{:S(2)}, u32[]{:S(2)}) %collective-permute-start.7) | collective-permute-done | bytes 57376 | tf_op jit(solution)/shard_map/ppermute | solution.py:601
  103.7 1.0 copy.19
  104.7 1.0 copy.20
  105.8 1.2 collective-permute-done.8
  107.1 0.8 broadcast_in_dim.137
  107.8 3.5 %all-to-all-start.2 = ((f16[16,80,128]{2,1,0:T(8,128)(2,1)}), f16[16,80,128]{2,1,0:T(8,128)(2,1)S(1)}, u32[]{:S(2)}, u32[]{:S(2)}) async-start(f16[16,80,128]{2,1,0:T(8,128)(2,1)} %broadcast_in_dim.137), calls=%async_computation.2 | async-start | bytes 655360 | tf_op jit(solution)/shard_map/all_to_all | solution.py:469
  111.4 7.6 %all-to-all-done.2 = f16[16,80,128]{2,1,0:T(8,128)(2,1)S(1)} async-done(((f16[16,80,128]{2,1,0:T(8,128)(2,1)}), f16[16,80,128]{2,1,0:T(8,128)(2,1)S(1)}, u32[]{:S(2)}, u32[]{:S(2)}) %all-to-all-start.2) | async-done | bytes 327712 | tf_op jit(solution)/shard_map/all_to_all | solution.py:469
  119.0 5.3 %collective-permute-start.9 = (f16[16,80,128]{2,1,0:T(8,128)(2,1)S(1)}, f16[16,80,128]{2,1,0:T(8,128)(2,1)S(1)}, u32[]{:S(2)}, u32[]{:S(2)}) collective-permute-start(f16[16,80,128]{2,1,0:T(8,128)(2,1)S(1)} %all-to-all-done.2), channel_id=1, source_target_pairs={{0,1},{1,0},{2,3},{3,2},{4,5},{5,4},{6,7},{7,6},{8,9},{9,8},{10,11... | collective-permute-start | bytes 983048 | tf_op jit(solution)/shard_map/ppermute | solution.py:477
  124.3 1.0 fusion.3
  125.3 1.0 fusion.1
  127.0 1.1 slice_bitcast_fusion
  (79 shorter events, 6.4 us)
Async XLA Ops:
  1.9 6.0 %copy-start.4 = (bf16[8,192,128]{2,1,0:T(8,128)(2,1)}, bf16[8,192,128]{2,1,0:T(8,128)(2,1)S(1)}, u32[]{:S(2)}) copy-start(bf16[8,192,128]{2,1,0:T(8,128)(2,1)S(1)} %get-tuple-element.69.x_ref) | copy-start | bytes 1179652
  1.9 6.0 %copy-start.5 = (bf16[8,192,128]{2,1,0:T(8,128)(2,1)}, bf16[8,192,128]{2,1,0:T(8,128)(2,1)S(1)}, u32[]{:S(2)}) copy-start(bf16[8,192,128]{2,1,0:T(8,128)(2,1)S(1)} %get-tuple-element.68.c_ref) | copy-start | bytes 1179652
  2.0 12.1 %collective-permute-start.1 = (bf16[3,192,128]{2,1,0:T(8,128)(2,1)S(1)}, bf16[3,192,128]{2,1,0:T(8,128)(2,1)S(1)}, u32[]{:S(2)}, u32[]{:S(2)}) collective-permute-start(bf16[3,192,128]{2,1,0:T(8,128)(2,1)S(1)} %pad_maximum_fusion.2), channel_id=1, source_target_pairs={{4,0},{8,4},{12,8},{16,12},{20,16},{24,20},{28,24},{5,1},{9,5},{13... | collective-permute-start | bytes 442376 | tf_op jit(solution)/shard_map/ppermute | solution.py:490
  3.3 10.8 %collective-permute-start = (bf16[3,192,128]{2,1,0:T(8,128)(2,1)S(1)}, bf16[3,192,128]{2,1,0:T(8,128)(2,1)S(1)}, u32[]{:S(2)}, u32[]{:S(2)}) collective-permute-start(bf16[3,192,128]{2,1,0:T(8,128)(2,1)S(1)} %pad_maximum_fusion.1), channel_id=1, source_target_pairs={{0,4},{4,8},{8,12},{12,16},{16,20},{20,24},{24,28},{1,5},{5,9},{9,... | collective-permute-start | bytes 442376 | tf_op jit(solution)/shard_map/ppermute | solution.py:489
  14.1 11.0 %copy-start = (bf16[3,192,128]{2,1,0:T(8,128)(2,1)}, bf16[3,192,128]{2,1,0:T(8,128)(2,1)S(1)}, u32[]{:S(2)}) copy-start(bf16[3,192,128]{2,1,0:T(8,128)(2,1)S(1)} %collective-permute-done.1.bot_ref) | copy-start | bytes 442372
  14.2 11.0 %copy-start.1 = (bf16[3,192,128]{2,1,0:T(8,128)(2,1)}, bf16[3,192,128]{2,1,0:T(8,128)(2,1)S(1)}, u32[]{:S(2)}) copy-start(bf16[3,192,128]{2,1,0:T(8,128)(2,1)S(1)} %collective-permute-done.top_ref) | copy-start | bytes 442372
  14.2 0.9 copy-start.3
  15.2 10.0 %copy-start.2 = (bf16[192,128]{1,0:T(8,128)(2,1)}, bf16[192,128]{1,0:T(8,128)(2,1)S(1)}, u32[]{:S(2)}) copy-start(bf16[192,128]{1,0:T(8,128)(2,1)S(1)} %strip.1.own_ref) | copy-start | bytes 147460
  15.2 6.5 %collective-permute-start.2 = (bf16[192,128]{1,0:T(8,128)(2,1)S(1)}, bf16[192,128]{1,0:T(8,128)(2,1)S(1)}, u32[]{:S(2)}, u32[]{:S(2)}) collective-permute-start(bf16[192,128]{1,0:T(8,128)(2,1)S(1)} %strip.1.own_ref), channel_id=1, source_target_pairs={{0,1},{1,2},{2,3},{4,5},{5,6},{6,7},{8,9},{9,10},{10,11},{12,13},{... | collective-permute-start | bytes 147464 | tf_op jit(solution)/shard_map/ppermute | solution.py:523
  19.8 5.4 %collective-permute-start.3 = (bf16[192,128]{1,0:T(8,128)(2,1)S(1)}, bf16[192,128]{1,0:T(8,128)(2,1)S(1)}, u32[]{:S(2)}, u32[]{:S(2)}) collective-permute-start(bf16[192,128]{1,0:T(8,128)(2,1)S(1)} %strip.1.own_ref), channel_id=1, source_target_pairs={{1,0},{2,1},{3,2},{5,4},{6,5},{7,6},{9,8},{10,9},{11,10},{13,12},{... | collective-permute-start | bytes 147464 | tf_op jit(solution)/shard_map/ppermute | solution.py:524
  21.7 3.5 %copy-start.9 = (bf16[192,128]{1,0:T(8,128)(2,1)}, bf16[192,128]{1,0:T(8,128)(2,1)S(1)}, u32[]{:S(2)}) copy-start(bf16[192,128]{1,0:T(8,128)(2,1)S(1)} %collective-permute-done.2.left_ref) | copy-start | bytes 147460
  25.2 0.6 copy-start.10
  35.9 1.5 %collective-permute-start.4 = (f32[16,128]{1,0:T(8,128)}, f32[16,128]{1,0:T(8,128)S(1)}, u32[]{:S(2)}, u32[]{:S(2)}) collective-permute-start(f32[16,128]{1,0:T(8,128)} %get-tuple-element.24), channel_id=1, source_target_pairs={{0,1},{1,0},{2,3},{3,2},{4,5},{5,4},{6,7},{7,6},{8,9},{9,8},{10,11... | collective-permute-start | bytes 24584 | tf_op jit(solution)/shard_map/ppermute | solution.py:477
  38.7 14.7 %all-to-all-start = ((f32[16,16,128]{2,1,0:T(8,128)}), f32[16,16,128]{2,1,0:T(8,128)S(1)}, u32[]{:S(2)}, u32[]{:S(2)}) async-start(f32[16,16,128]{2,1,0:T(8,128)} %broadcast_in_dim.120), calls=%async_computation | async-start | bytes 262144 | tf_op jit(solution)/shard_map/all_to_all | solution.py:469
  53.4 0.7 copy-start.6
  72.4 3.6 %collective-permute-start.5 = (f32[1280,128]{1,0:T(8,128)}, f32[1280,128]{1,0:T(8,128)S(1)}, u32[]{:S(2)}, u32[]{:S(2)}) collective-permute-start(f32[1280,128]{1,0:T(8,128)} %get-tuple-element.32), channel_id=1, source_target_pairs={{0,1},{1,0},{2,3},{3,2},{4,5},{5,4},{6,7},{7,6},{8,9},{9,8},{10,11... | collective-permute-start | bytes 1966088 | tf_op jit(solution)/shard_map/ppermute | solution.py:477
  77.5 12.4 %copy-start.11 = (f32[16,128]{1,0:T(8,128)S(1)}, f32[16,128]{1,0:T(8,128)}, u32[]{:S(2)}) copy-start(f32[16,128]{1,0:T(8,128)} %get-tuple-element.33) | copy-start | bytes 24580
  77.9 25.8 %copy-start.8 = (bf16[8,192,128]{2,1,0:T(8,128)(2,1)S(1)}, bf16[8,192,128]{2,1,0:T(8,128)(2,1)}, u32[]{:S(2)}) copy-start(bf16[8,192,128]{2,1,0:T(8,128)(2,1)} %get-tuple-element.29) | copy-start | bytes 1179652
  89.5 15.2 %copy-start.7 = (bf16[8,192,128]{2,1,0:T(8,128)(2,1)S(1)}, bf16[8,192,128]{2,1,0:T(8,128)(2,1)}, u32[]{:S(2)}) copy-start(bf16[8,192,128]{2,1,0:T(8,128)(2,1)} %get-tuple-element.30) | copy-start | bytes 1179652
  89.9 8.5 %collective-permute-start.6 = (f32[96,128]{1,0:T(8,128)S(1)}, f32[96,128]{1,0:T(8,128)S(1)}, u32[]{:S(2)}, u32[]{:S(2)}) collective-permute-start(f32[96,128]{1,0:T(8,128)S(1)} %pad_maximum_fusion.5), channel_id=1, source_target_pairs={{0,128},{32,160},{64,192},{96,224},{128,0},{160,32},{192,64},{224,... | collective-permute-start | bytes 147464 | tf_op jit(solution)/shard_map/ppermute | solution.py:601
  98.4 5.1 %collective-permute-start.7 = (f32[112,128]{1,0:T(8,128)S(1)}, f32[112,128]{1,0:T(8,128)S(1)}, u32[]{:S(2)}, u32[]{:S(2)}) collective-permute-start(f32[112,128]{1,0:T(8,128)S(1)} %pad_maximum_fusion.4), channel_id=1, source_target_pairs={{0,64},{32,96},{64,0},{96,32},{128,192},{160,224},{192,128},{224,1... | collective-permute-start | bytes 172040 | tf_op jit(solution)/shard_map/ppermute | solution.py:601
  103.6 3.3 %collective-permute-start.8 = (f32[144,128]{1,0:T(8,128)S(1)}, f32[144,128]{1,0:T(8,128)S(1)}, u32[]{:S(2)}, u32[]{:S(2)}) collective-permute-start(f32[144,128]{1,0:T(8,128)S(1)} %pad_maximum_fusion.3), channel_id=1, source_target_pairs={{0,32},{32,0},{64,96},{96,64},{128,160},{160,128},{192,224},{224,1... | collective-permute-start | bytes 221192 | tf_op jit(solution)/shard_map/ppermute | solution.py:601
  107.8 11.2 %all-to-all-start.2 = ((f16[16,80,128]{2,1,0:T(8,128)(2,1)}), f16[16,80,128]{2,1,0:T(8,128)(2,1)S(1)}, u32[]{:S(2)}, u32[]{:S(2)}) async-start(f16[16,80,128]{2,1,0:T(8,128)(2,1)} %broadcast_in_dim.137), calls=%async_computation.2 | async-start | bytes 655360 | tf_op jit(solution)/shard_map/all_to_all | solution.py:469
  119.0 7.3 %collective-permute-start.9 = (f16[16,80,128]{2,1,0:T(8,128)(2,1)S(1)}, f16[16,80,128]{2,1,0:T(8,128)(2,1)S(1)}, u32[]{:S(2)}, u32[]{:S(2)}) collective-permute-start(f16[16,80,128]{2,1,0:T(8,128)(2,1)S(1)} %all-to-all-done.2), channel_id=1, source_target_pairs={{0,1},{1,0},{2,3},{3,2},{4,5},{5,4},{6,7},{7,6},{8,9},{9,8},{10,11... | collective-permute-start | bytes 983048 | tf_op jit(solution)/shard_map/ppermute | solution.py:477

commit v14 on v13

--- a/solution.py
+++ b/solution.py
@@ -414,6 +414,19 @@
             copy.wait()
 
 
+def spread_kernel(own_ref, other_ref, out_ref):
+    total = own_ref[...] + other_ref[...]
+    for q in range(PARTS // 2):
+        out_ref[q] = total
+
+
+def taps_kernel(rows_ref, out_ref):
+    for t in range(9):
+        for n in range(BLOCKS):
+            q = BLOCKS * t + n
+            out_ref[t : t + 1, slab(n)] = rows_ref[q // 2, q % 2 : q % 2 + 1, :]
+
+
 def scale_kernel(x_ref, out_ref):
     def exponent(v):
         top = jnp.max(jnp.max(jnp.abs(v), axis=0, keepdims=True), axis=1, keepdims=True)
@@ -552,7 +565,15 @@
         name="forward",
     )(top, bot, own, left, right, gain, w_expand, taps, hid, gg)
 
-    sums = gathered(sums + partner(sums))
+    sums = exchanged(
+        pl.pallas_call(
+            spread_kernel,
+            out_shape=shape(PARTS // 2, 16, LANES),
+            compiler_params=params(False, 4096),
+            cost_estimate=cost(1e5, 1e5),
+            name="spread",
+        )(sums, partner(sums))
+    )
     core = (col % 2).astype(jnp.int32).reshape(1)
     out, gin, keep, send, vec = pl.pallas_call(
         backward_kernel,
@@ -628,13 +649,21 @@
     ).reshape(PARTS, PACK, LANES).astype(F32)
     big = (every[:, :72] * jnp.exp2(every[:, 74:75])).reshape(2, CH // 8, BLOCKS, 8, LANES)
     big = big.transpose(0, 1, 3, 2, 4).reshape(2, CH, EX)
-    small = (every[:, 72:74] * jnp.exp2(every[:, 77:78])).reshape(8192)
+    small = every[:, 72:74] * jnp.exp2(every[:, 77:78])
+    grad_taps = pl.pallas_call(
+        taps_kernel,
+        out_shape=shape(9, EX),
+        compiler_params=params(False, 4096),
+        cost_estimate=cost(1e5, 1e5),
+        name="taps",
+    )(small)
+    small = small.reshape(8192)
     return (
         out.transpose(1, 0, 2)[None],
         gin.transpose(1, 0, 2)[None],
         small[6912:7104],
         big[0],
-        small[:6912].reshape(9, 768).T,
+        grad_taps.T,
         grad_wsq,
         grad_wexc,
         big[1].T,

time: 130 us -> 130 us (level)
  Pallas kernels: 34.8 us -> 36.1 us
    pallas_call x0 -> x2, Pallas kernels: none -> 1.3 us  [the longest x1 0.66 us: local(): pl.pallas_call(spread_kernel, out_shape=shape(PARTS // 2, 16, LANES), com...]
    unnamed x26 -> x28, local copies, waits for them, and re-layouts: 4.16 us -> 4.85 us
where the time goes in v14:
time: 130 us; the launch traced here: 129 us
  starting transfers between devices  39.6 us (30%)
  Pallas kernels  36.1 us (28%)
  waiting for transfers between devices  26.5 us (20%)
  blocking collectives  11.6 us (9%)
  local copies, waits for them, and re-layouts  8.59 us (7%)
  other arithmetic  3.82 us (3%)
  matrix products  1.98 us (2%)
    pallas_call x1, Pallas kernels, local(): pl.pallas_call(backward_kernel, grid=(STEPS,), in_specs=[pl.BlockSpec(mem...  18.3 us
    all_to_all x2, waiting for transfers between devices, exchanged(): return lax.all_to_all(blocks, RC, 0, 0, tiled=True, axis_index_groups=CHIPS)  13.6 us
    all_to_all x2, starting transfers between devices, exchanged(): return lax.all_to_all(blocks, RC, 0, 0, tiled=True, axis_index_groups=CHIPS)  11.6 us
    all_to_all x1, blocking collectives, exchanged(): return lax.all_to_all(blocks, RC, 0, 0, tiled=True, axis_index_groups=CHIPS)  11.6 us
    pallas_call x1, Pallas kernels, local(): pl.pallas_call(forward_kernel, grid=(STEPS,), in_specs=[halo, halo, edge,...  10.1 us
    ppermute x3, starting transfers between devices, local(): lax.ppermute(jnp.concatenate([total, vecs.reshape(16 * members, LANES)],...  8.63 us
    ppermute x3, starting transfers between devices, partner(): return lax.ppermute(block, 'col', [(i, i ^ 1) for i in range(4)])  7.05 us
    ppermute x3, waiting for transfers between devices, local(): lax.ppermute(jnp.concatenate([total, vecs.reshape(16 * members, LANES)],...  6.24 us
  transfers between devices with their start and end apart: 12, of which 8 were waited for; matrix products, arithmetic and copies ran while one was open for 4% of the time, Pallas kernels for 5%

profile of v14, /device:TPU:1, one launch (start us, length us, event | category | flops | bytes accessed | tf_op | source)
XLA Modules:
  0.0 129.3 jit_solution(11122352597701267165)
XLA Ops:
  0.6 1.3 copy_bitcast_fusion
  2.0 1.3 collective-permute-start.1
  3.3 4.6 %collective-permute-start = (bf16[3,192,128]{2,1,0:T(8,128)(2,1)S(1)}, bf16[3,192,128]{2,1,0:T(8,128)(2,1)S(1)}, u32[]{:S(2)}, u32[]{:S(2)}) collective-permute-start(bf16[3,192,128]{2,1,0:T(8,128)(2,1)S(1)} %pad_maximum_fusion.1), channel_id=1, source_target_pairs={{0,4},{4,8},{8,12},{12,16},{16,20},{20,24},{24,28},{1,5},{5,9},{9,... | collective-permute-start | bytes 442376 | tf_op jit(solution)/shard_map/ppermute | solution.py:502
  7.9 6.2 %expand.1 = (bf16[192,1024]{1,0:T(8,128)(2,1)}, f32[8,128]{1,0:T(8,128)}, bf16[192,128]{1,0:T(8,128)(2,1)}, f32[768,1024]{1,0:T(8,128)}, bf16[768,1024]{1,0:T(8,128)(2,1)}, /*index=5*/f32[768,1024]{1,0:T(8,128)}) custom-call(bf16[8,192,128]{2,1,0:T(8,128)(2,1)} %copy-done.5, bf16[8,192,128]{2,1,0:T(8,128)(2,1)} %copy-done.6, f32[1,192]{1,0:T(1,128)} %bitcast.76, ...), custom_call_target="tpu_custom_call" | custom-call | flops 600000000 | bytes 10000000 | tf_op jit(solution)/shard_map/expand/pallas_call | solution.py:514
  14.1 0.8 copy-done.3
  15.2 4.6 %collective-permute-start.2 = (bf16[192,128]{1,0:T(8,128)(2,1)S(1)}, bf16[192,128]{1,0:T(8,128)(2,1)S(1)}, u32[]{:S(2)}, u32[]{:S(2)}) collective-permute-start(bf16[192,128]{1,0:T(8,128)(2,1)S(1)} %strip.1.own_ref), channel_id=1, source_target_pairs={{0,1},{1,2},{2,3},{4,5},{5,6},{6,7},{8,9},{9,10},{10,11},{12,13},{... | collective-permute-start | bytes 147464 | tf_op jit(solution)/shard_map/ppermute | solution.py:536
  19.7 1.9 %collective-permute-start.3 = (bf16[192,128]{1,0:T(8,128)(2,1)S(1)}, bf16[192,128]{1,0:T(8,128)(2,1)S(1)}, u32[]{:S(2)}, u32[]{:S(2)}) collective-permute-start(bf16[192,128]{1,0:T(8,128)(2,1)S(1)} %strip.1.own_ref), channel_id=1, source_target_pairs={{1,0},{2,1},{3,2},{5,4},{6,5},{7,6},{9,8},{10,9},{11,10},{13,12},{... | collective-permute-start | bytes 147464 | tf_op jit(solution)/shard_map/ppermute | solution.py:537
  21.7 3.4 %collective-permute-done.3.right_ref = bf16[192,128]{1,0:T(8,128)(2,1)S(1)} collective-permute-done((bf16[192,128]{1,0:T(8,128)(2,1)S(1)}, bf16[192,128]{1,0:T(8,128)(2,1)S(1)}, u32[]{:S(2)}, u32[]{:S(2)}) %collective-permute-start.3) | collective-permute-done | bytes 49184 | tf_op jit(solution)/shard_map/ppermute | solution.py:537
  25.8 10.1 %forward.1 = (f32[768,1408]{1,0:T(8,128)}, f32[16,128]{1,0:T(8,128)}) custom-call(bf16[3,192,128]{2,1,0:T(8,128)(2,1)} %copy-done.1, bf16[3,192,128]{2,1,0:T(8,128)(2,1)} %copy-done, bf16[192,128]{1,0:T(8,128)(2,1)} %copy-done.2, bf16[192,128]{1,0:T(8,128)(2,1)} %copy-done.10, bf16[192,128]{1,0:T(8,128)(2,1)} %copy-done.11, f32[1,192]{1,0:T(1,128)} %bitcast.77, ...), custom_call_target="tpu_custom_call" | custom-call | flops 200000000 | bytes 12000000 | tf_op jit(solution)/shard_map/forward/pallas_call | solution.py:547
  36.0 1.3 %collective-permute-done.4.other_ref = f32[16,128]{1,0:T(8,128)S(1)} collective-permute-done((f32[16,128]{1,0:T(8,128)}, f32[16,128]{1,0:T(8,128)S(1)}, u32[]{:S(2)}, u32[]{:S(2)}) %collective-permute-start.4) | collective-permute-done | bytes 8224 | tf_op jit(solution)/shard_map/ppermute | solution.py:490
  37.3 0.7 copy-done.4
  38.7 8.0 %all-to-all-start = ((f32[16,16,128]{2,1,0:T(8,128)}), f32[16,16,128]{2,1,0:T(8,128)S(1)}, u32[]{:S(2)}, u32[]{:S(2)}) async-start(f32[16,16,128]{2,1,0:T(8,128)} %spread.1), calls=%async_computation | async-start | bytes 262144 | tf_op jit(solution)/shard_map/all_to_all | solution.py:482
  47.4 6.0 %all-to-all-done.parts_ref = f32[16,16,128]{2,1,0:T(8,128)S(1)} async-done(((f32[16,16,128]{2,1,0:T(8,128)}), f32[16,16,128]{2,1,0:T(8,128)S(1)}, u32[]{:S(2)}, u32[]{:S(2)}) %all-to-all-start) | async-done | bytes 131104 | tf_op jit(solution)/shard_map/all_to_all | solution.py:482
  54.1 18.3 %backward.1 = (bf16[8,192,128]{2,1,0:T(8,128)(2,1)}, bf16[8,192,128]{2,1,0:T(8,128)(2,1)}, f32[1280,128]{1,0:T(8,128)}, f32[1280,128]{1,0:T(8,128)}, f32[16,128]{1,0:T(8,128)}) custom-call(s32[1]{0:T(128)} %bitcast.core_ref, f32[16,16,128]{2,1,0:T(8,128)} %copy-done.7, f32[48,768]{1,0:T(8,128)} %bitcast.62, f32[48,768]{1,0:T(8,128)} %wexc_ref.1, ...), custom_call_target="tpu_custom_call" | custom-call | flops 1500000000 | bytes 16000000 | tf_op jit(solution)/shard_map/backward/pallas_call | solution.py:578
  72.4 1.7 %collective-permute-start.5 = (f32[1280,128]{1,0:T(8,128)}, f32[1280,128]{1,0:T(8,128)S(1)}, u32[]{:S(2)}, u32[]{:S(2)}) collective-permute-start(f32[1280,128]{1,0:T(8,128)} %get-tuple-element.32), channel_id=1, source_target_pairs={{0,1},{1,0},{2,3},{3,2},{4,5},{5,4},{6,7},{7,6},{8,9},{9,8},{10,11... | collective-permute-start | bytes 1966088 | tf_op jit(solution)/shard_map/ppermute | solution.py:490
  74.0 1.9 %collective-permute-done.5 = f32[1280,128]{1,0:T(8,128)S(1)} collective-permute-done((f32[1280,128]{1,0:T(8,128)}, f32[1280,128]{1,0:T(8,128)S(1)}, u32[]{:S(2)}, u32[]{:S(2)}) %collective-permute-start.5) | collective-permute-done | bytes 655392 | tf_op jit(solution)/shard_map/ppermute | solution.py:490
  76.0 1.2 add.29
  77.9 11.6 %all_to_all.15 = f16[16,80,128]{2,1,0:T(8,128)(2,1)S(1)} all-to-all(f16[16,80,128]{2,1,0:T(8,128)(2,1)S(1)} %select_convert_fusion), channel_id=1, replica_groups={{0,2,4,6,8,10,12,14,16,18,20,22,24,26,28,30},{1,3,5,7,9,11,13,15,17,19,..., dimensions={0} | all-to-all | bytes 655360 | tf_op jit(solution)/shard_map/all_to_all | solution.py:482
  89.9 7.0 %collective-permute-start.6 = (f32[96,128]{1,0:T(8,128)S(1)}, f32[96,128]{1,0:T(8,128)S(1)}, u32[]{:S(2)}, u32[]{:S(2)}) collective-permute-start(f32[96,128]{1,0:T(8,128)S(1)} %pad_maximum_fusion.5), channel_id=1, source_target_pairs={{0,128},{32,160},{64,192},{96,224},{128,0},{160,32},{192,64},{224,... | collective-permute-start | bytes 147464 | tf_op jit(solution)/shard_map/ppermute | solution.py:622
  96.9 1.5 %collective-permute-done.6 = f32[96,128]{1,0:T(8,128)S(1)} collective-permute-done((f32[96,128]{1,0:T(8,128)S(1)}, f32[96,128]{1,0:T(8,128)S(1)}, u32[]{:S(2)}, u32[]{:S(2)}) %collective-permute-start.6) | collective-permute-done | bytes 49184 | tf_op jit(solution)/shard_map/ppermute | solution.py:622
  98.4 1.5 %collective-permute-start.7 = (f32[112,128]{1,0:T(8,128)S(1)}, f32[112,128]{1,0:T(8,128)S(1)}, u32[]{:S(2)}, u32[]{:S(2)}) collective-permute-start(f32[112,128]{1,0:T(8,128)S(1)} %pad_maximum_fusion.4), channel_id=1, source_target_pairs={{0,64},{32,96},{64,0},{96,32},{128,192},{160,224},{192,128},{224,1... | collective-permute-start | bytes 172040 | tf_op jit(solution)/shard_map/ppermute | solution.py:622
  100.0 3.6 %collective-permute-done.7 = f32[112,128]{1,0:T(8,128)S(1)} collective-permute-done((f32[112,128]{1,0:T(8,128)S(1)}, f32[112,128]{1,0:T(8,128)S(1)}, u32[]{:S(2)}, u32[]{:S(2)}) %collective-permute-start.7) | collective-permute-done | bytes 57376 | tf_op jit(solution)/shard_map/ppermute | solution.py:622
  103.7 1.0 copy.19
  104.7 1.0 copy.20
  105.7 1.2 collective-permute-done.8
  107.0 0.8 broadcast_in_dim.130
  107.8 3.5 %all-to-all-start.2 = ((f16[16,80,128]{2,1,0:T(8,128)(2,1)}), f16[16,80,128]{2,1,0:T(8,128)(2,1)S(1)}, u32[]{:S(2)}, u32[]{:S(2)}) async-start(f16[16,80,128]{2,1,0:T(8,128)(2,1)} %broadcast_in_dim.130), calls=%async_computation.2 | async-start | bytes 655360 | tf_op jit(solution)/shard_map/all_to_all | solution.py:482
  111.4 7.6 %all-to-all-done.2 = f16[16,80,128]{2,1,0:T(8,128)(2,1)S(1)} async-done(((f16[16,80,128]{2,1,0:T(8,128)(2,1)}), f16[16,80,128]{2,1,0:T(8,128)(2,1)S(1)}, u32[]{:S(2)}, u32[]{:S(2)}) %all-to-all-start.2) | async-done | bytes 327712 | tf_op jit(solution)/shard_map/all_to_all | solution.py:482
  119.0 5.3 %collective-permute-start.9 = (f16[16,80,128]{2,1,0:T(8,128)(2,1)S(1)}, f16[16,80,128]{2,1,0:T(8,128)(2,1)S(1)}, u32[]{:S(2)}, u32[]{:S(2)}) collective-permute-start(f16[16,80,128]{2,1,0:T(8,128)(2,1)S(1)} %all-to-all-done.2), channel_id=1, source_target_pairs={{0,1},{1,0},{2,3},{3,2},{4,5},{5,4},{6,7},{7,6},{8,9},{9,8},{10,11... | collective-permute-start | bytes 983048 | tf_op jit(solution)/shard_map/ppermute | solution.py:490
  124.3 1.0 fusion.3
  125.3 1.0 fusion.1
  127.0 1.1 slice_bitcast_fusion
  (79 shorter events, 6.3 us)
Async XLA Ops:
  1.9 6.0 %copy-start.5 = (bf16[8,192,128]{2,1,0:T(8,128)(2,1)}, bf16[8,192,128]{2,1,0:T(8,128)(2,1)S(1)}, u32[]{:S(2)}) copy-start(bf16[8,192,128]{2,1,0:T(8,128)(2,1)S(1)} %get-tuple-element.69.x_ref) | copy-start | bytes 1179652
  1.9 6.0 %copy-start.6 = (bf16[8,192,128]{2,1,0:T(8,128)(2,1)}, bf16[8,192,128]{2,1,0:T(8,128)(2,1)S(1)}, u32[]{:S(2)}) copy-start(bf16[8,192,128]{2,1,0:T(8,128)(2,1)S(1)} %get-tuple-element.68.c_ref) | copy-start | bytes 1179652
  2.0 12.1 %collective-permute-start.1 = (bf16[3,192,128]{2,1,0:T(8,128)(2,1)S(1)}, bf16[3,192,128]{2,1,0:T(8,128)(2,1)S(1)}, u32[]{:S(2)}, u32[]{:S(2)}) collective-permute-start(bf16[3,192,128]{2,1,0:T(8,128)(2,1)S(1)} %pad_maximum_fusion.2), channel_id=1, source_target_pairs={{4,0},{8,4},{12,8},{16,12},{20,16},{24,20},{28,24},{5,1},{9,5},{13... | collective-permute-start | bytes 442376 | tf_op jit(solution)/shard_map/ppermute | solution.py:503
  3.3 10.8 %collective-permute-start = (bf16[3,192,128]{2,1,0:T(8,128)(2,1)S(1)}, bf16[3,192,128]{2,1,0:T(8,128)(2,1)S(1)}, u32[]{:S(2)}, u32[]{:S(2)}) collective-permute-start(bf16[3,192,128]{2,1,0:T(8,128)(2,1)S(1)} %pad_maximum_fusion.1), channel_id=1, source_target_pairs={{0,4},{4,8},{8,12},{12,16},{16,20},{20,24},{24,28},{1,5},{5,9},{9,... | collective-permute-start | bytes 442376 | tf_op jit(solution)/shard_map/ppermute | solution.py:502
  14.1 11.0 %copy-start = (bf16[3,192,128]{2,1,0:T(8,128)(2,1)}, bf16[3,192,128]{2,1,0:T(8,128)(2,1)S(1)}, u32[]{:S(2)}) copy-start(bf16[3,192,128]{2,1,0:T(8,128)(2,1)S(1)} %collective-permute-done.1.bot_ref) | copy-start | bytes 442372
  14.1 11.0 %copy-start.1 = (bf16[3,192,128]{2,1,0:T(8,128)(2,1)}, bf16[3,192,128]{2,1,0:T(8,128)(2,1)S(1)}, u32[]{:S(2)}) copy-start(bf16[3,192,128]{2,1,0:T(8,128)(2,1)S(1)} %collective-permute-done.top_ref) | copy-start | bytes 442372
  14.1 0.9 copy-start.3
  15.1 10.0 %copy-start.2 = (bf16[192,128]{1,0:T(8,128)(2,1)}, bf16[192,128]{1,0:T(8,128)(2,1)S(1)}, u32[]{:S(2)}) copy-start(bf16[192,128]{1,0:T(8,128)(2,1)S(1)} %strip.1.own_ref) | copy-start | bytes 147460
  15.2 6.5 %collective-permute-start.2 = (bf16[192,128]{1,0:T(8,128)(2,1)S(1)}, bf16[192,128]{1,0:T(8,128)(2,1)S(1)}, u32[]{:S(2)}, u32[]{:S(2)}) collective-permute-start(bf16[192,128]{1,0:T(8,128)(2,1)S(1)} %strip.1.own_ref), channel_id=1, source_target_pairs={{0,1},{1,2},{2,3},{4,5},{5,6},{6,7},{8,9},{9,10},{10,11},{12,13},{... | collective-permute-start | bytes 147464 | tf_op jit(solution)/shard_map/ppermute | solution.py:536
  19.7 5.4 %collective-permute-start.3 = (bf16[192,128]{1,0:T(8,128)(2,1)S(1)}, bf16[192,128]{1,0:T(8,128)(2,1)S(1)}, u32[]{:S(2)}, u32[]{:S(2)}) collective-permute-start(bf16[192,128]{1,0:T(8,128)(2,1)S(1)} %strip.1.own_ref), channel_id=1, source_target_pairs={{1,0},{2,1},{3,2},{5,4},{6,5},{7,6},{9,8},{10,9},{11,10},{13,12},{... | collective-permute-start | bytes 147464 | tf_op jit(solution)/shard_map/ppermute | solution.py:537
  21.7 3.5 %copy-start.10 = (bf16[192,128]{1,0:T(8,128)(2,1)}, bf16[192,128]{1,0:T(8,128)(2,1)S(1)}, u32[]{:S(2)}) copy-start(bf16[192,128]{1,0:T(8,128)(2,1)S(1)} %collective-permute-done.2.left_ref) | copy-start | bytes 147460
  25.1 0.6 copy-start.11
  35.9 1.5 %collective-permute-start.4 = (f32[16,128]{1,0:T(8,128)}, f32[16,128]{1,0:T(8,128)S(1)}, u32[]{:S(2)}, u32[]{:S(2)}) collective-permute-start(f32[16,128]{1,0:T(8,128)} %get-tuple-element.24.own_ref), channel_id=1, source_target_pairs={{0,1},{1,0},{2,3},{3,2},{4,5},{5,4},{6,7},{7,6},{8,9},{9,8},{10,11... | collective-permute-start | bytes 24584 | tf_op jit(solution)/shard_map/ppermute | solution.py:490
  37.3 0.7 copy-start.4
  38.7 14.7 %all-to-all-start = ((f32[16,16,128]{2,1,0:T(8,128)}), f32[16,16,128]{2,1,0:T(8,128)S(1)}, u32[]{:S(2)}, u32[]{:S(2)}) async-start(f32[16,16,128]{2,1,0:T(8,128)} %spread.1), calls=%async_computation | async-start | bytes 262144 | tf_op jit(solution)/shard_map/all_to_all | solution.py:482
  53.4 0.7 copy-start.7
  72.4 3.6 %collective-permute-start.5 = (f32[1280,128]{1,0:T(8,128)}, f32[1280,128]{1,0:T(8,128)S(1)}, u32[]{:S(2)}, u32[]{:S(2)}) collective-permute-start(f32[1280,128]{1,0:T(8,128)} %get-tuple-element.32), channel_id=1, source_target_pairs={{0,1},{1,0},{2,3},{3,2},{4,5},{5,4},{6,7},{7,6},{8,9},{9,8},{10,11... | collective-permute-start | bytes 1966088 | tf_op jit(solution)/shard_map/ppermute | solution.py:490
  77.5 12.4 %copy-start.12 = (f32[16,128]{1,0:T(8,128)S(1)}, f32[16,128]{1,0:T(8,128)}, u32[]{:S(2)}) copy-start(f32[16,128]{1,0:T(8,128)} %get-tuple-element.33) | copy-start | bytes 24580
  77.9 25.8 %copy-start.9 = (bf16[8,192,128]{2,1,0:T(8,128)(2,1)S(1)}, bf16[8,192,128]{2,1,0:T(8,128)(2,1)}, u32[]{:S(2)}) copy-start(bf16[8,192,128]{2,1,0:T(8,128)(2,1)} %get-tuple-element.29) | copy-start | bytes 1179652
  89.5 15.2 %copy-start.8 = (bf16[8,192,128]{2,1,0:T(8,128)(2,1)S(1)}, bf16[8,192,128]{2,1,0:T(8,128)(2,1)}, u32[]{:S(2)}) copy-start(bf16[8,192,128]{2,1,0:T(8,128)(2,1)} %get-tuple-element.30) | copy-start | bytes 1179652
  89.9 8.5 %collective-permute-start.6 = (f32[96,128]{1,0:T(8,128)S(1)}, f32[96,128]{1,0:T(8,128)S(1)}, u32[]{:S(2)}, u32[]{:S(2)}) collective-permute-start(f32[96,128]{1,0:T(8,128)S(1)} %pad_maximum_fusion.5), channel_id=1, source_target_pairs={{0,128},{32,160},{64,192},{96,224},{128,0},{160,32},{192,64},{224,... | collective-permute-start | bytes 147464 | tf_op jit(solution)/shard_map/ppermute | solution.py:622
  98.4 5.1 %collective-permute-start.7 = (f32[112,128]{1,0:T(8,128)S(1)}, f32[112,128]{1,0:T(8,128)S(1)}, u32[]{:S(2)}, u32[]{:S(2)}) collective-permute-start(f32[112,128]{1,0:T(8,128)S(1)} %pad_maximum_fusion.4), channel_id=1, source_target_pairs={{0,64},{32,96},{64,0},{96,32},{128,192},{160,224},{192,128},{224,1... | collective-permute-start | bytes 172040 | tf_op jit(solution)/shard_map/ppermute | solution.py:622
  103.6 3.3 %collective-permute-start.8 = (f32[144,128]{1,0:T(8,128)S(1)}, f32[144,128]{1,0:T(8,128)S(1)}, u32[]{:S(2)}, u32[]{:S(2)}) collective-permute-start(f32[144,128]{1,0:T(8,128)S(1)} %pad_maximum_fusion.3), channel_id=1, source_target_pairs={{0,32},{32,0},{64,96},{96,64},{128,160},{160,128},{192,224},{224,1... | collective-permute-start | bytes 221192 | tf_op jit(solution)/shard_map/ppermute | solution.py:622
  107.8 11.2 %all-to-all-start.2 = ((f16[16,80,128]{2,1,0:T(8,128)(2,1)}), f16[16,80,128]{2,1,0:T(8,128)(2,1)S(1)}, u32[]{:S(2)}, u32[]{:S(2)}) async-start(f16[16,80,128]{2,1,0:T(8,128)(2,1)} %broadcast_in_dim.130), calls=%async_computation.2 | async-start | bytes 655360 | tf_op jit(solution)/shard_map/all_to_all | solution.py:482
  119.0 7.3 %collective-permute-start.9 = (f16[16,80,128]{2,1,0:T(8,128)(2,1)S(1)}, f16[16,80,128]{2,1,0:T(8,128)(2,1)S(1)}, u32[]{:S(2)}, u32[]{:S(2)}) collective-permute-start(f16[16,80,128]{2,1,0:T(8,128)(2,1)S(1)} %all-to-all-done.2), channel_id=1, source_target_pairs={{0,1},{1,0},{2,3},{3,2},{4,5},{5,4},{6,7},{7,6},{8,9},{9,8},{10,11... | collective-permute-start | bytes 983048 | tf_op jit(solution)/shard_map/ppermute | solution.py:490
